TPU v7x, 32 devices: a whole 2x2x4 slice. The times are simulated.
32 devices in a mesh: dp: 16 (over z, x, core), fsdp: 2 (over y).
Axes of the slice: x: 2, y: 2, z: 4, core: 2. Of those that a mesh axis runs over, the one named last changes fastest.
Arguments:
- grads: bfloat16 [16, 2, 8192, 1024], P('dp', None, 'fsdp'), may hold values from -1.1953125 to 1.1953125
- raw_proj: float32 [2, 1024, 512], P(None, 'fsdp'), may hold values from -6 to 6
- bucket_owner: int32 [2, 512], P(None, 'fsdp'), may hold values from 0 to 15, as said below
- first_moment: float32 [2, 2, 512, 16, 512], P(None, 'fsdp', 'dp'), may hold values from -0.6 to 0.6
- second_moment: float32 [2, 2, 512, 16, 512], P(None, 'fsdp', 'dp'), may hold values from 0.01 to 0.05
Outputs:
- weight_delta: bfloat16 [2, 8192, 1024], P(None, 'fsdp')
- first_out: float32 [2, 2, 512, 16, 512], P(None, 'fsdp', 'dp')
- second_out: float32 [2, 2, 512, 16, 512], P(None, 'fsdp', 'dp')
Inputs may be any that keep to these rules, and one draw needn't show every extreme that they name: `bucket_owner`: within each matrix and each block of 256 buckets of one fsdp index, no owner holds more than 32 buckets, and one owner holds exactly 32.
All inputs are finite; a program needn't handle non-finite values.
Results may differ from a plain program's by a relative error of at most 0.0062.
Values may be sent and summed in bfloat16 or wider, within the bound.
No kernel may reach another device: no remote copies, remote signals or barrier semaphores. Data moves between devices by JAX's collectives and lax.ppermute only.
A program may use at most 128 MiB of HBM per device.

v0:
```python
import functools

import jax
import jax.numpy as jnp
from jax import lax
from jax.experimental import pallas as pl
from jax.experimental.pallas import tpu as pltpu
from jax.sharding import PartitionSpec as P


PANEL = 8
BLOCK = 128
WIDE = 256
QUAD = 4
F32 = jnp.float32
BF16 = jnp.bfloat16


def dot_f32(a, b, dims):
    return lax.dot_general(
        a, b, (dims, ((), ())), precision=lax.Precision.HIGHEST, preferred_element_type=F32
    )


def dot_bf16(a, b, dims):
    return lax.dot_general(a, b, (dims, ((), ())), preferred_element_type=F32)


def halves(x):
    high = x.astype(BF16)
    return high, (x - high.astype(F32)).astype(BF16)


def dot_split(a, b, dims):
    (a_high, a_low), (b_high, b_low) = halves(a), halves(b)
    return (
        dot_bf16(a_low, b_high, dims)
        + dot_bf16(a_high, b_low, dims)
        + dot_bf16(a_high, b_high, dims)
    )


def eliminate_panel(block_ref, inverse_ref, scale_ref, m, start):
    rows = block_ref[m, pl.ds(start, PANEL), :]
    inv_rows = inverse_ref[m, pl.ds(start, PANEL), :]
    sub = lax.broadcasted_iota(jnp.int32, rows.shape, 0)
    cols = [
        jnp.take_along_axis(
            rows, jnp.full(rows.shape, start + j, jnp.int32), axis=1, mode="promise_in_bounds"
        )
        for j in range(PANEL)
    ]
    recip = jnp.zeros_like(rows)
    for j in range(PANEL):
        r = 1.0 / jnp.broadcast_to(cols[j][j : j + 1, :], rows.shape)
        recip = jnp.where(sub == j, r, recip)
        if j + 1 < PANEL:
            mult = jnp.where(sub > j, cols[j] * r, 0.0)
            for k in range(j + 1, PANEL):
                cols[k] = cols[k] - mult * jnp.broadcast_to(cols[k][j : j + 1, :], rows.shape)
            rows = rows - mult * jnp.broadcast_to(rows[j : j + 1, :], rows.shape)
            inv_rows = inv_rows - mult * jnp.broadcast_to(inv_rows[j : j + 1, :], rows.shape)
    inverse_ref[m, pl.ds(start, PANEL), :] = inv_rows
    scale_ref[m, pl.ds(start, PANEL), :] = recip
    return rows, inv_rows, recip


def eliminate_block(block_ref, inverse_ref, scale_ref, mats, size):
    row_id = lax.broadcasted_iota(jnp.int32, (size, size), 0)
    lane_id = lax.broadcasted_iota(jnp.int32, (size, size), 1)
    for m in range(mats):
        inverse_ref[m] = jnp.where(row_id == lane_id, 1.0, 0.0)

    def panel(p, _):
        start = pl.multiple_of(p * PANEL, PANEL)
        done = [eliminate_panel(block_ref, inverse_ref, scale_ref, m, start) for m in range(mats)]
        below = row_id >= start + PANEL
        for m in range(mats):
            rows, inv_rows, recip = done[m]
            both = jnp.concatenate([rows, inv_rows], axis=1)
            change = dot_f32(rows * recip, both, ((0,), (0,)))
            block_ref[m] = block_ref[m] - jnp.where(below, change[:, :size], 0.0)
            inverse_ref[m] = inverse_ref[m] - jnp.where(below, change[:, size:], 0.0)
        return 0

    lax.fori_loop(0, size // PANEL, panel, 0)


def basis_kernel(offsets, *refs, pieces):
    own_ref = refs[0]
    piece_refs = refs[1 : 1 + pieces]
    basis_ref = refs[1 + pieces]
    raw, gram, low, inv, block, binv, scale = refs[2 + pieces :]
    mats, _, rank = raw.shape
    n = rank // BLOCK

    def sl(i):
        return slice(i * BLOCK, (i + 1) * BLOCK)

    for i, ref in enumerate((own_ref, *piece_refs)):
        at = pl.multiple_of(offsets[i], 8)
        raw[:, pl.ds(at, ref.shape[1]), :] = ref[...]

    def grams(m, _):
        for j in range(0, rank, WIDE):
            gram[m, j:, j : j + WIDE] = dot_f32(raw[m, :, j:], raw[m, :, j : j + WIDE], ((0,), (0,)))
        return 0

    lax.fori_loop(0, mats, grams, 0)
    for b in range(n):
        below = (b + 1) * BLOCK
        for m in range(mats):
            block[m] = gram[m, sl(b), sl(b)]
        eliminate_block(block, binv, scale, mats, BLOCK)
        for m in range(mats):
            d_inv = binv[m] * jnp.sqrt(scale[m])
            inv[m, sl(b), sl(b)] = d_inv
            if b > 0:
                acc = dot_f32(
                    low[m, sl(b), : b * BLOCK], inv[m, : b * BLOCK, : b * BLOCK], ((1,), (0,))
                )
                inv[m, sl(b), : b * BLOCK] = -dot_f32(d_inv, acc, ((1,), (0,)))
            if b + 1 < n:
                low[m, below:, sl(b)] = dot_f32(gram[m, below:, sl(b)], d_inv, ((1,), (1,)))
                inv[m, sl(b), below:] = jnp.zeros((BLOCK, rank - below), F32)
                for j in range(b + 1, n):
                    gram[m, j * BLOCK :, sl(j)] = gram[m, j * BLOCK :, sl(j)] - dot_f32(
                        low[m, j * BLOCK :, sl(b)], low[m, sl(j), sl(b)], ((1,), (1,))
                    )

    def bases(m, _):
        for j in range(0, rank, WIDE):
            end = j + WIDE
            basis_ref[m, :, j:end] = dot_split(
                raw[m, :, :end], inv[m, j:end, :end], ((1,), (1,))
            ).astype(BF16)
        return 0

    lax.fori_loop(0, mats, bases, 0)


def orthonormal_basis(own, pieces, offsets, feats):
    mats, _, rank = own.shape
    vmem = pl.BlockSpec(memory_space=pltpu.VMEM)
    smem = pl.BlockSpec(memory_space=pltpu.SMEM)
    return pl.pallas_call(
        functools.partial(basis_kernel, pieces=len(pieces)),
        out_shape=jax.ShapeDtypeStruct((mats, feats, rank), BF16),
        in_specs=[smem] + [vmem] * (1 + len(pieces)),
        out_specs=vmem,
        scratch_shapes=[pltpu.VMEM((mats, feats, rank), F32)]
        + [pltpu.VMEM((mats, rank, rank), F32)] * 3
        + [pltpu.VMEM((mats, BLOCK, BLOCK), F32)] * 3,
        cost_estimate=pl.CostEstimate(
            flops=90_000_000_000, bytes_accessed=6 * mats * feats * rank, transcendentals=0
        ),
        name="basis",
    )(offsets, own, *pieces)


def collect_kernel(places, *refs):
    m = pl.program_id(1)
    owner_refs, group_refs = refs[:QUAD], refs[QUAD:]
    capacity, bucket_rows = owner_refs[0].shape[2], owner_refs[0].shape[3]
    unit_rows = group_refs[0].shape[2]
    for ref in group_refs:
        ref[...] = jnp.zeros(ref.shape, BF16)
    for i, owner_ref in enumerate(owner_refs):

        def pick(s, _):
            place = places[i, m, s]
            at = pl.multiple_of(lax.rem(jnp.maximum(place, 0), unit_rows), bucket_rows)
            for k, ref in enumerate(group_refs):

                @pl.when(jnp.logical_and(place >= k * unit_rows, place < (k + 1) * unit_rows))
                def _():
                    ref[0, 0, pl.ds(at, bucket_rows), :] = owner_ref[0, 0, s]

            return 0

        lax.fori_loop(0, capacity, pick, 0)


def collect_moments(owners, places, depth, unit_rows):
    kinds, mats, capacity, bucket_rows, rank = owners[0].shape
    slots = pl.BlockSpec((1, 1, capacity, bucket_rows, rank), lambda a, m, p: (a, m, 0, 0, 0))
    group = pl.BlockSpec((1, 1, unit_rows, rank), lambda a, m, p: (a, m, 0, 0))
    return pl.pallas_call(
        collect_kernel,
        out_shape=(jax.ShapeDtypeStruct((kinds, mats, unit_rows, rank), BF16),) * depth,
        grid_spec=pltpu.PrefetchScalarGridSpec(
            num_scalar_prefetch=1,
            grid=(kinds, mats),
            in_specs=[slots] * QUAD,
            out_specs=(group,) * depth,
        ),
        cost_estimate=pl.CostEstimate(
            flops=0, bytes_accessed=4 * QUAD * owners[0].size, transcendentals=0
        ),
        name="collect",
    )(places, *owners)


def project_kernel(quads, group, grads_ref, basis_ref, other_ref, own_ref, result):
    unit_rows = other_ref.shape[2]
    result[...] = dot_bf16(grads_ref[0, 0], basis_ref[0], ((1,), (0,))).astype(BF16)
    for i, ref in ((0, other_ref), (1, other_ref), (2, own_ref), (3, own_ref)):
        at = pl.multiple_of(quads[i] * unit_rows, unit_rows)
        ref[i % 2, 0] = result[pl.ds(at, unit_rows), :]


def project(grads, basis, quads, group, unit_rows):
    _, mats, _, feats = grads.shape
    rank = basis.shape[2]
    rows = QUAD * unit_rows
    out = jax.ShapeDtypeStruct((2, mats, unit_rows, rank), BF16)
    out_spec = pl.BlockSpec((2, 1, unit_rows, rank), lambda m, q, g: (0, m, 0, 0))
    return pl.pallas_call(
        project_kernel,
        out_shape=(out, out),
        grid_spec=pltpu.PrefetchScalarGridSpec(
            num_scalar_prefetch=2,
            grid=(mats,),
            in_specs=[
                pl.BlockSpec((1, 1, rows, feats), lambda m, q, g: (0, m, g[0], 0)),
                pl.BlockSpec((1, feats, rank), lambda m, q, g: (m, 0, 0)),
            ],
            out_specs=(out_spec, out_spec),
            scratch_shapes=[pltpu.VMEM((rows, rank), BF16)],
        ),
        cost_estimate=pl.CostEstimate(
            flops=2 * mats * rows * feats * rank,
            bytes_accessed=2 * mats * rows * (feats + rank),
            transcendentals=0,
        ),
        name="project",
    )(quads, group, grads, basis)


def expand_kernel(quads, group, *refs):
    parts, basis_ref = refs[:QUAD], refs[QUAD]
    out_ref, joined = refs[-2:]
    unit_rows = parts[0].shape[1]
    for i, ref in enumerate(parts):
        at = pl.multiple_of(quads[i] * unit_rows, unit_rows)
        joined[pl.ds(at, unit_rows), :] = ref[0]
    out_ref[0] = dot_bf16(joined[...], basis_ref[0], ((1,), (1,))).astype(BF16)


def expand(parts, basis, quads, group, target, local_rows):
    mats, unit_rows, rank = parts[0].shape
    feats = basis.shape[1]
    rows = QUAD * unit_rows
    part = pl.BlockSpec((1, unit_rows, rank), lambda m, q, g: (m, 0, 0))
    in_specs = [part] * QUAD + [pl.BlockSpec((1, feats, rank), lambda m, q, g: (m, 0, 0))]
    args = [quads, group, *parts, basis]
    aliases = {}
    if target is not None:
        in_specs.append(pl.BlockSpec(memory_space=pl.ANY))
        aliases = {len(args): 0}
        args.append(target)
    return pl.pallas_call(
        expand_kernel,
        out_shape=jax.ShapeDtypeStruct((mats, local_rows, feats), BF16),
        grid_spec=pltpu.PrefetchScalarGridSpec(
            num_scalar_prefetch=2,
            grid=(mats,),
            in_specs=in_specs,
            out_specs=pl.BlockSpec((1, rows, feats), lambda m, q, g: (m, g[0], 0)),
            scratch_shapes=[pltpu.VMEM((rows, rank), BF16)],
        ),
        input_output_aliases=aliases,
        cost_estimate=pl.CostEstimate(
            flops=2 * mats * rows * feats * rank,
            bytes_accessed=2 * mats * rows * (feats + rank),
            transcendentals=0,
        ),
        name="expand",
    )(*args)


def new_moments(first, second, grad_rows):
    new_first = 0.9 * first + 0.1 * grad_rows
    new_second = 0.999 * second + 0.001 * grad_rows * grad_rows
    return new_first, new_second


def settle_kernel(piece_of, row_of, held, *refs, pieces):
    piece_refs = refs[:pieces]
    first_ref, second_ref, first_out, second_out, rows, sem = refs[pieces:]
    m = pl.program_id(0)
    capacity, bucket_rows = rows.shape[0], rows.shape[1]

    def fetch(s, _):
        piece = piece_of[m, s]
        at = pl.multiple_of(row_of[m, s], bucket_rows)
        for i, ref in enumerate(piece_refs):

            @pl.when(piece == i)
            def _():
                pltpu.make_async_copy(ref.at[m, pl.ds(at, bucket_rows), :], rows.at[s], sem).start()

        return 0

    lax.fori_loop(0, capacity, fetch, 0)
    pltpu.make_async_copy(rows, rows, sem).wait()

    def settle(s, _):
        first, second = first_ref[0, 0, s], second_ref[0, 0, s]
        new_first, new_second = new_moments(first, second, rows[s].astype(F32))
        keep = held[m, s] > 0
        first_out[0, 0, s] = jnp.where(keep, new_first, first)
        second_out[0, 0, s] = jnp.where(keep, new_second, second)
        return 0

    lax.fori_loop(0, capacity, settle, 0)


def settle_moments(first, second, pieces, piece_of, row_of, held):
    mats, _, capacity, bucket_rows, rank = first.shape
    spec = pl.BlockSpec((1, 1, capacity, bucket_rows, rank), lambda m, *_: (m, 0, 0, 0, 0))
    return pl.pallas_call(
        functools.partial(settle_kernel, pieces=len(pieces)),
        out_shape=(
            jax.ShapeDtypeStruct(first.shape, F32),
            jax.ShapeDtypeStruct(second.shape, F32),
        ),
        grid_spec=pltpu.PrefetchScalarGridSpec(
            num_scalar_prefetch=3,
            grid=(mats,),
            in_specs=[pl.BlockSpec(memory_space=pl.ANY)] * len(pieces) + [spec, spec],
            out_specs=(spec, spec),
            scratch_shapes=[
                pltpu.VMEM((capacity, bucket_rows, rank), BF16),
                pltpu.SemaphoreType.DMA,
            ],
        ),
        cost_estimate=pl.CostEstimate(
            flops=8 * first.size, bytes_accessed=18 * first.size, transcendentals=0
        ),
        name="settle",
    )(piece_of, row_of, held, *pieces, first, second)


def adam_update(first, second, grad_rows):
    new_first, new_second = new_moments(first, second, grad_rows)
    scaled = (
        6.0 * (new_first / (1.0 - 0.9**10)) / (jnp.sqrt(new_second / (1.0 - 0.999**10)) + 1e-08)
    )
    return scaled.astype(BF16)


def shards(grads, raw_proj, bucket_owner, first_moment, second_moment):
    local_rows = grads.shape[2]
    local_feats = raw_proj.shape[1]
    buckets = bucket_owner.shape[1]
    capacity = first_moment.shape[2]
    bucket_rows = local_rows // buckets
    replicas = lax.axis_size("dp")
    splits = lax.axis_size("fsdp")
    depth = replicas // QUAD
    unit_rows = local_rows // replicas
    unit_buckets = buckets // replicas
    me = lax.axis_index("dp")
    my_z, my_quad = me // QUAD, me % QUAD

    def permute(v, target):
        return lax.ppermute(v, "dp", [(i, target(i)) for i in range(replicas)])

    def to_core(v):
        return permute(v, lambda i: i ^ 1)

    def to_x(v):
        return permute(v, lambda i: i ^ 2)

    def to_z(v):
        return permute(v, lambda i: (i + QUAD) % replicas)

    quarter = local_feats // QUAD
    part = lax.dynamic_slice_in_dim(raw_proj, my_quad * quarter, quarter, 1)
    my_f = lax.axis_index("fsdp")
    pieces, offsets = [], [my_f * local_feats]
    for shift in range(1, splits):
        fetched = lax.ppermute(part, "fsdp", [(i, (i + shift) % splits) for i in range(splits)])
        across = to_x(fetched)
        base = ((my_f + splits - shift) % splits) * local_feats
        for piece, flip in ((fetched, 0), (across, 2), (to_core(fetched), 1), (to_core(across), 3)):
            pieces.append(piece)
            offsets.append(base + (my_quad ^ flip) * quarter)
    offsets = jnp.stack(offsets).astype(jnp.int32)

    same = bucket_owner[:, :, None] == bucket_owner[:, None, :]
    order = jnp.arange(buckets, dtype=jnp.int32)
    earlier = order[None, :] < order[:, None]
    ranks = jnp.sum(jnp.logical_and(same, earlier).astype(jnp.int32), axis=-1)
    owner_ids = jnp.stack([me ^ flip for flip in (0, 2, 1, 3)])
    local_slot = jnp.where(bucket_owner[None] == owner_ids[:, None, None], ranks[None], -1)
    slot_ids = jnp.arange(capacity, dtype=jnp.int32)
    matches = local_slot[:, :, None, :] == slot_ids[None, None, :, None]
    quad_occupied = jnp.any(matches, axis=3)
    quad_buckets = jnp.sum(jnp.where(matches, order[None, None, None, :], 0), axis=3)
    occupied, bucket_of = quad_occupied[0], quad_buckets[0]
    quad_units = quad_buckets // unit_buckets
    steps = (my_z + depth - 1 - quad_units // QUAD) % depth
    places = steps * unit_rows + (quad_buckets % unit_buckets) * bucket_rows
    wanted = jnp.logical_and(quad_occupied, quad_units % QUAD == my_quad)
    places = jnp.where(wanted, places, -1).astype(jnp.int32)

    slots = jnp.stack([first_moment[:, 0], second_moment[:, 0]]).astype(BF16)
    slots, pieces = lax.optimization_barrier((slots, pieces))
    slots_across = to_x(slots)
    slots_core = to_core(slots)

    basis = orthonormal_basis(raw_proj, pieces, offsets, splits * local_feats)

    owners = (slots, slots_across, slots_core, to_core(slots_across))
    moment_groups = collect_moments(owners, places, depth, unit_rows)
    unit_moments = moment_groups[0]
    for k in range(1, depth):
        unit_moments = to_z(unit_moments) + moment_groups[k]

    send_quads = jnp.stack([my_quad ^ flip for flip in (3, 1, 2, 0)]).astype(jnp.int32)
    held = None
    for k in range(1, depth + 1):
        group = ((my_z + depth - k) % depth).astype(jnp.int32)[None]
        other, own = project(grads, basis, send_quads, group, unit_rows)
        arrived = to_core(other)
        send = (own[0].astype(F32) + arrived[0].astype(F32)).astype(BF16)
        crossed = to_x(send)
        total = own[1].astype(F32) + arrived[1].astype(F32) + crossed.astype(F32)
        if held is not None:
            total = total + to_z(held).astype(F32)
        held = total.astype(BF16)
    held, grad_rows = lax.optimization_barrier((held, total))

    def ring(unit):
        groups = []
        for k in range(depth):
            across = to_x(unit)
            core = to_core(unit)
            groups.append((unit, across, core, to_core(across)))
            if k + 1 < depth:
                unit = to_z(unit)
        return groups

    grad_groups = ring(held)
    update = adam_update(unit_moments[0].astype(F32), unit_moments[1].astype(F32), grad_rows)
    update_groups = ring(update)

    part_quads = jnp.stack([my_quad ^ flip for flip in (0, 2, 1, 3)]).astype(jnp.int32)
    weight_delta = None
    for k, parts in enumerate(update_groups):
        group = ((my_z + depth - k) % depth).astype(jnp.int32)[None]
        weight_delta = expand(parts, basis, part_quads, group, weight_delta, local_rows)

    unit = bucket_of // unit_buckets
    back = (my_z + depth - unit // QUAD) % depth
    flip = (unit % QUAD) ^ my_quad
    piece_of = back * QUAD + (flip % 2) * 2 + flip // 2
    row_of = (bucket_of % unit_buckets) * bucket_rows
    first_out, second_out = settle_moments(
        first_moment,
        second_moment,
        [p for parts in grad_groups for p in parts],
        piece_of.astype(jnp.int32),
        row_of.astype(jnp.int32),
        occupied.astype(jnp.int32),
    )
    return weight_delta, first_out, second_out


def solution(mesh):
    return jax.shard_map(
        shards,
        mesh=mesh,
        in_specs=(
            P("dp", None, "fsdp", None),
            P(None, "fsdp", None),
            P(None, "fsdp"),
            P(None, "fsdp", "dp", None, None),
            P(None, "fsdp", "dp", None, None),
        ),
        out_specs=(
            P(None, "fsdp", None),
            P(None, "fsdp", "dp", None, None),
            P(None, "fsdp", "dp", None, None),
        ),
        check_vma=False,
    )
```

profile of v0, /device:TPU:0, one launch (start us, length us, event | category | flops | bytes accessed | tf_op | source)
XLA Modules:
  0.0 378.0 jit_solution(3945377104758179980)
XLA Ops:
  0.6 1.1 constant_dynamic-slice_fusion
  1.7 3.1 collective-permute-start
  4.8 11.9 %collective-permute-done.refs_1_ = f32[2,128,512]{2,1,0:T(8,128)S(1)} collective-permute-done((f32[2,128,512]{2,1,0:T(8,128)S(1)}, f32[2,128,512]{2,1,0:T(8,128)S(1)}, u32[]{:S(2)}, u32[]{:S(2)}) %collective-permute-start) | collective-permute-done | bytes 524320 | tf_op jit(solution)/shard_map/ppermute | solution.py:384
  16.7 1.7 collective-permute-start.1
  19.7 10.2 %collective-permute-done.1.refs_2_ = f32[2,128,512]{2,1,0:T(8,128)S(1)} collective-permute-done((f32[2,128,512]{2,1,0:T(8,128)S(1)}, f32[2,128,512]{2,1,0:T(8,128)S(1)}, u32[]{:S(2)}, u32[]{:S(2)}) %collective-permute-start.1) | collective-permute-done | bytes 524320 | tf_op jit(solution)/shard_map/ppermute | solution.py:368
  29.8 2.7 fusion.5
  32.8 0.8 copy-done.36
  33.6 0.8 copy-done.37
  34.5 1.4 collective-permute-start.4
  35.9 55.3 %basis.1.basis_ref.refs_4_ = bf16[2,1024,512]{2,1,0:T(8,128)(2,1)} custom-call(s32[5]{0:T(128)} %stack.76.offsets, f32[2,512,512]{2,1,0:T(8,128)} %refs_0_.1, f32[2,128,512]{2,1,0:T(8,128)} %copy-done.34, f32[2,128,512]{2,1,0:T(8,128)} %copy-done.35, f32[2,128,512]{2,1,0:T(8,128)} %copy-done.36, f32[2,128,512]{2,1,0:T(8,128)} %copy-done.37), custom_call_target="tpu_custom_call" | custom-call | flops 89999998976 | bytes 6291456 | tf_op jit(solution)/shard_map/basis/pallas_call | solution.py:146
  91.2 6.3 %project.7 = (bf16[2,2,256,512]{3,2,1,0:T(8,128)(2,1)}, bf16[2,2,256,512]{3,2,1,0:T(8,128)(2,1)}) custom-call(s32[4]{0:T(128)} %pad_add_fusion.2.quads, s32[1]{0:T(128)} %bitcast.27.group, bf16[1,2,4096,1024]{3,2,1,0:T(8,128)(2,1)} %grads_ref.7, bf16[2,1024,512]{2,1,0:T(8,128)(2,1)} %basis.1.basis_ref.refs_4_), custom_call_target="tpu_custom_call" | custom-call | flops 2147483648 | bytes 6291456 | tf_op jit(solution)/shard_map/project/pallas_call | solution.py:218
  98.5 6.3 %project.6 = (bf16[2,2,256,512]{3,2,1,0:T(8,128)(2,1)}, bf16[2,2,256,512]{3,2,1,0:T(8,128)(2,1)}) custom-call(s32[4]{0:T(128)} %pad_add_fusion.2.quads, s32[1]{0:T(128)} %bitcast.24.group, bf16[1,2,4096,1024]{3,2,1,0:T(8,128)(2,1)} %grads_ref.7, bf16[2,1024,512]{2,1,0:T(8,128)(2,1)} %basis.1.basis_ref.refs_4_), custom_call_target="tpu_custom_call" | custom-call | flops 2147483648 | bytes 6291456 | tf_op jit(solution)/shard_map/project/pallas_call | solution.py:218
  105.6 2.0 fusion.18
  108.2 6.2 %project.5 = (bf16[2,2,256,512]{3,2,1,0:T(8,128)(2,1)}, bf16[2,2,256,512]{3,2,1,0:T(8,128)(2,1)}) custom-call(s32[4]{0:T(128)} %pad_add_fusion.2.quads, s32[1]{0:T(128)} %bitcast.4.group, bf16[1,2,4096,1024]{3,2,1,0:T(8,128)(2,1)} %grads_ref.7, bf16[2,1024,512]{2,1,0:T(8,128)(2,1)} %basis.1.basis_ref.refs_4_), custom_call_target="tpu_custom_call" | custom-call | flops 2147483648 | bytes 6291456 | tf_op jit(solution)/shard_map/project/pallas_call | solution.py:218
  114.3 6.3 %project.4 = (bf16[2,2,256,512]{3,2,1,0:T(8,128)(2,1)}, bf16[2,2,256,512]{3,2,1,0:T(8,128)(2,1)}) custom-call(s32[4]{0:T(128)} %pad_add_fusion.2.quads, s32[1]{0:T(128)} %bitcast.14.group, bf16[1,2,4096,1024]{3,2,1,0:T(8,128)(2,1)} %grads_ref.7, bf16[2,1024,512]{2,1,0:T(8,128)(2,1)} %basis.1.basis_ref.refs_4_), custom_call_target="tpu_custom_call" | custom-call | flops 2147483648 | bytes 6291456 | tf_op jit(solution)/shard_map/project/pallas_call | solution.py:218
  121.2 2.0 fusion.17
  123.1 1.5 collective-permute-start.15
  124.6 2.3 fusion.7
  127.0 1.6 collective-permute-start.18
  129.4 22.0 %collect.1 = (bf16[2,2,256,512]{3,2,1,0:T(8,128)(2,1)}, bf16[2,2,256,512]{3,2,1,0:T(8,128)(2,1)}, bf16[2,2,256,512]{3,2,1,0:T(8,128)(2,1)}, bf16[2,2,256,512]{3,2,1,0:T(8,128)(2,1)}) custom-call(s32[4,2,32]{2,1,0:T(2,128)} %and_select_fusion.3.places, bf16[2,2,32,16,512]{4,3,2,1,0:T(8,128)(2,1)} %copy-done, ...), custom_call_target="tpu_custom_call" | custom-call | bytes 16777216 | tf_op jit(solution)/shard_map/collect/pallas_call | solution.py:188
  151.3 1.6 collective-permute-start.7
  152.9 1.3 fusion.16
  154.8 1.6 fusion.9
  156.4 1.6 collective-permute-start.19
  158.1 1.2 fusion.15
  159.2 1.6 collective-permute-start.11
  160.8 18.6 %collective-permute-done.7 = bf16[2,2,256,512]{3,2,1,0:T(8,128)(2,1)S(1)} collective-permute-done((bf16[2,2,256,512]{3,2,1,0:T(8,128)(2,1)}, bf16[2,2,256,512]{3,2,1,0:T(8,128)(2,1)S(1)}, u32[]{:S(2)}, u32[]{:S(2)}) %collective-permute-start.7) | collective-permute-done | bytes 1048608 | tf_op jit(solution)/shard_map/ppermute | solution.py:368
  179.8 10.8 %collective-permute-done.19 = bf16[2,256,512]{2,1,0:T(8,128)(2,1)S(1)} collective-permute-done((bf16[2,256,512]{2,1,0:T(8,128)(2,1)S(1)}, bf16[2,256,512]{2,1,0:T(8,128)(2,1)S(1)}, u32[]{:S(2)}, u32[]{:S(2)}) %collective-permute-start.19) | collective-permute-done | bytes 524320 | tf_op jit(solution)/shard_map/ppermute | solution.py:368
  190.6 1.3 fusion.11
  192.0 30.8 %collective-permute-done.20 = bf16[2,256,512]{2,1,0:T(8,128)(2,1)S(1)} collective-permute-done((bf16[2,256,512]{2,1,0:T(8,128)(2,1)S(1)}, bf16[2,256,512]{2,1,0:T(8,128)(2,1)S(1)}, u32[]{:S(2)}, u32[]{:S(2)}) %collective-permute-start.20) | collective-permute-done | bytes 524320 | tf_op jit(solution)/shard_map/ppermute | solution.py:368
  222.8 1.3 fusion.33
  224.6 1.4 collective-permute-start.9
  226.5 14.3 %collective-permute-done.39.refs_4_ = bf16[2,256,512]{2,1,0:T(8,128)(2,1)S(1)} collective-permute-done((bf16[2,256,512]{2,1,0:T(8,128)(2,1)S(1)}, bf16[2,256,512]{2,1,0:T(8,128)(2,1)S(1)}, u32[]{:S(2)}, u32[]{:S(2)}) %collective-permute-start.39) | collective-permute-done | bytes 524320 | tf_op jit(solution)/shard_map/ppermute | solution.py:368
  241.6 30.6 %collective-permute-done.43.refs_8_ = bf16[2,256,512]{2,1,0:T(8,128)(2,1)S(1)} collective-permute-done((bf16[2,256,512]{2,1,0:T(8,128)(2,1)S(1)}, bf16[2,256,512]{2,1,0:T(8,128)(2,1)S(1)}, u32[]{:S(2)}, u32[]{:S(2)}) %collective-permute-start.43) | collective-permute-done | bytes 524320 | tf_op jit(solution)/shard_map/ppermute | solution.py:368
  274.7 14.1 %collective-permute-done.47.refs_12_ = bf16[2,256,512]{2,1,0:T(8,128)(2,1)S(1)} collective-permute-done((bf16[2,256,512]{2,1,0:T(8,128)(2,1)S(1)}, bf16[2,256,512]{2,1,0:T(8,128)(2,1)S(1)}, u32[]{:S(2)}, u32[]{:S(2)}) %collective-permute-start.47) | collective-permute-done | bytes 524320 | tf_op jit(solution)/shard_map/ppermute | solution.py:368
  289.4 10.2 %collective-permute-done.21.refs_0_ = bf16[2,256,512]{2,1,0:T(8,128)(2,1)S(1)} collective-permute-done((bf16[2,256,512]{2,1,0:T(8,128)(2,1)S(1)}, bf16[2,256,512]{2,1,0:T(8,128)(2,1)S(1)}, u32[]{:S(2)}, u32[]{:S(2)}) %collective-permute-start.21) | collective-permute-done | bytes 524320 | tf_op jit(solution)/shard_map/ppermute | solution.py:368
  300.2 1.6 collective-permute-done.48.refs_13_
  302.2 12.5 %collective-permute-done.22.refs_0_ = bf16[2,256,512]{2,1,0:T(8,128)(2,1)S(1)} collective-permute-done((bf16[2,256,512]{2,1,0:T(8,128)(2,1)S(1)}, bf16[2,256,512]{2,1,0:T(8,128)(2,1)S(1)}, u32[]{:S(2)}, u32[]{:S(2)}) %collective-permute-start.22) | collective-permute-done | bytes 524320 | tf_op jit(solution)/shard_map/ppermute | solution.py:368
  315.8 0.8 copy-done.31
  316.6 1.3 collective-permute-start.27
  318.7 10.5 %collective-permute-done.23.refs_0_ = bf16[2,256,512]{2,1,0:T(8,128)(2,1)S(1)} collective-permute-done((bf16[2,256,512]{2,1,0:T(8,128)(2,1)S(1)}, bf16[2,256,512]{2,1,0:T(8,128)(2,1)S(1)}, u32[]{:S(2)}, u32[]{:S(2)}) %collective-permute-start.23) | collective-permute-done | bytes 524320 | tf_op jit(solution)/shard_map/ppermute | solution.py:368
  330.8 10.2 %collective-permute-done.27.refs_1_ = bf16[2,256,512]{2,1,0:T(8,128)(2,1)S(1)} collective-permute-done((bf16[2,256,512]{2,1,0:T(8,128)(2,1)S(1)}, bf16[2,256,512]{2,1,0:T(8,128)(2,1)S(1)}, u32[]{:S(2)}, u32[]{:S(2)}) %collective-permute-start.27) | collective-permute-done | bytes 524320 | tf_op jit(solution)/shard_map/ppermute | solution.py:368
  342.2 8.2 %settle.1 = (f32[2,1,32,16,512]{4,3,2,1,0:T(8,128)}, f32[2,1,32,16,512]{4,3,2,1,0:T(8,128)}) custom-call(s32[2,32]{1,0:T(2,128)} %get-tuple-element.48.piece_of, s32[2,32]{1,0:T(2,128)} %get-tuple-element.47.row_of, s32[2,32]{1,0:T(2,128)} %fusion.30.held, bf16[2,256,512]{2,1,0:T(8,128)(2,1)} %copy-done.1, bf16[2,256,512]{2,1,0:T(8,128)(2,1)} %copy-done.18, ...), custom_call_target="tpu_custom_call" | custom-call | flops 4194304 | bytes 9437184 | tf_op jit(solution)/shard_map/settle/pallas_call | solution.py:322
  351.7 6.2 %expand.4.refs_5_ = bf16[2,4096,1024]{2,1,0:T(8,128)(2,1)} custom-call(s32[4]{0:T(128)} %pad_add_fusion.quads, s32[1]{0:T(128)} %bitcast.31.group, bf16[2,256,512]{2,1,0:T(8,128)(2,1)} %copy-done.2, bf16[2,256,512]{2,1,0:T(8,128)(2,1)} %collective-permute-done.33.refs_1_, bf16[2,256,512]{2,1,0:T(8,128)(2,1)} %copy-done.32, ...), custom_call_target="tpu_custom_call" | custom-call | flops 2147483648 | bytes 6291456 | tf_op jit(solution)/shard_map/expand/pallas_call | solution.py:262
  357.8 6.2 %expand.5.refs_5_ = bf16[2,4096,1024]{2,1,0:T(8,128)(2,1)} custom-call(s32[4]{0:T(128)} %pad_add_fusion.quads, s32[1]{0:T(128)} %bitcast.27.group, bf16[2,256,512]{2,1,0:T(8,128)(2,1)} %copy-done.10, bf16[2,256,512]{2,1,0:T(8,128)(2,1)} %collective-permute-done.30.refs_1_, ...), custom_call_target="tpu_custom_call", output_to_operand_aliasing={{}: (7, {})} | custom-call | flops 2147483648 | bytes 6291456 | tf_op jit(solution)/shard_map/expand/pallas_call | solution.py:262
  364.0 6.2 %expand.6.refs_5_ = bf16[2,4096,1024]{2,1,0:T(8,128)(2,1)} custom-call(s32[4]{0:T(128)} %pad_add_fusion.quads, s32[1]{0:T(128)} %bitcast.24.group, bf16[2,256,512]{2,1,0:T(8,128)(2,1)} %copy-done.11, bf16[2,256,512]{2,1,0:T(8,128)(2,1)} %copy-done.13, bf16[2,256,512]{2,1,0:T(8,128)(2,1)} %collective-permute-done.28.refs_2_, ...), custom_call_target="tpu_custom_call", output_to_operand_aliasing={{}: (7, {})} | custom-call | flops 2147483648 | bytes 6291456 | tf_op jit(solution)/shard_map/expand/pallas_call | solution.py:262
  371.0 0.8 copy-done.16
  371.8 6.2 %expand.7 = bf16[2,4096,1024]{2,1,0:T(8,128)(2,1)} custom-call(s32[4]{0:T(128)} %pad_add_fusion.quads, s32[1]{0:T(128)} %bitcast.4.group, bf16[2,256,512]{2,1,0:T(8,128)(2,1)} %copy-done.12, bf16[2,256,512]{2,1,0:T(8,128)(2,1)} %copy-done.14, bf16[2,256,512]{2,1,0:T(8,128)(2,1)} %copy-done.15, ...), custom_call_target="tpu_custom_call", output_to_operand_aliasing={{}: (7, {})} | custom-call | flops 2147483648 | bytes 6291456 | tf_op jit(solution)/shard_map/expand/pallas_call | solution.py:262
  (168 shorter events, 18.6 us)
Async XLA Ops:
  1.7 15.0 %collective-permute-start = (f32[2,128,512]{2,1,0:T(8,128)S(1)}, f32[2,128,512]{2,1,0:T(8,128)S(1)}, u32[]{:S(2)}, u32[]{:S(2)}) collective-permute-start(f32[2,128,512]{2,1,0:T(8,128)S(1)} %constant_dynamic-slice_fusion), channel_id=1, source_target_pairs={{0,1},{1,0},{2,3},{3,2},{4,5},{5,4},{6,7},{7,6},{8,9},{9,8},{10,11... | collective-permute-start | bytes 1572872 | tf_op jit(solution)/shard_map/ppermute | solution.py:384
  16.7 13.1 %collective-permute-start.1 = (f32[2,128,512]{2,1,0:T(8,128)S(1)}, f32[2,128,512]{2,1,0:T(8,128)S(1)}, u32[]{:S(2)}, u32[]{:S(2)}) collective-permute-start(f32[2,128,512]{2,1,0:T(8,128)S(1)} %collective-permute-done.refs_1_), channel_id=1, source_target_pairs={{0,4},{2,6},{4,0},{6,2},{8,12},{10,14},{12,8},{14,10},{16,20},{18,... | collective-permute-start | bytes 1572872 | tf_op jit(solution)/shard_map/ppermute | solution.py:368
  19.7 13.1 %collective-permute-start.2 = (f32[2,128,512]{2,1,0:T(8,128)S(1)}, f32[2,128,512]{2,1,0:T(8,128)S(1)}, u32[]{:S(2)}, u32[]{:S(2)}) collective-permute-start(f32[2,128,512]{2,1,0:T(8,128)S(1)} %collective-permute-done.refs_1_), channel_id=1, source_target_pairs={{0,2},{2,0},{4,6},{6,4},{8,10},{10,8},{12,14},{14,12},{16,18},{18,... | collective-permute-start | bytes 1572872 | tf_op jit(solution)/shard_map/ppermute | solution.py:368
  34.5 63.9 %collective-permute-start.4 = (bf16[2,2,32,16,512]{4,3,2,1,0:T(8,128)(2,1)S(1)}, bf16[2,2,32,16,512]{4,3,2,1,0:T(8,128)(2,1)}, u32[]{:S(2)}, u32[]{:S(2)}) collective-permute-start(bf16[2,2,32,16,512]{4,3,2,1,0:T(8,128)(2,1)S(1)} %pad_maximum_fusion.refs_0_), channel_id=1, source_target_pairs={{0,4},{2,6},{4,0},{6,2},{8,12},{10,14},{12,8},{14,10},{16,20},{18,... | collective-permute-start | bytes 6291464 | tf_op jit(solution)/shard_map/ppermute | solution.py:368
  97.6 29.4 %collective-permute-start.5 = (bf16[2,2,32,16,512]{4,3,2,1,0:T(8,128)(2,1)S(1)}, bf16[2,2,32,16,512]{4,3,2,1,0:T(8,128)(2,1)}, u32[]{:S(2)}, u32[]{:S(2)}) collective-permute-start(bf16[2,2,32,16,512]{4,3,2,1,0:T(8,128)(2,1)S(1)} %pad_maximum_fusion.refs_0_), channel_id=1, source_target_pairs={{0,2},{2,0},{4,6},{6,4},{8,10},{10,8},{12,14},{14,12},{16,18},{18,... | collective-permute-start | bytes 6291464 | tf_op jit(solution)/shard_map/ppermute | solution.py:368
  98.3 31.0 %collective-permute-start.6 = (bf16[2,2,32,16,512]{4,3,2,1,0:T(8,128)(2,1)}, bf16[2,2,32,16,512]{4,3,2,1,0:T(8,128)(2,1)}, u32[]{:S(2)}, u32[]{:S(2)}) collective-permute-start(bf16[2,2,32,16,512]{4,3,2,1,0:T(8,128)(2,1)} %collective-permute-done.4.refs_1_), channel_id=1, source_target_pairs={{0,2},{2,0},{4,6},{6,4},{8,10},{10,8},{12,14},{14,12},{16,18},{18,... | collective-permute-start | bytes 6291464 | tf_op jit(solution)/shard_map/ppermute | solution.py:368
  104.8 15.9 %collective-permute-start.14 = (bf16[2,2,256,512]{3,2,1,0:T(8,128)(2,1)}, bf16[2,2,256,512]{3,2,1,0:T(8,128)(2,1)}, u32[]{:S(2)}, u32[]{:S(2)}) collective-permute-start(bf16[2,2,256,512]{3,2,1,0:T(8,128)(2,1)} %get-tuple-element.38), channel_id=1, source_target_pairs={{0,2},{2,0},{4,6},{6,4},{8,10},{10,8},{12,14},{14,12},{16,18},{18,... | collective-permute-start | bytes 3145736 | tf_op jit(solution)/shard_map/ppermute | solution.py:368
  107.6 15.5 %collective-permute-start.17 = (bf16[2,256,512]{2,1,0:T(8,128)(2,1)}, bf16[2,256,512]{2,1,0:T(8,128)(2,1)}, u32[]{:S(2)}, u32[]{:S(2)}) collective-permute-start(bf16[2,256,512]{2,1,0:T(8,128)(2,1)} %fusion.18), channel_id=1, source_target_pairs={{0,4},{2,6},{4,0},{6,2},{8,12},{10,14},{12,8},{14,10},{16,20},{18,... | collective-permute-start | bytes 1572872 | tf_op jit(solution)/shard_map/ppermute | solution.py:368
  114.3 38.6 %collective-permute-start.12 = (bf16[2,2,256,512]{3,2,1,0:T(8,128)(2,1)}, bf16[2,2,256,512]{3,2,1,0:T(8,128)(2,1)}, u32[]{:S(2)}, u32[]{:S(2)}) collective-permute-start(bf16[2,2,256,512]{3,2,1,0:T(8,128)(2,1)} %get-tuple-element.36), channel_id=1, source_target_pairs={{0,2},{2,0},{4,6},{6,4},{8,10},{10,8},{12,14},{14,12},{16,18},{18,... | collective-permute-start | bytes 3145736 | tf_op jit(solution)/shard_map/ppermute | solution.py:368
  120.7 37.4 %collective-permute-start.10 = (bf16[2,2,256,512]{3,2,1,0:T(8,128)(2,1)}, bf16[2,2,256,512]{3,2,1,0:T(8,128)(2,1)}, u32[]{:S(2)}, u32[]{:S(2)}) collective-permute-start(bf16[2,2,256,512]{3,2,1,0:T(8,128)(2,1)} %get-tuple-element.34), channel_id=1, source_target_pairs={{0,2},{2,0},{4,6},{6,4},{8,10},{10,8},{12,14},{14,12},{16,18},{18,... | collective-permute-start | bytes 3145736 | tf_op jit(solution)/shard_map/ppermute | solution.py:368
  123.1 31.7 %collective-permute-start.15 = (bf16[2,256,512]{2,1,0:T(8,128)(2,1)}, bf16[2,256,512]{2,1,0:T(8,128)(2,1)}, u32[]{:S(2)}, u32[]{:S(2)}) collective-permute-start(bf16[2,256,512]{2,1,0:T(8,128)(2,1)} %fusion.17), channel_id=1, source_target_pairs={{0,4},{2,6},{4,0},{6,2},{8,12},{10,14},{12,8},{14,10},{16,20},{18,... | collective-permute-start | bytes 1572872 | tf_op jit(solution)/shard_map/ppermute | solution.py:368
  127.0 27.8 %collective-permute-start.18 = (bf16[2,256,512]{2,1,0:T(8,128)(2,1)}, bf16[2,256,512]{2,1,0:T(8,128)(2,1)}, u32[]{:S(2)}, u32[]{:S(2)}) collective-permute-start(bf16[2,256,512]{2,1,0:T(8,128)(2,1)} %fusion.7), channel_id=1, source_target_pairs={{0,8},{2,10},{4,12},{6,14},{8,16},{10,18},{12,20},{14,22},{16,24},... | collective-permute-start | bytes 1572872 | tf_op jit(solution)/shard_map/ppermute | solution.py:368
  151.3 28.0 %collective-permute-start.7 = (bf16[2,2,256,512]{3,2,1,0:T(8,128)(2,1)}, bf16[2,2,256,512]{3,2,1,0:T(8,128)(2,1)S(1)}, u32[]{:S(2)}, u32[]{:S(2)}) collective-permute-start(bf16[2,2,256,512]{3,2,1,0:T(8,128)(2,1)} %get-tuple-element.25), channel_id=1, source_target_pairs={{0,8},{2,10},{4,12},{6,14},{8,16},{10,18},{12,20},{14,22},{16,24},... | collective-permute-start | bytes 3145736 | tf_op jit(solution)/shard_map/ppermute | solution.py:368
  154.2 25.6 %collective-permute-start.13 = (bf16[2,256,512]{2,1,0:T(8,128)(2,1)S(1)}, bf16[2,256,512]{2,1,0:T(8,128)(2,1)S(1)}, u32[]{:S(2)}, u32[]{:S(2)}) collective-permute-start(bf16[2,256,512]{2,1,0:T(8,128)(2,1)S(1)} %fusion.16), channel_id=1, source_target_pairs={{0,4},{2,6},{4,0},{6,2},{8,12},{10,14},{12,8},{14,10},{16,20},{18,... | collective-permute-start | bytes 1572872 | tf_op jit(solution)/shard_map/ppermute | solution.py:368
  156.4 34.2 %collective-permute-start.19 = (bf16[2,256,512]{2,1,0:T(8,128)(2,1)S(1)}, bf16[2,256,512]{2,1,0:T(8,128)(2,1)S(1)}, u32[]{:S(2)}, u32[]{:S(2)}) collective-permute-start(bf16[2,256,512]{2,1,0:T(8,128)(2,1)S(1)} %fusion.9), channel_id=1, source_target_pairs={{0,8},{2,10},{4,12},{6,14},{8,16},{10,18},{12,20},{14,22},{16,24},... | collective-permute-start | bytes 1572872 | tf_op jit(solution)/shard_map/ppermute | solution.py:368
  159.2 32.8 %collective-permute-start.11 = (bf16[2,256,512]{2,1,0:T(8,128)(2,1)S(1)}, bf16[2,256,512]{2,1,0:T(8,128)(2,1)S(1)}, u32[]{:S(2)}, u32[]{:S(2)}) collective-permute-start(bf16[2,256,512]{2,1,0:T(8,128)(2,1)S(1)} %fusion.15), channel_id=1, source_target_pairs={{0,4},{2,6},{4,0},{6,2},{8,12},{10,14},{12,8},{14,10},{16,20},{18,... | collective-permute-start | bytes 1572872 | tf_op jit(solution)/shard_map/ppermute | solution.py:368
  179.7 44.5 %collective-permute-start.8 = (bf16[2,2,256,512]{3,2,1,0:T(8,128)(2,1)S(1)}, bf16[2,2,256,512]{3,2,1,0:T(8,128)(2,1)S(1)}, u32[]{:S(2)}, u32[]{:S(2)}) collective-permute-start(bf16[2,2,256,512]{3,2,1,0:T(8,128)(2,1)S(1)} %add.204), channel_id=1, source_target_pairs={{0,8},{2,10},{4,12},{6,14},{8,16},{10,18},{12,20},{14,22},{16,24},... | collective-permute-start | bytes 3145736 | tf_op jit(solution)/shard_map/ppermute | solution.py:368
  191.9 30.9 %collective-permute-start.20 = (bf16[2,256,512]{2,1,0:T(8,128)(2,1)S(1)}, bf16[2,256,512]{2,1,0:T(8,128)(2,1)S(1)}, u32[]{:S(2)}, u32[]{:S(2)}) collective-permute-start(bf16[2,256,512]{2,1,0:T(8,128)(2,1)S(1)} %fusion.11), channel_id=1, source_target_pairs={{0,8},{2,10},{4,12},{6,14},{8,16},{10,18},{12,20},{14,22},{16,24},... | collective-permute-start | bytes 1572872 | tf_op jit(solution)/shard_map/ppermute | solution.py:368
  224.2 16.6 %collective-permute-start.39 = (bf16[2,256,512]{2,1,0:T(8,128)(2,1)S(1)}, bf16[2,256,512]{2,1,0:T(8,128)(2,1)S(1)}, u32[]{:S(2)}, u32[]{:S(2)}) collective-permute-start(bf16[2,256,512]{2,1,0:T(8,128)(2,1)S(1)} %get-tuple-element.42.refs_0_), channel_id=1, source_target_pairs={{0,8},{2,10},{4,12},{6,14},{8,16},{10,18},{12,20},{14,22},{16,24},... | collective-permute-start | bytes 1572872 | tf_op jit(solution)/shard_map/ppermute | solution.py:368
  224.6 47.6 %collective-permute-start.9 = (bf16[2,2,256,512]{3,2,1,0:T(8,128)(2,1)S(1)}, bf16[2,2,256,512]{3,2,1,0:T(8,128)(2,1)S(1)}, u32[]{:S(2)}, u32[]{:S(2)}) collective-permute-start(bf16[2,2,256,512]{3,2,1,0:T(8,128)(2,1)S(1)} %add.205), channel_id=1, source_target_pairs={{0,8},{2,10},{4,12},{6,14},{8,16},{10,18},{12,20},{14,22},{16,24},... | collective-permute-start | bytes 3145736 | tf_op jit(solution)/shard_map/ppermute | solution.py:368
  226.0 15.5 %collective-permute-start.36 = (bf16[2,256,512]{2,1,0:T(8,128)(2,1)S(1)}, bf16[2,256,512]{2,1,0:T(8,128)(2,1)S(1)}, u32[]{:S(2)}, u32[]{:S(2)}) collective-permute-start(bf16[2,256,512]{2,1,0:T(8,128)(2,1)S(1)} %get-tuple-element.42.refs_0_), channel_id=1, source_target_pairs={{0,4},{2,6},{4,0},{6,2},{8,12},{10,14},{12,8},{14,10},{16,20},{18,... | collective-permute-start | bytes 1572872 | tf_op jit(solution)/shard_map/ppermute | solution.py:368
  240.8 31.3 %collective-permute-start.43 = (bf16[2,256,512]{2,1,0:T(8,128)(2,1)S(1)}, bf16[2,256,512]{2,1,0:T(8,128)(2,1)S(1)}, u32[]{:S(2)}, u32[]{:S(2)}) collective-permute-start(bf16[2,256,512]{2,1,0:T(8,128)(2,1)S(1)} %collective-permute-done.39.refs_4_), channel_id=1, source_target_pairs={{0,8},{2,10},{4,12},{6,14},{8,16},{10,18},{12,20},{14,22},{16,24},... | collective-permute-start | bytes 1572872 | tf_op jit(solution)/shard_map/ppermute | solution.py:368
  240.8 32.6 %collective-permute-start.37 = (bf16[2,256,512]{2,1,0:T(8,128)(2,1)S(1)}, bf16[2,256,512]{2,1,0:T(8,128)(2,1)S(1)}, u32[]{:S(2)}, u32[]{:S(2)}) collective-permute-start(bf16[2,256,512]{2,1,0:T(8,128)(2,1)S(1)} %get-tuple-element.42.refs_0_), channel_id=1, source_target_pairs={{0,2},{2,0},{4,6},{6,4},{8,10},{10,8},{12,14},{14,12},{16,18},{18,... | collective-permute-start | bytes 1572872 | tf_op jit(solution)/shard_map/ppermute | solution.py:368
  240.8 33.2 %collective-permute-start.40 = (bf16[2,256,512]{2,1,0:T(8,128)(2,1)S(1)}, bf16[2,256,512]{2,1,0:T(8,128)(2,1)S(1)}, u32[]{:S(2)}, u32[]{:S(2)}) collective-permute-start(bf16[2,256,512]{2,1,0:T(8,128)(2,1)S(1)} %collective-permute-done.39.refs_4_), channel_id=1, source_target_pairs={{0,4},{2,6},{4,0},{6,2},{8,12},{10,14},{12,8},{14,10},{16,20},{18,... | collective-permute-start | bytes 1572872 | tf_op jit(solution)/shard_map/ppermute | solution.py:368
  241.4 32.8 %collective-permute-start.41 = (bf16[2,256,512]{2,1,0:T(8,128)(2,1)S(1)}, bf16[2,256,512]{2,1,0:T(8,128)(2,1)S(1)}, u32[]{:S(2)}, u32[]{:S(2)}) collective-permute-start(bf16[2,256,512]{2,1,0:T(8,128)(2,1)S(1)} %collective-permute-done.39.refs_4_), channel_id=1, source_target_pairs={{0,2},{2,0},{4,6},{6,4},{8,10},{10,8},{12,14},{14,12},{16,18},{18,... | collective-permute-start | bytes 1572872 | tf_op jit(solution)/shard_map/ppermute | solution.py:368
  272.2 16.6 %collective-permute-start.47 = (bf16[2,256,512]{2,1,0:T(8,128)(2,1)S(1)}, bf16[2,256,512]{2,1,0:T(8,128)(2,1)S(1)}, u32[]{:S(2)}, u32[]{:S(2)}) collective-permute-start(bf16[2,256,512]{2,1,0:T(8,128)(2,1)S(1)} %collective-permute-done.43.refs_8_), channel_id=1, source_target_pairs={{0,8},{2,10},{4,12},{6,14},{8,16},{10,18},{12,20},{14,22},{16,24},... | collective-permute-start | bytes 1572872 | tf_op jit(solution)/shard_map/ppermute | solution.py:368
  273.4 15.9 %collective-permute-start.44 = (bf16[2,256,512]{2,1,0:T(8,128)(2,1)S(1)}, bf16[2,256,512]{2,1,0:T(8,128)(2,1)S(1)}, u32[]{:S(2)}, u32[]{:S(2)}) collective-permute-start(bf16[2,256,512]{2,1,0:T(8,128)(2,1)S(1)} %collective-permute-done.43.refs_8_), channel_id=1, source_target_pairs={{0,4},{2,6},{4,0},{6,2},{8,12},{10,14},{12,8},{14,10},{16,20},{18,... | collective-permute-start | bytes 1572872 | tf_op jit(solution)/shard_map/ppermute | solution.py:368
  274.0 25.5 %collective-permute-start.21 = (bf16[2,256,512]{2,1,0:T(8,128)(2,1)S(1)}, bf16[2,256,512]{2,1,0:T(8,128)(2,1)S(1)}, u32[]{:S(2)}, u32[]{:S(2)}) collective-permute-start(bf16[2,256,512]{2,1,0:T(8,128)(2,1)S(1)} %fusion.14.refs_0_), channel_id=1, source_target_pairs={{0,8},{2,10},{4,12},{6,14},{8,16},{10,18},{12,20},{14,22},{16,24},... | collective-permute-start | bytes 1572872 | tf_op jit(solution)/shard_map/ppermute | solution.py:368
  274.1 25.5 %collective-permute-start.42 = (bf16[2,256,512]{2,1,0:T(8,128)(2,1)S(1)}, bf16[2,256,512]{2,1,0:T(8,128)(2,1)S(1)}, u32[]{:S(2)}, u32[]{:S(2)}) collective-permute-start(bf16[2,256,512]{2,1,0:T(8,128)(2,1)S(1)} %collective-permute-done.40.refs_5_), channel_id=1, source_target_pairs={{0,2},{2,0},{4,6},{6,4},{8,10},{10,8},{12,14},{14,12},{16,18},{18,... | collective-permute-start | bytes 1572872 | tf_op jit(solution)/shard_map/ppermute | solution.py:368
  274.3 25.9 %collective-permute-start.45 = (bf16[2,256,512]{2,1,0:T(8,128)(2,1)S(1)}, bf16[2,256,512]{2,1,0:T(8,128)(2,1)S(1)}, u32[]{:S(2)}, u32[]{:S(2)}) collective-permute-start(bf16[2,256,512]{2,1,0:T(8,128)(2,1)S(1)} %collective-permute-done.43.refs_8_), channel_id=1, source_target_pairs={{0,2},{2,0},{4,6},{6,4},{8,10},{10,8},{12,14},{14,12},{16,18},{18,... | collective-permute-start | bytes 1572872 | tf_op jit(solution)/shard_map/ppermute | solution.py:368
  288.8 12.9 %collective-permute-start.48 = (bf16[2,256,512]{2,1,0:T(8,128)(2,1)S(1)}, bf16[2,256,512]{2,1,0:T(8,128)(2,1)S(1)}, u32[]{:S(2)}, u32[]{:S(2)}) collective-permute-start(bf16[2,256,512]{2,1,0:T(8,128)(2,1)S(1)} %collective-permute-done.47.refs_12_), channel_id=1, source_target_pairs={{0,4},{2,6},{4,0},{6,2},{8,12},{10,14},{12,8},{14,10},{16,20},{18,... | collective-permute-start | bytes 1572872 | tf_op jit(solution)/shard_map/ppermute | solution.py:368
  289.4 12.4 %collective-permute-start.46 = (bf16[2,256,512]{2,1,0:T(8,128)(2,1)S(1)}, bf16[2,256,512]{2,1,0:T(8,128)(2,1)S(1)}, u32[]{:S(2)}, u32[]{:S(2)}) collective-permute-start(bf16[2,256,512]{2,1,0:T(8,128)(2,1)S(1)} %collective-permute-done.44.refs_9_), channel_id=1, source_target_pairs={{0,2},{2,0},{4,6},{6,4},{8,10},{10,8},{12,14},{14,12},{16,18},{18,... | collective-permute-start | bytes 1572872 | tf_op jit(solution)/shard_map/ppermute | solution.py:368
  299.5 15.2 %collective-permute-start.22 = (bf16[2,256,512]{2,1,0:T(8,128)(2,1)S(1)}, bf16[2,256,512]{2,1,0:T(8,128)(2,1)S(1)}, u32[]{:S(2)}, u32[]{:S(2)}) collective-permute-start(bf16[2,256,512]{2,1,0:T(8,128)(2,1)S(1)} %collective-permute-done.21.refs_0_), channel_id=1, source_target_pairs={{0,8},{2,10},{4,12},{6,14},{8,16},{10,18},{12,20},{14,22},{16,24},... | collective-permute-start | bytes 1572872 | tf_op jit(solution)/shard_map/ppermute | solution.py:368
  299.6 15.2 %collective-permute-start.33 = (bf16[2,256,512]{2,1,0:T(8,128)(2,1)S(1)}, bf16[2,256,512]{2,1,0:T(8,128)(2,1)}, u32[]{:S(2)}, u32[]{:S(2)}) collective-permute-start(bf16[2,256,512]{2,1,0:T(8,128)(2,1)S(1)} %fusion.14.refs_0_), channel_id=1, source_target_pairs={{0,4},{2,6},{4,0},{6,2},{8,12},{10,14},{12,8},{14,10},{16,20},{18,... | collective-permute-start | bytes 1572872 | tf_op jit(solution)/shard_map/ppermute | solution.py:368
  300.2 14.7 %collective-permute-start.49 = (bf16[2,256,512]{2,1,0:T(8,128)(2,1)S(1)}, bf16[2,256,512]{2,1,0:T(8,128)(2,1)S(1)}, u32[]{:S(2)}, u32[]{:S(2)}) collective-permute-start(bf16[2,256,512]{2,1,0:T(8,128)(2,1)S(1)} %collective-permute-done.47.refs_12_), channel_id=1, source_target_pairs={{0,2},{2,0},{4,6},{6,4},{8,10},{10,8},{12,14},{14,12},{16,18},{18,... | collective-permute-start | bytes 1572872 | tf_op jit(solution)/shard_map/ppermute | solution.py:368
  301.7 13.7 %collective-permute-start.50 = (bf16[2,256,512]{2,1,0:T(8,128)(2,1)S(1)}, bf16[2,256,512]{2,1,0:T(8,128)(2,1)S(1)}, u32[]{:S(2)}, u32[]{:S(2)}) collective-permute-start(bf16[2,256,512]{2,1,0:T(8,128)(2,1)S(1)} %collective-permute-done.48.refs_13_), channel_id=1, source_target_pairs={{0,2},{2,0},{4,6},{6,4},{8,10},{10,8},{12,14},{14,12},{16,18},{18,... | collective-permute-start | bytes 1572872 | tf_op jit(solution)/shard_map/ppermute | solution.py:368
  301.8 16.1 %collective-permute-start.34 = (bf16[2,256,512]{2,1,0:T(8,128)(2,1)S(1)}, bf16[2,256,512]{2,1,0:T(8,128)(2,1)S(1)}, u32[]{:S(2)}, u32[]{:S(2)}) collective-permute-start(bf16[2,256,512]{2,1,0:T(8,128)(2,1)S(1)} %fusion.14.refs_0_), channel_id=1, source_target_pairs={{0,2},{2,0},{4,6},{6,4},{8,10},{10,8},{12,14},{14,12},{16,18},{18,... | collective-permute-start | bytes 1572872 | tf_op jit(solution)/shard_map/ppermute | solution.py:368
  314.8 14.4 %collective-permute-start.23 = (bf16[2,256,512]{2,1,0:T(8,128)(2,1)S(1)}, bf16[2,256,512]{2,1,0:T(8,128)(2,1)S(1)}, u32[]{:S(2)}, u32[]{:S(2)}) collective-permute-start(bf16[2,256,512]{2,1,0:T(8,128)(2,1)S(1)} %collective-permute-done.22.refs_0_), channel_id=1, source_target_pairs={{0,8},{2,10},{4,12},{6,14},{8,16},{10,18},{12,20},{14,22},{16,24},... | collective-permute-start | bytes 1572872 | tf_op jit(solution)/shard_map/ppermute | solution.py:368
  314.8 15.5 %collective-permute-start.35 = (bf16[2,256,512]{2,1,0:T(8,128)(2,1)}, bf16[2,256,512]{2,1,0:T(8,128)(2,1)}, u32[]{:S(2)}, u32[]{:S(2)}) collective-permute-start(bf16[2,256,512]{2,1,0:T(8,128)(2,1)} %collective-permute-done.33.refs_1_), channel_id=1, source_target_pairs={{0,2},{2,0},{4,6},{6,4},{8,10},{10,8},{12,14},{14,12},{16,18},{18,... | collective-permute-start | bytes 1572872 | tf_op jit(solution)/shard_map/ppermute | solution.py:368
  314.9 15.4 %collective-permute-start.30 = (bf16[2,256,512]{2,1,0:T(8,128)(2,1)S(1)}, bf16[2,256,512]{2,1,0:T(8,128)(2,1)}, u32[]{:S(2)}, u32[]{:S(2)}) collective-permute-start(bf16[2,256,512]{2,1,0:T(8,128)(2,1)S(1)} %collective-permute-done.21.refs_0_), channel_id=1, source_target_pairs={{0,4},{2,6},{4,0},{6,2},{8,12},{10,14},{12,8},{14,10},{16,20},{18,... | collective-permute-start | bytes 1572872 | tf_op jit(solution)/shard_map/ppermute | solution.py:368
  316.6 24.4 %collective-permute-start.27 = (bf16[2,256,512]{2,1,0:T(8,128)(2,1)S(1)}, bf16[2,256,512]{2,1,0:T(8,128)(2,1)S(1)}, u32[]{:S(2)}, u32[]{:S(2)}) collective-permute-start(bf16[2,256,512]{2,1,0:T(8,128)(2,1)S(1)} %collective-permute-done.22.refs_0_), channel_id=1, source_target_pairs={{0,4},{2,6},{4,0},{6,2},{8,12},{10,14},{12,8},{14,10},{16,20},{18,... | collective-permute-start | bytes 1572872 | tf_op jit(solution)/shard_map/ppermute | solution.py:368
  317.9 32.6 %collective-permute-start.31 = (bf16[2,256,512]{2,1,0:T(8,128)(2,1)S(1)}, bf16[2,256,512]{2,1,0:T(8,128)(2,1)}, u32[]{:S(2)}, u32[]{:S(2)}) collective-permute-start(bf16[2,256,512]{2,1,0:T(8,128)(2,1)S(1)} %collective-permute-done.21.refs_0_), channel_id=1, source_target_pairs={{0,2},{2,0},{4,6},{6,4},{8,10},{10,8},{12,14},{14,12},{16,18},{18,... | collective-permute-start | bytes 1572872 | tf_op jit(solution)/shard_map/ppermute | solution.py:368
  329.1 22.5 %collective-permute-start.24 = (bf16[2,256,512]{2,1,0:T(8,128)(2,1)S(1)}, bf16[2,256,512]{2,1,0:T(8,128)(2,1)S(1)}, u32[]{:S(2)}, u32[]{:S(2)}) collective-permute-start(bf16[2,256,512]{2,1,0:T(8,128)(2,1)S(1)} %collective-permute-done.23.refs_0_), channel_id=1, source_target_pairs={{0,4},{2,6},{4,0},{6,2},{8,12},{10,14},{12,8},{14,10},{16,20},{18,... | collective-permute-start | bytes 1572872 | tf_op jit(solution)/shard_map/ppermute | solution.py:368
  330.3 33.8 %collective-permute-start.28 = (bf16[2,256,512]{2,1,0:T(8,128)(2,1)S(1)}, bf16[2,256,512]{2,1,0:T(8,128)(2,1)}, u32[]{:S(2)}, u32[]{:S(2)}) collective-permute-start(bf16[2,256,512]{2,1,0:T(8,128)(2,1)S(1)} %collective-permute-done.22.refs_0_), channel_id=1, source_target_pairs={{0,2},{2,0},{4,6},{6,4},{8,10},{10,8},{12,14},{14,12},{16,18},{18,... | collective-permute-start | bytes 1572872 | tf_op jit(solution)/shard_map/ppermute | solution.py:368
  330.3 27.6 %collective-permute-start.32 = (bf16[2,256,512]{2,1,0:T(8,128)(2,1)}, bf16[2,256,512]{2,1,0:T(8,128)(2,1)}, u32[]{:S(2)}, u32[]{:S(2)}) collective-permute-start(bf16[2,256,512]{2,1,0:T(8,128)(2,1)} %collective-permute-done.30.refs_1_), channel_id=1, source_target_pairs={{0,2},{2,0},{4,6},{6,4},{8,10},{10,8},{12,14},{14,12},{16,18},{18,... | collective-permute-start | bytes 1572872 | tf_op jit(solution)/shard_map/ppermute | solution.py:368
  341.0 23.1 %collective-permute-start.29 = (bf16[2,256,512]{2,1,0:T(8,128)(2,1)S(1)}, bf16[2,256,512]{2,1,0:T(8,128)(2,1)}, u32[]{:S(2)}, u32[]{:S(2)}) collective-permute-start(bf16[2,256,512]{2,1,0:T(8,128)(2,1)S(1)} %collective-permute-done.27.refs_1_), channel_id=1, source_target_pairs={{0,2},{2,0},{4,6},{6,4},{8,10},{10,8},{12,14},{14,12},{16,18},{18,... | collective-permute-start | bytes 1572872 | tf_op jit(solution)/shard_map/ppermute | solution.py:368
  350.5 19.8 %collective-permute-start.25 = (bf16[2,256,512]{2,1,0:T(8,128)(2,1)S(1)}, bf16[2,256,512]{2,1,0:T(8,128)(2,1)S(1)}, u32[]{:S(2)}, u32[]{:S(2)}) collective-permute-start(bf16[2,256,512]{2,1,0:T(8,128)(2,1)S(1)} %collective-permute-done.23.refs_0_), channel_id=1, source_target_pairs={{0,2},{2,0},{4,6},{6,4},{8,10},{10,8},{12,14},{14,12},{16,18},{18,... | collective-permute-start | bytes 1572872 | tf_op jit(solution)/shard_map/ppermute | solution.py:368
  351.7 18.6 %collective-permute-start.26 = (bf16[2,256,512]{2,1,0:T(8,128)(2,1)S(1)}, bf16[2,256,512]{2,1,0:T(8,128)(2,1)S(1)}, u32[]{:S(2)}, u32[]{:S(2)}) collective-permute-start(bf16[2,256,512]{2,1,0:T(8,128)(2,1)S(1)} %collective-permute-done.24.refs_1_), channel_id=1, source_target_pairs={{0,2},{2,0},{4,6},{6,4},{8,10},{10,8},{12,14},{14,12},{16,18},{18,... | collective-permute-start | bytes 1572872 | tf_op jit(solution)/shard_map/ppermute | solution.py:368
  (41 other events, 850.8 us)
where the time goes:
time: 379 us; the launch traced here: 378 us
  waiting for transfers between devices  187 us (49%)
  Pallas kernels  135 us (36%)
  starting transfers between devices  26 us (7%)
  other arithmetic  21.7 us (6%)
  local copies, waits for them, and re-layouts  6.8 us (2%)
    ppermute x50, waiting for transfers between devices, permute(): return lax.ppermute(v, 'dp', [(i, target(i)) for i in range(replicas)])  175 us
    pallas_call x1, Pallas kernels, orthonormal_basis(): pl.pallas_call(functools.partial(basis_kernel, pieces=len(pieces)), out_s...  55.3 us
    pallas_call x4, Pallas kernels, project(): pl.pallas_call(project_kernel, out_shape=(out, out), grid_spec=pltpu.Pref...  25.1 us
    pallas_call x4, Pallas kernels, expand(): pl.pallas_call(expand_kernel, out_shape=jax.ShapeDtypeStruct((mats, local...  24.7 us
    ppermute x50, starting transfers between devices, permute(): return lax.ppermute(v, 'dp', [(i, target(i)) for i in range(replicas)])  22.9 us
    pallas_call x1, Pallas kernels, collect_moments(): pl.pallas_call(collect_kernel, out_shape=(jax.ShapeDtypeStruct((kinds, ma...  22 us
    ppermute x1, waiting for transfers between devices, shards(): lax.ppermute(part, 'fsdp', [(i, (i + shift) % splits) for i in range(spli...  11.9 us
    pallas_call x1, Pallas kernels, settle_moments(): pl.pallas_call(functools.partial(settle_kernel, pieces=len(pieces)), out_...  8.16 us
  transfers between devices with their start and end apart: 51, of which 14 were waited for; matrix products, arithmetic and copies ran while one was open for 6% of the time, Pallas kernels for 34%

commit v1 on v0

--- a/solution.py
+++ b/solution.py
@@ -38,6 +38,22 @@
         + dot_bf16(a_high, b_low, dims)
         + dot_bf16(a_high, b_high, dims)
     )
+
+
+def thirds(x):
+    first = x.astype(BF16).astype(F32)
+    rest = x - first
+    second = rest.astype(BF16).astype(F32)
+    return first, second, rest - second
+
+
+def dot_packed(a, b, dims):
+    a1, a2, a3 = thirds(a)
+    b1, b2, b3 = thirds(b)
+    (a_dim,), (b_dim,) = dims
+    left = jnp.concatenate([a1, a2, a1, a3, a2, a1], axis=a_dim).astype(BF16)
+    right = jnp.concatenate([b3, b2, b2, b1, b1, b1], axis=b_dim).astype(BF16)
+    return dot_bf16(left, right, dims)
 
 
 def eliminate_panel(block_ref, inverse_ref, scale_ref, m, start):
@@ -78,7 +94,7 @@
         for m in range(mats):
             rows, inv_rows, recip = done[m]
             both = jnp.concatenate([rows, inv_rows], axis=1)
-            change = dot_f32(rows * recip, both, ((0,), (0,)))
+            change = dot_packed(rows * recip, both, ((0,), (0,)))
             block_ref[m] = block_ref[m] - jnp.where(below, change[:, :size], 0.0)
             inverse_ref[m] = inverse_ref[m] - jnp.where(below, change[:, size:], 0.0)
         return 0
@@ -86,11 +102,50 @@
     lax.fori_loop(0, size // PANEL, panel, 0)
 
 
-def basis_kernel(offsets, *refs, pieces):
+def add_gram(gram, pieces, held):
+    mats, rank, _ = gram.shape
+
+    def one(m, _):
+        for j in range(0, rank, WIDE):
+            total = None if held is None else held[m, j:, j : j + WIDE]
+            for ref in pieces:
+                part = dot_f32(ref[m, :, j:], ref[m, :, j : j + WIDE], ((0,), (0,)))
+                total = part if total is None else total + part
+            gram[m, j:, j : j + WIDE] = total
+        return 0
+
+    lax.fori_loop(0, mats, one, 0)
+
+
+def gram_kernel(*refs, pieces):
+    held = refs[pieces] if len(refs) > pieces + 1 else None
+    add_gram(refs[-1], refs[:pieces], held)
+
+
+def gram_of(pieces, held=None):
+    mats, _, rank = pieces[0].shape
+    args = list(pieces) + ([] if held is None else [held])
+    depth = sum(p.shape[1] for p in pieces)
+    vmem = pl.BlockSpec(memory_space=pltpu.VMEM)
+    return pl.pallas_call(
+        functools.partial(gram_kernel, pieces=len(pieces)),
+        out_shape=jax.ShapeDtypeStruct((mats, rank, rank), F32),
+        in_specs=[vmem] * len(args),
+        out_specs=vmem,
+        cost_estimate=pl.CostEstimate(
+            flops=12 * mats * depth * rank * rank,
+            bytes_accessed=4 * mats * rank * (rank + depth),
+            transcendentals=0,
+        ),
+        name="gram",
+    )(*args)
+
+
+def basis_kernel(offsets, *refs, pieces, fresh):
     own_ref = refs[0]
     piece_refs = refs[1 : 1 + pieces]
-    basis_ref = refs[1 + pieces]
-    raw, gram, low, inv, block, binv, scale = refs[2 + pieces :]
+    held, basis_ref = refs[1 + pieces : 3 + pieces]
+    raw, gram, low, inv, block, binv, scale = refs[3 + pieces :]
     mats, _, rank = raw.shape
     n = rank // BLOCK
 
@@ -101,12 +156,7 @@
         at = pl.multiple_of(offsets[i], 8)
         raw[:, pl.ds(at, ref.shape[1]), :] = ref[...]
 
-    def grams(m, _):
-        for j in range(0, rank, WIDE):
-            gram[m, j:, j : j + WIDE] = dot_f32(raw[m, :, j:], raw[m, :, j : j + WIDE], ((0,), (0,)))
-        return 0
-
-    lax.fori_loop(0, mats, grams, 0)
+    add_gram(gram, [piece_refs[i] for i in fresh], held)
     for b in range(n):
         below = (b + 1) * BLOCK
         for m in range(mats):
@@ -116,15 +166,15 @@
             d_inv = binv[m] * jnp.sqrt(scale[m])
             inv[m, sl(b), sl(b)] = d_inv
             if b > 0:
-                acc = dot_f32(
+                acc = dot_packed(
                     low[m, sl(b), : b * BLOCK], inv[m, : b * BLOCK, : b * BLOCK], ((1,), (0,))
                 )
-                inv[m, sl(b), : b * BLOCK] = -dot_f32(d_inv, acc, ((1,), (0,)))
+                inv[m, sl(b), : b * BLOCK] = -dot_packed(d_inv, acc, ((1,), (0,)))
             if b + 1 < n:
-                low[m, below:, sl(b)] = dot_f32(gram[m, below:, sl(b)], d_inv, ((1,), (1,)))
+                low[m, below:, sl(b)] = dot_packed(gram[m, below:, sl(b)], d_inv, ((1,), (1,)))
                 inv[m, sl(b), below:] = jnp.zeros((BLOCK, rank - below), F32)
                 for j in range(b + 1, n):
-                    gram[m, j * BLOCK :, sl(j)] = gram[m, j * BLOCK :, sl(j)] - dot_f32(
+                    gram[m, j * BLOCK :, sl(j)] = gram[m, j * BLOCK :, sl(j)] - dot_packed(
                         low[m, j * BLOCK :, sl(b)], low[m, sl(j), sl(b)], ((1,), (1,))
                     )
 
@@ -139,66 +189,62 @@
     lax.fori_loop(0, mats, bases, 0)
 
 
-def orthonormal_basis(own, pieces, offsets, feats):
+def orthonormal_basis(own, pieces, offsets, held, fresh, feats):
     mats, _, rank = own.shape
     vmem = pl.BlockSpec(memory_space=pltpu.VMEM)
     smem = pl.BlockSpec(memory_space=pltpu.SMEM)
     return pl.pallas_call(
-        functools.partial(basis_kernel, pieces=len(pieces)),
+        functools.partial(basis_kernel, pieces=len(pieces), fresh=tuple(fresh)),
         out_shape=jax.ShapeDtypeStruct((mats, feats, rank), BF16),
-        in_specs=[smem] + [vmem] * (1 + len(pieces)),
+        in_specs=[smem] + [vmem] * (2 + len(pieces)),
         out_specs=vmem,
         scratch_shapes=[pltpu.VMEM((mats, feats, rank), F32)]
         + [pltpu.VMEM((mats, rank, rank), F32)] * 3
         + [pltpu.VMEM((mats, BLOCK, BLOCK), F32)] * 3,
         cost_estimate=pl.CostEstimate(
-            flops=90_000_000_000, bytes_accessed=6 * mats * feats * rank, transcendentals=0
+            flops=40_000_000_000, bytes_accessed=6 * mats * feats * rank, transcendentals=0
         ),
         name="basis",
-    )(offsets, own, *pieces)
-
-
-def collect_kernel(places, *refs):
+    )(offsets, own, *pieces, held)
+
+
+def collect_kernel(places, counts, *refs):
     m = pl.program_id(1)
-    owner_refs, group_refs = refs[:QUAD], refs[QUAD:]
-    capacity, bucket_rows = owner_refs[0].shape[2], owner_refs[0].shape[3]
-    unit_rows = group_refs[0].shape[2]
-    for ref in group_refs:
-        ref[...] = jnp.zeros(ref.shape, BF16)
+    owner_refs, group_ref = refs[:QUAD], refs[QUAD]
+    bucket_rows = owner_refs[0].shape[3]
+    group_ref[...] = jnp.zeros(group_ref.shape, BF16)
     for i, owner_ref in enumerate(owner_refs):
 
         def pick(s, _):
             place = places[i, m, s]
-            at = pl.multiple_of(lax.rem(jnp.maximum(place, 0), unit_rows), bucket_rows)
-            for k, ref in enumerate(group_refs):
-
-                @pl.when(jnp.logical_and(place >= k * unit_rows, place < (k + 1) * unit_rows))
-                def _():
-                    ref[0, 0, pl.ds(at, bucket_rows), :] = owner_ref[0, 0, s]
+
+            @pl.when(place >= 0)
+            def _():
+                at = pl.multiple_of(jnp.maximum(place, 0), bucket_rows)
+                group_ref[0, 0, pl.ds(at, bucket_rows), :] = owner_ref[0, 0, s]
 
             return 0
 
-        lax.fori_loop(0, capacity, pick, 0)
-
-
-def collect_moments(owners, places, depth, unit_rows):
+        lax.fori_loop(0, counts[i, m], pick, 0)
+
+
+def collect_moments(owners, places, counts, column_rows):
     kinds, mats, capacity, bucket_rows, rank = owners[0].shape
-    slots = pl.BlockSpec((1, 1, capacity, bucket_rows, rank), lambda a, m, p: (a, m, 0, 0, 0))
-    group = pl.BlockSpec((1, 1, unit_rows, rank), lambda a, m, p: (a, m, 0, 0))
+    slots = pl.BlockSpec((1, 1, capacity, bucket_rows, rank), lambda a, m, *_: (a, m, 0, 0, 0))
     return pl.pallas_call(
         collect_kernel,
-        out_shape=(jax.ShapeDtypeStruct((kinds, mats, unit_rows, rank), BF16),) * depth,
+        out_shape=jax.ShapeDtypeStruct((kinds, mats, column_rows, rank), BF16),
         grid_spec=pltpu.PrefetchScalarGridSpec(
-            num_scalar_prefetch=1,
+            num_scalar_prefetch=2,
             grid=(kinds, mats),
             in_specs=[slots] * QUAD,
-            out_specs=(group,) * depth,
+            out_specs=pl.BlockSpec((1, 1, column_rows, rank), lambda a, m, *_: (a, m, 0, 0)),
         ),
         cost_estimate=pl.CostEstimate(
             flops=0, bytes_accessed=4 * QUAD * owners[0].size, transcendentals=0
         ),
         name="collect",
-    )(places, *owners)
+    )(places, counts, *owners)
 
 
 def project_kernel(quads, group, grads_ref, basis_ref, other_ref, own_ref, result):
@@ -351,7 +397,7 @@
 
 
 def shards(grads, raw_proj, bucket_owner, first_moment, second_moment):
-    local_rows = grads.shape[2]
+    mats, local_rows = grads.shape[1], grads.shape[2]
     local_feats = raw_proj.shape[1]
     buckets = bucket_owner.shape[1]
     capacity = first_moment.shape[2]
@@ -379,15 +425,19 @@
     quarter = local_feats // QUAD
     part = lax.dynamic_slice_in_dim(raw_proj, my_quad * quarter, quarter, 1)
     my_f = lax.axis_index("fsdp")
-    pieces, offsets = [], [my_f * local_feats]
+    gram = gram_of([raw_proj])
+    pieces, offsets, early, fresh = [], [my_f * local_feats], [], []
     for shift in range(1, splits):
         fetched = lax.ppermute(part, "fsdp", [(i, (i + shift) % splits) for i in range(splits)])
         across = to_x(fetched)
         base = ((my_f + splits - shift) % splits) * local_feats
         for piece, flip in ((fetched, 0), (across, 2), (to_core(fetched), 1), (to_core(across), 3)):
+            (fresh if flip & 2 else early).append(len(pieces))
             pieces.append(piece)
             offsets.append(base + (my_quad ^ flip) * quarter)
     offsets = jnp.stack(offsets).astype(jnp.int32)
+    if early:
+        gram = gram_of([pieces[i] for i in early], gram)
 
     same = bucket_owner[:, :, None] == bucket_owner[:, None, :]
     order = jnp.arange(buckets, dtype=jnp.int32)
@@ -399,6 +449,7 @@
     matches = local_slot[:, :, None, :] == slot_ids[None, None, :, None]
     quad_occupied = jnp.any(matches, axis=3)
     quad_buckets = jnp.sum(jnp.where(matches, order[None, None, None, :], 0), axis=3)
+    quad_counts = jnp.sum(quad_occupied.astype(jnp.int32), axis=2)
     occupied, bucket_of = quad_occupied[0], quad_buckets[0]
     quad_units = quad_buckets // unit_buckets
     steps = (my_z + depth - 1 - quad_units // QUAD) % depth
@@ -411,10 +462,11 @@
     slots_across = to_x(slots)
     slots_core = to_core(slots)
 
-    basis = orthonormal_basis(raw_proj, pieces, offsets, splits * local_feats)
+    basis = orthonormal_basis(raw_proj, pieces, offsets, gram, fresh, splits * local_feats)
 
     owners = (slots, slots_across, slots_core, to_core(slots_across))
-    moment_groups = collect_moments(owners, places, depth, unit_rows)
+    column = collect_moments(owners, places, quad_counts, depth * unit_rows)
+    moment_groups = [column[:, :, k * unit_rows : (k + 1) * unit_rows] for k in range(depth)]
     unit_moments = moment_groups[0]
     for k in range(1, depth):
         unit_moments = to_z(unit_moments) + moment_groups[k]
@@ -435,8 +487,14 @@
 
     def ring(unit):
         groups = []
+        across = None
+        half = mats // 2
         for k in range(depth):
-            across = to_x(unit)
+            if 0 < k == depth - 1:
+                over_z = to_z(across[half:])
+                across = jnp.concatenate([to_x(unit[:half]), over_z])
+            else:
+                across = to_x(unit)
             core = to_core(unit)
             groups.append((unit, across, core, to_core(across)))
             if k + 1 < depth:

time: 379 us -> 369 us (0.974)
  Pallas kernels: 135 us -> 119 us
  waiting for transfers between devices: 187 us -> 191 us
    pallas_call x2 -> x4, Pallas kernels: 77.3 us -> 61 us  [the longest x1 40.4 us: orthonormal_basis(): pl.pallas_call(functools.partial(basis_kernel, pieces=len(pieces), fresh=...]
    ppermute x50 -> x52, waiting for transfers between devices: 175 us -> 180 us  [permute(): return lax.ppermute(v, 'dp', [(i, target(i)) for i in range(replicas)])]
    ppermute x50 -> x52, starting transfers between devices: 22.9 us -> 24.6 us  [permute(): return lax.ppermute(v, 'dp', [(i, target(i)) for i in range(replicas)])]
  transfers between devices with their start and end apart: 51 -> 53, of which waited for: 14 -> 16; matrix products, arithmetic and copies ran while one was open for 6% -> 7% of each run, Pallas kernels for 34% -> 31%
where the time goes in v1:
time: 369 us; the launch traced here: 368 us
  waiting for transfers between devices  191 us (52%)
  Pallas kernels  119 us (32%)
  starting transfers between devices  27.7 us (8%)
  other arithmetic  19.9 us (5%)
  local copies, waits for them, and re-layouts  9.35 us (3%)
    ppermute x52, waiting for transfers between devices, permute(): return lax.ppermute(v, 'dp', [(i, target(i)) for i in range(replicas)])  180 us
    pallas_call x1, Pallas kernels, orthonormal_basis(): pl.pallas_call(functools.partial(basis_kernel, pieces=len(pieces), fresh=...  40.4 us
    pallas_call x4, Pallas kernels, project(): pl.pallas_call(project_kernel, out_shape=(out, out), grid_spec=pltpu.Pref...  24.8 us
    pallas_call x4, Pallas kernels, expand(): pl.pallas_call(expand_kernel, out_shape=jax.ShapeDtypeStruct((mats, local...  24.7 us
    ppermute x52, starting transfers between devices, permute(): return lax.ppermute(v, 'dp', [(i, target(i)) for i in range(replicas)])  24.6 us
    pallas_call x2, Pallas kernels, gram_of(): pl.pallas_call(functools.partial(gram_kernel, pieces=len(pieces)), out_sh...  12 us
    ppermute x1, waiting for transfers between devices, shards(): lax.ppermute(part, 'fsdp', [(i, (i + shift) % splits) for i in range(spli...  11.3 us
    pallas_call x1, Pallas kernels, collect_moments(): pl.pallas_call(collect_kernel, out_shape=jax.ShapeDtypeStruct((kinds, mat...  8.59 us
  transfers between devices with their start and end apart: 53, of which 16 were waited for; matrix products, arithmetic and copies ran while one was open for 7% of the time, Pallas kernels for 31%

profile of v1, /device:TPU:0, one launch (start us, length us, event | category | flops | bytes accessed | tf_op | source)
XLA Modules:
  0.0 367.9 jit_solution(611410877932408902)
XLA Ops:
  1.7 3.1 collective-permute-start
  5.4 11.3 %collective-permute-done.refs_0_.refs_1_ = f32[2,128,512]{2,1,0:T(8,128)S(1)} collective-permute-done((f32[2,128,512]{2,1,0:T(8,128)S(1)}, f32[2,128,512]{2,1,0:T(8,128)S(1)}, u32[]{:S(2)}, u32[]{:S(2)}) %collective-permute-start) | collective-permute-done | bytes 524320 | tf_op jit(solution)/shard_map/ppermute | solution.py:431
  16.7 1.7 collective-permute-start.1
  18.4 2.6 fusion.5
  21.3 8.5 %collective-permute-done.1.refs_2_ = f32[2,128,512]{2,1,0:T(8,128)S(1)} collective-permute-done((f32[2,128,512]{2,1,0:T(8,128)S(1)}, f32[2,128,512]{2,1,0:T(8,128)S(1)}, u32[]{:S(2)}, u32[]{:S(2)}) %collective-permute-start.1) | collective-permute-done | bytes 524320 | tf_op jit(solution)/shard_map/ppermute | solution.py:414
  30.5 5.9 %gram.2.refs_2_ = f32[2,512,512]{2,1,0:T(8,128)} custom-call(f32[2,512,512]{2,1,0:T(8,128)} %refs_0_.3), custom_call_target="tpu_custom_call" | custom-call | flops 3221225472 | bytes 4194304 | tf_op jit(solution)/shard_map/gram/pallas_call | solution.py:130
  36.4 6.1 %gram.3.refs_5_ = f32[2,512,512]{2,1,0:T(8,128)} custom-call(f32[2,128,512]{2,1,0:T(8,128)} %copy-done.30, f32[2,128,512]{2,1,0:T(8,128)} %collective-permute-done.2.refs_1_.refs_3_, f32[2,512,512]{2,1,0:T(8,128)} %gram.2.refs_2_), custom_call_target="tpu_custom_call" | custom-call | flops 1610612736 | bytes 3145728 | tf_op jit(solution)/shard_map/gram/pallas_call | solution.py:130
  42.5 1.4 collective-permute-start.4
  44.0 40.4 %basis.1.basis_ref.refs_4_ = bf16[2,1024,512]{2,1,0:T(8,128)(2,1)} custom-call(s32[5]{0:T(128)} %stack.76.offsets, f32[2,512,512]{2,1,0:T(8,128)} %refs_0_.3, f32[2,128,512]{2,1,0:T(8,128)} %copy-done.30, f32[2,128,512]{2,1,0:T(8,128)} %copy-done.31, f32[2,128,512]{2,1,0:T(8,128)} %collective-permute-done.2.refs_1_.refs_3_, ...), custom_call_target="tpu_custom_call" | custom-call | flops 40000000000 | bytes 6291456 | tf_op jit(solution)/shard_map/basis/pallas_call | solution.py:196
  84.4 6.3 %project.7 = (bf16[2,2,256,512]{3,2,1,0:T(8,128)(2,1)}, bf16[2,2,256,512]{3,2,1,0:T(8,128)(2,1)}) custom-call(s32[4]{0:T(128)} %pad_add_fusion.2.quads, s32[1]{0:T(128)} %bitcast.27.group, bf16[1,2,4096,1024]{3,2,1,0:T(8,128)(2,1)} %grads_ref.7, bf16[2,1024,512]{2,1,0:T(8,128)(2,1)} %basis.1.basis_ref.refs_4_), custom_call_target="tpu_custom_call" | custom-call | flops 2147483648 | bytes 6291456 | tf_op jit(solution)/shard_map/project/pallas_call | solution.py:264
  91.8 6.2 %project.6 = (bf16[2,2,256,512]{3,2,1,0:T(8,128)(2,1)}, bf16[2,2,256,512]{3,2,1,0:T(8,128)(2,1)}) custom-call(s32[4]{0:T(128)} %pad_add_fusion.2.quads, s32[1]{0:T(128)} %bitcast.24.group, bf16[1,2,4096,1024]{3,2,1,0:T(8,128)(2,1)} %grads_ref.7, bf16[2,1024,512]{2,1,0:T(8,128)(2,1)} %basis.1.basis_ref.refs_4_), custom_call_target="tpu_custom_call" | custom-call | flops 2147483648 | bytes 6291456 | tf_op jit(solution)/shard_map/project/pallas_call | solution.py:264
  98.9 2.1 fusion.18
  101.6 6.2 %project.5 = (bf16[2,2,256,512]{3,2,1,0:T(8,128)(2,1)}, bf16[2,2,256,512]{3,2,1,0:T(8,128)(2,1)}) custom-call(s32[4]{0:T(128)} %pad_add_fusion.2.quads, s32[1]{0:T(128)} %bitcast.4.group, bf16[1,2,4096,1024]{3,2,1,0:T(8,128)(2,1)} %grads_ref.7, bf16[2,1024,512]{2,1,0:T(8,128)(2,1)} %basis.1.basis_ref.refs_4_), custom_call_target="tpu_custom_call" | custom-call | flops 2147483648 | bytes 6291456 | tf_op jit(solution)/shard_map/project/pallas_call | solution.py:264
  107.8 6.2 %project.4 = (bf16[2,2,256,512]{3,2,1,0:T(8,128)(2,1)}, bf16[2,2,256,512]{3,2,1,0:T(8,128)(2,1)}) custom-call(s32[4]{0:T(128)} %pad_add_fusion.2.quads, s32[1]{0:T(128)} %bitcast.14.group, bf16[1,2,4096,1024]{3,2,1,0:T(8,128)(2,1)} %grads_ref.7, bf16[2,1024,512]{2,1,0:T(8,128)(2,1)} %basis.1.basis_ref.refs_4_), custom_call_target="tpu_custom_call" | custom-call | flops 2147483648 | bytes 6291456 | tf_op jit(solution)/shard_map/project/pallas_call | solution.py:264
  115.5 2.1 fusion.17
  117.6 1.4 collective-permute-start.15
  119.1 2.4 fusion.7
  121.4 1.6 collective-permute-start.18
  123.0 1.3 convert_reduce_fusion.1
  124.3 8.6 %collect.1 = bf16[2,2,1024,512]{3,2,1,0:T(8,128)(2,1)} custom-call(s32[4,2,32]{2,1,0:T(2,128)} %get-tuple-element.42.places, s32[4,2]{1,0:T(4,128)} %get-tuple-element.41.counts, bf16[2,2,32,16,512]{4,3,2,1,0:T(8,128)(2,1)} %copy-done.1, bf16[2,2,32,16,512]{4,3,2,1,0:T(8,128)(2,1)} %collective-permute-done.4.refs_1_, ...), custom_call_target="tpu_custom_call" | custom-call | bytes 16777216 | tf_op jit(solution)/shard_map/collect/pallas_call | solution.py:234
  132.9 1.4 slice.112
  134.3 2.3 collective-permute-start.7
  136.7 1.3 fusion.16
  138.5 1.8 fusion.9
  140.3 1.7 collective-permute-start.19
  142.1 1.2 collective-permute-start.11
  143.3 18.9 %collective-permute-done.7 = bf16[2,2,256,512]{3,2,1,0:T(8,128)(2,1)S(1)} collective-permute-done((bf16[2,2,256,512]{3,2,1,0:T(8,128)(2,1)S(1)}, bf16[2,2,256,512]{3,2,1,0:T(8,128)(2,1)S(1)}, u32[]{:S(2)}, u32[]{:S(2)}) %collective-permute-start.7) | collective-permute-done | bytes 1048608 | tf_op jit(solution)/shard_map/ppermute | solution.py:414
  162.8 10.6 %collective-permute-done.19 = bf16[2,256,512]{2,1,0:T(8,128)(2,1)S(1)} collective-permute-done((bf16[2,256,512]{2,1,0:T(8,128)(2,1)S(1)}, bf16[2,256,512]{2,1,0:T(8,128)(2,1)S(1)}, u32[]{:S(2)}, u32[]{:S(2)}) %collective-permute-start.19) | collective-permute-done | bytes 524320 | tf_op jit(solution)/shard_map/ppermute | solution.py:414
  173.4 1.3 fusion.11
  175.3 30.3 %collective-permute-done.20 = bf16[2,256,512]{2,1,0:T(8,128)(2,1)S(1)} collective-permute-done((bf16[2,256,512]{2,1,0:T(8,128)(2,1)S(1)}, bf16[2,256,512]{2,1,0:T(8,128)(2,1)S(1)}, u32[]{:S(2)}, u32[]{:S(2)}) %collective-permute-start.20) | collective-permute-done | bytes 524320 | tf_op jit(solution)/shard_map/ppermute | solution.py:414
  206.6 1.6 collective-permute-start.9
  208.2 14.4 %collective-permute-done.40.refs_4_ = bf16[2,256,512]{2,1,0:T(8,128)(2,1)S(1)} collective-permute-done((bf16[2,256,512]{2,1,0:T(8,128)(2,1)S(1)}, bf16[2,256,512]{2,1,0:T(8,128)(2,1)S(1)}, u32[]{:S(2)}, u32[]{:S(2)}) %collective-permute-start.40) | collective-permute-done | bytes 524320 | tf_op jit(solution)/shard_map/ppermute | solution.py:414
  223.1 30.8 %collective-permute-done.44.refs_8_ = bf16[2,256,512]{2,1,0:T(8,128)(2,1)S(1)} collective-permute-done((bf16[2,256,512]{2,1,0:T(8,128)(2,1)S(1)}, bf16[2,256,512]{2,1,0:T(8,128)(2,1)S(1)}, u32[]{:S(2)}, u32[]{:S(2)}) %collective-permute-start.44) | collective-permute-done | bytes 524320 | tf_op jit(solution)/shard_map/ppermute | solution.py:414
  255.7 1.5 collective-permute-start.41
  257.2 13.4 %collective-permute-done.48.refs_12_ = bf16[2,256,512]{2,1,0:T(8,128)(2,1)S(1)} collective-permute-done((bf16[2,256,512]{2,1,0:T(8,128)(2,1)S(1)}, bf16[2,256,512]{2,1,0:T(8,128)(2,1)S(1)}, u32[]{:S(2)}, u32[]{:S(2)}) %collective-permute-start.48) | collective-permute-done | bytes 524320 | tf_op jit(solution)/shard_map/ppermute | solution.py:414
  270.5 8.1 %collective-permute-done.21.refs_0_ = bf16[2,256,512]{2,1,0:T(8,128)(2,1)} collective-permute-done((bf16[2,256,512]{2,1,0:T(8,128)(2,1)S(1)}, bf16[2,256,512]{2,1,0:T(8,128)(2,1)}, u32[]{:S(2)}, u32[]{:S(2)}) %collective-permute-start.21) | collective-permute-done | bytes 524320 | tf_op jit(solution)/shard_map/ppermute | solution.py:414
  280.0 5.1 %collective-permute-done.49 = bf16[1,256,512]{2,1,0:T(8,128)(2,1)S(1)} collective-permute-done((bf16[1,256,512]{2,1,0:T(8,128)(2,1)S(1)}, bf16[1,256,512]{2,1,0:T(8,128)(2,1)S(1)}, u32[]{:S(2)}, u32[]{:S(2)}) %collective-permute-start.49) | collective-permute-done | bytes 262176 | tf_op jit(solution)/shard_map/ppermute | solution.py:414
  285.1 9.0 %collective-permute-done.22.refs_0_ = bf16[2,256,512]{2,1,0:T(8,128)(2,1)S(1)} collective-permute-done((bf16[2,256,512]{2,1,0:T(8,128)(2,1)}, bf16[2,256,512]{2,1,0:T(8,128)(2,1)S(1)}, u32[]{:S(2)}, u32[]{:S(2)}) %collective-permute-start.22) | collective-permute-done | bytes 524320 | tf_op jit(solution)/shard_map/ppermute | solution.py:414
  294.6 2.4 collective-permute-done.50
  297.8 8.7 %collective-permute-done.25.refs_1_ = bf16[2,256,512]{2,1,0:T(8,128)(2,1)S(1)} collective-permute-done((bf16[2,256,512]{2,1,0:T(8,128)(2,1)S(1)}, bf16[2,256,512]{2,1,0:T(8,128)(2,1)S(1)}, u32[]{:S(2)}, u32[]{:S(2)}) %collective-permute-start.25) | collective-permute-done | bytes 524320 | tf_op jit(solution)/shard_map/ppermute | solution.py:414
  306.5 2.2 collective-permute-done.23.refs_0_
  310.6 7.2 %collective-permute-done.34.refs_1_ = bf16[2,256,512]{2,1,0:T(8,128)(2,1)} collective-permute-done((bf16[2,256,512]{2,1,0:T(8,128)(2,1)S(1)}, bf16[2,256,512]{2,1,0:T(8,128)(2,1)}, u32[]{:S(2)}, u32[]{:S(2)}) %collective-permute-start.34) | collective-permute-done | bytes 524320 | tf_op jit(solution)/shard_map/ppermute | solution.py:414
  318.8 9.9 %collective-permute-done.31.refs_1_ = bf16[2,256,512]{2,1,0:T(8,128)(2,1)} collective-permute-done((bf16[2,256,512]{2,1,0:T(8,128)(2,1)}, bf16[2,256,512]{2,1,0:T(8,128)(2,1)}, u32[]{:S(2)}, u32[]{:S(2)}) %collective-permute-start.31) | collective-permute-done | bytes 524320 | tf_op jit(solution)/shard_map/ppermute | solution.py:414
  329.4 8.2 %settle.1 = (f32[2,1,32,16,512]{4,3,2,1,0:T(8,128)}, f32[2,1,32,16,512]{4,3,2,1,0:T(8,128)}) custom-call(s32[2,32]{1,0:T(2,128)} %get-tuple-element.40.piece_of, s32[2,32]{1,0:T(2,128)} %get-tuple-element.39.row_of, s32[2,32]{1,0:T(2,128)} %fusion.30.held, bf16[2,256,512]{2,1,0:T(8,128)(2,1)} %copy-done.2, bf16[2,256,512]{2,1,0:T(8,128)(2,1)} %copy-done.21, ...), custom_call_target="tpu_custom_call" | custom-call | flops 4194304 | bytes 9437184 | tf_op jit(solution)/shard_map/settle/pallas_call | solution.py:368
  340.7 6.2 %expand.4.refs_5_ = bf16[2,4096,1024]{2,1,0:T(8,128)(2,1)} custom-call(s32[4]{0:T(128)} %pad_add_fusion.quads, s32[1]{0:T(128)} %bitcast.31.group, bf16[2,256,512]{2,1,0:T(8,128)(2,1)} %copy-done.3, bf16[2,256,512]{2,1,0:T(8,128)(2,1)} %collective-permute-done.34.refs_1_, bf16[2,256,512]{2,1,0:T(8,128)(2,1)} %collective-permute-done.35.refs_2_, ...), custom_call_target="tpu_custom_call" | custom-call | flops 2147483648 | bytes 6291456 | tf_op jit(solution)/shard_map/expand/pallas_call | solution.py:308
  346.9 6.2 %expand.5.refs_5_ = bf16[2,4096,1024]{2,1,0:T(8,128)(2,1)} custom-call(s32[4]{0:T(128)} %pad_add_fusion.quads, s32[1]{0:T(128)} %bitcast.27.group, bf16[2,256,512]{2,1,0:T(8,128)(2,1)} %collective-permute-done.21.refs_0_, bf16[2,256,512]{2,1,0:T(8,128)(2,1)} %collective-permute-done.31.refs_1_, ...), custom_call_target="tpu_custom_call", output_to_operand_aliasing={{}: (7, {})} | custom-call | flops 2147483648 | bytes 6291456 | tf_op jit(solution)/shard_map/expand/pallas_call | solution.py:308
  354.7 6.2 %expand.6.refs_5_ = bf16[2,4096,1024]{2,1,0:T(8,128)(2,1)} custom-call(s32[4]{0:T(128)} %pad_add_fusion.quads, s32[1]{0:T(128)} %bitcast.24.group, bf16[2,256,512]{2,1,0:T(8,128)(2,1)} %copy-done.15, bf16[2,256,512]{2,1,0:T(8,128)(2,1)} %copy-done.5, bf16[2,256,512]{2,1,0:T(8,128)(2,1)} %copy-done.16, ...), custom_call_target="tpu_custom_call", output_to_operand_aliasing={{}: (7, {})} | custom-call | flops 2147483648 | bytes 6291456 | tf_op jit(solution)/shard_map/expand/pallas_call | solution.py:308
  361.7 6.2 %expand.7 = bf16[2,4096,1024]{2,1,0:T(8,128)(2,1)} custom-call(s32[4]{0:T(128)} %pad_add_fusion.quads, s32[1]{0:T(128)} %bitcast.4.group, bf16[2,256,512]{2,1,0:T(8,128)(2,1)} %copy-done.4, bf16[2,256,512]{2,1,0:T(8,128)(2,1)} %copy-done.6, bf16[2,256,512]{2,1,0:T(8,128)(2,1)} %copy-done.17, ...), custom_call_target="tpu_custom_call", output_to_operand_aliasing={{}: (7, {})} | custom-call | flops 2147483648 | bytes 6291456 | tf_op jit(solution)/shard_map/expand/pallas_call | solution.py:308
  (171 shorter events, 23.3 us)
Async XLA Ops:
  1.7 15.0 %collective-permute-start = (f32[2,128,512]{2,1,0:T(8,128)S(1)}, f32[2,128,512]{2,1,0:T(8,128)S(1)}, u32[]{:S(2)}, u32[]{:S(2)}) collective-permute-start(f32[2,128,512]{2,1,0:T(8,128)S(1)} %constant_dynamic-slice_fusion), channel_id=1, source_target_pairs={{0,1},{1,0},{2,3},{3,2},{4,5},{5,4},{6,7},{7,6},{8,9},{9,8},{10,11... | collective-permute-start | bytes 1572872 | tf_op jit(solution)/shard_map/ppermute | solution.py:431
  16.7 13.1 %collective-permute-start.1 = (f32[2,128,512]{2,1,0:T(8,128)S(1)}, f32[2,128,512]{2,1,0:T(8,128)S(1)}, u32[]{:S(2)}, u32[]{:S(2)}) collective-permute-start(f32[2,128,512]{2,1,0:T(8,128)S(1)} %collective-permute-done.refs_0_.refs_1_), channel_id=1, source_target_pairs={{0,4},{2,6},{4,0},{6,2},{8,12},{10,14},{12,8},{14,10},{16,20},{18,... | collective-permute-start | bytes 1572872 | tf_op jit(solution)/shard_map/ppermute | solution.py:414
  21.0 15.4 %collective-permute-start.2 = (f32[2,128,512]{2,1,0:T(8,128)S(1)}, f32[2,128,512]{2,1,0:T(8,128)}, u32[]{:S(2)}, u32[]{:S(2)}) collective-permute-start(f32[2,128,512]{2,1,0:T(8,128)S(1)} %collective-permute-done.refs_0_.refs_1_), channel_id=1, source_target_pairs={{0,2},{2,0},{4,6},{6,4},{8,10},{10,8},{12,14},{14,12},{16,18},{18,... | collective-permute-start | bytes 1572872 | tf_op jit(solution)/shard_map/ppermute | solution.py:414
  29.8 12.7 %collective-permute-start.3 = (f32[2,128,512]{2,1,0:T(8,128)S(1)}, f32[2,128,512]{2,1,0:T(8,128)}, u32[]{:S(2)}, u32[]{:S(2)}) collective-permute-start(f32[2,128,512]{2,1,0:T(8,128)S(1)} %collective-permute-done.1.refs_2_), channel_id=1, source_target_pairs={{0,2},{2,0},{4,6},{6,4},{8,10},{10,8},{12,14},{14,12},{16,18},{18,... | collective-permute-start | bytes 1572872 | tf_op jit(solution)/shard_map/ppermute | solution.py:414
  42.5 49.0 %collective-permute-start.4 = (bf16[2,2,32,16,512]{4,3,2,1,0:T(8,128)(2,1)S(1)}, bf16[2,2,32,16,512]{4,3,2,1,0:T(8,128)(2,1)}, u32[]{:S(2)}, u32[]{:S(2)}) collective-permute-start(bf16[2,2,32,16,512]{4,3,2,1,0:T(8,128)(2,1)S(1)} %pad_maximum_fusion.refs_0_), channel_id=1, source_target_pairs={{0,4},{2,6},{4,0},{6,2},{8,12},{10,14},{12,8},{14,10},{16,20},{18,... | collective-permute-start | bytes 6291464 | tf_op jit(solution)/shard_map/ppermute | solution.py:414
  90.9 30.6 %collective-permute-start.5 = (bf16[2,2,32,16,512]{4,3,2,1,0:T(8,128)(2,1)S(1)}, bf16[2,2,32,16,512]{4,3,2,1,0:T(8,128)(2,1)}, u32[]{:S(2)}, u32[]{:S(2)}) collective-permute-start(bf16[2,2,32,16,512]{4,3,2,1,0:T(8,128)(2,1)S(1)} %pad_maximum_fusion.refs_0_), channel_id=1, source_target_pairs={{0,2},{2,0},{4,6},{6,4},{8,10},{10,8},{12,14},{14,12},{16,18},{18,... | collective-permute-start | bytes 6291464 | tf_op jit(solution)/shard_map/ppermute | solution.py:414
  91.5 32.7 %collective-permute-start.6 = (bf16[2,2,32,16,512]{4,3,2,1,0:T(8,128)(2,1)}, bf16[2,2,32,16,512]{4,3,2,1,0:T(8,128)(2,1)}, u32[]{:S(2)}, u32[]{:S(2)}) collective-permute-start(bf16[2,2,32,16,512]{4,3,2,1,0:T(8,128)(2,1)} %collective-permute-done.4.refs_1_), channel_id=1, source_target_pairs={{0,2},{2,0},{4,6},{6,4},{8,10},{10,8},{12,14},{14,12},{16,18},{18,... | collective-permute-start | bytes 6291464 | tf_op jit(solution)/shard_map/ppermute | solution.py:414
  98.0 16.0 %collective-permute-start.14 = (bf16[2,2,256,512]{3,2,1,0:T(8,128)(2,1)}, bf16[2,2,256,512]{3,2,1,0:T(8,128)(2,1)S(1)}, u32[]{:S(2)}, u32[]{:S(2)}) collective-permute-start(bf16[2,2,256,512]{3,2,1,0:T(8,128)(2,1)} %get-tuple-element.30), channel_id=1, source_target_pairs={{0,2},{2,0},{4,6},{6,4},{8,10},{10,8},{12,14},{14,12},{16,18},{18,... | collective-permute-start | bytes 3145736 | tf_op jit(solution)/shard_map/ppermute | solution.py:414
  101.0 16.6 %collective-permute-start.17 = (bf16[2,256,512]{2,1,0:T(8,128)(2,1)}, bf16[2,256,512]{2,1,0:T(8,128)(2,1)}, u32[]{:S(2)}, u32[]{:S(2)}) collective-permute-start(bf16[2,256,512]{2,1,0:T(8,128)(2,1)} %fusion.18), channel_id=1, source_target_pairs={{0,4},{2,6},{4,0},{6,2},{8,12},{10,14},{12,8},{14,10},{16,20},{18,... | collective-permute-start | bytes 1572872 | tf_op jit(solution)/shard_map/ppermute | solution.py:414
  107.8 28.8 %collective-permute-start.12 = (bf16[2,2,256,512]{3,2,1,0:T(8,128)(2,1)}, bf16[2,2,256,512]{3,2,1,0:T(8,128)(2,1)}, u32[]{:S(2)}, u32[]{:S(2)}) collective-permute-start(bf16[2,2,256,512]{3,2,1,0:T(8,128)(2,1)} %get-tuple-element.28), channel_id=1, source_target_pairs={{0,2},{2,0},{4,6},{6,4},{8,10},{10,8},{12,14},{14,12},{16,18},{18,... | collective-permute-start | bytes 3145736 | tf_op jit(solution)/shard_map/ppermute | solution.py:414
  115.0 27.0 %collective-permute-start.10 = (bf16[2,2,256,512]{3,2,1,0:T(8,128)(2,1)}, bf16[2,2,256,512]{3,2,1,0:T(8,128)(2,1)S(1)}, u32[]{:S(2)}, u32[]{:S(2)}) collective-permute-start(bf16[2,2,256,512]{3,2,1,0:T(8,128)(2,1)} %get-tuple-element.26), channel_id=1, source_target_pairs={{0,2},{2,0},{4,6},{6,4},{8,10},{10,8},{12,14},{14,12},{16,18},{18,... | collective-permute-start | bytes 3145736 | tf_op jit(solution)/shard_map/ppermute | solution.py:414
  117.6 20.9 %collective-permute-start.15 = (bf16[2,256,512]{2,1,0:T(8,128)(2,1)}, bf16[2,256,512]{2,1,0:T(8,128)(2,1)}, u32[]{:S(2)}, u32[]{:S(2)}) collective-permute-start(bf16[2,256,512]{2,1,0:T(8,128)(2,1)} %fusion.17), channel_id=1, source_target_pairs={{0,4},{2,6},{4,0},{6,2},{8,12},{10,14},{12,8},{14,10},{16,20},{18,... | collective-permute-start | bytes 1572872 | tf_op jit(solution)/shard_map/ppermute | solution.py:414
  121.4 17.1 %collective-permute-start.18 = (bf16[2,256,512]{2,1,0:T(8,128)(2,1)}, bf16[2,256,512]{2,1,0:T(8,128)(2,1)}, u32[]{:S(2)}, u32[]{:S(2)}) collective-permute-start(bf16[2,256,512]{2,1,0:T(8,128)(2,1)} %fusion.7), channel_id=1, source_target_pairs={{0,8},{2,10},{4,12},{6,14},{8,16},{10,18},{12,20},{14,22},{16,24},... | collective-permute-start | bytes 1572872 | tf_op jit(solution)/shard_map/ppermute | solution.py:414
  134.3 27.9 %collective-permute-start.7 = (bf16[2,2,256,512]{3,2,1,0:T(8,128)(2,1)S(1)}, bf16[2,2,256,512]{3,2,1,0:T(8,128)(2,1)S(1)}, u32[]{:S(2)}, u32[]{:S(2)}) collective-permute-start(bf16[2,2,256,512]{3,2,1,0:T(8,128)(2,1)S(1)} %slice.112), channel_id=1, source_target_pairs={{0,8},{2,10},{4,12},{6,14},{8,16},{10,18},{12,20},{14,22},{16,24},... | collective-permute-start | bytes 3145736 | tf_op jit(solution)/shard_map/ppermute | solution.py:414
  137.9 24.9 %collective-permute-start.13 = (bf16[2,256,512]{2,1,0:T(8,128)(2,1)S(1)}, bf16[2,256,512]{2,1,0:T(8,128)(2,1)S(1)}, u32[]{:S(2)}, u32[]{:S(2)}) collective-permute-start(bf16[2,256,512]{2,1,0:T(8,128)(2,1)S(1)} %fusion.16), channel_id=1, source_target_pairs={{0,4},{2,6},{4,0},{6,2},{8,12},{10,14},{12,8},{14,10},{16,20},{18,... | collective-permute-start | bytes 1572872 | tf_op jit(solution)/shard_map/ppermute | solution.py:414
  140.3 33.1 %collective-permute-start.19 = (bf16[2,256,512]{2,1,0:T(8,128)(2,1)S(1)}, bf16[2,256,512]{2,1,0:T(8,128)(2,1)S(1)}, u32[]{:S(2)}, u32[]{:S(2)}) collective-permute-start(bf16[2,256,512]{2,1,0:T(8,128)(2,1)S(1)} %fusion.9), channel_id=1, source_target_pairs={{0,8},{2,10},{4,12},{6,14},{8,16},{10,18},{12,20},{14,22},{16,24},... | collective-permute-start | bytes 1572872 | tf_op jit(solution)/shard_map/ppermute | solution.py:414
  142.1 33.2 %collective-permute-start.11 = (bf16[2,256,512]{2,1,0:T(8,128)(2,1)S(1)}, bf16[2,256,512]{2,1,0:T(8,128)(2,1)S(1)}, u32[]{:S(2)}, u32[]{:S(2)}) collective-permute-start(bf16[2,256,512]{2,1,0:T(8,128)(2,1)S(1)} %fusion.15), channel_id=1, source_target_pairs={{0,4},{2,6},{4,0},{6,2},{8,12},{10,14},{12,8},{14,10},{16,20},{18,... | collective-permute-start | bytes 1572872 | tf_op jit(solution)/shard_map/ppermute | solution.py:414
  162.3 44.1 %collective-permute-start.8 = (bf16[2,2,256,512]{3,2,1,0:T(8,128)(2,1)S(1)}, bf16[2,2,256,512]{3,2,1,0:T(8,128)(2,1)S(1)}, u32[]{:S(2)}, u32[]{:S(2)}) collective-permute-start(bf16[2,2,256,512]{3,2,1,0:T(8,128)(2,1)S(1)} %slice_add_fusion.2), channel_id=1, source_target_pairs={{0,8},{2,10},{4,12},{6,14},{8,16},{10,18},{12,20},{14,22},{16,24},... | collective-permute-start | bytes 3145736 | tf_op jit(solution)/shard_map/ppermute | solution.py:414
  174.8 30.9 %collective-permute-start.20 = (bf16[2,256,512]{2,1,0:T(8,128)(2,1)S(1)}, bf16[2,256,512]{2,1,0:T(8,128)(2,1)S(1)}, u32[]{:S(2)}, u32[]{:S(2)}) collective-permute-start(bf16[2,256,512]{2,1,0:T(8,128)(2,1)S(1)} %fusion.11), channel_id=1, source_target_pairs={{0,8},{2,10},{4,12},{6,14},{8,16},{10,18},{12,20},{14,22},{16,24},... | collective-permute-start | bytes 1572872 | tf_op jit(solution)/shard_map/ppermute | solution.py:414
  206.0 16.6 %collective-permute-start.40 = (bf16[2,256,512]{2,1,0:T(8,128)(2,1)S(1)}, bf16[2,256,512]{2,1,0:T(8,128)(2,1)S(1)}, u32[]{:S(2)}, u32[]{:S(2)}) collective-permute-start(bf16[2,256,512]{2,1,0:T(8,128)(2,1)S(1)} %get-tuple-element.34.refs_0_), channel_id=1, source_target_pairs={{0,8},{2,10},{4,12},{6,14},{8,16},{10,18},{12,20},{14,22},{16,24},... | collective-permute-start | bytes 1572872 | tf_op jit(solution)/shard_map/ppermute | solution.py:414
  206.6 47.4 %collective-permute-start.9 = (bf16[2,2,256,512]{3,2,1,0:T(8,128)(2,1)S(1)}, bf16[2,2,256,512]{3,2,1,0:T(8,128)(2,1)S(1)}, u32[]{:S(2)}, u32[]{:S(2)}) collective-permute-start(bf16[2,2,256,512]{3,2,1,0:T(8,128)(2,1)S(1)} %slice_add_fusion.1), channel_id=1, source_target_pairs={{0,8},{2,10},{4,12},{6,14},{8,16},{10,18},{12,20},{14,22},{16,24},... | collective-permute-start | bytes 3145736 | tf_op jit(solution)/shard_map/ppermute | solution.py:414
  222.6 31.3 %collective-permute-start.44 = (bf16[2,256,512]{2,1,0:T(8,128)(2,1)S(1)}, bf16[2,256,512]{2,1,0:T(8,128)(2,1)S(1)}, u32[]{:S(2)}, u32[]{:S(2)}) collective-permute-start(bf16[2,256,512]{2,1,0:T(8,128)(2,1)S(1)} %collective-permute-done.40.refs_4_), channel_id=1, source_target_pairs={{0,8},{2,10},{4,12},{6,14},{8,16},{10,18},{12,20},{14,22},{16,24},... | collective-permute-start | bytes 1572872 | tf_op jit(solution)/shard_map/ppermute | solution.py:414
  222.6 33.1 %collective-permute-start.37 = (bf16[2,256,512]{2,1,0:T(8,128)(2,1)S(1)}, bf16[2,256,512]{2,1,0:T(8,128)(2,1)S(1)}, u32[]{:S(2)}, u32[]{:S(2)}) collective-permute-start(bf16[2,256,512]{2,1,0:T(8,128)(2,1)S(1)} %get-tuple-element.34.refs_0_), channel_id=1, source_target_pairs={{0,4},{2,6},{4,0},{6,2},{8,12},{10,14},{12,8},{14,10},{16,20},{18,... | collective-permute-start | bytes 1572872 | tf_op jit(solution)/shard_map/ppermute | solution.py:414
  223.1 34.0 %collective-permute-start.38 = (bf16[2,256,512]{2,1,0:T(8,128)(2,1)S(1)}, bf16[2,256,512]{2,1,0:T(8,128)(2,1)S(1)}, u32[]{:S(2)}, u32[]{:S(2)}) collective-permute-start(bf16[2,256,512]{2,1,0:T(8,128)(2,1)S(1)} %get-tuple-element.34.refs_0_), channel_id=1, source_target_pairs={{0,2},{2,0},{4,6},{6,4},{8,10},{10,8},{12,14},{14,12},{16,18},{18,... | collective-permute-start | bytes 1572872 | tf_op jit(solution)/shard_map/ppermute | solution.py:414
  253.9 16.6 %collective-permute-start.48 = (bf16[2,256,512]{2,1,0:T(8,128)(2,1)S(1)}, bf16[2,256,512]{2,1,0:T(8,128)(2,1)S(1)}, u32[]{:S(2)}, u32[]{:S(2)}) collective-permute-start(bf16[2,256,512]{2,1,0:T(8,128)(2,1)S(1)} %collective-permute-done.44.refs_8_), channel_id=1, source_target_pairs={{0,8},{2,10},{4,12},{6,14},{8,16},{10,18},{12,20},{14,22},{16,24},... | collective-permute-start | bytes 1572872 | tf_op jit(solution)/shard_map/ppermute | solution.py:414
  254.9 23.8 %collective-permute-start.21 = (bf16[2,256,512]{2,1,0:T(8,128)(2,1)S(1)}, bf16[2,256,512]{2,1,0:T(8,128)(2,1)}, u32[]{:S(2)}, u32[]{:S(2)}) collective-permute-start(bf16[2,256,512]{2,1,0:T(8,128)(2,1)S(1)} %fusion.14.refs_0_), channel_id=1, source_target_pairs={{0,8},{2,10},{4,12},{6,14},{8,16},{10,18},{12,20},{14,22},{16,24},... | collective-permute-start | bytes 1572872 | tf_op jit(solution)/shard_map/ppermute | solution.py:414
  255.1 23.6 %collective-permute-start.45 = (bf16[2,256,512]{2,1,0:T(8,128)(2,1)S(1)}, bf16[2,256,512]{2,1,0:T(8,128)(2,1)S(1)}, u32[]{:S(2)}, u32[]{:S(2)}) collective-permute-start(bf16[2,256,512]{2,1,0:T(8,128)(2,1)S(1)} %collective-permute-done.44.refs_8_), channel_id=1, source_target_pairs={{0,4},{2,6},{4,0},{6,2},{8,12},{10,14},{12,8},{14,10},{16,20},{18,... | collective-permute-start | bytes 1572872 | tf_op jit(solution)/shard_map/ppermute | solution.py:414
  255.7 23.5 %collective-permute-start.41 = (bf16[2,256,512]{2,1,0:T(8,128)(2,1)S(1)}, bf16[2,256,512]{2,1,0:T(8,128)(2,1)S(1)}, u32[]{:S(2)}, u32[]{:S(2)}) collective-permute-start(bf16[2,256,512]{2,1,0:T(8,128)(2,1)S(1)} %collective-permute-done.40.refs_4_), channel_id=1, source_target_pairs={{0,4},{2,6},{4,0},{6,2},{8,12},{10,14},{12,8},{14,10},{16,20},{18,... | collective-permute-start | bytes 1572872 | tf_op jit(solution)/shard_map/ppermute | solution.py:414
  257.2 22.3 %collective-permute-start.39 = (bf16[2,256,512]{2,1,0:T(8,128)(2,1)S(1)}, bf16[2,256,512]{2,1,0:T(8,128)(2,1)S(1)}, u32[]{:S(2)}, u32[]{:S(2)}) collective-permute-start(bf16[2,256,512]{2,1,0:T(8,128)(2,1)S(1)} %collective-permute-done.37.refs_1_), channel_id=1, source_target_pairs={{0,2},{2,0},{4,6},{6,4},{8,10},{10,8},{12,14},{14,12},{16,18},{18,... | collective-permute-start | bytes 1572872 | tf_op jit(solution)/shard_map/ppermute | solution.py:414
  278.7 15.5 %collective-permute-start.22 = (bf16[2,256,512]{2,1,0:T(8,128)(2,1)}, bf16[2,256,512]{2,1,0:T(8,128)(2,1)S(1)}, u32[]{:S(2)}, u32[]{:S(2)}) collective-permute-start(bf16[2,256,512]{2,1,0:T(8,128)(2,1)} %collective-permute-done.21.refs_0_), channel_id=1, source_target_pairs={{0,8},{2,10},{4,12},{6,14},{8,16},{10,18},{12,20},{14,22},{16,24},... | collective-permute-start | bytes 1572872 | tf_op jit(solution)/shard_map/ppermute | solution.py:414
  279.2 17.8 %collective-permute-start.50 = (bf16[1,256,512]{2,1,0:T(8,128)(2,1)S(1)}, bf16[1,256,512]{2,1,0:T(8,128)(2,1)S(1)}, u32[]{:S(2)}, u32[]{:S(2)}) collective-permute-start(bf16[1,256,512]{2,1,0:T(8,128)(2,1)S(1)} %slice.131), channel_id=1, source_target_pairs={{0,8},{2,10},{4,12},{6,14},{8,16},{10,18},{12,20},{14,22},{16,24},... | collective-permute-start | bytes 786440 | tf_op jit(solution)/shard_map/ppermute | solution.py:414
  279.4 17.6 %collective-permute-start.43 = (bf16[2,256,512]{2,1,0:T(8,128)(2,1)S(1)}, bf16[2,256,512]{2,1,0:T(8,128)(2,1)S(1)}, u32[]{:S(2)}, u32[]{:S(2)}) collective-permute-start(bf16[2,256,512]{2,1,0:T(8,128)(2,1)S(1)} %collective-permute-done.41.refs_5_), channel_id=1, source_target_pairs={{0,2},{2,0},{4,6},{6,4},{8,10},{10,8},{12,14},{14,12},{16,18},{18,... | collective-permute-start | bytes 1572872 | tf_op jit(solution)/shard_map/ppermute | solution.py:414
  279.5 17.7 %collective-permute-start.46 = (bf16[2,256,512]{2,1,0:T(8,128)(2,1)S(1)}, bf16[2,256,512]{2,1,0:T(8,128)(2,1)S(1)}, u32[]{:S(2)}, u32[]{:S(2)}) collective-permute-start(bf16[2,256,512]{2,1,0:T(8,128)(2,1)S(1)} %collective-permute-done.44.refs_8_), channel_id=1, source_target_pairs={{0,2},{2,0},{4,6},{6,4},{8,10},{10,8},{12,14},{14,12},{16,18},{18,... | collective-permute-start | bytes 1572872 | tf_op jit(solution)/shard_map/ppermute | solution.py:414
  285.1 12.5 %collective-permute-start.47 = (bf16[2,256,512]{2,1,0:T(8,128)(2,1)S(1)}, bf16[2,256,512]{2,1,0:T(8,128)(2,1)S(1)}, u32[]{:S(2)}, u32[]{:S(2)}) collective-permute-start(bf16[2,256,512]{2,1,0:T(8,128)(2,1)S(1)} %collective-permute-done.45.refs_9_), channel_id=1, source_target_pairs={{0,2},{2,0},{4,6},{6,4},{8,10},{10,8},{12,14},{14,12},{16,18},{18,... | collective-permute-start | bytes 1572872 | tf_op jit(solution)/shard_map/ppermute | solution.py:414
  294.2 12.3 %collective-permute-start.25 = (bf16[2,256,512]{2,1,0:T(8,128)(2,1)S(1)}, bf16[2,256,512]{2,1,0:T(8,128)(2,1)S(1)}, u32[]{:S(2)}, u32[]{:S(2)}) collective-permute-start(bf16[2,256,512]{2,1,0:T(8,128)(2,1)S(1)} %collective-permute-done.22.refs_0_), channel_id=1, source_target_pairs={{0,4},{2,6},{4,0},{6,2},{8,12},{10,14},{12,8},{14,10},{16,20},{18,... | collective-permute-start | bytes 1572872 | tf_op jit(solution)/shard_map/ppermute | solution.py:414
  297.1 13.4 %collective-permute-start.51 = (bf16[2,256,512]{2,1,0:T(8,128)(2,1)S(1)}, bf16[2,256,512]{2,1,0:T(8,128)(2,1)}, u32[]{:S(2)}, u32[]{:S(2)}) collective-permute-start(bf16[2,256,512]{2,1,0:T(8,128)(2,1)S(1)} %collective-permute-done.48.refs_12_), channel_id=1, source_target_pairs={{0,2},{2,0},{4,6},{6,4},{8,10},{10,8},{12,14},{14,12},{16,18},{18,... | collective-permute-start | bytes 1572872 | tf_op jit(solution)/shard_map/ppermute | solution.py:414
  297.2 20.6 %collective-permute-start.34 = (bf16[2,256,512]{2,1,0:T(8,128)(2,1)S(1)}, bf16[2,256,512]{2,1,0:T(8,128)(2,1)}, u32[]{:S(2)}, u32[]{:S(2)}) collective-permute-start(bf16[2,256,512]{2,1,0:T(8,128)(2,1)S(1)} %fusion.14.refs_0_), channel_id=1, source_target_pairs={{0,4},{2,6},{4,0},{6,2},{8,12},{10,14},{12,8},{14,10},{16,20},{18,... | collective-permute-start | bytes 1572872 | tf_op jit(solution)/shard_map/ppermute | solution.py:414
  297.6 20.2 %collective-permute-start.52 = (bf16[2,256,512]{2,1,0:T(8,128)(2,1)S(1)}, bf16[2,256,512]{2,1,0:T(8,128)(2,1)}, u32[]{:S(2)}, u32[]{:S(2)}) collective-permute-start(bf16[2,256,512]{2,1,0:T(8,128)(2,1)S(1)} %constant_dynamic-update-slice_fusion.2.refs_13_), channel_id=1, source_target_pairs={{0,2},{2,0},{4,6},{6,4},{8,10},{10,8},{12,14},{14,12},{16,18},{18,... | collective-permute-start | bytes 1572872 | tf_op jit(solution)/shard_map/ppermute | solution.py:414
  308.7 20.0 %collective-permute-start.31 = (bf16[2,256,512]{2,1,0:T(8,128)(2,1)}, bf16[2,256,512]{2,1,0:T(8,128)(2,1)}, u32[]{:S(2)}, u32[]{:S(2)}) collective-permute-start(bf16[2,256,512]{2,1,0:T(8,128)(2,1)} %collective-permute-done.21.refs_0_), channel_id=1, source_target_pairs={{0,4},{2,6},{4,0},{6,2},{8,12},{10,14},{12,8},{14,10},{16,20},{18,... | collective-permute-start | bytes 1572872 | tf_op jit(solution)/shard_map/ppermute | solution.py:414
  310.5 30.1 %collective-permute-start.32 = (bf16[2,256,512]{2,1,0:T(8,128)(2,1)}, bf16[2,256,512]{2,1,0:T(8,128)(2,1)}, u32[]{:S(2)}, u32[]{:S(2)}) collective-permute-start(bf16[2,256,512]{2,1,0:T(8,128)(2,1)} %collective-permute-done.21.refs_0_), channel_id=1, source_target_pairs={{0,2},{2,0},{4,6},{6,4},{8,10},{10,8},{12,14},{14,12},{16,18},{18,... | collective-permute-start | bytes 1572872 | tf_op jit(solution)/shard_map/ppermute | solution.py:414
  317.8 22.3 %collective-permute-start.36 = (bf16[2,256,512]{2,1,0:T(8,128)(2,1)}, bf16[2,256,512]{2,1,0:T(8,128)(2,1)}, u32[]{:S(2)}, u32[]{:S(2)}) collective-permute-start(bf16[2,256,512]{2,1,0:T(8,128)(2,1)} %collective-permute-done.34.refs_1_), channel_id=1, source_target_pairs={{0,2},{2,0},{4,6},{6,4},{8,10},{10,8},{12,14},{14,12},{16,18},{18,... | collective-permute-start | bytes 1572872 | tf_op jit(solution)/shard_map/ppermute | solution.py:414
  317.8 19.7 %collective-permute-start.24 = (bf16[1,256,512]{2,1,0:T(8,128)(2,1)}, bf16[1,256,512]{2,1,0:T(8,128)(2,1)}, u32[]{:S(2)}, u32[]{:S(2)}) collective-permute-start(bf16[1,256,512]{2,1,0:T(8,128)(2,1)} %slice.126), channel_id=1, source_target_pairs={{0,4},{2,6},{4,0},{6,2},{8,12},{10,14},{12,8},{14,10},{16,20},{18,... | collective-permute-start | bytes 786440 | tf_op jit(solution)/shard_map/ppermute | solution.py:414
  318.2 19.9 %collective-permute-start.26 = (bf16[1,256,512]{2,1,0:T(8,128)(2,1)S(1)}, bf16[1,256,512]{2,1,0:T(8,128)(2,1)}, u32[]{:S(2)}, u32[]{:S(2)}) collective-permute-start(bf16[1,256,512]{2,1,0:T(8,128)(2,1)S(1)} %slice.127), channel_id=1, source_target_pairs={{0,8},{2,10},{4,12},{6,14},{8,16},{10,18},{12,20},{14,22},{16,24},... | collective-permute-start | bytes 786440 | tf_op jit(solution)/shard_map/ppermute | solution.py:414
  328.8 18.2 %collective-permute-start.33 = (bf16[2,256,512]{2,1,0:T(8,128)(2,1)}, bf16[2,256,512]{2,1,0:T(8,128)(2,1)}, u32[]{:S(2)}, u32[]{:S(2)}) collective-permute-start(bf16[2,256,512]{2,1,0:T(8,128)(2,1)} %collective-permute-done.31.refs_1_), channel_id=1, source_target_pairs={{0,2},{2,0},{4,6},{6,4},{8,10},{10,8},{12,14},{14,12},{16,18},{18,... | collective-permute-start | bytes 1572872 | tf_op jit(solution)/shard_map/ppermute | solution.py:414
  337.6 15.5 %collective-permute-start.29 = (bf16[2,256,512]{2,1,0:T(8,128)(2,1)}, bf16[2,256,512]{2,1,0:T(8,128)(2,1)S(1)}, u32[]{:S(2)}, u32[]{:S(2)}) collective-permute-start(bf16[2,256,512]{2,1,0:T(8,128)(2,1)} %copy-done.15), channel_id=1, source_target_pairs={{0,2},{2,0},{4,6},{6,4},{8,10},{10,8},{12,14},{14,12},{16,18},{18,... | collective-permute-start | bytes 1572872 | tf_op jit(solution)/shard_map/ppermute | solution.py:414
  338.1 15.0 %collective-permute-start.30 = (bf16[2,256,512]{2,1,0:T(8,128)(2,1)S(1)}, bf16[2,256,512]{2,1,0:T(8,128)(2,1)S(1)}, u32[]{:S(2)}, u32[]{:S(2)}) collective-permute-start(bf16[2,256,512]{2,1,0:T(8,128)(2,1)S(1)} %collective-permute-done.25.refs_1_), channel_id=1, source_target_pairs={{0,2},{2,0},{4,6},{6,4},{8,10},{10,8},{12,14},{14,12},{16,18},{18,... | collective-permute-start | bytes 1572872 | tf_op jit(solution)/shard_map/ppermute | solution.py:414
  340.2 20.7 %collective-permute-start.27 = (bf16[2,256,512]{2,1,0:T(8,128)(2,1)S(1)}, bf16[2,256,512]{2,1,0:T(8,128)(2,1)S(1)}, u32[]{:S(2)}, u32[]{:S(2)}) collective-permute-start(bf16[2,256,512]{2,1,0:T(8,128)(2,1)S(1)} %collective-permute-done.23.refs_0_), channel_id=1, source_target_pairs={{0,2},{2,0},{4,6},{6,4},{8,10},{10,8},{12,14},{14,12},{16,18},{18,... | collective-permute-start | bytes 1572872 | tf_op jit(solution)/shard_map/ppermute | solution.py:414
  340.6 20.3 %collective-permute-start.28 = (bf16[2,256,512]{2,1,0:T(8,128)(2,1)S(1)}, bf16[2,256,512]{2,1,0:T(8,128)(2,1)}, u32[]{:S(2)}, u32[]{:S(2)}) collective-permute-start(bf16[2,256,512]{2,1,0:T(8,128)(2,1)S(1)} %constant_dynamic-update-slice_fusion.refs_1_), channel_id=1, source_target_pairs={{0,2},{2,0},{4,6},{6,4},{8,10},{10,8},{12,14},{14,12},{16,18},{18,... | collective-permute-start | bytes 1572872 | tf_op jit(solution)/shard_map/ppermute | solution.py:414
  (37 other events, 848.0 us)

commit v2 on v1

--- a/solution.py
+++ b/solution.py
@@ -210,35 +210,46 @@
 
 def collect_kernel(places, counts, *refs):
     m = pl.program_id(1)
-    owner_refs, group_ref = refs[:QUAD], refs[QUAD]
-    bucket_rows = owner_refs[0].shape[3]
-    group_ref[...] = jnp.zeros(group_ref.shape, BF16)
+    owner_refs, (head_ref, rest_ref) = refs[:QUAD], refs[QUAD:]
+    bucket_rows, head_rows = owner_refs[0].shape[3], head_ref.shape[2]
+    for ref in (head_ref, rest_ref):
+        ref[...] = jnp.zeros(ref.shape, BF16)
     for i, owner_ref in enumerate(owner_refs):
 
         def pick(s, _):
             place = places[i, m, s]
 
-            @pl.when(place >= 0)
+            @pl.when(jnp.logical_and(place >= 0, place < head_rows))
             def _():
                 at = pl.multiple_of(jnp.maximum(place, 0), bucket_rows)
-                group_ref[0, 0, pl.ds(at, bucket_rows), :] = owner_ref[0, 0, s]
+                head_ref[0, 0, pl.ds(at, bucket_rows), :] = owner_ref[0, 0, s]
+
+            @pl.when(place >= head_rows)
+            def _():
+                at = pl.multiple_of(jnp.maximum(place - head_rows, 0), bucket_rows)
+                rest_ref[0, 0, pl.ds(at, bucket_rows), :] = owner_ref[0, 0, s]
 
             return 0
 
         lax.fori_loop(0, counts[i, m], pick, 0)
 
 
-def collect_moments(owners, places, counts, column_rows):
+def collect_moments(owners, places, counts, head_rows, rest_rows):
     kinds, mats, capacity, bucket_rows, rank = owners[0].shape
     slots = pl.BlockSpec((1, 1, capacity, bucket_rows, rank), lambda a, m, *_: (a, m, 0, 0, 0))
     return pl.pallas_call(
         collect_kernel,
-        out_shape=jax.ShapeDtypeStruct((kinds, mats, column_rows, rank), BF16),
+        out_shape=tuple(
+            jax.ShapeDtypeStruct((kinds, mats, rows, rank), BF16) for rows in (head_rows, rest_rows)
+        ),
         grid_spec=pltpu.PrefetchScalarGridSpec(
             num_scalar_prefetch=2,
             grid=(kinds, mats),
             in_specs=[slots] * QUAD,
-            out_specs=pl.BlockSpec((1, 1, column_rows, rank), lambda a, m, *_: (a, m, 0, 0)),
+            out_specs=tuple(
+                pl.BlockSpec((1, 1, rows, rank), lambda a, m, *_: (a, m, 0, 0))
+                for rows in (head_rows, rest_rows)
+            ),
         ),
         cost_estimate=pl.CostEstimate(
             flops=0, bytes_accessed=4 * QUAD * owners[0].size, transcendentals=0
@@ -423,18 +434,23 @@
         return permute(v, lambda i: (i + QUAD) % replicas)
 
     quarter = local_feats // QUAD
-    part = lax.dynamic_slice_in_dim(raw_proj, my_quad * quarter, quarter, 1)
+    my_core = me % 2
+    parts = [
+        lax.dynamic_slice_in_dim(raw_proj, (2 * my_core + i) * quarter, quarter, 1) for i in range(2)
+    ]
     my_f = lax.axis_index("fsdp")
     gram = gram_of([raw_proj])
     pieces, offsets, early, fresh = [], [my_f * local_feats], [], []
     for shift in range(1, splits):
-        fetched = lax.ppermute(part, "fsdp", [(i, (i + shift) % splits) for i in range(splits)])
-        across = to_x(fetched)
         base = ((my_f + splits - shift) % splits) * local_feats
-        for piece, flip in ((fetched, 0), (across, 2), (to_core(fetched), 1), (to_core(across), 3)):
-            (fresh if flip & 2 else early).append(len(pieces))
-            pieces.append(piece)
-            offsets.append(base + (my_quad ^ flip) * quarter)
+        for i, indices in ((0, early), (1, fresh)):
+            fetched = lax.ppermute(
+                parts[i], "fsdp", [(j, (j + shift) % splits) for j in range(splits)]
+            )
+            for piece, core in ((fetched, my_core), (to_core(fetched), 1 - my_core)):
+                indices.append(len(pieces))
+                pieces.append(piece)
+                offsets.append(base + (2 * core + i) * quarter)
     offsets = jnp.stack(offsets).astype(jnp.int32)
     if early:
         gram = gram_of([pieces[i] for i in early], gram)
@@ -458,18 +474,17 @@
     places = jnp.where(wanted, places, -1).astype(jnp.int32)
 
     slots = jnp.stack([first_moment[:, 0], second_moment[:, 0]]).astype(BF16)
-    slots, pieces = lax.optimization_barrier((slots, pieces))
     slots_across = to_x(slots)
     slots_core = to_core(slots)
 
     basis = orthonormal_basis(raw_proj, pieces, offsets, gram, fresh, splits * local_feats)
 
     owners = (slots, slots_across, slots_core, to_core(slots_across))
-    column = collect_moments(owners, places, quad_counts, depth * unit_rows)
-    moment_groups = [column[:, :, k * unit_rows : (k + 1) * unit_rows] for k in range(depth)]
-    unit_moments = moment_groups[0]
+    unit_moments, rest = collect_moments(
+        owners, places, quad_counts, unit_rows, (depth - 1) * unit_rows
+    )
     for k in range(1, depth):
-        unit_moments = to_z(unit_moments) + moment_groups[k]
+        unit_moments = to_z(unit_moments) + rest[:, :, (k - 1) * unit_rows : k * unit_rows]
 
     send_quads = jnp.stack([my_quad ^ flip for flip in (3, 1, 2, 0)]).astype(jnp.int32)
     held = None

time: 369 us -> 367 us (level)
  waiting for transfers between devices: 191 us -> 183 us
  starting transfers between devices: 27.7 us -> 33.9 us
    ppermute x52 -> x51, waiting for transfers between devices: 180 us -> 165 us  [permute(): return lax.ppermute(v, 'dp', [(i, target(i)) for i in range(replicas)])]
    ppermute x1 -> x2, waiting for transfers between devices: 11.3 us -> 17.9 us  [shards(): lax.ppermute(parts[i], 'fsdp', [(j, (j + shift) % splits) for j in range(...]
    ppermute x52 -> x51, starting transfers between devices: 24.6 us -> 30.8 us  [permute(): return lax.ppermute(v, 'dp', [(i, target(i)) for i in range(replicas)])]
  transfers between devices with their start and end apart: 53 -> 53, of which waited for: 16 -> 16; matrix products, arithmetic and copies ran while one was open for 7% -> 6% of each run, Pallas kernels for 31% -> 31%
where the time goes in v2:
time: 367 us; the launch traced here: 366 us
  waiting for transfers between devices  183 us (50%)
  Pallas kernels  119 us (32%)
  starting transfers between devices  33.9 us (9%)
  other arithmetic  19.2 us (5%)
  local copies, waits for them, and re-layouts  9.58 us (3%)
    ppermute x51, waiting for transfers between devices, permute(): return lax.ppermute(v, 'dp', [(i, target(i)) for i in range(replicas)])  165 us
    pallas_call x1, Pallas kernels, orthonormal_basis(): pl.pallas_call(functools.partial(basis_kernel, pieces=len(pieces), fresh=...  40.4 us
    ppermute x51, starting transfers between devices, permute(): return lax.ppermute(v, 'dp', [(i, target(i)) for i in range(replicas)])  30.8 us
    pallas_call x4, Pallas kernels, project(): pl.pallas_call(project_kernel, out_shape=(out, out), grid_spec=pltpu.Pref...  24.8 us
    pallas_call x4, Pallas kernels, expand(): pl.pallas_call(expand_kernel, out_shape=jax.ShapeDtypeStruct((mats, local...  24.7 us
    ppermute x2, waiting for transfers between devices, shards(): lax.ppermute(parts[i], 'fsdp', [(j, (j + shift) % splits) for j in range(...  17.9 us
    pallas_call x2, Pallas kernels, gram_of(): pl.pallas_call(functools.partial(gram_kernel, pieces=len(pieces)), out_sh...  12 us
    pallas_call x1, Pallas kernels, collect_moments(): pl.pallas_call(collect_kernel, out_shape=tuple((jax.ShapeDtypeStruct((kin...  9.33 us
  transfers between devices with their start and end apart: 53, of which 16 were waited for; matrix products, arithmetic and copies ran while one was open for 6% of the time, Pallas kernels for 31%

profile of v2, /device:TPU:0, one launch (start us, length us, event | category | flops | bytes accessed | tf_op | source)
XLA Modules:
  0.0 366.0 jit_solution(17977159569119897970)
XLA Ops:
  0.7 1.4 constant_dynamic-slice_fusion
  2.1 3.1 collective-permute-start.6
  5.3 1.9 fusion.5
  7.2 10.8 %collective-permute-done.6.refs_0_.refs_1_ = f32[2,128,512]{2,1,0:T(8,128)S(1)} collective-permute-done((f32[2,128,512]{2,1,0:T(8,128)S(1)}, f32[2,128,512]{2,1,0:T(8,128)S(1)}, u32[]{:S(2)}, u32[]{:S(2)}) %collective-permute-start.6) | collective-permute-done | bytes 524320 | tf_op jit(solution)/shard_map/ppermute | solution.py:447
  18.7 2.0 collective-permute-start
  21.3 7.1 %collective-permute-done.8.refs_3_ = f32[2,128,512]{2,1,0:T(8,128)} collective-permute-done((f32[2,128,512]{2,1,0:T(8,128)S(1)}, f32[2,128,512]{2,1,0:T(8,128)}, u32[]{:S(2)}, u32[]{:S(2)}) %collective-permute-start.8) | collective-permute-done | bytes 524320 | tf_op jit(solution)/shard_map/ppermute | solution.py:447
  29.0 5.9 %gram.2.refs_2_ = f32[2,512,512]{2,1,0:T(8,128)} custom-call(f32[2,512,512]{2,1,0:T(8,128)} %refs_0_.3), custom_call_target="tpu_custom_call" | custom-call | flops 3221225472 | bytes 4194304 | tf_op jit(solution)/shard_map/gram/pallas_call | solution.py:130
  34.9 6.1 %gram.3.refs_5_ = f32[2,512,512]{2,1,0:T(8,128)} custom-call(f32[2,128,512]{2,1,0:T(8,128)} %copy-done.29, f32[2,128,512]{2,1,0:T(8,128)} %collective-permute-done.7.refs_1_.refs_2_, f32[2,512,512]{2,1,0:T(8,128)} %gram.2.refs_2_), custom_call_target="tpu_custom_call" | custom-call | flops 1610612736 | bytes 3145728 | tf_op jit(solution)/shard_map/gram/pallas_call | solution.py:130
  41.8 40.4 %basis.1.basis_ref.refs_4_ = bf16[2,1024,512]{2,1,0:T(8,128)(2,1)} custom-call(s32[5]{0:T(128)} %stack.76.offsets, f32[2,512,512]{2,1,0:T(8,128)} %refs_0_.3, f32[2,128,512]{2,1,0:T(8,128)} %copy-done.29, f32[2,128,512]{2,1,0:T(8,128)} %collective-permute-done.7.refs_1_.refs_2_, f32[2,128,512]{2,1,0:T(8,128)} %collective-permute-done.8.refs_3_, ...), custom_call_target="tpu_custom_call" | custom-call | flops 40000000000 | bytes 6291456 | tf_op jit(solution)/shard_map/basis/pallas_call | solution.py:196
  82.2 6.3 %project.7 = (bf16[2,2,256,512]{3,2,1,0:T(8,128)(2,1)}, bf16[2,2,256,512]{3,2,1,0:T(8,128)(2,1)}) custom-call(s32[4]{0:T(128)} %pad_add_fusion.2.quads, s32[1]{0:T(128)} %bitcast.27.group, bf16[1,2,4096,1024]{3,2,1,0:T(8,128)(2,1)} %grads_ref.7, bf16[2,1024,512]{2,1,0:T(8,128)(2,1)} %basis.1.basis_ref.refs_4_), custom_call_target="tpu_custom_call" | custom-call | flops 2147483648 | bytes 6291456 | tf_op jit(solution)/shard_map/project/pallas_call | solution.py:275
  89.9 6.2 %project.6 = (bf16[2,2,256,512]{3,2,1,0:T(8,128)(2,1)}, bf16[2,2,256,512]{3,2,1,0:T(8,128)(2,1)}) custom-call(s32[4]{0:T(128)} %pad_add_fusion.2.quads, s32[1]{0:T(128)} %bitcast.24.group, bf16[1,2,4096,1024]{3,2,1,0:T(8,128)(2,1)} %grads_ref.7, bf16[2,1024,512]{2,1,0:T(8,128)(2,1)} %basis.1.basis_ref.refs_4_), custom_call_target="tpu_custom_call" | custom-call | flops 2147483648 | bytes 6291456 | tf_op jit(solution)/shard_map/project/pallas_call | solution.py:275
  96.7 2.1 fusion.18
  98.8 1.7 collective-permute-start.17
  100.6 6.2 %project.5 = (bf16[2,2,256,512]{3,2,1,0:T(8,128)(2,1)}, bf16[2,2,256,512]{3,2,1,0:T(8,128)(2,1)}) custom-call(s32[4]{0:T(128)} %pad_add_fusion.2.quads, s32[1]{0:T(128)} %bitcast.4.group, bf16[1,2,4096,1024]{3,2,1,0:T(8,128)(2,1)} %grads_ref.7, bf16[2,1024,512]{2,1,0:T(8,128)(2,1)} %basis.1.basis_ref.refs_4_), custom_call_target="tpu_custom_call" | custom-call | flops 2147483648 | bytes 6291456 | tf_op jit(solution)/shard_map/project/pallas_call | solution.py:275
  106.9 6.2 %project.4 = (bf16[2,2,256,512]{3,2,1,0:T(8,128)(2,1)}, bf16[2,2,256,512]{3,2,1,0:T(8,128)(2,1)}) custom-call(s32[4]{0:T(128)} %pad_add_fusion.2.quads, s32[1]{0:T(128)} %bitcast.14.group, bf16[1,2,4096,1024]{3,2,1,0:T(8,128)(2,1)} %grads_ref.7, bf16[2,1024,512]{2,1,0:T(8,128)(2,1)} %basis.1.basis_ref.refs_4_), custom_call_target="tpu_custom_call" | custom-call | flops 2147483648 | bytes 6291456 | tf_op jit(solution)/shard_map/project/pallas_call | solution.py:275
  114.4 2.1 fusion.17
  116.8 2.4 fusion.7
  119.2 1.8 collective-permute-start.18
  122.3 9.3 %collect.1 = (bf16[2,2,256,512]{3,2,1,0:T(8,128)(2,1)}, bf16[2,2,768,512]{3,2,1,0:T(8,128)(2,1)}) custom-call(s32[4,2,32]{2,1,0:T(2,128)} %get-tuple-element.38.places, s32[4,2]{1,0:T(4,128)} %get-tuple-element.37.counts, bf16[2,2,32,16,512]{4,3,2,1,0:T(8,128)(2,1)} %copy-done.1, bf16[2,2,32,16,512]{4,3,2,1,0:T(8,128)(2,1)} %collective-permute-done.refs_1_, ...), custom_call_target="tpu_custom_call" | custom-call | bytes 16777216 | tf_op jit(solution)/shard_map/collect/pallas_call | solution.py:240
  131.6 2.4 collective-permute-start.3
  135.3 1.5 collective-permute-start.13
  136.8 1.8 fusion.9
  138.6 1.8 collective-permute-start.19
  141.4 18.2 %collective-permute-done.3 = bf16[2,2,256,512]{3,2,1,0:T(8,128)(2,1)S(1)} collective-permute-done((bf16[2,2,256,512]{3,2,1,0:T(8,128)(2,1)}, bf16[2,2,256,512]{3,2,1,0:T(8,128)(2,1)S(1)}, u32[]{:S(2)}, u32[]{:S(2)}) %collective-permute-start.3) | collective-permute-done | bytes 1048608 | tf_op jit(solution)/shard_map/ppermute | solution.py:425
  160.4 10.5 %collective-permute-done.19 = bf16[2,256,512]{2,1,0:T(8,128)(2,1)S(1)} collective-permute-done((bf16[2,256,512]{2,1,0:T(8,128)(2,1)S(1)}, bf16[2,256,512]{2,1,0:T(8,128)(2,1)S(1)}, u32[]{:S(2)}, u32[]{:S(2)}) %collective-permute-start.19) | collective-permute-done | bytes 524320 | tf_op jit(solution)/shard_map/ppermute | solution.py:425
  172.9 30.4 %collective-permute-done.20 = bf16[2,256,512]{2,1,0:T(8,128)(2,1)S(1)} collective-permute-done((bf16[2,256,512]{2,1,0:T(8,128)(2,1)S(1)}, bf16[2,256,512]{2,1,0:T(8,128)(2,1)S(1)}, u32[]{:S(2)}, u32[]{:S(2)}) %collective-permute-start.20) | collective-permute-done | bytes 524320 | tf_op jit(solution)/shard_map/ppermute | solution.py:425
  204.3 1.8 collective-permute-start.5
  206.0 14.2 %collective-permute-done.40.refs_4_ = bf16[2,256,512]{2,1,0:T(8,128)(2,1)S(1)} collective-permute-done((bf16[2,256,512]{2,1,0:T(8,128)(2,1)S(1)}, bf16[2,256,512]{2,1,0:T(8,128)(2,1)S(1)}, u32[]{:S(2)}, u32[]{:S(2)}) %collective-permute-start.40) | collective-permute-done | bytes 524320 | tf_op jit(solution)/shard_map/ppermute | solution.py:425
  220.2 1.5 collective-permute-start.37
  221.7 30.0 %collective-permute-done.44.refs_8_ = bf16[2,256,512]{2,1,0:T(8,128)(2,1)S(1)} collective-permute-done((bf16[2,256,512]{2,1,0:T(8,128)(2,1)S(1)}, bf16[2,256,512]{2,1,0:T(8,128)(2,1)S(1)}, u32[]{:S(2)}, u32[]{:S(2)}) %collective-permute-start.44) | collective-permute-done | bytes 524320 | tf_op jit(solution)/shard_map/ppermute | solution.py:425
  253.1 1.5 collective-permute-start.45
  255.2 13.1 %collective-permute-done.48.refs_12_ = bf16[2,256,512]{2,1,0:T(8,128)(2,1)S(1)} collective-permute-done((bf16[2,256,512]{2,1,0:T(8,128)(2,1)S(1)}, bf16[2,256,512]{2,1,0:T(8,128)(2,1)S(1)}, u32[]{:S(2)}, u32[]{:S(2)}) %collective-permute-start.48) | collective-permute-done | bytes 524320 | tf_op jit(solution)/shard_map/ppermute | solution.py:425
  268.3 8.3 %collective-permute-done.21.refs_0_ = bf16[2,256,512]{2,1,0:T(8,128)(2,1)} collective-permute-done((bf16[2,256,512]{2,1,0:T(8,128)(2,1)S(1)}, bf16[2,256,512]{2,1,0:T(8,128)(2,1)}, u32[]{:S(2)}, u32[]{:S(2)}) %collective-permute-start.21) | collective-permute-done | bytes 524320 | tf_op jit(solution)/shard_map/ppermute | solution.py:425
  276.6 1.4 collective-permute-start.49
  278.8 4.2 %collective-permute-done.49 = bf16[1,256,512]{2,1,0:T(8,128)(2,1)S(1)} collective-permute-done((bf16[1,256,512]{2,1,0:T(8,128)(2,1)S(1)}, bf16[1,256,512]{2,1,0:T(8,128)(2,1)S(1)}, u32[]{:S(2)}, u32[]{:S(2)}) %collective-permute-start.49) | collective-permute-done | bytes 262176 | tf_op jit(solution)/shard_map/ppermute | solution.py:425
  283.1 9.2 %collective-permute-done.22.refs_0_ = bf16[2,256,512]{2,1,0:T(8,128)(2,1)S(1)} collective-permute-done((bf16[2,256,512]{2,1,0:T(8,128)(2,1)}, bf16[2,256,512]{2,1,0:T(8,128)(2,1)S(1)}, u32[]{:S(2)}, u32[]{:S(2)}) %collective-permute-start.22) | collective-permute-done | bytes 524320 | tf_op jit(solution)/shard_map/ppermute | solution.py:425
  293.6 1.5 collective-permute-done.50
  295.3 1.4 collective-permute-start.34
  296.8 7.8 %collective-permute-done.25.refs_1_ = bf16[2,256,512]{2,1,0:T(8,128)(2,1)S(1)} collective-permute-done((bf16[2,256,512]{2,1,0:T(8,128)(2,1)S(1)}, bf16[2,256,512]{2,1,0:T(8,128)(2,1)S(1)}, u32[]{:S(2)}, u32[]{:S(2)}) %collective-permute-start.25) | collective-permute-done | bytes 524320 | tf_op jit(solution)/shard_map/ppermute | solution.py:425
  304.6 2.3 collective-permute-done.23.refs_0_
  307.0 1.3 collective-permute-start.31
  309.8 6.1 %collective-permute-done.34.refs_1_ = bf16[2,256,512]{2,1,0:T(8,128)(2,1)} collective-permute-done((bf16[2,256,512]{2,1,0:T(8,128)(2,1)S(1)}, bf16[2,256,512]{2,1,0:T(8,128)(2,1)}, u32[]{:S(2)}, u32[]{:S(2)}) %collective-permute-start.34) | collective-permute-done | bytes 524320 | tf_op jit(solution)/shard_map/ppermute | solution.py:425
  317.8 9.0 %collective-permute-done.31.refs_1_ = bf16[2,256,512]{2,1,0:T(8,128)(2,1)} collective-permute-done((bf16[2,256,512]{2,1,0:T(8,128)(2,1)}, bf16[2,256,512]{2,1,0:T(8,128)(2,1)}, u32[]{:S(2)}, u32[]{:S(2)}) %collective-permute-start.31) | collective-permute-done | bytes 524320 | tf_op jit(solution)/shard_map/ppermute | solution.py:425
  327.5 8.2 %settle.1 = (f32[2,1,32,16,512]{4,3,2,1,0:T(8,128)}, f32[2,1,32,16,512]{4,3,2,1,0:T(8,128)}) custom-call(s32[2,32]{1,0:T(2,128)} %get-tuple-element.36.piece_of, s32[2,32]{1,0:T(2,128)} %get-tuple-element.35.row_of, s32[2,32]{1,0:T(2,128)} %fusion.30.held, bf16[2,256,512]{2,1,0:T(8,128)(2,1)} %copy-done.3, bf16[2,256,512]{2,1,0:T(8,128)(2,1)} %copy-done.20, ...), custom_call_target="tpu_custom_call" | custom-call | flops 4194304 | bytes 9437184 | tf_op jit(solution)/shard_map/settle/pallas_call | solution.py:379
  338.9 6.2 %expand.4.refs_5_ = bf16[2,4096,1024]{2,1,0:T(8,128)(2,1)} custom-call(s32[4]{0:T(128)} %pad_add_fusion.quads, s32[1]{0:T(128)} %bitcast.31.group, bf16[2,256,512]{2,1,0:T(8,128)(2,1)} %copy-done.4, bf16[2,256,512]{2,1,0:T(8,128)(2,1)} %collective-permute-done.34.refs_1_, bf16[2,256,512]{2,1,0:T(8,128)(2,1)} %collective-permute-done.35.refs_2_, ...), custom_call_target="tpu_custom_call" | custom-call | flops 2147483648 | bytes 6291456 | tf_op jit(solution)/shard_map/expand/pallas_call | solution.py:319
  345.1 6.2 %expand.5.refs_5_ = bf16[2,4096,1024]{2,1,0:T(8,128)(2,1)} custom-call(s32[4]{0:T(128)} %pad_add_fusion.quads, s32[1]{0:T(128)} %bitcast.27.group, bf16[2,256,512]{2,1,0:T(8,128)(2,1)} %collective-permute-done.21.refs_0_, bf16[2,256,512]{2,1,0:T(8,128)(2,1)} %collective-permute-done.31.refs_1_, ...), custom_call_target="tpu_custom_call", output_to_operand_aliasing={{}: (7, {})} | custom-call | flops 2147483648 | bytes 6291456 | tf_op jit(solution)/shard_map/expand/pallas_call | solution.py:319
  352.9 6.2 %expand.6.refs_5_ = bf16[2,4096,1024]{2,1,0:T(8,128)(2,1)} custom-call(s32[4]{0:T(128)} %pad_add_fusion.quads, s32[1]{0:T(128)} %bitcast.24.group, bf16[2,256,512]{2,1,0:T(8,128)(2,1)} %copy-done.14, bf16[2,256,512]{2,1,0:T(8,128)(2,1)} %copy-done.6, bf16[2,256,512]{2,1,0:T(8,128)(2,1)} %copy-done.15, ...), custom_call_target="tpu_custom_call", output_to_operand_aliasing={{}: (7, {})} | custom-call | flops 2147483648 | bytes 6291456 | tf_op jit(solution)/shard_map/expand/pallas_call | solution.py:319
  359.8 6.2 %expand.7 = bf16[2,4096,1024]{2,1,0:T(8,128)(2,1)} custom-call(s32[4]{0:T(128)} %pad_add_fusion.quads, s32[1]{0:T(128)} %bitcast.4.group, bf16[2,256,512]{2,1,0:T(8,128)(2,1)} %copy-done.5, bf16[2,256,512]{2,1,0:T(8,128)(2,1)} %copy-done.7, bf16[2,256,512]{2,1,0:T(8,128)(2,1)} %copy-done.16, ...), custom_call_target="tpu_custom_call", output_to_operand_aliasing={{}: (7, {})} | custom-call | flops 2147483648 | bytes 6291456 | tf_op jit(solution)/shard_map/expand/pallas_call | solution.py:319
  (168 shorter events, 27.8 us)
Async XLA Ops:
  2.1 15.8 %collective-permute-start.6 = (f32[2,128,512]{2,1,0:T(8,128)S(1)}, f32[2,128,512]{2,1,0:T(8,128)S(1)}, u32[]{:S(2)}, u32[]{:S(2)}) collective-permute-start(f32[2,128,512]{2,1,0:T(8,128)S(1)} %get-tuple-element.34), channel_id=1, source_target_pairs={{0,1},{1,0},{2,3},{3,2},{4,5},{5,4},{6,7},{7,6},{8,9},{9,8},{10,11... | collective-permute-start | bytes 1572872 | tf_op jit(solution)/shard_map/ppermute | solution.py:447
  5.2 23.3 %collective-permute-start.8 = (f32[2,128,512]{2,1,0:T(8,128)S(1)}, f32[2,128,512]{2,1,0:T(8,128)}, u32[]{:S(2)}, u32[]{:S(2)}) collective-permute-start(f32[2,128,512]{2,1,0:T(8,128)S(1)} %get-tuple-element.33), channel_id=1, source_target_pairs={{0,1},{1,0},{2,3},{3,2},{4,5},{5,4},{6,7},{7,6},{8,9},{9,8},{10,11... | collective-permute-start | bytes 1572872 | tf_op jit(solution)/shard_map/ppermute | solution.py:447
  18.0 16.9 %collective-permute-start.7 = (f32[2,128,512]{2,1,0:T(8,128)S(1)}, f32[2,128,512]{2,1,0:T(8,128)}, u32[]{:S(2)}, u32[]{:S(2)}) collective-permute-start(f32[2,128,512]{2,1,0:T(8,128)S(1)} %collective-permute-done.6.refs_0_.refs_1_), channel_id=1, source_target_pairs={{0,2},{2,0},{4,6},{6,4},{8,10},{10,8},{12,14},{14,12},{16,18},{18,... | collective-permute-start | bytes 1572872 | tf_op jit(solution)/shard_map/ppermute | solution.py:425
  18.7 70.6 %collective-permute-start = (bf16[2,2,32,16,512]{4,3,2,1,0:T(8,128)(2,1)S(1)}, bf16[2,2,32,16,512]{4,3,2,1,0:T(8,128)(2,1)}, u32[]{:S(2)}, u32[]{:S(2)}) collective-permute-start(bf16[2,2,32,16,512]{4,3,2,1,0:T(8,128)(2,1)S(1)} %pad_maximum_fusion.refs_0_), channel_id=1, source_target_pairs={{0,4},{2,6},{4,0},{6,2},{8,12},{10,14},{12,8},{14,10},{16,20},{18,... | collective-permute-start | bytes 6291464 | tf_op jit(solution)/shard_map/ppermute | solution.py:425
  28.4 12.6 %collective-permute-start.9 = (f32[2,128,512]{2,1,0:T(8,128)}, f32[2,128,512]{2,1,0:T(8,128)S(1)}, u32[]{:S(2)}, u32[]{:S(2)}) collective-permute-start(f32[2,128,512]{2,1,0:T(8,128)} %collective-permute-done.8.refs_3_), channel_id=1, source_target_pairs={{0,2},{2,0},{4,6},{6,4},{8,10},{10,8},{12,14},{14,12},{16,18},{18,... | collective-permute-start | bytes 1572872 | tf_op jit(solution)/shard_map/ppermute | solution.py:425
  89.0 30.2 %collective-permute-start.1 = (bf16[2,2,32,16,512]{4,3,2,1,0:T(8,128)(2,1)S(1)}, bf16[2,2,32,16,512]{4,3,2,1,0:T(8,128)(2,1)}, u32[]{:S(2)}, u32[]{:S(2)}) collective-permute-start(bf16[2,2,32,16,512]{4,3,2,1,0:T(8,128)(2,1)S(1)} %pad_maximum_fusion.refs_0_), channel_id=1, source_target_pairs={{0,2},{2,0},{4,6},{6,4},{8,10},{10,8},{12,14},{14,12},{16,18},{18,... | collective-permute-start | bytes 6291464 | tf_op jit(solution)/shard_map/ppermute | solution.py:425
  89.3 32.9 %collective-permute-start.2 = (bf16[2,2,32,16,512]{4,3,2,1,0:T(8,128)(2,1)}, bf16[2,2,32,16,512]{4,3,2,1,0:T(8,128)(2,1)}, u32[]{:S(2)}, u32[]{:S(2)}) collective-permute-start(bf16[2,2,32,16,512]{4,3,2,1,0:T(8,128)(2,1)} %collective-permute-done.refs_1_), channel_id=1, source_target_pairs={{0,2},{2,0},{4,6},{6,4},{8,10},{10,8},{12,14},{14,12},{16,18},{18,... | collective-permute-start | bytes 6291464 | tf_op jit(solution)/shard_map/ppermute | solution.py:425
  96.1 17.0 %collective-permute-start.14 = (bf16[2,2,256,512]{3,2,1,0:T(8,128)(2,1)}, bf16[2,2,256,512]{3,2,1,0:T(8,128)(2,1)S(1)}, u32[]{:S(2)}, u32[]{:S(2)}) collective-permute-start(bf16[2,2,256,512]{3,2,1,0:T(8,128)(2,1)} %get-tuple-element.24), channel_id=1, source_target_pairs={{0,2},{2,0},{4,6},{6,4},{8,10},{10,8},{12,14},{14,12},{16,18},{18,... | collective-permute-start | bytes 3145736 | tf_op jit(solution)/shard_map/ppermute | solution.py:425
  98.8 17.7 %collective-permute-start.17 = (bf16[2,256,512]{2,1,0:T(8,128)(2,1)}, bf16[2,256,512]{2,1,0:T(8,128)(2,1)}, u32[]{:S(2)}, u32[]{:S(2)}) collective-permute-start(bf16[2,256,512]{2,1,0:T(8,128)(2,1)} %fusion.18), channel_id=1, source_target_pairs={{0,4},{2,6},{4,0},{6,2},{8,12},{10,14},{12,8},{14,10},{16,20},{18,... | collective-permute-start | bytes 1572872 | tf_op jit(solution)/shard_map/ppermute | solution.py:425
  106.7 27.3 %collective-permute-start.12 = (bf16[2,2,256,512]{3,2,1,0:T(8,128)(2,1)}, bf16[2,2,256,512]{3,2,1,0:T(8,128)(2,1)}, u32[]{:S(2)}, u32[]{:S(2)}) collective-permute-start(bf16[2,2,256,512]{3,2,1,0:T(8,128)(2,1)} %get-tuple-element.22), channel_id=1, source_target_pairs={{0,2},{2,0},{4,6},{6,4},{8,10},{10,8},{12,14},{14,12},{16,18},{18,... | collective-permute-start | bytes 3145736 | tf_op jit(solution)/shard_map/ppermute | solution.py:425
  114.1 26.3 %collective-permute-start.10 = (bf16[2,2,256,512]{3,2,1,0:T(8,128)(2,1)}, bf16[2,2,256,512]{3,2,1,0:T(8,128)(2,1)S(1)}, u32[]{:S(2)}, u32[]{:S(2)}) collective-permute-start(bf16[2,2,256,512]{3,2,1,0:T(8,128)(2,1)} %get-tuple-element.20), channel_id=1, source_target_pairs={{0,2},{2,0},{4,6},{6,4},{8,10},{10,8},{12,14},{14,12},{16,18},{18,... | collective-permute-start | bytes 3145736 | tf_op jit(solution)/shard_map/ppermute | solution.py:425
  116.5 20.3 %collective-permute-start.15 = (bf16[2,256,512]{2,1,0:T(8,128)(2,1)}, bf16[2,256,512]{2,1,0:T(8,128)(2,1)}, u32[]{:S(2)}, u32[]{:S(2)}) collective-permute-start(bf16[2,256,512]{2,1,0:T(8,128)(2,1)} %fusion.17), channel_id=1, source_target_pairs={{0,4},{2,6},{4,0},{6,2},{8,12},{10,14},{12,8},{14,10},{16,20},{18,... | collective-permute-start | bytes 1572872 | tf_op jit(solution)/shard_map/ppermute | solution.py:425
  119.2 17.6 %collective-permute-start.18 = (bf16[2,256,512]{2,1,0:T(8,128)(2,1)}, bf16[2,256,512]{2,1,0:T(8,128)(2,1)}, u32[]{:S(2)}, u32[]{:S(2)}) collective-permute-start(bf16[2,256,512]{2,1,0:T(8,128)(2,1)} %fusion.7), channel_id=1, source_target_pairs={{0,8},{2,10},{4,12},{6,14},{8,16},{10,18},{12,20},{14,22},{16,24},... | collective-permute-start | bytes 1572872 | tf_op jit(solution)/shard_map/ppermute | solution.py:425
  131.6 28.0 %collective-permute-start.3 = (bf16[2,2,256,512]{3,2,1,0:T(8,128)(2,1)}, bf16[2,2,256,512]{3,2,1,0:T(8,128)(2,1)S(1)}, u32[]{:S(2)}, u32[]{:S(2)}) collective-permute-start(bf16[2,2,256,512]{3,2,1,0:T(8,128)(2,1)} %get-tuple-element.17), channel_id=1, source_target_pairs={{0,8},{2,10},{4,12},{6,14},{8,16},{10,18},{12,20},{14,22},{16,24},... | collective-permute-start | bytes 3145736 | tf_op jit(solution)/shard_map/ppermute | solution.py:425
  135.3 25.1 %collective-permute-start.13 = (bf16[2,256,512]{2,1,0:T(8,128)(2,1)S(1)}, bf16[2,256,512]{2,1,0:T(8,128)(2,1)S(1)}, u32[]{:S(2)}, u32[]{:S(2)}) collective-permute-start(bf16[2,256,512]{2,1,0:T(8,128)(2,1)S(1)} %fusion.16), channel_id=1, source_target_pairs={{0,4},{2,6},{4,0},{6,2},{8,12},{10,14},{12,8},{14,10},{16,20},{18,... | collective-permute-start | bytes 1572872 | tf_op jit(solution)/shard_map/ppermute | solution.py:425
  138.6 32.3 %collective-permute-start.19 = (bf16[2,256,512]{2,1,0:T(8,128)(2,1)S(1)}, bf16[2,256,512]{2,1,0:T(8,128)(2,1)S(1)}, u32[]{:S(2)}, u32[]{:S(2)}) collective-permute-start(bf16[2,256,512]{2,1,0:T(8,128)(2,1)S(1)} %fusion.9), channel_id=1, source_target_pairs={{0,8},{2,10},{4,12},{6,14},{8,16},{10,18},{12,20},{14,22},{16,24},... | collective-permute-start | bytes 1572872 | tf_op jit(solution)/shard_map/ppermute | solution.py:425
  140.5 32.3 %collective-permute-start.11 = (bf16[2,256,512]{2,1,0:T(8,128)(2,1)S(1)}, bf16[2,256,512]{2,1,0:T(8,128)(2,1)S(1)}, u32[]{:S(2)}, u32[]{:S(2)}) collective-permute-start(bf16[2,256,512]{2,1,0:T(8,128)(2,1)S(1)} %fusion.15), channel_id=1, source_target_pairs={{0,4},{2,6},{4,0},{6,2},{8,12},{10,14},{12,8},{14,10},{16,20},{18,... | collective-permute-start | bytes 1572872 | tf_op jit(solution)/shard_map/ppermute | solution.py:425
  159.7 44.4 %collective-permute-start.4 = (bf16[2,2,256,512]{3,2,1,0:T(8,128)(2,1)S(1)}, bf16[2,2,256,512]{3,2,1,0:T(8,128)(2,1)S(1)}, u32[]{:S(2)}, u32[]{:S(2)}) collective-permute-start(bf16[2,2,256,512]{3,2,1,0:T(8,128)(2,1)S(1)} %slice_add_fusion.2), channel_id=1, source_target_pairs={{0,8},{2,10},{4,12},{6,14},{8,16},{10,18},{12,20},{14,22},{16,24},... | collective-permute-start | bytes 3145736 | tf_op jit(solution)/shard_map/ppermute | solution.py:425
  172.2 31.0 %collective-permute-start.20 = (bf16[2,256,512]{2,1,0:T(8,128)(2,1)S(1)}, bf16[2,256,512]{2,1,0:T(8,128)(2,1)S(1)}, u32[]{:S(2)}, u32[]{:S(2)}) collective-permute-start(bf16[2,256,512]{2,1,0:T(8,128)(2,1)S(1)} %fusion.11), channel_id=1, source_target_pairs={{0,8},{2,10},{4,12},{6,14},{8,16},{10,18},{12,20},{14,22},{16,24},... | collective-permute-start | bytes 1572872 | tf_op jit(solution)/shard_map/ppermute | solution.py:425
  203.5 16.6 %collective-permute-start.40 = (bf16[2,256,512]{2,1,0:T(8,128)(2,1)S(1)}, bf16[2,256,512]{2,1,0:T(8,128)(2,1)S(1)}, u32[]{:S(2)}, u32[]{:S(2)}) collective-permute-start(bf16[2,256,512]{2,1,0:T(8,128)(2,1)S(1)} %get-tuple-element.28.refs_0_), channel_id=1, source_target_pairs={{0,8},{2,10},{4,12},{6,14},{8,16},{10,18},{12,20},{14,22},{16,24},... | collective-permute-start | bytes 1572872 | tf_op jit(solution)/shard_map/ppermute | solution.py:425
  204.3 47.4 %collective-permute-start.5 = (bf16[2,2,256,512]{3,2,1,0:T(8,128)(2,1)S(1)}, bf16[2,2,256,512]{3,2,1,0:T(8,128)(2,1)S(1)}, u32[]{:S(2)}, u32[]{:S(2)}) collective-permute-start(bf16[2,2,256,512]{3,2,1,0:T(8,128)(2,1)S(1)} %slice_add_fusion.1), channel_id=1, source_target_pairs={{0,8},{2,10},{4,12},{6,14},{8,16},{10,18},{12,20},{14,22},{16,24},... | collective-permute-start | bytes 3145736 | tf_op jit(solution)/shard_map/ppermute | solution.py:425
  220.2 31.5 %collective-permute-start.44 = (bf16[2,256,512]{2,1,0:T(8,128)(2,1)S(1)}, bf16[2,256,512]{2,1,0:T(8,128)(2,1)S(1)}, u32[]{:S(2)}, u32[]{:S(2)}) collective-permute-start(bf16[2,256,512]{2,1,0:T(8,128)(2,1)S(1)} %collective-permute-done.40.refs_4_), channel_id=1, source_target_pairs={{0,8},{2,10},{4,12},{6,14},{8,16},{10,18},{12,20},{14,22},{16,24},... | collective-permute-start | bytes 1572872 | tf_op jit(solution)/shard_map/ppermute | solution.py:425
  220.2 34.5 %collective-permute-start.37 = (bf16[2,256,512]{2,1,0:T(8,128)(2,1)S(1)}, bf16[2,256,512]{2,1,0:T(8,128)(2,1)S(1)}, u32[]{:S(2)}, u32[]{:S(2)}) collective-permute-start(bf16[2,256,512]{2,1,0:T(8,128)(2,1)S(1)} %get-tuple-element.28.refs_0_), channel_id=1, source_target_pairs={{0,4},{2,6},{4,0},{6,2},{8,12},{10,14},{12,8},{14,10},{16,20},{18,... | collective-permute-start | bytes 1572872 | tf_op jit(solution)/shard_map/ppermute | solution.py:425
  221.7 33.5 %collective-permute-start.38 = (bf16[2,256,512]{2,1,0:T(8,128)(2,1)S(1)}, bf16[2,256,512]{2,1,0:T(8,128)(2,1)S(1)}, u32[]{:S(2)}, u32[]{:S(2)}) collective-permute-start(bf16[2,256,512]{2,1,0:T(8,128)(2,1)S(1)} %get-tuple-element.28.refs_0_), channel_id=1, source_target_pairs={{0,2},{2,0},{4,6},{6,4},{8,10},{10,8},{12,14},{14,12},{16,18},{18,... | collective-permute-start | bytes 1572872 | tf_op jit(solution)/shard_map/ppermute | solution.py:425
  251.7 16.6 %collective-permute-start.48 = (bf16[2,256,512]{2,1,0:T(8,128)(2,1)S(1)}, bf16[2,256,512]{2,1,0:T(8,128)(2,1)S(1)}, u32[]{:S(2)}, u32[]{:S(2)}) collective-permute-start(bf16[2,256,512]{2,1,0:T(8,128)(2,1)S(1)} %collective-permute-done.44.refs_8_), channel_id=1, source_target_pairs={{0,8},{2,10},{4,12},{6,14},{8,16},{10,18},{12,20},{14,22},{16,24},... | collective-permute-start | bytes 1572872 | tf_op jit(solution)/shard_map/ppermute | solution.py:425
  252.6 24.0 %collective-permute-start.21 = (bf16[2,256,512]{2,1,0:T(8,128)(2,1)S(1)}, bf16[2,256,512]{2,1,0:T(8,128)(2,1)}, u32[]{:S(2)}, u32[]{:S(2)}) collective-permute-start(bf16[2,256,512]{2,1,0:T(8,128)(2,1)S(1)} %fusion.14.refs_0_), channel_id=1, source_target_pairs={{0,8},{2,10},{4,12},{6,14},{8,16},{10,18},{12,20},{14,22},{16,24},... | collective-permute-start | bytes 1572872 | tf_op jit(solution)/shard_map/ppermute | solution.py:425
  253.1 23.5 %collective-permute-start.45 = (bf16[2,256,512]{2,1,0:T(8,128)(2,1)S(1)}, bf16[2,256,512]{2,1,0:T(8,128)(2,1)S(1)}, u32[]{:S(2)}, u32[]{:S(2)}) collective-permute-start(bf16[2,256,512]{2,1,0:T(8,128)(2,1)S(1)} %collective-permute-done.44.refs_8_), channel_id=1, source_target_pairs={{0,4},{2,6},{4,0},{6,2},{8,12},{10,14},{12,8},{14,10},{16,20},{18,... | collective-permute-start | bytes 1572872 | tf_op jit(solution)/shard_map/ppermute | solution.py:425
  254.7 23.4 %collective-permute-start.41 = (bf16[2,256,512]{2,1,0:T(8,128)(2,1)S(1)}, bf16[2,256,512]{2,1,0:T(8,128)(2,1)S(1)}, u32[]{:S(2)}, u32[]{:S(2)}) collective-permute-start(bf16[2,256,512]{2,1,0:T(8,128)(2,1)S(1)} %collective-permute-done.40.refs_4_), channel_id=1, source_target_pairs={{0,4},{2,6},{4,0},{6,2},{8,12},{10,14},{12,8},{14,10},{16,20},{18,... | collective-permute-start | bytes 1572872 | tf_op jit(solution)/shard_map/ppermute | solution.py:425
  255.2 23.0 %collective-permute-start.39 = (bf16[2,256,512]{2,1,0:T(8,128)(2,1)S(1)}, bf16[2,256,512]{2,1,0:T(8,128)(2,1)S(1)}, u32[]{:S(2)}, u32[]{:S(2)}) collective-permute-start(bf16[2,256,512]{2,1,0:T(8,128)(2,1)S(1)} %collective-permute-done.37.refs_1_), channel_id=1, source_target_pairs={{0,2},{2,0},{4,6},{6,4},{8,10},{10,8},{12,14},{14,12},{16,18},{18,... | collective-permute-start | bytes 1572872 | tf_op jit(solution)/shard_map/ppermute | solution.py:425
  276.6 15.7 %collective-permute-start.22 = (bf16[2,256,512]{2,1,0:T(8,128)(2,1)}, bf16[2,256,512]{2,1,0:T(8,128)(2,1)S(1)}, u32[]{:S(2)}, u32[]{:S(2)}) collective-permute-start(bf16[2,256,512]{2,1,0:T(8,128)(2,1)} %collective-permute-done.21.refs_0_), channel_id=1, source_target_pairs={{0,8},{2,10},{4,12},{6,14},{8,16},{10,18},{12,20},{14,22},{16,24},... | collective-permute-start | bytes 1572872 | tf_op jit(solution)/shard_map/ppermute | solution.py:425
  278.1 17.0 %collective-permute-start.50 = (bf16[1,256,512]{2,1,0:T(8,128)(2,1)S(1)}, bf16[1,256,512]{2,1,0:T(8,128)(2,1)S(1)}, u32[]{:S(2)}, u32[]{:S(2)}) collective-permute-start(bf16[1,256,512]{2,1,0:T(8,128)(2,1)S(1)} %slice.123), channel_id=1, source_target_pairs={{0,8},{2,10},{4,12},{6,14},{8,16},{10,18},{12,20},{14,22},{16,24},... | collective-permute-start | bytes 786440 | tf_op jit(solution)/shard_map/ppermute | solution.py:425
  278.2 17.0 %collective-permute-start.43 = (bf16[2,256,512]{2,1,0:T(8,128)(2,1)S(1)}, bf16[2,256,512]{2,1,0:T(8,128)(2,1)S(1)}, u32[]{:S(2)}, u32[]{:S(2)}) collective-permute-start(bf16[2,256,512]{2,1,0:T(8,128)(2,1)S(1)} %collective-permute-done.41.refs_5_), channel_id=1, source_target_pairs={{0,2},{2,0},{4,6},{6,4},{8,10},{10,8},{12,14},{14,12},{16,18},{18,... | collective-permute-start | bytes 1572872 | tf_op jit(solution)/shard_map/ppermute | solution.py:425
  278.3 16.9 %collective-permute-start.46 = (bf16[2,256,512]{2,1,0:T(8,128)(2,1)S(1)}, bf16[2,256,512]{2,1,0:T(8,128)(2,1)S(1)}, u32[]{:S(2)}, u32[]{:S(2)}) collective-permute-start(bf16[2,256,512]{2,1,0:T(8,128)(2,1)S(1)} %collective-permute-done.44.refs_8_), channel_id=1, source_target_pairs={{0,2},{2,0},{4,6},{6,4},{8,10},{10,8},{12,14},{14,12},{16,18},{18,... | collective-permute-start | bytes 1572872 | tf_op jit(solution)/shard_map/ppermute | solution.py:425
  283.1 13.6 %collective-permute-start.47 = (bf16[2,256,512]{2,1,0:T(8,128)(2,1)S(1)}, bf16[2,256,512]{2,1,0:T(8,128)(2,1)S(1)}, u32[]{:S(2)}, u32[]{:S(2)}) collective-permute-start(bf16[2,256,512]{2,1,0:T(8,128)(2,1)S(1)} %collective-permute-done.45.refs_9_), channel_id=1, source_target_pairs={{0,2},{2,0},{4,6},{6,4},{8,10},{10,8},{12,14},{14,12},{16,18},{18,... | collective-permute-start | bytes 1572872 | tf_op jit(solution)/shard_map/ppermute | solution.py:425
  295.2 14.5 %collective-permute-start.51 = (bf16[2,256,512]{2,1,0:T(8,128)(2,1)S(1)}, bf16[2,256,512]{2,1,0:T(8,128)(2,1)}, u32[]{:S(2)}, u32[]{:S(2)}) collective-permute-start(bf16[2,256,512]{2,1,0:T(8,128)(2,1)S(1)} %collective-permute-done.48.refs_12_), channel_id=1, source_target_pairs={{0,2},{2,0},{4,6},{6,4},{8,10},{10,8},{12,14},{14,12},{16,18},{18,... | collective-permute-start | bytes 1572872 | tf_op jit(solution)/shard_map/ppermute | solution.py:425
  295.3 20.6 %collective-permute-start.34 = (bf16[2,256,512]{2,1,0:T(8,128)(2,1)S(1)}, bf16[2,256,512]{2,1,0:T(8,128)(2,1)}, u32[]{:S(2)}, u32[]{:S(2)}) collective-permute-start(bf16[2,256,512]{2,1,0:T(8,128)(2,1)S(1)} %fusion.14.refs_0_), channel_id=1, source_target_pairs={{0,4},{2,6},{4,0},{6,2},{8,12},{10,14},{12,8},{14,10},{16,20},{18,... | collective-permute-start | bytes 1572872 | tf_op jit(solution)/shard_map/ppermute | solution.py:425
  296.7 19.3 %collective-permute-start.52 = (bf16[2,256,512]{2,1,0:T(8,128)(2,1)S(1)}, bf16[2,256,512]{2,1,0:T(8,128)(2,1)}, u32[]{:S(2)}, u32[]{:S(2)}) collective-permute-start(bf16[2,256,512]{2,1,0:T(8,128)(2,1)S(1)} %constant_dynamic-update-slice_fusion.2.refs_13_), channel_id=1, source_target_pairs={{0,2},{2,0},{4,6},{6,4},{8,10},{10,8},{12,14},{14,12},{16,18},{18,... | collective-permute-start | bytes 1572872 | tf_op jit(solution)/shard_map/ppermute | solution.py:425
  304.6 12.7 %collective-permute-start.35 = (bf16[2,256,512]{2,1,0:T(8,128)(2,1)S(1)}, bf16[2,256,512]{2,1,0:T(8,128)(2,1)}, u32[]{:S(2)}, u32[]{:S(2)}) collective-permute-start(bf16[2,256,512]{2,1,0:T(8,128)(2,1)S(1)} %fusion.14.refs_0_), channel_id=1, source_target_pairs={{0,2},{2,0},{4,6},{6,4},{8,10},{10,8},{12,14},{14,12},{16,18},{18,... | collective-permute-start | bytes 1572872 | tf_op jit(solution)/shard_map/ppermute | solution.py:425
  307.0 19.9 %collective-permute-start.31 = (bf16[2,256,512]{2,1,0:T(8,128)(2,1)}, bf16[2,256,512]{2,1,0:T(8,128)(2,1)}, u32[]{:S(2)}, u32[]{:S(2)}) collective-permute-start(bf16[2,256,512]{2,1,0:T(8,128)(2,1)} %collective-permute-done.21.refs_0_), channel_id=1, source_target_pairs={{0,4},{2,6},{4,0},{6,2},{8,12},{10,14},{12,8},{14,10},{16,20},{18,... | collective-permute-start | bytes 1572872 | tf_op jit(solution)/shard_map/ppermute | solution.py:425
  309.7 29.1 %collective-permute-start.32 = (bf16[2,256,512]{2,1,0:T(8,128)(2,1)}, bf16[2,256,512]{2,1,0:T(8,128)(2,1)}, u32[]{:S(2)}, u32[]{:S(2)}) collective-permute-start(bf16[2,256,512]{2,1,0:T(8,128)(2,1)} %collective-permute-done.21.refs_0_), channel_id=1, source_target_pairs={{0,2},{2,0},{4,6},{6,4},{8,10},{10,8},{12,14},{14,12},{16,18},{18,... | collective-permute-start | bytes 1572872 | tf_op jit(solution)/shard_map/ppermute | solution.py:425
  315.9 22.3 %collective-permute-start.36 = (bf16[2,256,512]{2,1,0:T(8,128)(2,1)}, bf16[2,256,512]{2,1,0:T(8,128)(2,1)}, u32[]{:S(2)}, u32[]{:S(2)}) collective-permute-start(bf16[2,256,512]{2,1,0:T(8,128)(2,1)} %collective-permute-done.34.refs_1_), channel_id=1, source_target_pairs={{0,2},{2,0},{4,6},{6,4},{8,10},{10,8},{12,14},{14,12},{16,18},{18,... | collective-permute-start | bytes 1572872 | tf_op jit(solution)/shard_map/ppermute | solution.py:425
  315.9 19.8 %collective-permute-start.24 = (bf16[1,256,512]{2,1,0:T(8,128)(2,1)}, bf16[1,256,512]{2,1,0:T(8,128)(2,1)}, u32[]{:S(2)}, u32[]{:S(2)}) collective-permute-start(bf16[1,256,512]{2,1,0:T(8,128)(2,1)} %slice.118), channel_id=1, source_target_pairs={{0,4},{2,6},{4,0},{6,2},{8,12},{10,14},{12,8},{14,10},{16,20},{18,... | collective-permute-start | bytes 786440 | tf_op jit(solution)/shard_map/ppermute | solution.py:425
  317.3 19.0 %collective-permute-start.26 = (bf16[1,256,512]{2,1,0:T(8,128)(2,1)S(1)}, bf16[1,256,512]{2,1,0:T(8,128)(2,1)}, u32[]{:S(2)}, u32[]{:S(2)}) collective-permute-start(bf16[1,256,512]{2,1,0:T(8,128)(2,1)S(1)} %slice.119), channel_id=1, source_target_pairs={{0,8},{2,10},{4,12},{6,14},{8,16},{10,18},{12,20},{14,22},{16,24},... | collective-permute-start | bytes 786440 | tf_op jit(solution)/shard_map/ppermute | solution.py:425
  326.8 18.2 %collective-permute-start.33 = (bf16[2,256,512]{2,1,0:T(8,128)(2,1)}, bf16[2,256,512]{2,1,0:T(8,128)(2,1)}, u32[]{:S(2)}, u32[]{:S(2)}) collective-permute-start(bf16[2,256,512]{2,1,0:T(8,128)(2,1)} %collective-permute-done.31.refs_1_), channel_id=1, source_target_pairs={{0,2},{2,0},{4,6},{6,4},{8,10},{10,8},{12,14},{14,12},{16,18},{18,... | collective-permute-start | bytes 1572872 | tf_op jit(solution)/shard_map/ppermute | solution.py:425
  335.7 15.5 %collective-permute-start.29 = (bf16[2,256,512]{2,1,0:T(8,128)(2,1)}, bf16[2,256,512]{2,1,0:T(8,128)(2,1)S(1)}, u32[]{:S(2)}, u32[]{:S(2)}) collective-permute-start(bf16[2,256,512]{2,1,0:T(8,128)(2,1)} %copy-done.14), channel_id=1, source_target_pairs={{0,2},{2,0},{4,6},{6,4},{8,10},{10,8},{12,14},{14,12},{16,18},{18,... | collective-permute-start | bytes 1572872 | tf_op jit(solution)/shard_map/ppermute | solution.py:425
  336.2 15.0 %collective-permute-start.30 = (bf16[2,256,512]{2,1,0:T(8,128)(2,1)S(1)}, bf16[2,256,512]{2,1,0:T(8,128)(2,1)S(1)}, u32[]{:S(2)}, u32[]{:S(2)}) collective-permute-start(bf16[2,256,512]{2,1,0:T(8,128)(2,1)S(1)} %collective-permute-done.25.refs_1_), channel_id=1, source_target_pairs={{0,2},{2,0},{4,6},{6,4},{8,10},{10,8},{12,14},{14,12},{16,18},{18,... | collective-permute-start | bytes 1572872 | tf_op jit(solution)/shard_map/ppermute | solution.py:425
  338.3 20.7 %collective-permute-start.27 = (bf16[2,256,512]{2,1,0:T(8,128)(2,1)S(1)}, bf16[2,256,512]{2,1,0:T(8,128)(2,1)S(1)}, u32[]{:S(2)}, u32[]{:S(2)}) collective-permute-start(bf16[2,256,512]{2,1,0:T(8,128)(2,1)S(1)} %collective-permute-done.23.refs_0_), channel_id=1, source_target_pairs={{0,2},{2,0},{4,6},{6,4},{8,10},{10,8},{12,14},{14,12},{16,18},{18,... | collective-permute-start | bytes 1572872 | tf_op jit(solution)/shard_map/ppermute | solution.py:425
  338.8 20.3 %collective-permute-start.28 = (bf16[2,256,512]{2,1,0:T(8,128)(2,1)S(1)}, bf16[2,256,512]{2,1,0:T(8,128)(2,1)}, u32[]{:S(2)}, u32[]{:S(2)}) collective-permute-start(bf16[2,256,512]{2,1,0:T(8,128)(2,1)S(1)} %constant_dynamic-update-slice_fusion.refs_1_), channel_id=1, source_target_pairs={{0,2},{2,0},{4,6},{6,4},{8,10},{10,8},{12,14},{14,12},{16,18},{18,... | collective-permute-start | bytes 1572872 | tf_op jit(solution)/shard_map/ppermute | solution.py:425
  (36 other events, 834.9 us)

commit v3 on v2

--- a/solution.py
+++ b/solution.py
@@ -141,22 +141,13 @@
     )(*args)
 
 
-def basis_kernel(offsets, *refs, pieces, fresh):
-    own_ref = refs[0]
-    piece_refs = refs[1 : 1 + pieces]
-    held, basis_ref = refs[1 + pieces : 3 + pieces]
-    raw, gram, low, inv, block, binv, scale = refs[3 + pieces :]
-    mats, _, rank = raw.shape
-    n = rank // BLOCK
+def factor(gram, inv, low, block, binv, scale, size):
+    mats = block.shape[0]
+    n = size // BLOCK
 
     def sl(i):
         return slice(i * BLOCK, (i + 1) * BLOCK)
 
-    for i, ref in enumerate((own_ref, *piece_refs)):
-        at = pl.multiple_of(offsets[i], 8)
-        raw[:, pl.ds(at, ref.shape[1]), :] = ref[...]
-
-    add_gram(gram, [piece_refs[i] for i in fresh], held)
     for b in range(n):
         below = (b + 1) * BLOCK
         for m in range(mats):
@@ -171,47 +162,96 @@
                 )
                 inv[m, sl(b), : b * BLOCK] = -dot_packed(d_inv, acc, ((1,), (0,)))
             if b + 1 < n:
-                low[m, below:, sl(b)] = dot_packed(gram[m, below:, sl(b)], d_inv, ((1,), (1,)))
-                inv[m, sl(b), below:] = jnp.zeros((BLOCK, rank - below), F32)
+                low[m, below:size, sl(b)] = dot_packed(gram[m, below:size, sl(b)], d_inv, ((1,), (1,)))
+                inv[m, sl(b), below:size] = jnp.zeros((BLOCK, size - below), F32)
                 for j in range(b + 1, n):
-                    gram[m, j * BLOCK :, sl(j)] = gram[m, j * BLOCK :, sl(j)] - dot_packed(
-                        low[m, j * BLOCK :, sl(b)], low[m, sl(j), sl(b)], ((1,), (1,))
+                    gram[m, j * BLOCK : size, sl(j)] = gram[m, j * BLOCK : size, sl(j)] - dot_packed(
+                        low[m, j * BLOCK : size, sl(b)], low[m, sl(j), sl(b)], ((1,), (1,))
                     )
 
+
+def first_half_kernel(*refs, pieces):
+    held, inv_out, low_out, rest_out, gram, low, block, binv, scale = refs[pieces:]
+    mats, rank, _ = gram.shape
+    half = rank // 2
+    add_gram(gram, refs[:pieces], held)
+    factor(gram, inv_out, low, block, binv, scale, half)
+    for m in range(mats):
+        side = dot_f32(gram[m, half:, :half], inv_out[m], ((1,), (1,)))
+        low_out[m] = side
+        rest_out[m] = gram[m, half:, half:] - dot_f32(side, side, ((1,), (1,)))
+
+
+def second_half_kernel(offsets, *refs, pieces):
+    own_ref = refs[0]
+    piece_refs = refs[1 : 1 + pieces]
+    inv_ref, side_ref, rest_ref, basis_ref = refs[1 + pieces : 5 + pieces]
+    raw, gram, inv, low, block, binv, scale = refs[5 + pieces :]
+    mats, _, rank = raw.shape
+    half = rank // 2
+    for i, ref in enumerate((own_ref, *piece_refs)):
+        at = pl.multiple_of(offsets[i], 8)
+        raw[:, pl.ds(at, ref.shape[1]), :] = ref[...]
+    gram[...] = rest_ref[...]
+    factor(gram, inv, low, block, binv, scale, half)
+
     def bases(m, _):
-        for j in range(0, rank, WIDE):
-            end = j + WIDE
-            basis_ref[m, :, j:end] = dot_split(
-                raw[m, :, :end], inv[m, j:end, :end], ((1,), (1,))
-            ).astype(BF16)
+        acc = dot_f32(side_ref[m], inv_ref[m], ((1,), (0,)))
+        left = -dot_f32(inv[m], acc, ((1,), (0,)))
+        basis_ref[m, :, :half] = dot_split(raw[m, :, :half], inv_ref[m], ((1,), (1,))).astype(BF16)
+        both = jnp.concatenate([left, inv[m]], axis=1)
+        basis_ref[m, :, half:] = dot_split(raw[m], both, ((1,), (1,))).astype(BF16)
         return 0
 
     lax.fori_loop(0, mats, bases, 0)
 
 
-def orthonormal_basis(own, pieces, offsets, held, fresh, feats):
+def first_half(fresh, held):
+    mats, rank, _ = held.shape
+    half = rank // 2
+    vmem = pl.BlockSpec(memory_space=pltpu.VMEM)
+    state = jax.ShapeDtypeStruct((mats, half, half), F32)
+    return pl.pallas_call(
+        functools.partial(first_half_kernel, pieces=len(fresh)),
+        out_shape=(state,) * 3,
+        in_specs=[vmem] * (len(fresh) + 1),
+        out_specs=(vmem,) * 3,
+        scratch_shapes=[
+            pltpu.VMEM((mats, rank, rank), F32),
+            pltpu.VMEM((mats, half, half), F32),
+        ]
+        + [pltpu.VMEM((mats, BLOCK, BLOCK), F32)] * 3,
+        cost_estimate=pl.CostEstimate(
+            flops=20_000_000_000, bytes_accessed=4 * mats * rank * rank, transcendentals=0
+        ),
+        name="first_half",
+    )(*fresh, held)
+
+
+def second_half(own, pieces, offsets, state, feats):
     mats, _, rank = own.shape
+    half = rank // 2
     vmem = pl.BlockSpec(memory_space=pltpu.VMEM)
     smem = pl.BlockSpec(memory_space=pltpu.SMEM)
     return pl.pallas_call(
-        functools.partial(basis_kernel, pieces=len(pieces), fresh=tuple(fresh)),
+        functools.partial(second_half_kernel, pieces=len(pieces)),
         out_shape=jax.ShapeDtypeStruct((mats, feats, rank), BF16),
-        in_specs=[smem] + [vmem] * (2 + len(pieces)),
+        in_specs=[smem] + [vmem] * (4 + len(pieces)),
         out_specs=vmem,
         scratch_shapes=[pltpu.VMEM((mats, feats, rank), F32)]
-        + [pltpu.VMEM((mats, rank, rank), F32)] * 3
+        + [pltpu.VMEM((mats, half, half), F32)] * 3
         + [pltpu.VMEM((mats, BLOCK, BLOCK), F32)] * 3,
         cost_estimate=pl.CostEstimate(
-            flops=40_000_000_000, bytes_accessed=6 * mats * feats * rank, transcendentals=0
-        ),
-        name="basis",
-    )(offsets, own, *pieces, held)
+            flops=20_000_000_000, bytes_accessed=6 * mats * feats * rank, transcendentals=0
+        ),
+        name="second_half",
+    )(offsets, own, *pieces, *state)
 
 
 def collect_kernel(places, counts, *refs):
-    m = pl.program_id(1)
+    m = pl.program_id(0)
     owner_refs, (head_ref, rest_ref) = refs[:QUAD], refs[QUAD:]
-    bucket_rows, head_rows = owner_refs[0].shape[3], head_ref.shape[2]
+    bucket_rows, head_rows = owner_refs[0].shape[2], head_ref.shape[1]
     for ref in (head_ref, rest_ref):
         ref[...] = jnp.zeros(ref.shape, BF16)
     for i, owner_ref in enumerate(owner_refs):
@@ -222,12 +262,12 @@
             @pl.when(jnp.logical_and(place >= 0, place < head_rows))
             def _():
                 at = pl.multiple_of(jnp.maximum(place, 0), bucket_rows)
-                head_ref[0, 0, pl.ds(at, bucket_rows), :] = owner_ref[0, 0, s]
+                head_ref[0, pl.ds(at, bucket_rows), :] = owner_ref[0, s]
 
             @pl.when(place >= head_rows)
             def _():
                 at = pl.multiple_of(jnp.maximum(place - head_rows, 0), bucket_rows)
-                rest_ref[0, 0, pl.ds(at, bucket_rows), :] = owner_ref[0, 0, s]
+                rest_ref[0, pl.ds(at, bucket_rows), :] = owner_ref[0, s]
 
             return 0
 
@@ -235,19 +275,19 @@
 
 
 def collect_moments(owners, places, counts, head_rows, rest_rows):
-    kinds, mats, capacity, bucket_rows, rank = owners[0].shape
-    slots = pl.BlockSpec((1, 1, capacity, bucket_rows, rank), lambda a, m, *_: (a, m, 0, 0, 0))
+    mats, capacity, bucket_rows, rank = owners[0].shape
+    slots = pl.BlockSpec((1, capacity, bucket_rows, rank), lambda m, *_: (m, 0, 0, 0))
     return pl.pallas_call(
         collect_kernel,
         out_shape=tuple(
-            jax.ShapeDtypeStruct((kinds, mats, rows, rank), BF16) for rows in (head_rows, rest_rows)
+            jax.ShapeDtypeStruct((mats, rows, rank), BF16) for rows in (head_rows, rest_rows)
         ),
         grid_spec=pltpu.PrefetchScalarGridSpec(
             num_scalar_prefetch=2,
-            grid=(kinds, mats),
+            grid=(mats,),
             in_specs=[slots] * QUAD,
             out_specs=tuple(
-                pl.BlockSpec((1, 1, rows, rank), lambda a, m, *_: (a, m, 0, 0))
+                pl.BlockSpec((1, rows, rank), lambda m, *_: (m, 0, 0))
                 for rows in (head_rows, rest_rows)
             ),
         ),
@@ -473,18 +513,22 @@
     wanted = jnp.logical_and(quad_occupied, quad_units % QUAD == my_quad)
     places = jnp.where(wanted, places, -1).astype(jnp.int32)
 
-    slots = jnp.stack([first_moment[:, 0], second_moment[:, 0]]).astype(BF16)
-    slots_across = to_x(slots)
-    slots_core = to_core(slots)
-
-    basis = orthonormal_basis(raw_proj, pieces, offsets, gram, fresh, splits * local_feats)
-
-    owners = (slots, slots_across, slots_core, to_core(slots_across))
-    unit_moments, rest = collect_moments(
-        owners, places, quad_counts, unit_rows, (depth - 1) * unit_rows
-    )
-    for k in range(1, depth):
-        unit_moments = to_z(unit_moments) + rest[:, :, (k - 1) * unit_rows : k * unit_rows]
+    def unit_moments(moment):
+        slots = moment[:, 0].astype(BF16)
+        across = to_x(slots)
+        owners = (slots, across, to_core(slots), to_core(across))
+        held, rest = collect_moments(
+            owners, places, quad_counts, unit_rows, (depth - 1) * unit_rows
+        )
+        for k in range(1, depth):
+            held = to_z(held) + rest[:, (k - 1) * unit_rows : k * unit_rows]
+        return held
+
+    first_unit = unit_moments(first_moment)
+    second_unit = unit_moments(second_moment)
+
+    state = first_half([pieces[i] for i in fresh], gram)
+    basis = second_half(raw_proj, pieces, offsets, state, splits * local_feats)
 
     send_quads = jnp.stack([my_quad ^ flip for flip in (3, 1, 2, 0)]).astype(jnp.int32)
     held = None
@@ -517,7 +561,7 @@
         return groups
 
     grad_groups = ring(held)
-    update = adam_update(unit_moments[0].astype(F32), unit_moments[1].astype(F32), grad_rows)
+    update = adam_update(first_unit.astype(F32), second_unit.astype(F32), grad_rows)
     update_groups = ring(update)
 
     part_quads = jnp.stack([my_quad ^ flip for flip in (0, 2, 1, 3)]).astype(jnp.int32)

time: 367 us -> 369 us (level)
  Pallas kernels: 119 us -> 124 us
  starting transfers between devices: 33.9 us -> 29.4 us
  waiting for transfers between devices: 183 us -> 179 us
    ppermute x51 -> x57, waiting for transfers between devices: 165 us -> 159 us  [permute(): return lax.ppermute(v, 'dp', [(i, target(i)) for i in range(replicas)])]
    ppermute x51 -> x57, starting transfers between devices: 30.8 us -> 25.9 us  [permute(): return lax.ppermute(v, 'dp', [(i, target(i)) for i in range(replicas)])]
    pallas_call x2 -> x4, Pallas kernels: 49.7 us -> 54 us  [the longest x1 22.1 us: second_half(): pl.pallas_call(functools.partial(second_half_kernel, pieces=len(pieces)),...]
  transfers between devices with their start and end apart: 53 -> 59, of which waited for: 16 -> 22; matrix products, arithmetic and copies ran while one was open for 6% -> 7% of each run, Pallas kernels for 31% -> 31%
where the time goes in v3:
time: 369 us; the launch traced here: 368 us
  waiting for transfers between devices  179 us (49%)
  Pallas kernels  124 us (34%)
  starting transfers between devices  29.4 us (8%)
  other arithmetic  22.5 us (6%)
  local copies, waits for them, and re-layouts  11.7 us (3%)
    ppermute x57, waiting for transfers between devices, permute(): return lax.ppermute(v, 'dp', [(i, target(i)) for i in range(replicas)])  159 us
    ppermute x57, starting transfers between devices, permute(): return lax.ppermute(v, 'dp', [(i, target(i)) for i in range(replicas)])  25.9 us
    pallas_call x4, Pallas kernels, expand(): pl.pallas_call(expand_kernel, out_shape=jax.ShapeDtypeStruct((mats, local...  24.9 us
    pallas_call x4, Pallas kernels, project(): pl.pallas_call(project_kernel, out_shape=(out, out), grid_spec=pltpu.Pref...  24.7 us
    pallas_call x1, Pallas kernels, second_half(): pl.pallas_call(functools.partial(second_half_kernel, pieces=len(pieces)),...  22.1 us
    pallas_call x1, Pallas kernels, first_half(): pl.pallas_call(functools.partial(first_half_kernel, pieces=len(fresh)), o...  20.2 us
    ppermute x2, waiting for transfers between devices, shards(): lax.ppermute(parts[i], 'fsdp', [(j, (j + shift) % splits) for j in range(...  19.9 us
    pallas_call x2, Pallas kernels, gram_of(): pl.pallas_call(functools.partial(gram_kernel, pieces=len(pieces)), out_sh...  12 us
  transfers between devices with their start and end apart: 59, of which 22 were waited for; matrix products, arithmetic and copies ran while one was open for 7% of the time, Pallas kernels for 31%

profile of v3, /device:TPU:0, one launch (start us, length us, event | category | flops | bytes accessed | tf_op | source)
XLA Modules:
  0.0 367.6 jit_solution(10577488799516738842)
XLA Ops:
  0.7 2.4 constant_dynamic-slice_fusion
  3.1 3.0 collective-permute-start.6
  9.4 9.7 %collective-permute-done.6.refs_0_.refs_1_ = f32[2,128,512]{2,1,0:T(8,128)} collective-permute-done((f32[2,128,512]{2,1,0:T(8,128)}, f32[2,128,512]{2,1,0:T(8,128)}, u32[]{:S(2)}, u32[]{:S(2)}) %collective-permute-start.6) | collective-permute-done | bytes 524320 | tf_op jit(solution)/shard_map/ppermute | solution.py:487
  19.4 10.1 %collective-permute-done.8.refs_0_.refs_3_ = f32[2,128,512]{2,1,0:T(8,128)} collective-permute-done((f32[2,128,512]{2,1,0:T(8,128)}, f32[2,128,512]{2,1,0:T(8,128)}, u32[]{:S(2)}, u32[]{:S(2)}) %collective-permute-start.8) | collective-permute-done | bytes 524320 | tf_op jit(solution)/shard_map/ppermute | solution.py:487
  30.2 5.9 %gram.2.refs_2_ = f32[2,512,512]{2,1,0:T(8,128)} custom-call(f32[2,512,512]{2,1,0:T(8,128)} %refs_0_.3), custom_call_target="tpu_custom_call" | custom-call | flops 3221225472 | bytes 4194304 | tf_op jit(solution)/shard_map/gram/pallas_call | solution.py:130
  36.1 6.1 %gram.3.refs_2_ = f32[2,512,512]{2,1,0:T(8,128)} custom-call(f32[2,128,512]{2,1,0:T(8,128)} %collective-permute-done.6.refs_0_.refs_1_, f32[2,128,512]{2,1,0:T(8,128)} %collective-permute-done.7.refs_1_.refs_2_, f32[2,512,512]{2,1,0:T(8,128)} %gram.2.refs_2_), custom_call_target="tpu_custom_call" | custom-call | flops 1610612736 | bytes 3145728 | tf_op jit(solution)/shard_map/gram/pallas_call | solution.py:130
  42.2 20.2 %first_half.1 = (f32[2,256,256]{2,1,0:T(8,128)}, f32[2,256,256]{2,1,0:T(8,128)}, f32[2,256,256]{2,1,0:T(8,128)}) custom-call(f32[2,128,512]{2,1,0:T(8,128)} %collective-permute-done.8.refs_0_.refs_3_, f32[2,128,512]{2,1,0:T(8,128)} %collective-permute-done.9.refs_1_.refs_4_, f32[2,512,512]{2,1,0:T(8,128)} %gram.3.refs_2_), custom_call_target="tpu_custom_call" | custom-call | flops 20000000000 | bytes 2097152 | tf_op jit(solution)/shard_map/first_half/pallas_call | solution.py:214
  62.4 22.1 %second_half.1.basis_ref.refs_4_ = bf16[2,1024,512]{2,1,0:T(8,128)(2,1)} custom-call(s32[5]{0:T(128)} %stack.71.offsets, f32[2,512,512]{2,1,0:T(8,128)} %refs_0_.3, f32[2,128,512]{2,1,0:T(8,128)} %collective-permute-done.6.refs_0_.refs_1_, f32[2,128,512]{2,1,0:T(8,128)} %collective-permute-done.7.refs_1_.refs_2_, ...), custom_call_target="tpu_custom_call" | custom-call | flops 20000000000 | bytes 6291456 | tf_op jit(solution)/shard_map/second_half/pallas_call | solution.py:236
  84.5 6.2 %project.7 = (bf16[2,2,256,512]{3,2,1,0:T(8,128)(2,1)}, bf16[2,2,256,512]{3,2,1,0:T(8,128)(2,1)}) custom-call(s32[4]{0:T(128)} %pad_add_fusion.2.quads, s32[1]{0:T(128)} %bitcast.24.group, bf16[1,2,4096,1024]{3,2,1,0:T(8,128)(2,1)} %grads_ref.7, bf16[2,1024,512]{2,1,0:T(8,128)(2,1)} %second_half.1.basis_ref.refs_4_), custom_call_target="tpu_custom_call" | custom-call | flops 2147483648 | bytes 6291456 | tf_op jit(solution)/shard_map/project/pallas_call | solution.py:315
  91.4 6.2 %project.6 = (bf16[2,2,256,512]{3,2,1,0:T(8,128)(2,1)}, bf16[2,2,256,512]{3,2,1,0:T(8,128)(2,1)}) custom-call(s32[4]{0:T(128)} %pad_add_fusion.2.quads, s32[1]{0:T(128)} %bitcast.21.group, bf16[1,2,4096,1024]{3,2,1,0:T(8,128)(2,1)} %grads_ref.7, bf16[2,1024,512]{2,1,0:T(8,128)(2,1)} %second_half.1.basis_ref.refs_4_), custom_call_target="tpu_custom_call" | custom-call | flops 2147483648 | bytes 6291456 | tf_op jit(solution)/shard_map/project/pallas_call | solution.py:315
  98.3 6.2 %project.4 = (bf16[2,2,256,512]{3,2,1,0:T(8,128)(2,1)}, bf16[2,2,256,512]{3,2,1,0:T(8,128)(2,1)}) custom-call(s32[4]{0:T(128)} %pad_add_fusion.2.quads, s32[1]{0:T(128)} %bitcast.11.group, bf16[1,2,4096,1024]{3,2,1,0:T(8,128)(2,1)} %grads_ref.7, bf16[2,1024,512]{2,1,0:T(8,128)(2,1)} %second_half.1.basis_ref.refs_4_), custom_call_target="tpu_custom_call" | custom-call | flops 2147483648 | bytes 6291456 | tf_op jit(solution)/shard_map/project/pallas_call | solution.py:315
  104.5 6.2 %project.5 = (bf16[2,2,256,512]{3,2,1,0:T(8,128)(2,1)}, bf16[2,2,256,512]{3,2,1,0:T(8,128)(2,1)}) custom-call(s32[4]{0:T(128)} %pad_add_fusion.2.quads, s32[1]{0:T(128)} %bitcast.4.group, bf16[1,2,4096,1024]{3,2,1,0:T(8,128)(2,1)} %grads_ref.7, bf16[2,1024,512]{2,1,0:T(8,128)(2,1)} %second_half.1.basis_ref.refs_4_), custom_call_target="tpu_custom_call" | custom-call | flops 2147483648 | bytes 6291456 | tf_op jit(solution)/shard_map/project/pallas_call | solution.py:315
  110.7 2.1 fusion.17
  113.3 1.7 collective-permute-start.17
  116.6 5.8 %collect.3 = (bf16[2,256,512]{2,1,0:T(8,128)(2,1)}, bf16[2,768,512]{2,1,0:T(8,128)(2,1)}) custom-call(s32[4,2,32]{2,1,0:T(2,128)} %get-tuple-element.48.places, s32[4,2]{1,0:T(4,128)} %get-tuple-element.47.counts, bf16[2,32,16,512]{3,2,1,0:T(8,128)(2,1)} %copy-done.3, bf16[2,32,16,512]{3,2,1,0:T(8,128)(2,1)} %collective-permute-done.21.refs_1_, ...), custom_call_target="tpu_custom_call" | custom-call | bytes 8388608 | tf_op jit(solution)/shard_map/collect/pallas_call | solution.py:280
  123.0 2.2 fusion.16
  125.2 2.3 collective-permute-done.17
  127.5 1.7 collective-permute-start.15
  129.2 2.4 fusion.7
  133.2 2.0 fusion.14
  136.7 2.0 fusion.15
  141.8 5.8 %collect.2 = (bf16[2,256,512]{2,1,0:T(8,128)(2,1)}, bf16[2,768,512]{2,1,0:T(8,128)(2,1)}) custom-call(s32[4,2,32]{2,1,0:T(2,128)} %get-tuple-element.48.places, s32[4,2]{1,0:T(4,128)} %get-tuple-element.47.counts, bf16[2,32,16,512]{3,2,1,0:T(8,128)(2,1)} %copy-done.2, bf16[2,32,16,512]{3,2,1,0:T(8,128)(2,1)} %copy-done.14, ...), custom_call_target="tpu_custom_call" | custom-call | bytes 8388608 | tf_op jit(solution)/shard_map/collect/pallas_call | solution.py:280
  147.7 2.1 collective-permute-start.3
  149.8 1.6 fusion.9
  152.0 7.7 %collective-permute-done.24 = bf16[2,256,512]{2,1,0:T(8,128)(2,1)} collective-permute-done((bf16[2,256,512]{2,1,0:T(8,128)(2,1)}, bf16[2,256,512]{2,1,0:T(8,128)(2,1)}, u32[]{:S(2)}, u32[]{:S(2)}) %collective-permute-start.24) | collective-permute-done | bytes 524320 | tf_op jit(solution)/shard_map/ppermute | solution.py:465
  160.9 9.9 %collective-permute-done.3 = bf16[2,256,512]{2,1,0:T(8,128)(2,1)S(1)} collective-permute-done((bf16[2,256,512]{2,1,0:T(8,128)(2,1)}, bf16[2,256,512]{2,1,0:T(8,128)(2,1)S(1)}, u32[]{:S(2)}, u32[]{:S(2)}) %collective-permute-start.3) | collective-permute-done | bytes 524320 | tf_op jit(solution)/shard_map/ppermute | solution.py:465
  171.0 11.1 %collective-permute-done.19 = bf16[2,256,512]{2,1,0:T(8,128)(2,1)S(1)} collective-permute-done((bf16[2,256,512]{2,1,0:T(8,128)(2,1)S(1)}, bf16[2,256,512]{2,1,0:T(8,128)(2,1)S(1)}, u32[]{:S(2)}, u32[]{:S(2)}) %collective-permute-start.19) | collective-permute-done | bytes 524320 | tf_op jit(solution)/shard_map/ppermute | solution.py:465
  183.5 9.9 %collective-permute-done.25 = bf16[2,256,512]{2,1,0:T(8,128)(2,1)S(1)} collective-permute-done((bf16[2,256,512]{2,1,0:T(8,128)(2,1)S(1)}, bf16[2,256,512]{2,1,0:T(8,128)(2,1)S(1)}, u32[]{:S(2)}, u32[]{:S(2)}) %collective-permute-start.25) | collective-permute-done | bytes 524320 | tf_op jit(solution)/shard_map/ppermute | solution.py:465
  193.5 11.1 %collective-permute-done.4 = bf16[2,256,512]{2,1,0:T(8,128)(2,1)S(1)} collective-permute-done((bf16[2,256,512]{2,1,0:T(8,128)(2,1)S(1)}, bf16[2,256,512]{2,1,0:T(8,128)(2,1)S(1)}, u32[]{:S(2)}, u32[]{:S(2)}) %collective-permute-start.4) | collective-permute-done | bytes 524320 | tf_op jit(solution)/shard_map/ppermute | solution.py:465
  204.8 11.1 %collective-permute-done.20 = bf16[2,256,512]{2,1,0:T(8,128)(2,1)S(1)} collective-permute-done((bf16[2,256,512]{2,1,0:T(8,128)(2,1)S(1)}, bf16[2,256,512]{2,1,0:T(8,128)(2,1)S(1)}, u32[]{:S(2)}, u32[]{:S(2)}) %collective-permute-start.20) | collective-permute-done | bytes 524320 | tf_op jit(solution)/shard_map/ppermute | solution.py:465
  217.4 9.7 %collective-permute-done.26 = bf16[2,256,512]{2,1,0:T(8,128)(2,1)S(1)} collective-permute-done((bf16[2,256,512]{2,1,0:T(8,128)(2,1)S(1)}, bf16[2,256,512]{2,1,0:T(8,128)(2,1)S(1)}, u32[]{:S(2)}, u32[]{:S(2)}) %collective-permute-start.26) | collective-permute-done | bytes 524320 | tf_op jit(solution)/shard_map/ppermute | solution.py:465
  227.1 9.2 %collective-permute-done.5 = bf16[2,256,512]{2,1,0:T(8,128)(2,1)S(1)} collective-permute-done((bf16[2,256,512]{2,1,0:T(8,128)(2,1)S(1)}, bf16[2,256,512]{2,1,0:T(8,128)(2,1)S(1)}, u32[]{:S(2)}, u32[]{:S(2)}) %collective-permute-start.5) | collective-permute-done | bytes 524320 | tf_op jit(solution)/shard_map/ppermute | solution.py:465
  239.1 14.9 %collective-permute-done.27.refs_0_ = bf16[2,256,512]{2,1,0:T(8,128)(2,1)} collective-permute-done((bf16[2,256,512]{2,1,0:T(8,128)(2,1)S(1)}, bf16[2,256,512]{2,1,0:T(8,128)(2,1)}, u32[]{:S(2)}, u32[]{:S(2)}) %collective-permute-start.27) | collective-permute-done | bytes 524320 | tf_op jit(solution)/shard_map/ppermute | solution.py:465
  254.5 10.7 %collective-permute-done.46.refs_4_ = bf16[2,256,512]{2,1,0:T(8,128)(2,1)} collective-permute-done((bf16[2,256,512]{2,1,0:T(8,128)(2,1)S(1)}, bf16[2,256,512]{2,1,0:T(8,128)(2,1)}, u32[]{:S(2)}, u32[]{:S(2)}) %collective-permute-start.46) | collective-permute-done | bytes 524320 | tf_op jit(solution)/shard_map/ppermute | solution.py:465
  265.3 11.2 %collective-permute-done.28.refs_0_ = bf16[2,256,512]{2,1,0:T(8,128)(2,1)} collective-permute-done((bf16[2,256,512]{2,1,0:T(8,128)(2,1)}, bf16[2,256,512]{2,1,0:T(8,128)(2,1)}, u32[]{:S(2)}, u32[]{:S(2)}) %collective-permute-start.28) | collective-permute-done | bytes 524320 | tf_op jit(solution)/shard_map/ppermute | solution.py:465
  278.6 9.1 %collective-permute-done.50.refs_8_ = bf16[2,256,512]{2,1,0:T(8,128)(2,1)} collective-permute-done((bf16[2,256,512]{2,1,0:T(8,128)(2,1)}, bf16[2,256,512]{2,1,0:T(8,128)(2,1)}, u32[]{:S(2)}, u32[]{:S(2)}) %collective-permute-start.50) | collective-permute-done | bytes 524320 | tf_op jit(solution)/shard_map/ppermute | solution.py:465
  287.7 2.8 collective-permute-done.31.refs_1_
  290.5 8.3 %collective-permute-done.29.refs_0_ = bf16[2,256,512]{2,1,0:T(8,128)(2,1)S(1)} collective-permute-done((bf16[2,256,512]{2,1,0:T(8,128)(2,1)}, bf16[2,256,512]{2,1,0:T(8,128)(2,1)S(1)}, u32[]{:S(2)}, u32[]{:S(2)}) %collective-permute-start.29) | collective-permute-done | bytes 524320 | tf_op jit(solution)/shard_map/ppermute | solution.py:465
  303.3 6.7 %collective-permute-done.54.refs_12_ = bf16[2,256,512]{2,1,0:T(8,128)(2,1)S(1)} collective-permute-done((bf16[2,256,512]{2,1,0:T(8,128)(2,1)}, bf16[2,256,512]{2,1,0:T(8,128)(2,1)S(1)}, u32[]{:S(2)}, u32[]{:S(2)}) %collective-permute-start.54) | collective-permute-done | bytes 524320 | tf_op jit(solution)/shard_map/ppermute | solution.py:465
  310.0 3.9 %collective-permute-done.51.refs_9_ = bf16[2,256,512]{2,1,0:T(8,128)(2,1)S(1)} collective-permute-done((bf16[2,256,512]{2,1,0:T(8,128)(2,1)}, bf16[2,256,512]{2,1,0:T(8,128)(2,1)S(1)}, u32[]{:S(2)}, u32[]{:S(2)}) %collective-permute-start.51) | collective-permute-done | bytes 524320 | tf_op jit(solution)/shard_map/ppermute | solution.py:465
  316.0 2.6 collective-permute-done.30
  322.4 4.8 %collective-permute-done.37.refs_1_ = bf16[2,256,512]{2,1,0:T(8,128)(2,1)} collective-permute-done((bf16[2,256,512]{2,1,0:T(8,128)(2,1)}, bf16[2,256,512]{2,1,0:T(8,128)(2,1)}, u32[]{:S(2)}, u32[]{:S(2)}) %collective-permute-start.37) | collective-permute-done | bytes 524320 | tf_op jit(solution)/shard_map/ppermute | solution.py:465
  327.7 2.2 collective-permute-done.55
  331.0 6.4 %expand.4.refs_5_ = bf16[2,4096,1024]{2,1,0:T(8,128)(2,1)} custom-call(s32[4]{0:T(128)} %pad_add_fusion.quads, s32[1]{0:T(128)} %bitcast.29.group, bf16[2,256,512]{2,1,0:T(8,128)(2,1)} %copy-done.5, bf16[2,256,512]{2,1,0:T(8,128)(2,1)} %copy-done.28, bf16[2,256,512]{2,1,0:T(8,128)(2,1)} %copy-done.29, bf16[2,256,512]{2,1,0:T(8,128)(2,1)} %collective-permute-done.42.refs_3_, ...), custom_call_target="tpu_custom_call" | custom-call | flops 2147483648 | bytes 6291456 | tf_op jit(solution)/shard_map/expand/pallas_call | solution.py:359
  339.7 6.2 %expand.5.refs_5_ = bf16[2,4096,1024]{2,1,0:T(8,128)(2,1)} custom-call(s32[4]{0:T(128)} %pad_add_fusion.quads, s32[1]{0:T(128)} %bitcast.24.group, bf16[2,256,512]{2,1,0:T(8,128)(2,1)} %collective-permute-done.27.refs_0_, bf16[2,256,512]{2,1,0:T(8,128)(2,1)} %collective-permute-done.37.refs_1_, ...), custom_call_target="tpu_custom_call", output_to_operand_aliasing={{}: (7, {})} | custom-call | flops 2147483648 | bytes 6291456 | tf_op jit(solution)/shard_map/expand/pallas_call | solution.py:359
  345.9 6.2 %expand.6.refs_5_ = bf16[2,4096,1024]{2,1,0:T(8,128)(2,1)} custom-call(s32[4]{0:T(128)} %pad_add_fusion.quads, s32[1]{0:T(128)} %bitcast.21.group, bf16[2,256,512]{2,1,0:T(8,128)(2,1)} %collective-permute-done.28.refs_0_, bf16[2,256,512]{2,1,0:T(8,128)(2,1)} %copy-done.8, ...), custom_call_target="tpu_custom_call", output_to_operand_aliasing={{}: (7, {})} | custom-call | flops 2147483648 | bytes 6291456 | tf_op jit(solution)/shard_map/expand/pallas_call | solution.py:359
  352.0 6.2 %expand.7 = bf16[2,4096,1024]{2,1,0:T(8,128)(2,1)} custom-call(s32[4]{0:T(128)} %pad_add_fusion.quads, s32[1]{0:T(128)} %bitcast.4.group, bf16[2,256,512]{2,1,0:T(8,128)(2,1)} %copy-done.9, bf16[2,256,512]{2,1,0:T(8,128)(2,1)} %copy-done.10, bf16[2,256,512]{2,1,0:T(8,128)(2,1)} %collective-permute-done.33.refs_2_, ...), custom_call_target="tpu_custom_call", output_to_operand_aliasing={{}: (7, {})} | custom-call | flops 2147483648 | bytes 6291456 | tf_op jit(solution)/shard_map/expand/pallas_call | solution.py:359
  359.5 7.9 %settle.1 = (f32[2,1,32,16,512]{4,3,2,1,0:T(8,128)}, f32[2,1,32,16,512]{4,3,2,1,0:T(8,128)}) custom-call(s32[2,32]{1,0:T(2,128)} %get-tuple-element.46.piece_of, s32[2,32]{1,0:T(2,128)} %get-tuple-element.45.row_of, s32[2,32]{1,0:T(2,128)} %fusion.29.held, bf16[2,256,512]{2,1,0:T(8,128)(2,1)} %copy-done.4, bf16[2,256,512]{2,1,0:T(8,128)(2,1)} %copy-done.21, ...), custom_call_target="tpu_custom_call" | custom-call | flops 4194304 | bytes 9437184 | tf_op jit(solution)/shard_map/settle/pallas_call | solution.py:419
  (187 shorter events, 40.4 us)
Async XLA Ops:
  3.1 16.1 %collective-permute-start.6 = (f32[2,128,512]{2,1,0:T(8,128)}, f32[2,128,512]{2,1,0:T(8,128)}, u32[]{:S(2)}, u32[]{:S(2)}) collective-permute-start(f32[2,128,512]{2,1,0:T(8,128)} %get-tuple-element.44), channel_id=1, source_target_pairs={{0,1},{1,0},{2,3},{3,2},{4,5},{5,4},{6,7},{7,6},{8,9},{9,8},{10,11... | collective-permute-start | bytes 1572872 | tf_op jit(solution)/shard_map/ppermute | solution.py:487
  6.2 85.0 %collective-permute-start.21 = (bf16[2,32,16,512]{3,2,1,0:T(8,128)(2,1)S(1)}, bf16[2,32,16,512]{3,2,1,0:T(8,128)(2,1)}, u32[]{:S(2)}, u32[]{:S(2)}) collective-permute-start(bf16[2,32,16,512]{3,2,1,0:T(8,128)(2,1)S(1)} %fusion.6.refs_0_), channel_id=1, source_target_pairs={{0,4},{2,6},{4,0},{6,2},{8,12},{10,14},{12,8},{14,10},{16,20},{18,... | collective-permute-start | bytes 3145736 | tf_op jit(solution)/shard_map/ppermute | solution.py:465
  7.8 105.0 %collective-permute-start.22 = (bf16[2,32,16,512]{3,2,1,0:T(8,128)(2,1)S(1)}, bf16[2,32,16,512]{3,2,1,0:T(8,128)(2,1)}, u32[]{:S(2)}, u32[]{:S(2)}) collective-permute-start(bf16[2,32,16,512]{3,2,1,0:T(8,128)(2,1)S(1)} %fusion.6.refs_0_), channel_id=1, source_target_pairs={{0,2},{2,0},{4,6},{6,4},{8,10},{10,8},{12,14},{14,12},{16,18},{18,... | collective-permute-start | bytes 3145736 | tf_op jit(solution)/shard_map/ppermute | solution.py:465
  7.8 21.7 %collective-permute-start.8 = (f32[2,128,512]{2,1,0:T(8,128)}, f32[2,128,512]{2,1,0:T(8,128)}, u32[]{:S(2)}, u32[]{:S(2)}) collective-permute-start(f32[2,128,512]{2,1,0:T(8,128)} %get-tuple-element.43), channel_id=1, source_target_pairs={{0,1},{1,0},{2,3},{3,2},{4,5},{5,4},{6,7},{7,6},{8,9},{9,8},{10,11... | collective-permute-start | bytes 1572872 | tf_op jit(solution)/shard_map/ppermute | solution.py:487
  8.5 113.9 %collective-permute-start = (bf16[2,32,16,512]{3,2,1,0:T(8,128)(2,1)S(1)}, bf16[2,32,16,512]{3,2,1,0:T(8,128)(2,1)S(1)}, u32[]{:S(2)}, u32[]{:S(2)}) collective-permute-start(bf16[2,32,16,512]{3,2,1,0:T(8,128)(2,1)S(1)} %fusion.5.refs_0_), channel_id=1, source_target_pairs={{0,4},{2,6},{4,0},{6,2},{8,12},{10,14},{12,8},{14,10},{16,20},{18,... | collective-permute-start | bytes 3145736 | tf_op jit(solution)/shard_map/ppermute | solution.py:465
  19.1 16.9 %collective-permute-start.7 = (f32[2,128,512]{2,1,0:T(8,128)}, f32[2,128,512]{2,1,0:T(8,128)}, u32[]{:S(2)}, u32[]{:S(2)}) collective-permute-start(f32[2,128,512]{2,1,0:T(8,128)} %collective-permute-done.6.refs_0_.refs_1_), channel_id=1, source_target_pairs={{0,2},{2,0},{4,6},{6,4},{8,10},{10,8},{12,14},{14,12},{16,18},{18,... | collective-permute-start | bytes 1572872 | tf_op jit(solution)/shard_map/ppermute | solution.py:465
  90.7 20.0 %collective-permute-start.16 = (bf16[2,2,256,512]{3,2,1,0:T(8,128)(2,1)}, bf16[2,2,256,512]{3,2,1,0:T(8,128)(2,1)}, u32[]{:S(2)}, u32[]{:S(2)}) collective-permute-start(bf16[2,2,256,512]{3,2,1,0:T(8,128)(2,1)} %get-tuple-element.34), channel_id=1, source_target_pairs={{0,2},{2,0},{4,6},{6,4},{8,10},{10,8},{12,14},{14,12},{16,18},{18,... | collective-permute-start | bytes 3145736 | tf_op jit(solution)/shard_map/ppermute | solution.py:465
  91.3 22.0 %collective-permute-start.23 = (bf16[2,32,16,512]{3,2,1,0:T(8,128)(2,1)}, bf16[2,32,16,512]{3,2,1,0:T(8,128)(2,1)}, u32[]{:S(2)}, u32[]{:S(2)}) collective-permute-start(bf16[2,32,16,512]{3,2,1,0:T(8,128)(2,1)} %collective-permute-done.21.refs_1_), channel_id=1, source_target_pairs={{0,2},{2,0},{4,6},{6,4},{8,10},{10,8},{12,14},{14,12},{16,18},{18,... | collective-permute-start | bytes 3145736 | tf_op jit(solution)/shard_map/ppermute | solution.py:465
  97.5 24.9 %collective-permute-start.14 = (bf16[2,2,256,512]{3,2,1,0:T(8,128)(2,1)}, bf16[2,2,256,512]{3,2,1,0:T(8,128)(2,1)}, u32[]{:S(2)}, u32[]{:S(2)}) collective-permute-start(bf16[2,2,256,512]{3,2,1,0:T(8,128)(2,1)} %get-tuple-element.32), channel_id=1, source_target_pairs={{0,2},{2,0},{4,6},{6,4},{8,10},{10,8},{12,14},{14,12},{16,18},{18,... | collective-permute-start | bytes 3145736 | tf_op jit(solution)/shard_map/ppermute | solution.py:465
  110.7 21.0 %collective-permute-start.10 = (bf16[2,2,256,512]{3,2,1,0:T(8,128)(2,1)}, bf16[2,2,256,512]{3,2,1,0:T(8,128)(2,1)}, u32[]{:S(2)}, u32[]{:S(2)}) collective-permute-start(bf16[2,2,256,512]{3,2,1,0:T(8,128)(2,1)} %get-tuple-element.28), channel_id=1, source_target_pairs={{0,2},{2,0},{4,6},{6,4},{8,10},{10,8},{12,14},{14,12},{16,18},{18,... | collective-permute-start | bytes 3145736 | tf_op jit(solution)/shard_map/ppermute | solution.py:465
  112.8 22.4 %collective-permute-start.12 = (bf16[2,2,256,512]{3,2,1,0:T(8,128)(2,1)}, bf16[2,2,256,512]{3,2,1,0:T(8,128)(2,1)}, u32[]{:S(2)}, u32[]{:S(2)}) collective-permute-start(bf16[2,2,256,512]{3,2,1,0:T(8,128)(2,1)} %get-tuple-element.30), channel_id=1, source_target_pairs={{0,2},{2,0},{4,6},{6,4},{8,10},{10,8},{12,14},{14,12},{16,18},{18,... | collective-permute-start | bytes 3145736 | tf_op jit(solution)/shard_map/ppermute | solution.py:465
  122.4 16.3 %collective-permute-start.1 = (bf16[2,32,16,512]{3,2,1,0:T(8,128)(2,1)S(1)}, bf16[2,32,16,512]{3,2,1,0:T(8,128)(2,1)S(1)}, u32[]{:S(2)}, u32[]{:S(2)}) collective-permute-start(bf16[2,32,16,512]{3,2,1,0:T(8,128)(2,1)S(1)} %fusion.5.refs_0_), channel_id=1, source_target_pairs={{0,2},{2,0},{4,6},{6,4},{8,10},{10,8},{12,14},{14,12},{16,18},{18,... | collective-permute-start | bytes 3145736 | tf_op jit(solution)/shard_map/ppermute | solution.py:465
  122.5 16.8 %collective-permute-start.2 = (bf16[2,32,16,512]{3,2,1,0:T(8,128)(2,1)S(1)}, bf16[2,32,16,512]{3,2,1,0:T(8,128)(2,1)S(1)}, u32[]{:S(2)}, u32[]{:S(2)}) collective-permute-start(bf16[2,32,16,512]{3,2,1,0:T(8,128)(2,1)S(1)} %collective-permute-done.refs_1_), channel_id=1, source_target_pairs={{0,2},{2,0},{4,6},{6,4},{8,10},{10,8},{12,14},{14,12},{16,18},{18,... | collective-permute-start | bytes 3145736 | tf_op jit(solution)/shard_map/ppermute | solution.py:465
  127.5 20.1 %collective-permute-start.15 = (bf16[2,256,512]{2,1,0:T(8,128)(2,1)}, bf16[2,256,512]{2,1,0:T(8,128)(2,1)}, u32[]{:S(2)}, u32[]{:S(2)}) collective-permute-start(bf16[2,256,512]{2,1,0:T(8,128)(2,1)} %fusion.16), channel_id=1, source_target_pairs={{0,4},{2,6},{4,0},{6,2},{8,12},{10,14},{12,8},{14,10},{16,20},{18,... | collective-permute-start | bytes 1572872 | tf_op jit(solution)/shard_map/ppermute | solution.py:465
  131.6 18.2 %collective-permute-start.18 = (bf16[2,256,512]{2,1,0:T(8,128)(2,1)}, bf16[2,256,512]{2,1,0:T(8,128)(2,1)}, u32[]{:S(2)}, u32[]{:S(2)}) collective-permute-start(bf16[2,256,512]{2,1,0:T(8,128)(2,1)} %fusion.7), channel_id=1, source_target_pairs={{0,8},{2,10},{4,12},{6,14},{8,16},{10,18},{12,20},{14,22},{16,24},... | collective-permute-start | bytes 1572872 | tf_op jit(solution)/shard_map/ppermute | solution.py:465
  135.2 24.6 %collective-permute-start.24 = (bf16[2,256,512]{2,1,0:T(8,128)(2,1)}, bf16[2,256,512]{2,1,0:T(8,128)(2,1)}, u32[]{:S(2)}, u32[]{:S(2)}) collective-permute-start(bf16[2,256,512]{2,1,0:T(8,128)(2,1)} %get-tuple-element.36), channel_id=1, source_target_pairs={{0,8},{2,10},{4,12},{6,14},{8,16},{10,18},{12,20},{14,22},{16,24},... | collective-permute-start | bytes 1572872 | tf_op jit(solution)/shard_map/ppermute | solution.py:465
  138.7 66.0 %collective-permute-start.11 = (bf16[2,256,512]{2,1,0:T(8,128)(2,1)}, bf16[2,256,512]{2,1,0:T(8,128)(2,1)}, u32[]{:S(2)}, u32[]{:S(2)}) collective-permute-start(bf16[2,256,512]{2,1,0:T(8,128)(2,1)} %fusion.14), channel_id=1, source_target_pairs={{0,4},{2,6},{4,0},{6,2},{8,12},{10,14},{12,8},{14,10},{16,20},{18,... | collective-permute-start | bytes 1572872 | tf_op jit(solution)/shard_map/ppermute | solution.py:465
  140.7 30.3 %collective-permute-start.13 = (bf16[2,256,512]{2,1,0:T(8,128)(2,1)}, bf16[2,256,512]{2,1,0:T(8,128)(2,1)S(1)}, u32[]{:S(2)}, u32[]{:S(2)}) collective-permute-start(bf16[2,256,512]{2,1,0:T(8,128)(2,1)} %fusion.15), channel_id=1, source_target_pairs={{0,4},{2,6},{4,0},{6,2},{8,12},{10,14},{12,8},{14,10},{16,20},{18,... | collective-permute-start | bytes 1572872 | tf_op jit(solution)/shard_map/ppermute | solution.py:465
  147.7 23.2 %collective-permute-start.3 = (bf16[2,256,512]{2,1,0:T(8,128)(2,1)}, bf16[2,256,512]{2,1,0:T(8,128)(2,1)S(1)}, u32[]{:S(2)}, u32[]{:S(2)}) collective-permute-start(bf16[2,256,512]{2,1,0:T(8,128)(2,1)} %get-tuple-element.22), channel_id=1, source_target_pairs={{0,8},{2,10},{4,12},{6,14},{8,16},{10,18},{12,20},{14,22},{16,24},... | collective-permute-start | bytes 1572872 | tf_op jit(solution)/shard_map/ppermute | solution.py:465
  151.5 30.7 %collective-permute-start.19 = (bf16[2,256,512]{2,1,0:T(8,128)(2,1)S(1)}, bf16[2,256,512]{2,1,0:T(8,128)(2,1)S(1)}, u32[]{:S(2)}, u32[]{:S(2)}) collective-permute-start(bf16[2,256,512]{2,1,0:T(8,128)(2,1)S(1)} %fusion.9), channel_id=1, source_target_pairs={{0,8},{2,10},{4,12},{6,14},{8,16},{10,18},{12,20},{14,22},{16,24},... | collective-permute-start | bytes 1572872 | tf_op jit(solution)/shard_map/ppermute | solution.py:465
  160.9 32.5 %collective-permute-start.25 = (bf16[2,256,512]{2,1,0:T(8,128)(2,1)S(1)}, bf16[2,256,512]{2,1,0:T(8,128)(2,1)S(1)}, u32[]{:S(2)}, u32[]{:S(2)}) collective-permute-start(bf16[2,256,512]{2,1,0:T(8,128)(2,1)S(1)} %slice_add_fusion.1), channel_id=1, source_target_pairs={{0,8},{2,10},{4,12},{6,14},{8,16},{10,18},{12,20},{14,22},{16,24},... | collective-permute-start | bytes 1572872 | tf_op jit(solution)/shard_map/ppermute | solution.py:465
  171.0 33.6 %collective-permute-start.4 = (bf16[2,256,512]{2,1,0:T(8,128)(2,1)S(1)}, bf16[2,256,512]{2,1,0:T(8,128)(2,1)S(1)}, u32[]{:S(2)}, u32[]{:S(2)}) collective-permute-start(bf16[2,256,512]{2,1,0:T(8,128)(2,1)S(1)} %slice_add_fusion.3), channel_id=1, source_target_pairs={{0,8},{2,10},{4,12},{6,14},{8,16},{10,18},{12,20},{14,22},{16,24},... | collective-permute-start | bytes 1572872 | tf_op jit(solution)/shard_map/ppermute | solution.py:465
  183.4 32.4 %collective-permute-start.20 = (bf16[2,256,512]{2,1,0:T(8,128)(2,1)S(1)}, bf16[2,256,512]{2,1,0:T(8,128)(2,1)S(1)}, u32[]{:S(2)}, u32[]{:S(2)}) collective-permute-start(bf16[2,256,512]{2,1,0:T(8,128)(2,1)S(1)} %fusion.11), channel_id=1, source_target_pairs={{0,8},{2,10},{4,12},{6,14},{8,16},{10,18},{12,20},{14,22},{16,24},... | collective-permute-start | bytes 1572872 | tf_op jit(solution)/shard_map/ppermute | solution.py:465
  193.4 33.6 %collective-permute-start.26 = (bf16[2,256,512]{2,1,0:T(8,128)(2,1)S(1)}, bf16[2,256,512]{2,1,0:T(8,128)(2,1)S(1)}, u32[]{:S(2)}, u32[]{:S(2)}) collective-permute-start(bf16[2,256,512]{2,1,0:T(8,128)(2,1)S(1)} %slice_add_fusion), channel_id=1, source_target_pairs={{0,8},{2,10},{4,12},{6,14},{8,16},{10,18},{12,20},{14,22},{16,24},... | collective-permute-start | bytes 1572872 | tf_op jit(solution)/shard_map/ppermute | solution.py:465
  204.7 31.6 %collective-permute-start.5 = (bf16[2,256,512]{2,1,0:T(8,128)(2,1)S(1)}, bf16[2,256,512]{2,1,0:T(8,128)(2,1)S(1)}, u32[]{:S(2)}, u32[]{:S(2)}) collective-permute-start(bf16[2,256,512]{2,1,0:T(8,128)(2,1)S(1)} %slice_add_fusion.2), channel_id=1, source_target_pairs={{0,8},{2,10},{4,12},{6,14},{8,16},{10,18},{12,20},{14,22},{16,24},... | collective-permute-start | bytes 1572872 | tf_op jit(solution)/shard_map/ppermute | solution.py:465
  237.2 16.8 %collective-permute-start.27 = (bf16[2,256,512]{2,1,0:T(8,128)(2,1)S(1)}, bf16[2,256,512]{2,1,0:T(8,128)(2,1)}, u32[]{:S(2)}, u32[]{:S(2)}) collective-permute-start(bf16[2,256,512]{2,1,0:T(8,128)(2,1)S(1)} %fusion.13.refs_0_), channel_id=1, source_target_pairs={{0,8},{2,10},{4,12},{6,14},{8,16},{10,18},{12,20},{14,22},{16,24},... | collective-permute-start | bytes 1572872 | tf_op jit(solution)/shard_map/ppermute | solution.py:465
  237.3 27.9 %collective-permute-start.46 = (bf16[2,256,512]{2,1,0:T(8,128)(2,1)S(1)}, bf16[2,256,512]{2,1,0:T(8,128)(2,1)}, u32[]{:S(2)}, u32[]{:S(2)}) collective-permute-start(bf16[2,256,512]{2,1,0:T(8,128)(2,1)S(1)} %get-tuple-element.38.refs_0_), channel_id=1, source_target_pairs={{0,8},{2,10},{4,12},{6,14},{8,16},{10,18},{12,20},{14,22},{16,24},... | collective-permute-start | bytes 1572872 | tf_op jit(solution)/shard_map/ppermute | solution.py:465
  238.6 26.6 %collective-permute-start.43 = (bf16[2,256,512]{2,1,0:T(8,128)(2,1)S(1)}, bf16[2,256,512]{2,1,0:T(8,128)(2,1)S(1)}, u32[]{:S(2)}, u32[]{:S(2)}) collective-permute-start(bf16[2,256,512]{2,1,0:T(8,128)(2,1)S(1)} %get-tuple-element.38.refs_0_), channel_id=1, source_target_pairs={{0,4},{2,6},{4,0},{6,2},{8,12},{10,14},{12,8},{14,10},{16,20},{18,... | collective-permute-start | bytes 1572872 | tf_op jit(solution)/shard_map/ppermute | solution.py:465
  254.0 22.5 %collective-permute-start.28 = (bf16[2,256,512]{2,1,0:T(8,128)(2,1)}, bf16[2,256,512]{2,1,0:T(8,128)(2,1)}, u32[]{:S(2)}, u32[]{:S(2)}) collective-permute-start(bf16[2,256,512]{2,1,0:T(8,128)(2,1)} %collective-permute-done.27.refs_0_), channel_id=1, source_target_pairs={{0,8},{2,10},{4,12},{6,14},{8,16},{10,18},{12,20},{14,22},{16,24},... | collective-permute-start | bytes 1572872 | tf_op jit(solution)/shard_map/ppermute | solution.py:465
  254.0 23.0 %collective-permute-start.44 = (bf16[2,256,512]{2,1,0:T(8,128)(2,1)S(1)}, bf16[2,256,512]{2,1,0:T(8,128)(2,1)S(1)}, u32[]{:S(2)}, u32[]{:S(2)}) collective-permute-start(bf16[2,256,512]{2,1,0:T(8,128)(2,1)S(1)} %get-tuple-element.38.refs_0_), channel_id=1, source_target_pairs={{0,2},{2,0},{4,6},{6,4},{8,10},{10,8},{12,14},{14,12},{16,18},{18,... | collective-permute-start | bytes 1572872 | tf_op jit(solution)/shard_map/ppermute | solution.py:465
  254.0 23.0 %collective-permute-start.40 = (bf16[2,256,512]{2,1,0:T(8,128)(2,1)S(1)}, bf16[2,256,512]{2,1,0:T(8,128)(2,1)S(1)}, u32[]{:S(2)}, u32[]{:S(2)}) collective-permute-start(bf16[2,256,512]{2,1,0:T(8,128)(2,1)S(1)} %fusion.13.refs_0_), channel_id=1, source_target_pairs={{0,4},{2,6},{4,0},{6,2},{8,12},{10,14},{12,8},{14,10},{16,20},{18,... | collective-permute-start | bytes 1572872 | tf_op jit(solution)/shard_map/ppermute | solution.py:465
  265.2 22.5 %collective-permute-start.50 = (bf16[2,256,512]{2,1,0:T(8,128)(2,1)}, bf16[2,256,512]{2,1,0:T(8,128)(2,1)}, u32[]{:S(2)}, u32[]{:S(2)}) collective-permute-start(bf16[2,256,512]{2,1,0:T(8,128)(2,1)} %collective-permute-done.46.refs_4_), channel_id=1, source_target_pairs={{0,8},{2,10},{4,12},{6,14},{8,16},{10,18},{12,20},{14,22},{16,24},... | collective-permute-start | bytes 1572872 | tf_op jit(solution)/shard_map/ppermute | solution.py:465
  277.0 21.8 %collective-permute-start.29 = (bf16[2,256,512]{2,1,0:T(8,128)(2,1)}, bf16[2,256,512]{2,1,0:T(8,128)(2,1)S(1)}, u32[]{:S(2)}, u32[]{:S(2)}) collective-permute-start(bf16[2,256,512]{2,1,0:T(8,128)(2,1)} %collective-permute-done.28.refs_0_), channel_id=1, source_target_pairs={{0,8},{2,10},{4,12},{6,14},{8,16},{10,18},{12,20},{14,22},{16,24},... | collective-permute-start | bytes 1572872 | tf_op jit(solution)/shard_map/ppermute | solution.py:465
  277.0 23.2 %collective-permute-start.47 = (bf16[2,256,512]{2,1,0:T(8,128)(2,1)}, bf16[2,256,512]{2,1,0:T(8,128)(2,1)S(1)}, u32[]{:S(2)}, u32[]{:S(2)}) collective-permute-start(bf16[2,256,512]{2,1,0:T(8,128)(2,1)} %collective-permute-done.46.refs_4_), channel_id=1, source_target_pairs={{0,4},{2,6},{4,0},{6,2},{8,12},{10,14},{12,8},{14,10},{16,20},{18,... | collective-permute-start | bytes 1572872 | tf_op jit(solution)/shard_map/ppermute | solution.py:465
  278.6 23.2 %collective-permute-start.45 = (bf16[2,256,512]{2,1,0:T(8,128)(2,1)S(1)}, bf16[2,256,512]{2,1,0:T(8,128)(2,1)S(1)}, u32[]{:S(2)}, u32[]{:S(2)}) collective-permute-start(bf16[2,256,512]{2,1,0:T(8,128)(2,1)S(1)} %collective-permute-done.43.refs_1_), channel_id=1, source_target_pairs={{0,2},{2,0},{4,6},{6,4},{8,10},{10,8},{12,14},{14,12},{16,18},{18,... | collective-permute-start | bytes 1572872 | tf_op jit(solution)/shard_map/ppermute | solution.py:465
  287.7 14.9 %collective-permute-start.48 = (bf16[2,256,512]{2,1,0:T(8,128)(2,1)}, bf16[2,256,512]{2,1,0:T(8,128)(2,1)}, u32[]{:S(2)}, u32[]{:S(2)}) collective-permute-start(bf16[2,256,512]{2,1,0:T(8,128)(2,1)} %collective-permute-done.46.refs_4_), channel_id=1, source_target_pairs={{0,2},{2,0},{4,6},{6,4},{8,10},{10,8},{12,14},{14,12},{16,18},{18,... | collective-permute-start | bytes 1572872 | tf_op jit(solution)/shard_map/ppermute | solution.py:465
  290.5 19.5 %collective-permute-start.54 = (bf16[2,256,512]{2,1,0:T(8,128)(2,1)}, bf16[2,256,512]{2,1,0:T(8,128)(2,1)S(1)}, u32[]{:S(2)}, u32[]{:S(2)}) collective-permute-start(bf16[2,256,512]{2,1,0:T(8,128)(2,1)} %collective-permute-done.50.refs_8_), channel_id=1, source_target_pairs={{0,8},{2,10},{4,12},{6,14},{8,16},{10,18},{12,20},{14,22},{16,24},... | collective-permute-start | bytes 1572872 | tf_op jit(solution)/shard_map/ppermute | solution.py:465
  298.9 15.1 %collective-permute-start.51 = (bf16[2,256,512]{2,1,0:T(8,128)(2,1)}, bf16[2,256,512]{2,1,0:T(8,128)(2,1)S(1)}, u32[]{:S(2)}, u32[]{:S(2)}) collective-permute-start(bf16[2,256,512]{2,1,0:T(8,128)(2,1)} %collective-permute-done.50.refs_8_), channel_id=1, source_target_pairs={{0,4},{2,6},{4,0},{6,2},{8,12},{10,14},{12,8},{14,10},{16,20},{18,... | collective-permute-start | bytes 1572872 | tf_op jit(solution)/shard_map/ppermute | solution.py:465
  300.2 18.4 %collective-permute-start.30 = (bf16[1,256,512]{2,1,0:T(8,128)(2,1)S(1)}, bf16[1,256,512]{2,1,0:T(8,128)(2,1)S(1)}, u32[]{:S(2)}, u32[]{:S(2)}) collective-permute-start(bf16[1,256,512]{2,1,0:T(8,128)(2,1)S(1)} %slice.120), channel_id=1, source_target_pairs={{0,4},{2,6},{4,0},{6,2},{8,12},{10,14},{12,8},{14,10},{16,20},{18,... | collective-permute-start | bytes 786440 | tf_op jit(solution)/shard_map/ppermute | solution.py:465
  302.6 17.0 %collective-permute-start.32 = (bf16[1,256,512]{2,1,0:T(8,128)(2,1)}, bf16[1,256,512]{2,1,0:T(8,128)(2,1)S(1)}, u32[]{:S(2)}, u32[]{:S(2)}) collective-permute-start(bf16[1,256,512]{2,1,0:T(8,128)(2,1)} %slice.121), channel_id=1, source_target_pairs={{0,8},{2,10},{4,12},{6,14},{8,16},{10,18},{12,20},{14,22},{16,24},... | collective-permute-start | bytes 786440 | tf_op jit(solution)/shard_map/ppermute | solution.py:465
  302.6 24.6 %collective-permute-start.37 = (bf16[2,256,512]{2,1,0:T(8,128)(2,1)}, bf16[2,256,512]{2,1,0:T(8,128)(2,1)}, u32[]{:S(2)}, u32[]{:S(2)}) collective-permute-start(bf16[2,256,512]{2,1,0:T(8,128)(2,1)} %collective-permute-done.27.refs_0_), channel_id=1, source_target_pairs={{0,4},{2,6},{4,0},{6,2},{8,12},{10,14},{12,8},{14,10},{16,20},{18,... | collective-permute-start | bytes 1572872 | tf_op jit(solution)/shard_map/ppermute | solution.py:465
  310.0 17.1 %collective-permute-start.38 = (bf16[2,256,512]{2,1,0:T(8,128)(2,1)}, bf16[2,256,512]{2,1,0:T(8,128)(2,1)}, u32[]{:S(2)}, u32[]{:S(2)}) collective-permute-start(bf16[2,256,512]{2,1,0:T(8,128)(2,1)} %collective-permute-done.27.refs_0_), channel_id=1, source_target_pairs={{0,2},{2,0},{4,6},{6,4},{8,10},{10,8},{12,14},{14,12},{16,18},{18,... | collective-permute-start | bytes 1572872 | tf_op jit(solution)/shard_map/ppermute | solution.py:465
  322.3 16.3 %collective-permute-start.35 = (bf16[2,256,512]{2,1,0:T(8,128)(2,1)}, bf16[2,256,512]{2,1,0:T(8,128)(2,1)}, u32[]{:S(2)}, u32[]{:S(2)}) collective-permute-start(bf16[2,256,512]{2,1,0:T(8,128)(2,1)} %collective-permute-done.28.refs_0_), channel_id=1, source_target_pairs={{0,2},{2,0},{4,6},{6,4},{8,10},{10,8},{12,14},{14,12},{16,18},{18,... | collective-permute-start | bytes 1572872 | tf_op jit(solution)/shard_map/ppermute | solution.py:465
  338.5 19.7 %collective-permute-start.52 = (bf16[2,256,512]{2,1,0:T(8,128)(2,1)}, bf16[2,256,512]{2,1,0:T(8,128)(2,1)}, u32[]{:S(2)}, u32[]{:S(2)}) collective-permute-start(bf16[2,256,512]{2,1,0:T(8,128)(2,1)} %collective-permute-done.50.refs_8_), channel_id=1, source_target_pairs={{0,2},{2,0},{4,6},{6,4},{8,10},{10,8},{12,14},{14,12},{16,18},{18,... | collective-permute-start | bytes 1572872 | tf_op jit(solution)/shard_map/ppermute | solution.py:465
  338.6 19.6 %collective-permute-start.49 = (bf16[2,256,512]{2,1,0:T(8,128)(2,1)}, bf16[2,256,512]{2,1,0:T(8,128)(2,1)}, u32[]{:S(2)}, u32[]{:S(2)}) collective-permute-start(bf16[2,256,512]{2,1,0:T(8,128)(2,1)} %copy-done.23), channel_id=1, source_target_pairs={{0,2},{2,0},{4,6},{6,4},{8,10},{10,8},{12,14},{14,12},{16,18},{18,... | collective-permute-start | bytes 1572872 | tf_op jit(solution)/shard_map/ppermute | solution.py:465
  339.1 19.2 %collective-permute-start.53 = (bf16[2,256,512]{2,1,0:T(8,128)(2,1)S(1)}, bf16[2,256,512]{2,1,0:T(8,128)(2,1)S(1)}, u32[]{:S(2)}, u32[]{:S(2)}) collective-permute-start(bf16[2,256,512]{2,1,0:T(8,128)(2,1)S(1)} %collective-permute-done.51.refs_9_), channel_id=1, source_target_pairs={{0,2},{2,0},{4,6},{6,4},{8,10},{10,8},{12,14},{14,12},{16,18},{18,... | collective-permute-start | bytes 1572872 | tf_op jit(solution)/shard_map/ppermute | solution.py:465
  339.2 19.1 %collective-permute-start.57 = (bf16[2,256,512]{2,1,0:T(8,128)(2,1)S(1)}, bf16[2,256,512]{2,1,0:T(8,128)(2,1)S(1)}, u32[]{:S(2)}, u32[]{:S(2)}) collective-permute-start(bf16[2,256,512]{2,1,0:T(8,128)(2,1)S(1)} %collective-permute-done.54.refs_12_), channel_id=1, source_target_pairs={{0,2},{2,0},{4,6},{6,4},{8,10},{10,8},{12,14},{14,12},{16,18},{18,... | collective-permute-start | bytes 1572872 | tf_op jit(solution)/shard_map/ppermute | solution.py:465
  339.6 18.7 %collective-permute-start.58 = (bf16[2,256,512]{2,1,0:T(8,128)(2,1)S(1)}, bf16[2,256,512]{2,1,0:T(8,128)(2,1)S(1)}, u32[]{:S(2)}, u32[]{:S(2)}) collective-permute-start(bf16[2,256,512]{2,1,0:T(8,128)(2,1)S(1)} %constant_dynamic-update-slice_fusion.2.refs_13_), channel_id=1, source_target_pairs={{0,2},{2,0},{4,6},{6,4},{8,10},{10,8},{12,14},{14,12},{16,18},{18,... | collective-permute-start | bytes 1572872 | tf_op jit(solution)/shard_map/ppermute | solution.py:465
  (44 other events, 852.9 us)

commit v4 on v3

--- a/solution.py
+++ b/solution.py
@@ -250,46 +250,42 @@
 
 def collect_kernel(places, counts, *refs):
     m = pl.program_id(0)
-    owner_refs, (head_ref, rest_ref) = refs[:QUAD], refs[QUAD:]
-    bucket_rows, head_rows = owner_refs[0].shape[2], head_ref.shape[1]
-    for ref in (head_ref, rest_ref):
+    owner_refs, group_refs = refs[:QUAD], refs[QUAD:]
+    bucket_rows, unit_rows = owner_refs[0].shape[2], group_refs[0].shape[1]
+    for ref in group_refs:
         ref[...] = jnp.zeros(ref.shape, BF16)
     for i, owner_ref in enumerate(owner_refs):
 
         def pick(s, _):
             place = places[i, m, s]
 
-            @pl.when(jnp.logical_and(place >= 0, place < head_rows))
+            @pl.when(place >= 0)
             def _():
-                at = pl.multiple_of(jnp.maximum(place, 0), bucket_rows)
-                head_ref[0, pl.ds(at, bucket_rows), :] = owner_ref[0, s]
-
-            @pl.when(place >= head_rows)
-            def _():
-                at = pl.multiple_of(jnp.maximum(place - head_rows, 0), bucket_rows)
-                rest_ref[0, pl.ds(at, bucket_rows), :] = owner_ref[0, s]
+                group = place // unit_rows
+                at = pl.multiple_of(place - group * unit_rows, bucket_rows)
+                for k, ref in enumerate(group_refs):
+
+                    @pl.when(group == k)
+                    def _():
+                        ref[0, pl.ds(at, bucket_rows), :] = owner_ref[0, s]
 
             return 0
 
         lax.fori_loop(0, counts[i, m], pick, 0)
 
 
-def collect_moments(owners, places, counts, head_rows, rest_rows):
+def collect_moments(owners, places, counts, depth, unit_rows):
     mats, capacity, bucket_rows, rank = owners[0].shape
     slots = pl.BlockSpec((1, capacity, bucket_rows, rank), lambda m, *_: (m, 0, 0, 0))
+    group = pl.BlockSpec((1, unit_rows, rank), lambda m, *_: (m, 0, 0))
     return pl.pallas_call(
         collect_kernel,
-        out_shape=tuple(
-            jax.ShapeDtypeStruct((mats, rows, rank), BF16) for rows in (head_rows, rest_rows)
-        ),
+        out_shape=(jax.ShapeDtypeStruct((mats, unit_rows, rank), BF16),) * depth,
         grid_spec=pltpu.PrefetchScalarGridSpec(
             num_scalar_prefetch=2,
             grid=(mats,),
             in_specs=[slots] * QUAD,
-            out_specs=tuple(
-                pl.BlockSpec((1, rows, rank), lambda m, *_: (m, 0, 0))
-                for rows in (head_rows, rest_rows)
-            ),
+            out_specs=(group,) * depth,
         ),
         cost_estimate=pl.CostEstimate(
             flops=0, bytes_accessed=4 * QUAD * owners[0].size, transcendentals=0
@@ -334,30 +330,48 @@
     )(quads, group, grads, basis)
 
 
-def expand_kernel(quads, group, *refs):
-    parts, basis_ref = refs[:QUAD], refs[QUAD]
+def expand_kernel(quads, group, *refs, parts):
+    basis_ref = refs[parts]
     out_ref, joined = refs[-2:]
-    unit_rows = parts[0].shape[1]
-    for i, ref in enumerate(parts):
+    m = pl.program_id(0)
+    unit_rows = refs[0].shape[1]
+    used = 0
+    for i in range(QUAD):
         at = pl.multiple_of(quads[i] * unit_rows, unit_rows)
-        joined[pl.ds(at, unit_rows), :] = ref[0]
+        if parts == QUAD or i % 2 == 0:
+            joined[pl.ds(at, unit_rows), :] = refs[used][0]
+            used += 1
+        else:
+            low, high = refs[used], refs[used + 1]
+            used += 2
+            joined[pl.ds(at, unit_rows), :] = jnp.where(m < pl.num_programs(0) // 2, low[0], high[0])
     out_ref[0] = dot_bf16(joined[...], basis_ref[0], ((1,), (1,))).astype(BF16)
 
 
 def expand(parts, basis, quads, group, target, local_rows):
-    mats, unit_rows, rank = parts[0].shape
-    feats = basis.shape[1]
+    mats, feats, rank = basis.shape
+    unit_rows = parts[0][0].shape[1]
     rows = QUAD * unit_rows
-    part = pl.BlockSpec((1, unit_rows, rank), lambda m, q, g: (m, 0, 0))
-    in_specs = [part] * QUAD + [pl.BlockSpec((1, feats, rank), lambda m, q, g: (m, 0, 0))]
-    args = [quads, group, *parts, basis]
+    block = (1, unit_rows, rank)
+    half = mats // 2
+    in_specs, args = [], [quads, group]
+    for part in parts:
+        if len(part) == 1:
+            in_specs.append(pl.BlockSpec(block, lambda m, q, g: (m, 0, 0)))
+        else:
+            in_specs.append(pl.BlockSpec(block, lambda m, q, g: (jnp.minimum(m, half - 1), 0, 0)))
+            in_specs.append(pl.BlockSpec(block, lambda m, q, g: (jnp.maximum(m - half, 0), 0, 0)))
+        args += part
+    pieces = len(in_specs)
+    in_specs.append(pl.BlockSpec((1, feats, rank), lambda m, q, g: (m, 0, 0)))
+    args.append(basis)
     aliases = {}
     if target is not None:
         in_specs.append(pl.BlockSpec(memory_space=pl.ANY))
         aliases = {len(args): 0}
         args.append(target)
     return pl.pallas_call(
-        expand_kernel,
+        functools.partial(expand_kernel, parts=pieces),
         out_shape=jax.ShapeDtypeStruct((mats, local_rows, feats), BF16),
         grid_spec=pltpu.PrefetchScalarGridSpec(
             num_scalar_prefetch=2,
@@ -383,19 +397,28 @@
 
 
 def settle_kernel(piece_of, row_of, held, *refs, pieces):
-    piece_refs = refs[:pieces]
-    first_ref, second_ref, first_out, second_out, rows, sem = refs[pieces:]
+    count = sum(pieces)
+    first_ref, second_ref, first_out, second_out, rows, sem = refs[count:]
     m = pl.program_id(0)
+    half = pl.num_programs(0) // 2
+    sources = []
+    for i, parts in enumerate(pieces):
+        at = sum(pieces[:i])
+        if parts == 1:
+            sources.append((i, refs[at], None, 0))
+        else:
+            sources += [(i, refs[at], m < half, 0), (i, refs[at + 1], m >= half, half)]
     capacity, bucket_rows = rows.shape[0], rows.shape[1]
 
     def fetch(s, _):
         piece = piece_of[m, s]
         at = pl.multiple_of(row_of[m, s], bucket_rows)
-        for i, ref in enumerate(piece_refs):
-
-            @pl.when(piece == i)
+        for i, ref, mine, base in sources:
+
+            @pl.when(piece == i if mine is None else jnp.logical_and(piece == i, mine))
             def _():
-                pltpu.make_async_copy(ref.at[m, pl.ds(at, bucket_rows), :], rows.at[s], sem).start()
+                source = ref.at[m - base, pl.ds(at, bucket_rows), :]
+                pltpu.make_async_copy(source, rows.at[s], sem).start()
 
         return 0
 
@@ -417,7 +440,7 @@
     mats, _, capacity, bucket_rows, rank = first.shape
     spec = pl.BlockSpec((1, 1, capacity, bucket_rows, rank), lambda m, *_: (m, 0, 0, 0, 0))
     return pl.pallas_call(
-        functools.partial(settle_kernel, pieces=len(pieces)),
+        functools.partial(settle_kernel, pieces=tuple(len(p) for p in pieces)),
         out_shape=(
             jax.ShapeDtypeStruct(first.shape, F32),
             jax.ShapeDtypeStruct(second.shape, F32),
@@ -425,7 +448,7 @@
         grid_spec=pltpu.PrefetchScalarGridSpec(
             num_scalar_prefetch=3,
             grid=(mats,),
-            in_specs=[pl.BlockSpec(memory_space=pl.ANY)] * len(pieces) + [spec, spec],
+            in_specs=[pl.BlockSpec(memory_space=pl.ANY)] * sum(len(p) for p in pieces) + [spec, spec],
             out_specs=(spec, spec),
             scratch_shapes=[
                 pltpu.VMEM((capacity, bucket_rows, rank), BF16),
@@ -436,7 +459,7 @@
             flops=8 * first.size, bytes_accessed=18 * first.size, transcendentals=0
         ),
         name="settle",
-    )(piece_of, row_of, held, *pieces, first, second)
+    )(piece_of, row_of, held, *(v for p in pieces for v in p), first, second)
 
 
 def adam_update(first, second, grad_rows):
@@ -470,8 +493,8 @@
     def to_x(v):
         return permute(v, lambda i: i ^ 2)
 
-    def to_z(v):
-        return permute(v, lambda i: (i + QUAD) % replicas)
+    def to_z(v, layers=1):
+        return permute(v, lambda i: (i + layers * QUAD) % replicas)
 
     quarter = local_feats // QUAD
     my_core = me % 2
@@ -508,7 +531,7 @@
     quad_counts = jnp.sum(quad_occupied.astype(jnp.int32), axis=2)
     occupied, bucket_of = quad_occupied[0], quad_buckets[0]
     quad_units = quad_buckets // unit_buckets
-    steps = (my_z + depth - 1 - quad_units // QUAD) % depth
+    steps = (quad_units // QUAD + depth - my_z) % depth
     places = steps * unit_rows + (quad_buckets % unit_buckets) * bucket_rows
     wanted = jnp.logical_and(quad_occupied, quad_units % QUAD == my_quad)
     places = jnp.where(wanted, places, -1).astype(jnp.int32)
@@ -517,15 +540,14 @@
         slots = moment[:, 0].astype(BF16)
         across = to_x(slots)
         owners = (slots, across, to_core(slots), to_core(across))
-        held, rest = collect_moments(
-            owners, places, quad_counts, unit_rows, (depth - 1) * unit_rows
-        )
+        groups = collect_moments(owners, places, quad_counts, depth, unit_rows)
+        total = groups[0]
         for k in range(1, depth):
-            held = to_z(held) + rest[:, (k - 1) * unit_rows : k * unit_rows]
-        return held
-
-    first_unit = unit_moments(first_moment)
-    second_unit = unit_moments(second_moment)
+            total = total + to_z(groups[k], k)
+        return total
+
+    first_unit, second_unit = unit_moments(first_moment), unit_moments(second_moment)
+    first_unit, second_unit = lax.optimization_barrier((first_unit, second_unit))
 
     state = first_half([pieces[i] for i in fresh], gram)
     basis = second_half(raw_proj, pieces, offsets, state, splits * local_feats)
@@ -546,16 +568,17 @@
 
     def ring(unit):
         groups = []
-        across = None
+        across = (None,)
         half = mats // 2
         for k in range(depth):
             if 0 < k == depth - 1:
-                over_z = to_z(across[half:])
-                across = jnp.concatenate([to_x(unit[:half]), over_z])
+                over_z = to_z(across[0][half:])
+                across = (to_x(unit[:half]), over_z)
             else:
-                across = to_x(unit)
+                across = (to_x(unit),)
             core = to_core(unit)
-            groups.append((unit, across, core, to_core(across)))
+            both = tuple(to_core(v) for v in across)
+            groups.append(((unit,), across, (core,), both))
             if k + 1 < depth:
                 unit = to_z(unit)
         return groups

time: 369 us -> 432 us (1.17)
  starting transfers between devices: 29.4 us -> 121 us
  waiting for transfers between devices: 179 us -> 152 us
  local copies, waits for them, and re-layouts: 11.7 us -> 7.09 us
    ppermute x57 -> x59, starting transfers between devices: 25.9 us -> 118 us  [permute(): return lax.ppermute(v, 'dp', [(i, target(i)) for i in range(replicas)])]
    ppermute x57 -> x59, waiting for transfers between devices: 159 us -> 130 us  [permute(): return lax.ppermute(v, 'dp', [(i, target(i)) for i in range(replicas)])]
  transfers between devices with their start and end apart: 59 -> 61, of which waited for: 22 -> 17; matrix products, arithmetic and copies ran while one was open for 7% -> 6% of each run, Pallas kernels for 31% -> 16%
where the time goes in v4:
time: 432 us
  waiting for transfers between devices  152 us (35%)
  Pallas kernels  125 us (29%)
  starting transfers between devices  121 us (28%)
  other arithmetic  25.6 us (6%)
  local copies, waits for them, and re-layouts  7.09 us (2%)
    ppermute x59, waiting for transfers between devices, permute(): return lax.ppermute(v, 'dp', [(i, target(i)) for i in range(replicas)])  130 us
    ppermute x59, starting transfers between devices, permute(): return lax.ppermute(v, 'dp', [(i, target(i)) for i in range(replicas)])  118 us
    pallas_call x4, Pallas kernels, project(): pl.pallas_call(project_kernel, out_shape=(out, out), grid_spec=pltpu.Pref...  25.2 us
    pallas_call x4, Pallas kernels, expand(): pl.pallas_call(functools.partial(expand_kernel, parts=pieces), out_shape=...  25.2 us
    ppermute x2, waiting for transfers between devices, shards(): lax.ppermute(parts[i], 'fsdp', [(j, (j + shift) % splits) for j in range(...  22.4 us
    pallas_call x1, Pallas kernels, second_half(): pl.pallas_call(functools.partial(second_half_kernel, pieces=len(pieces)),...  22.1 us
    pallas_call x1, Pallas kernels, first_half(): pl.pallas_call(functools.partial(first_half_kernel, pieces=len(fresh)), o...  20.2 us
    pallas_call x2, Pallas kernels, collect_moments(): pl.pallas_call(collect_kernel, out_shape=(jax.ShapeDtypeStruct((mats, uni...  12.1 us
  transfers between devices with their start and end apart: 61, of which 17 were waited for; matrix products, arithmetic and copies ran while one was open for 6% of the time, Pallas kernels for 16%

profile of v4, /device:TPU:0, one launch (start us, length us, event | category | flops | bytes accessed | tf_op | source)
XLA Modules:
  0.0 431.5 jit_solution(7983429173699522871)
XLA Ops:
  2.0 3.1 collective-permute-start.12
  5.1 12.7 %collective-permute-done.12.refs_0_.refs_1_ = f32[2,128,512]{2,1,0:T(8,128)S(1)} collective-permute-done((f32[2,128,512]{2,1,0:T(8,128)S(1)}, f32[2,128,512]{2,1,0:T(8,128)S(1)}, u32[]{:S(2)}, u32[]{:S(2)}) %collective-permute-start.12) | collective-permute-done | bytes 524320 | tf_op jit(solution)/shard_map/ppermute | solution.py:510
  18.5 9.7 %collective-permute-done.14.refs_0_.refs_3_ = f32[2,128,512]{2,1,0:T(8,128)S(1)} collective-permute-done((f32[2,128,512]{2,1,0:T(8,128)S(1)}, f32[2,128,512]{2,1,0:T(8,128)S(1)}, u32[]{:S(2)}, u32[]{:S(2)}) %collective-permute-start.14) | collective-permute-done | bytes 524320 | tf_op jit(solution)/shard_map/ppermute | solution.py:510
  28.9 5.9 %gram.2.refs_2_ = f32[2,512,512]{2,1,0:T(8,128)} custom-call(f32[2,512,512]{2,1,0:T(8,128)} %refs_0_.3), custom_call_target="tpu_custom_call" | custom-call | flops 3221225472 | bytes 4194304 | tf_op jit(solution)/shard_map/gram/pallas_call | solution.py:130
  35.6 6.1 %gram.3.refs_2_ = f32[2,512,512]{2,1,0:T(8,128)} custom-call(f32[2,128,512]{2,1,0:T(8,128)} %copy-done.31, f32[2,128,512]{2,1,0:T(8,128)} %copy-done.33, f32[2,512,512]{2,1,0:T(8,128)} %gram.2.refs_2_), custom_call_target="tpu_custom_call" | custom-call | flops 1610612736 | bytes 3145728 | tf_op jit(solution)/shard_map/gram/pallas_call | solution.py:130
  42.5 20.2 %first_half.1 = (f32[2,256,256]{2,1,0:T(8,128)}, f32[2,256,256]{2,1,0:T(8,128)}, f32[2,256,256]{2,1,0:T(8,128)}) custom-call(f32[2,128,512]{2,1,0:T(8,128)} %copy-done.32, f32[2,128,512]{2,1,0:T(8,128)} %copy-done.34, f32[2,512,512]{2,1,0:T(8,128)} %gram.3.refs_2_), custom_call_target="tpu_custom_call" | custom-call | flops 20000000000 | bytes 2097152 | tf_op jit(solution)/shard_map/first_half/pallas_call | solution.py:214
  62.7 22.1 %second_half.1.basis_ref.refs_4_.refs_6_ = bf16[2,1024,512]{2,1,0:T(8,128)(2,1)} custom-call(s32[5]{0:T(128)} %stack.71.offsets, f32[2,512,512]{2,1,0:T(8,128)} %refs_0_.3, f32[2,128,512]{2,1,0:T(8,128)} %copy-done.31, f32[2,128,512]{2,1,0:T(8,128)} %copy-done.33, f32[2,128,512]{2,1,0:T(8,128)} %copy-done.32, f32[2,128,512]{2,1,0:T(8,128)} %copy-done.34, ...), custom_call_target="tpu_custom_call" | custom-call | flops 20000000000 | bytes 6291456 | tf_op jit(solution)/shard_map/second_half/pallas_call | solution.py:236
  84.8 6.3 %project.7 = (bf16[2,2,256,512]{3,2,1,0:T(8,128)(2,1)}, bf16[2,2,256,512]{3,2,1,0:T(8,128)(2,1)}) custom-call(s32[4]{0:T(128)} %pad_add_fusion.2.quads, s32[1]{0:T(128)} %bitcast.26.group, bf16[1,2,4096,1024]{3,2,1,0:T(8,128)(2,1)} %grads_ref.7, bf16[2,1024,512]{2,1,0:T(8,128)(2,1)} %second_half.1.basis_ref.refs_4_.refs_6_), custom_call_target="tpu_custom_call" | custom-call | flops 2147483648 | bytes 6291456 | tf_op jit(solution)/shard_map/project/pallas_call | solution.py:311
  94.3 6.4 %project.6 = (bf16[2,2,256,512]{3,2,1,0:T(8,128)(2,1)}, bf16[2,2,256,512]{3,2,1,0:T(8,128)(2,1)}) custom-call(s32[4]{0:T(128)} %pad_add_fusion.2.quads, s32[1]{0:T(128)} %bitcast.23.group, bf16[1,2,4096,1024]{3,2,1,0:T(8,128)(2,1)} %grads_ref.7, bf16[2,1024,512]{2,1,0:T(8,128)(2,1)} %second_half.1.basis_ref.refs_4_.refs_6_), custom_call_target="tpu_custom_call" | custom-call | flops 2147483648 | bytes 6291456 | tf_op jit(solution)/shard_map/project/pallas_call | solution.py:311
  101.3 2.2 fusion.17
  105.2 6.3 %project.5 = (bf16[2,2,256,512]{3,2,1,0:T(8,128)(2,1)}, bf16[2,2,256,512]{3,2,1,0:T(8,128)(2,1)}) custom-call(s32[4]{0:T(128)} %pad_add_fusion.2.quads, s32[1]{0:T(128)} %bitcast.4.group, bf16[1,2,4096,1024]{3,2,1,0:T(8,128)(2,1)} %grads_ref.7, bf16[2,1024,512]{2,1,0:T(8,128)(2,1)} %second_half.1.basis_ref.refs_4_.refs_6_), custom_call_target="tpu_custom_call" | custom-call | flops 2147483648 | bytes 6291456 | tf_op jit(solution)/shard_map/project/pallas_call | solution.py:311
  111.8 7.1 %collective-permute-done.6.refs_1_ = bf16[2,32,16,512]{3,2,1,0:T(8,128)(2,1)} collective-permute-done((bf16[2,32,16,512]{3,2,1,0:T(8,128)(2,1)}, bf16[2,32,16,512]{3,2,1,0:T(8,128)(2,1)}, u32[]{:S(2)}, u32[]{:S(2)}) %collective-permute-start.6) | collective-permute-done | bytes 1048608 | tf_op jit(solution)/shard_map/ppermute | solution.py:488
  119.5 2.0 fusion.16
  121.5 30.4 %collective-permute-done.23 = bf16[2,256,512]{2,1,0:T(8,128)(2,1)} collective-permute-done((bf16[2,256,512]{2,1,0:T(8,128)(2,1)}, bf16[2,256,512]{2,1,0:T(8,128)(2,1)}, u32[]{:S(2)}, u32[]{:S(2)}) %collective-permute-start.23) | collective-permute-done | bytes 524320 | tf_op jit(solution)/shard_map/ppermute | solution.py:488
  153.5 2.4 fusion.7
  157.6 6.2 %project.4 = (bf16[2,2,256,512]{3,2,1,0:T(8,128)(2,1)}, bf16[2,2,256,512]{3,2,1,0:T(8,128)(2,1)}) custom-call(s32[4]{0:T(128)} %pad_add_fusion.2.quads, s32[1]{0:T(128)} %bitcast.13.group, bf16[1,2,4096,1024]{3,2,1,0:T(8,128)(2,1)} %grads_ref.7, bf16[2,1024,512]{2,1,0:T(8,128)(2,1)} %second_half.1.basis_ref.refs_4_.refs_6_), custom_call_target="tpu_custom_call" | custom-call | flops 2147483648 | bytes 6291456 | tf_op jit(solution)/shard_map/project/pallas_call | solution.py:311
  163.8 2.1 fusion.15
  166.4 4.5 %collective-permute-done.24 = bf16[2,256,512]{2,1,0:T(8,128)(2,1)} collective-permute-done((bf16[2,256,512]{2,1,0:T(8,128)(2,1)}, bf16[2,256,512]{2,1,0:T(8,128)(2,1)}, u32[]{:S(2)}, u32[]{:S(2)}) %collective-permute-start.24) | collective-permute-done | bytes 524320 | tf_op jit(solution)/shard_map/ppermute | solution.py:488
  170.9 2.4 fusion.9
  175.7 6.1 %collect.3 = (bf16[2,256,512]{2,1,0:T(8,128)(2,1)}, bf16[2,256,512]{2,1,0:T(8,128)(2,1)}, bf16[2,256,512]{2,1,0:T(8,128)(2,1)}, bf16[2,256,512]{2,1,0:T(8,128)(2,1)}) custom-call(s32[4,2,32]{2,1,0:T(2,128)} %get-tuple-element.60.places, s32[4,2]{1,0:T(4,128)} %get-tuple-element.59.counts, bf16[2,32,16,512]{3,2,1,0:T(8,128)(2,1)} %fusion.6.refs_0_, ...), custom_call_target="tpu_custom_call" | custom-call | bytes 8388608 | tf_op jit(solution)/shard_map/collect/pallas_call | solution.py:281
  181.8 3.1 collective-permute-start.10
  184.9 3.1 collective-permute-done.19
  190.9 2.0 fusion.14
  192.9 2.6 fusion.11
  197.0 6.0 %collect.2 = (bf16[2,256,512]{2,1,0:T(8,128)(2,1)}, bf16[2,256,512]{2,1,0:T(8,128)(2,1)}, bf16[2,256,512]{2,1,0:T(8,128)(2,1)}, bf16[2,256,512]{2,1,0:T(8,128)(2,1)}) custom-call(s32[4,2,32]{2,1,0:T(2,128)} %get-tuple-element.60.places, s32[4,2]{1,0:T(4,128)} %get-tuple-element.59.counts, bf16[2,32,16,512]{3,2,1,0:T(8,128)(2,1)} %copy-done.2, ...), custom_call_target="tpu_custom_call" | custom-call | bytes 8388608 | tf_op jit(solution)/shard_map/collect/pallas_call | solution.py:281
  203.0 10.4 %collective-permute-done.10 = bf16[2,256,512]{2,1,0:T(8,128)(2,1)} collective-permute-done((bf16[2,256,512]{2,1,0:T(8,128)(2,1)}, bf16[2,256,512]{2,1,0:T(8,128)(2,1)}, u32[]{:S(2)}, u32[]{:S(2)}) %collective-permute-start.10) | collective-permute-done | bytes 524320 | tf_op jit(solution)/shard_map/ppermute | solution.py:488
  213.4 7.9 %collective-permute-start.3 = (bf16[2,256,512]{2,1,0:T(8,128)(2,1)}, bf16[2,256,512]{2,1,0:T(8,128)(2,1)S(1)}, u32[]{:S(2)}, u32[]{:S(2)}) collective-permute-start(bf16[2,256,512]{2,1,0:T(8,128)(2,1)} %get-tuple-element.29), channel_id=1, source_target_pairs={{0,8},{2,10},{4,12},{6,14},{8,16},{10,18},{12,20},{14,22},{16,24},... | collective-permute-start | bytes 1572872 | tf_op jit(solution)/shard_map/ppermute | solution.py:488
  221.3 25.6 %collective-permute-done.11 = bf16[2,256,512]{2,1,0:T(8,128)(2,1)} collective-permute-done((bf16[2,256,512]{2,1,0:T(8,128)(2,1)}, bf16[2,256,512]{2,1,0:T(8,128)(2,1)}, u32[]{:S(2)}, u32[]{:S(2)}) %collective-permute-start.11) | collective-permute-done | bytes 524320 | tf_op jit(solution)/shard_map/ppermute | solution.py:488
  246.8 10.2 %collective-permute-start.4 = (bf16[2,256,512]{2,1,0:T(8,128)(2,1)}, bf16[2,256,512]{2,1,0:T(8,128)(2,1)S(1)}, u32[]{:S(2)}, u32[]{:S(2)}) collective-permute-start(bf16[2,256,512]{2,1,0:T(8,128)(2,1)} %get-tuple-element.30), channel_id=1, source_target_pairs={{0,16},{2,18},{4,20},{6,22},{8,24},{10,26},{12,28},{14,30},{16,0},... | collective-permute-start | bytes 1572872 | tf_op jit(solution)/shard_map/ppermute | solution.py:488
  257.1 3.4 collective-permute-start.5
  263.6 17.7 %collective-permute-done.4 = bf16[2,256,512]{2,1,0:T(8,128)(2,1)S(1)} collective-permute-done((bf16[2,256,512]{2,1,0:T(8,128)(2,1)}, bf16[2,256,512]{2,1,0:T(8,128)(2,1)S(1)}, u32[]{:S(2)}, u32[]{:S(2)}) %collective-permute-start.4) | collective-permute-done | bytes 524320 | tf_op jit(solution)/shard_map/ppermute | solution.py:488
  284.6 10.5 %collective-permute-done.47.refs_4_ = bf16[2,256,512]{2,1,0:T(8,128)(2,1)S(1)} collective-permute-done((bf16[2,256,512]{2,1,0:T(8,128)(2,1)S(1)}, bf16[2,256,512]{2,1,0:T(8,128)(2,1)S(1)}, u32[]{:S(2)}, u32[]{:S(2)}) %collective-permute-start.47) | collective-permute-done | bytes 524320 | tf_op jit(solution)/shard_map/ppermute | solution.py:488
  295.1 23.1 %collective-permute-start.27 = (bf16[2,256,512]{2,1,0:T(8,128)(2,1)S(1)}, bf16[2,256,512]{2,1,0:T(8,128)(2,1)S(1)}, u32[]{:S(2)}, u32[]{:S(2)}) collective-permute-start(bf16[2,256,512]{2,1,0:T(8,128)(2,1)S(1)} %fusion.13.refs_0_), channel_id=1, source_target_pairs={{0,8},{2,10},{4,12},{6,14},{8,16},{10,18},{12,20},{14,22},{16,24},... | collective-permute-start | bytes 1572872 | tf_op jit(solution)/shard_map/ppermute | solution.py:488
  318.2 11.7 %collective-permute-start.51 = (bf16[2,256,512]{2,1,0:T(8,128)(2,1)S(1)}, bf16[2,256,512]{2,1,0:T(8,128)(2,1)}, u32[]{:S(2)}, u32[]{:S(2)}) collective-permute-start(bf16[2,256,512]{2,1,0:T(8,128)(2,1)S(1)} %collective-permute-done.47.refs_4_), channel_id=1, source_target_pairs={{0,8},{2,10},{4,12},{6,14},{8,16},{10,18},{12,20},{14,22},{16,24},... | collective-permute-start | bytes 1572872 | tf_op jit(solution)/shard_map/ppermute | solution.py:488
  331.9 9.7 %collective-permute-start.28 = (bf16[2,256,512]{2,1,0:T(8,128)(2,1)S(1)}, bf16[2,256,512]{2,1,0:T(8,128)(2,1)}, u32[]{:S(2)}, u32[]{:S(2)}) collective-permute-start(bf16[2,256,512]{2,1,0:T(8,128)(2,1)S(1)} %collective-permute-done.27.refs_0_), channel_id=1, source_target_pairs={{0,8},{2,10},{4,12},{6,14},{8,16},{10,18},{12,20},{14,22},{16,24},... | collective-permute-start | bytes 1572872 | tf_op jit(solution)/shard_map/ppermute | solution.py:488
  344.0 9.2 %collective-permute-start.55 = (bf16[2,256,512]{2,1,0:T(8,128)(2,1)}, bf16[2,256,512]{2,1,0:T(8,128)(2,1)S(1)}, u32[]{:S(2)}, u32[]{:S(2)}) collective-permute-start(bf16[2,256,512]{2,1,0:T(8,128)(2,1)} %collective-permute-done.51.refs_8_), channel_id=1, source_target_pairs={{0,8},{2,10},{4,12},{6,14},{8,16},{10,18},{12,20},{14,22},{16,24},... | collective-permute-start | bytes 1572872 | tf_op jit(solution)/shard_map/ppermute | solution.py:488
  353.3 1.9 collective-permute-start.31
  355.2 2.6 collective-permute-start.29
  358.1 7.8 %collective-permute-done.55.refs_12_ = bf16[2,256,512]{2,1,0:T(8,128)(2,1)S(1)} collective-permute-done((bf16[2,256,512]{2,1,0:T(8,128)(2,1)}, bf16[2,256,512]{2,1,0:T(8,128)(2,1)S(1)}, u32[]{:S(2)}, u32[]{:S(2)}) %collective-permute-start.55) | collective-permute-done | bytes 524320 | tf_op jit(solution)/shard_map/ppermute | solution.py:488
  365.9 2.4 collective-permute-done.31.refs_1_
  369.2 6.8 %collective-permute-done.29.refs_0_ = bf16[2,256,512]{2,1,0:T(8,128)(2,1)S(1)} collective-permute-done((bf16[2,256,512]{2,1,0:T(8,128)(2,1)}, bf16[2,256,512]{2,1,0:T(8,128)(2,1)S(1)}, u32[]{:S(2)}, u32[]{:S(2)}) %collective-permute-start.29) | collective-permute-done | bytes 524320 | tf_op jit(solution)/shard_map/ppermute | solution.py:488
  380.5 9.3 %collective-permute-start.32 = (bf16[1,256,512]{2,1,0:T(8,128)(2,1)S(1)}, bf16[1,256,512]{2,1,0:T(8,128)(2,1)}, u32[]{:S(2)}, u32[]{:S(2)}) collective-permute-start(bf16[1,256,512]{2,1,0:T(8,128)(2,1)S(1)} %slice.97), channel_id=1, source_target_pairs={{0,8},{2,10},{4,12},{6,14},{8,16},{10,18},{12,20},{14,22},{16,24},... | collective-permute-start | bytes 786440 | tf_op jit(solution)/shard_map/ppermute | solution.py:488
  391.6 2.4 collective-permute-start.57
  395.1 6.4 %expand.4.refs_5_ = bf16[2,4096,1024]{2,1,0:T(8,128)(2,1)} custom-call(s32[4]{0:T(128)} %pad_add_fusion.quads, s32[1]{0:T(128)} %bitcast.29.group, bf16[2,256,512]{2,1,0:T(8,128)(2,1)} %copy-done.4, bf16[2,256,512]{2,1,0:T(8,128)(2,1)} %copy-done.24, bf16[2,256,512]{2,1,0:T(8,128)(2,1)} %copy-done.25, bf16[2,256,512]{2,1,0:T(8,128)(2,1)} %copy-done.26, ...), custom_call_target="tpu_custom_call" | custom-call | flops 2147483648 | bytes 6291456 | tf_op jit(solution)/shard_map/expand/pallas_call | solution.py:373
  402.6 6.2 %expand.5.refs_5_ = bf16[2,4096,1024]{2,1,0:T(8,128)(2,1)} custom-call(s32[4]{0:T(128)} %pad_add_fusion.quads, s32[1]{0:T(128)} %bitcast.26.group, bf16[2,256,512]{2,1,0:T(8,128)(2,1)} %copy-done.12, bf16[2,256,512]{2,1,0:T(8,128)(2,1)} %collective-permute-done.38.refs_1_, bf16[2,256,512]{2,1,0:T(8,128)(2,1)} %copy-done.13, ...), custom_call_target="tpu_custom_call", output_to_operand_aliasing={{}: (7, {})} | custom-call | flops 2147483648 | bytes 6291456 | tf_op jit(solution)/shard_map/expand/pallas_call | solution.py:373
  409.3 6.2 %expand.6.refs_7_ = bf16[2,4096,1024]{2,1,0:T(8,128)(2,1)} custom-call(s32[4]{0:T(128)} %pad_add_fusion.quads, s32[1]{0:T(128)} %bitcast.23.group, bf16[2,256,512]{2,1,0:T(8,128)(2,1)} %collective-permute-done.28.refs_0_, bf16[2,256,512]{2,1,0:T(8,128)(2,1)} %copy-done.5, ...), custom_call_target="tpu_custom_call", output_to_operand_aliasing={{}: (7, {})} | custom-call | flops 2147483648 | bytes 6291456 | tf_op jit(solution)/shard_map/expand/pallas_call | solution.py:373
  415.5 6.4 %expand.7 = bf16[2,4096,1024]{2,1,0:T(8,128)(2,1)} custom-call(s32[4]{0:T(128)} %pad_add_fusion.quads, s32[1]{0:T(128)} %bitcast.4.group, bf16[2,256,512]{2,1,0:T(8,128)(2,1)} %copy-done.6, bf16[1,256,512]{2,1,0:T(8,128)(2,1)} %copy-done.27, bf16[1,256,512]{2,1,0:T(8,128)(2,1)} %collective-permute-done.32.refs_2_, ...), custom_call_target="tpu_custom_call", output_to_operand_aliasing={{}: (9, {})} | custom-call | flops 2147483648 | bytes 6291456 | tf_op jit(solution)/shard_map/expand/pallas_call | solution.py:373
  423.3 8.1 %settle.1 = (f32[2,1,32,16,512]{4,3,2,1,0:T(8,128)}, f32[2,1,32,16,512]{4,3,2,1,0:T(8,128)}) custom-call(s32[2,32]{1,0:T(2,128)} %get-tuple-element.58.piece_of, s32[2,32]{1,0:T(2,128)} %get-tuple-element.57.row_of, s32[2,32]{1,0:T(2,128)} %fusion.29.held, bf16[2,256,512]{2,1,0:T(8,128)(2,1)} %copy-done.3, bf16[2,256,512]{2,1,0:T(8,128)(2,1)} %copy-done.15, ...), custom_call_target="tpu_custom_call" | custom-call | flops 4194304 | bytes 9437184 | tf_op jit(solution)/shard_map/settle/pallas_call | solution.py:442
  (189 shorter events, 43.6 us)
Async XLA Ops:
  2.0 15.8 %collective-permute-start.12 = (f32[2,128,512]{2,1,0:T(8,128)S(1)}, f32[2,128,512]{2,1,0:T(8,128)S(1)}, u32[]{:S(2)}, u32[]{:S(2)}) collective-permute-start(f32[2,128,512]{2,1,0:T(8,128)S(1)} %get-tuple-element.56), channel_id=1, source_target_pairs={{0,1},{1,0},{2,3},{3,2},{4,5},{5,4},{6,7},{7,6},{8,9},{9,8},{10,11... | collective-permute-start | bytes 1572872 | tf_op jit(solution)/shard_map/ppermute | solution.py:510
  5.0 23.2 %collective-permute-start.14 = (f32[2,128,512]{2,1,0:T(8,128)S(1)}, f32[2,128,512]{2,1,0:T(8,128)S(1)}, u32[]{:S(2)}, u32[]{:S(2)}) collective-permute-start(f32[2,128,512]{2,1,0:T(8,128)S(1)} %get-tuple-element.55), channel_id=1, source_target_pairs={{0,1},{1,0},{2,3},{3,2},{4,5},{5,4},{6,7},{7,6},{8,9},{9,8},{10,11... | collective-permute-start | bytes 1572872 | tf_op jit(solution)/shard_map/ppermute | solution.py:510
  17.8 17.0 %collective-permute-start.13 = (f32[2,128,512]{2,1,0:T(8,128)S(1)}, f32[2,128,512]{2,1,0:T(8,128)S(1)}, u32[]{:S(2)}, u32[]{:S(2)}) collective-permute-start(f32[2,128,512]{2,1,0:T(8,128)S(1)} %collective-permute-done.12.refs_0_.refs_1_), channel_id=1, source_target_pairs={{0,2},{2,0},{4,6},{6,4},{8,10},{10,8},{12,14},{14,12},{16,18},{18,... | collective-permute-start | bytes 1572872 | tf_op jit(solution)/shard_map/ppermute | solution.py:488
  92.6 26.3 %collective-permute-start.6 = (bf16[2,32,16,512]{3,2,1,0:T(8,128)(2,1)}, bf16[2,32,16,512]{3,2,1,0:T(8,128)(2,1)}, u32[]{:S(2)}, u32[]{:S(2)}) collective-permute-start(bf16[2,32,16,512]{3,2,1,0:T(8,128)(2,1)} %fusion.6.refs_0_), channel_id=1, source_target_pairs={{0,4},{2,6},{4,0},{6,2},{8,12},{10,14},{12,8},{14,10},{16,20},{18,... | collective-permute-start | bytes 3145736 | tf_op jit(solution)/shard_map/ppermute | solution.py:488
  100.8 18.2 %collective-permute-start.20 = (bf16[2,2,256,512]{3,2,1,0:T(8,128)(2,1)}, bf16[2,2,256,512]{3,2,1,0:T(8,128)(2,1)}, u32[]{:S(2)}, u32[]{:S(2)}) collective-permute-start(bf16[2,2,256,512]{3,2,1,0:T(8,128)(2,1)} %get-tuple-element.45), channel_id=1, source_target_pairs={{0,2},{2,0},{4,6},{6,4},{8,10},{10,8},{12,14},{14,12},{16,18},{18,... | collective-permute-start | bytes 3145736 | tf_op jit(solution)/shard_map/ppermute | solution.py:488
  100.9 55.0 %collective-permute-start = (bf16[2,32,16,512]{3,2,1,0:T(8,128)(2,1)S(1)}, bf16[2,32,16,512]{3,2,1,0:T(8,128)(2,1)S(1)}, u32[]{:S(2)}, u32[]{:S(2)}) collective-permute-start(bf16[2,32,16,512]{3,2,1,0:T(8,128)(2,1)S(1)} %fusion.5.refs_0_), channel_id=1, source_target_pairs={{0,4},{2,6},{4,0},{6,2},{8,12},{10,14},{12,8},{14,10},{16,20},{18,... | collective-permute-start | bytes 3145736 | tf_op jit(solution)/shard_map/ppermute | solution.py:488
  103.5 48.4 %collective-permute-start.23 = (bf16[2,256,512]{2,1,0:T(8,128)(2,1)}, bf16[2,256,512]{2,1,0:T(8,128)(2,1)}, u32[]{:S(2)}, u32[]{:S(2)}) collective-permute-start(bf16[2,256,512]{2,1,0:T(8,128)(2,1)} %fusion.17), channel_id=1, source_target_pairs={{0,4},{2,6},{4,0},{6,2},{8,12},{10,14},{12,8},{14,10},{16,20},{18,... | collective-permute-start | bytes 1572872 | tf_op jit(solution)/shard_map/ppermute | solution.py:488
  111.5 52.2 %collective-permute-start.18 = (bf16[2,2,256,512]{3,2,1,0:T(8,128)(2,1)}, bf16[2,2,256,512]{3,2,1,0:T(8,128)(2,1)}, u32[]{:S(2)}, u32[]{:S(2)}) collective-permute-start(bf16[2,2,256,512]{3,2,1,0:T(8,128)(2,1)} %get-tuple-element.43), channel_id=1, source_target_pairs={{0,2},{2,0},{4,6},{6,4},{8,10},{10,8},{12,14},{14,12},{16,18},{18,... | collective-permute-start | bytes 3145736 | tf_op jit(solution)/shard_map/ppermute | solution.py:488
  119.0 54.4 %collective-permute-start.7 = (bf16[2,32,16,512]{3,2,1,0:T(8,128)(2,1)}, bf16[2,32,16,512]{3,2,1,0:T(8,128)(2,1)}, u32[]{:S(2)}, u32[]{:S(2)}) collective-permute-start(bf16[2,32,16,512]{3,2,1,0:T(8,128)(2,1)} %fusion.6.refs_0_), channel_id=1, source_target_pairs={{0,2},{2,0},{4,6},{6,4},{8,10},{10,8},{12,14},{14,12},{16,18},{18,... | collective-permute-start | bytes 3145736 | tf_op jit(solution)/shard_map/ppermute | solution.py:488
  119.0 54.9 %collective-permute-start.8 = (bf16[2,32,16,512]{3,2,1,0:T(8,128)(2,1)}, bf16[2,32,16,512]{3,2,1,0:T(8,128)(2,1)}, u32[]{:S(2)}, u32[]{:S(2)}) collective-permute-start(bf16[2,32,16,512]{3,2,1,0:T(8,128)(2,1)} %collective-permute-done.6.refs_1_), channel_id=1, source_target_pairs={{0,2},{2,0},{4,6},{6,4},{8,10},{10,8},{12,14},{14,12},{16,18},{18,... | collective-permute-start | bytes 3145736 | tf_op jit(solution)/shard_map/ppermute | solution.py:488
  155.9 15.0 %collective-permute-start.24 = (bf16[2,256,512]{2,1,0:T(8,128)(2,1)}, bf16[2,256,512]{2,1,0:T(8,128)(2,1)}, u32[]{:S(2)}, u32[]{:S(2)}) collective-permute-start(bf16[2,256,512]{2,1,0:T(8,128)(2,1)} %fusion.7), channel_id=1, source_target_pairs={{0,8},{2,10},{4,12},{6,14},{8,16},{10,18},{12,20},{14,22},{16,24},... | collective-permute-start | bytes 1572872 | tf_op jit(solution)/shard_map/ppermute | solution.py:488
  163.8 18.0 %collective-permute-start.16 = (bf16[2,2,256,512]{3,2,1,0:T(8,128)(2,1)}, bf16[2,2,256,512]{3,2,1,0:T(8,128)(2,1)}, u32[]{:S(2)}, u32[]{:S(2)}) collective-permute-start(bf16[2,2,256,512]{3,2,1,0:T(8,128)(2,1)} %get-tuple-element.41), channel_id=1, source_target_pairs={{0,2},{2,0},{4,6},{6,4},{8,10},{10,8},{12,14},{14,12},{16,18},{18,... | collective-permute-start | bytes 3145736 | tf_op jit(solution)/shard_map/ppermute | solution.py:488
  165.9 29.5 %collective-permute-start.1 = (bf16[2,32,16,512]{3,2,1,0:T(8,128)(2,1)S(1)}, bf16[2,32,16,512]{3,2,1,0:T(8,128)(2,1)}, u32[]{:S(2)}, u32[]{:S(2)}) collective-permute-start(bf16[2,32,16,512]{3,2,1,0:T(8,128)(2,1)S(1)} %fusion.5.refs_0_), channel_id=1, source_target_pairs={{0,2},{2,0},{4,6},{6,4},{8,10},{10,8},{12,14},{14,12},{16,18},{18,... | collective-permute-start | bytes 3145736 | tf_op jit(solution)/shard_map/ppermute | solution.py:488
  170.9 26.0 %collective-permute-start.2 = (bf16[2,32,16,512]{3,2,1,0:T(8,128)(2,1)S(1)}, bf16[2,32,16,512]{3,2,1,0:T(8,128)(2,1)}, u32[]{:S(2)}, u32[]{:S(2)}) collective-permute-start(bf16[2,32,16,512]{3,2,1,0:T(8,128)(2,1)S(1)} %collective-permute-done.refs_1_), channel_id=1, source_target_pairs={{0,2},{2,0},{4,6},{6,4},{8,10},{10,8},{12,14},{14,12},{16,18},{18,... | collective-permute-start | bytes 3145736 | tf_op jit(solution)/shard_map/ppermute | solution.py:488
  173.4 14.7 %collective-permute-start.19 = (bf16[2,256,512]{2,1,0:T(8,128)(2,1)}, bf16[2,256,512]{2,1,0:T(8,128)(2,1)}, u32[]{:S(2)}, u32[]{:S(2)}) collective-permute-start(bf16[2,256,512]{2,1,0:T(8,128)(2,1)} %fusion.15), channel_id=1, source_target_pairs={{0,4},{2,6},{4,0},{6,2},{8,12},{10,14},{12,8},{14,10},{16,20},{18,... | collective-permute-start | bytes 1572872 | tf_op jit(solution)/shard_map/ppermute | solution.py:488
  173.9 17.0 %collective-permute-start.25 = (bf16[2,256,512]{2,1,0:T(8,128)(2,1)}, bf16[2,256,512]{2,1,0:T(8,128)(2,1)}, u32[]{:S(2)}, u32[]{:S(2)}) collective-permute-start(bf16[2,256,512]{2,1,0:T(8,128)(2,1)} %fusion.9), channel_id=1, source_target_pairs={{0,8},{2,10},{4,12},{6,14},{8,16},{10,18},{12,20},{14,22},{16,24},... | collective-permute-start | bytes 1572872 | tf_op jit(solution)/shard_map/ppermute | solution.py:488
  181.8 31.6 %collective-permute-start.10 = (bf16[2,256,512]{2,1,0:T(8,128)(2,1)}, bf16[2,256,512]{2,1,0:T(8,128)(2,1)}, u32[]{:S(2)}, u32[]{:S(2)}) collective-permute-start(bf16[2,256,512]{2,1,0:T(8,128)(2,1)} %get-tuple-element.34), channel_id=1, source_target_pairs={{0,16},{2,18},{4,20},{6,22},{8,24},{10,26},{12,28},{14,30},{16,0},... | collective-permute-start | bytes 1572872 | tf_op jit(solution)/shard_map/ppermute | solution.py:488
  188.0 58.8 %collective-permute-start.11 = (bf16[2,256,512]{2,1,0:T(8,128)(2,1)}, bf16[2,256,512]{2,1,0:T(8,128)(2,1)}, u32[]{:S(2)}, u32[]{:S(2)}) collective-permute-start(bf16[2,256,512]{2,1,0:T(8,128)(2,1)} %get-tuple-element.35), channel_id=1, source_target_pairs={{0,24},{2,26},{4,28},{6,30},{8,0},{10,2},{12,4},{14,6},{16,8},{18,... | collective-permute-start | bytes 1572872 | tf_op jit(solution)/shard_map/ppermute | solution.py:488
  190.9 66.2 %collective-permute-start.9 = (bf16[2,256,512]{2,1,0:T(8,128)(2,1)}, bf16[2,256,512]{2,1,0:T(8,128)(2,1)}, u32[]{:S(2)}, u32[]{:S(2)}) collective-permute-start(bf16[2,256,512]{2,1,0:T(8,128)(2,1)} %get-tuple-element.33), channel_id=1, source_target_pairs={{0,8},{2,10},{4,12},{6,14},{8,16},{10,18},{12,20},{14,22},{16,24},... | collective-permute-start | bytes 1572872 | tf_op jit(solution)/shard_map/ppermute | solution.py:488
  195.5 66.5 %collective-permute-start.17 = (bf16[2,256,512]{2,1,0:T(8,128)(2,1)}, bf16[2,256,512]{2,1,0:T(8,128)(2,1)S(1)}, u32[]{:S(2)}, u32[]{:S(2)}) collective-permute-start(bf16[2,256,512]{2,1,0:T(8,128)(2,1)} %fusion.14), channel_id=1, source_target_pairs={{0,4},{2,6},{4,0},{6,2},{8,12},{10,14},{12,8},{14,10},{16,20},{18,... | collective-permute-start | bytes 1572872 | tf_op jit(solution)/shard_map/ppermute | solution.py:488
  197.0 65.0 %collective-permute-start.26 = (bf16[2,256,512]{2,1,0:T(8,128)(2,1)}, bf16[2,256,512]{2,1,0:T(8,128)(2,1)}, u32[]{:S(2)}, u32[]{:S(2)}) collective-permute-start(bf16[2,256,512]{2,1,0:T(8,128)(2,1)} %fusion.11), channel_id=1, source_target_pairs={{0,8},{2,10},{4,12},{6,14},{8,16},{10,18},{12,20},{14,22},{16,24},... | collective-permute-start | bytes 1572872 | tf_op jit(solution)/shard_map/ppermute | solution.py:488
  213.4 50.2 %collective-permute-start.3 = (bf16[2,256,512]{2,1,0:T(8,128)(2,1)}, bf16[2,256,512]{2,1,0:T(8,128)(2,1)S(1)}, u32[]{:S(2)}, u32[]{:S(2)}) collective-permute-start(bf16[2,256,512]{2,1,0:T(8,128)(2,1)} %get-tuple-element.29), channel_id=1, source_target_pairs={{0,8},{2,10},{4,12},{6,14},{8,16},{10,18},{12,20},{14,22},{16,24},... | collective-permute-start | bytes 1572872 | tf_op jit(solution)/shard_map/ppermute | solution.py:488
  246.8 34.5 %collective-permute-start.4 = (bf16[2,256,512]{2,1,0:T(8,128)(2,1)}, bf16[2,256,512]{2,1,0:T(8,128)(2,1)S(1)}, u32[]{:S(2)}, u32[]{:S(2)}) collective-permute-start(bf16[2,256,512]{2,1,0:T(8,128)(2,1)} %get-tuple-element.30), channel_id=1, source_target_pairs={{0,16},{2,18},{4,20},{6,22},{8,24},{10,26},{12,28},{14,30},{16,0},... | collective-permute-start | bytes 1572872 | tf_op jit(solution)/shard_map/ppermute | solution.py:488
  257.1 24.2 %collective-permute-start.5 = (bf16[2,256,512]{2,1,0:T(8,128)(2,1)}, bf16[2,256,512]{2,1,0:T(8,128)(2,1)S(1)}, u32[]{:S(2)}, u32[]{:S(2)}) collective-permute-start(bf16[2,256,512]{2,1,0:T(8,128)(2,1)} %get-tuple-element.31), channel_id=1, source_target_pairs={{0,24},{2,26},{4,28},{6,30},{8,0},{10,2},{12,4},{14,6},{16,8},{18,... | collective-permute-start | bytes 1572872 | tf_op jit(solution)/shard_map/ppermute | solution.py:488
  263.5 31.6 %collective-permute-start.47 = (bf16[2,256,512]{2,1,0:T(8,128)(2,1)S(1)}, bf16[2,256,512]{2,1,0:T(8,128)(2,1)S(1)}, u32[]{:S(2)}, u32[]{:S(2)}) collective-permute-start(bf16[2,256,512]{2,1,0:T(8,128)(2,1)S(1)} %get-tuple-element.50.refs_0_), channel_id=1, source_target_pairs={{0,8},{2,10},{4,12},{6,14},{8,16},{10,18},{12,20},{14,22},{16,24},... | collective-permute-start | bytes 1572872 | tf_op jit(solution)/shard_map/ppermute | solution.py:488
  281.4 36.8 %collective-permute-start.44 = (bf16[2,256,512]{2,1,0:T(8,128)(2,1)S(1)}, bf16[2,256,512]{2,1,0:T(8,128)(2,1)S(1)}, u32[]{:S(2)}, u32[]{:S(2)}) collective-permute-start(bf16[2,256,512]{2,1,0:T(8,128)(2,1)S(1)} %get-tuple-element.50.refs_0_), channel_id=1, source_target_pairs={{0,4},{2,6},{4,0},{6,2},{8,12},{10,14},{12,8},{14,10},{16,20},{18,... | collective-permute-start | bytes 1572872 | tf_op jit(solution)/shard_map/ppermute | solution.py:488
  283.0 46.9 %collective-permute-start.45 = (bf16[2,256,512]{2,1,0:T(8,128)(2,1)S(1)}, bf16[2,256,512]{2,1,0:T(8,128)(2,1)S(1)}, u32[]{:S(2)}, u32[]{:S(2)}) collective-permute-start(bf16[2,256,512]{2,1,0:T(8,128)(2,1)S(1)} %get-tuple-element.50.refs_0_), channel_id=1, source_target_pairs={{0,2},{2,0},{4,6},{6,4},{8,10},{10,8},{12,14},{14,12},{16,18},{18,... | collective-permute-start | bytes 1572872 | tf_op jit(solution)/shard_map/ppermute | solution.py:488
  283.8 47.6 %collective-permute-start.41 = (bf16[2,256,512]{2,1,0:T(8,128)(2,1)S(1)}, bf16[2,256,512]{2,1,0:T(8,128)(2,1)S(1)}, u32[]{:S(2)}, u32[]{:S(2)}) collective-permute-start(bf16[2,256,512]{2,1,0:T(8,128)(2,1)S(1)} %fusion.13.refs_0_), channel_id=1, source_target_pairs={{0,4},{2,6},{4,0},{6,2},{8,12},{10,14},{12,8},{14,10},{16,20},{18,... | collective-permute-start | bytes 1572872 | tf_op jit(solution)/shard_map/ppermute | solution.py:488
  284.4 47.0 %collective-permute-start.42 = (bf16[2,256,512]{2,1,0:T(8,128)(2,1)S(1)}, bf16[2,256,512]{2,1,0:T(8,128)(2,1)S(1)}, u32[]{:S(2)}, u32[]{:S(2)}) collective-permute-start(bf16[2,256,512]{2,1,0:T(8,128)(2,1)S(1)} %fusion.13.refs_0_), channel_id=1, source_target_pairs={{0,2},{2,0},{4,6},{6,4},{8,10},{10,8},{12,14},{14,12},{16,18},{18,... | collective-permute-start | bytes 1572872 | tf_op jit(solution)/shard_map/ppermute | solution.py:488
  295.1 36.8 %collective-permute-start.27 = (bf16[2,256,512]{2,1,0:T(8,128)(2,1)S(1)}, bf16[2,256,512]{2,1,0:T(8,128)(2,1)S(1)}, u32[]{:S(2)}, u32[]{:S(2)}) collective-permute-start(bf16[2,256,512]{2,1,0:T(8,128)(2,1)S(1)} %fusion.13.refs_0_), channel_id=1, source_target_pairs={{0,8},{2,10},{4,12},{6,14},{8,16},{10,18},{12,20},{14,22},{16,24},... | collective-permute-start | bytes 1572872 | tf_op jit(solution)/shard_map/ppermute | solution.py:488
  318.2 23.4 %collective-permute-start.51 = (bf16[2,256,512]{2,1,0:T(8,128)(2,1)S(1)}, bf16[2,256,512]{2,1,0:T(8,128)(2,1)}, u32[]{:S(2)}, u32[]{:S(2)}) collective-permute-start(bf16[2,256,512]{2,1,0:T(8,128)(2,1)S(1)} %collective-permute-done.47.refs_4_), channel_id=1, source_target_pairs={{0,8},{2,10},{4,12},{6,14},{8,16},{10,18},{12,20},{14,22},{16,24},... | collective-permute-start | bytes 1572872 | tf_op jit(solution)/shard_map/ppermute | solution.py:488
  331.9 21.4 %collective-permute-start.28 = (bf16[2,256,512]{2,1,0:T(8,128)(2,1)S(1)}, bf16[2,256,512]{2,1,0:T(8,128)(2,1)}, u32[]{:S(2)}, u32[]{:S(2)}) collective-permute-start(bf16[2,256,512]{2,1,0:T(8,128)(2,1)S(1)} %collective-permute-done.27.refs_0_), channel_id=1, source_target_pairs={{0,8},{2,10},{4,12},{6,14},{8,16},{10,18},{12,20},{14,22},{16,24},... | collective-permute-start | bytes 1572872 | tf_op jit(solution)/shard_map/ppermute | solution.py:488
  341.7 16.2 %collective-permute-start.38 = (bf16[2,256,512]{2,1,0:T(8,128)(2,1)S(1)}, bf16[2,256,512]{2,1,0:T(8,128)(2,1)}, u32[]{:S(2)}, u32[]{:S(2)}) collective-permute-start(bf16[2,256,512]{2,1,0:T(8,128)(2,1)S(1)} %collective-permute-done.27.refs_0_), channel_id=1, source_target_pairs={{0,4},{2,6},{4,0},{6,2},{8,12},{10,14},{12,8},{14,10},{16,20},{18,... | collective-permute-start | bytes 1572872 | tf_op jit(solution)/shard_map/ppermute | solution.py:488
  343.2 14.9 %collective-permute-start.39 = (bf16[2,256,512]{2,1,0:T(8,128)(2,1)S(1)}, bf16[2,256,512]{2,1,0:T(8,128)(2,1)S(1)}, u32[]{:S(2)}, u32[]{:S(2)}) collective-permute-start(bf16[2,256,512]{2,1,0:T(8,128)(2,1)S(1)} %collective-permute-done.27.refs_0_), channel_id=1, source_target_pairs={{0,2},{2,0},{4,6},{6,4},{8,10},{10,8},{12,14},{14,12},{16,18},{18,... | collective-permute-start | bytes 1572872 | tf_op jit(solution)/shard_map/ppermute | solution.py:488
  344.0 21.9 %collective-permute-start.55 = (bf16[2,256,512]{2,1,0:T(8,128)(2,1)}, bf16[2,256,512]{2,1,0:T(8,128)(2,1)S(1)}, u32[]{:S(2)}, u32[]{:S(2)}) collective-permute-start(bf16[2,256,512]{2,1,0:T(8,128)(2,1)} %collective-permute-done.51.refs_8_), channel_id=1, source_target_pairs={{0,8},{2,10},{4,12},{6,14},{8,16},{10,18},{12,20},{14,22},{16,24},... | collective-permute-start | bytes 1572872 | tf_op jit(solution)/shard_map/ppermute | solution.py:488
  353.3 15.0 %collective-permute-start.31 = (bf16[2,256,512]{2,1,0:T(8,128)(2,1)}, bf16[2,256,512]{2,1,0:T(8,128)(2,1)S(1)}, u32[]{:S(2)}, u32[]{:S(2)}) collective-permute-start(bf16[2,256,512]{2,1,0:T(8,128)(2,1)} %collective-permute-done.28.refs_0_), channel_id=1, source_target_pairs={{0,4},{2,6},{4,0},{6,2},{8,12},{10,14},{12,8},{14,10},{16,20},{18,... | collective-permute-start | bytes 1572872 | tf_op jit(solution)/shard_map/ppermute | solution.py:488
  355.2 20.8 %collective-permute-start.29 = (bf16[2,256,512]{2,1,0:T(8,128)(2,1)}, bf16[2,256,512]{2,1,0:T(8,128)(2,1)S(1)}, u32[]{:S(2)}, u32[]{:S(2)}) collective-permute-start(bf16[2,256,512]{2,1,0:T(8,128)(2,1)} %collective-permute-done.28.refs_0_), channel_id=1, source_target_pairs={{0,8},{2,10},{4,12},{6,14},{8,16},{10,18},{12,20},{14,22},{16,24},... | collective-permute-start | bytes 1572872 | tf_op jit(solution)/shard_map/ppermute | solution.py:488
  357.8 21.4 %collective-permute-start.52 = (bf16[2,256,512]{2,1,0:T(8,128)(2,1)}, bf16[2,256,512]{2,1,0:T(8,128)(2,1)S(1)}, u32[]{:S(2)}, u32[]{:S(2)}) collective-permute-start(bf16[2,256,512]{2,1,0:T(8,128)(2,1)} %collective-permute-done.51.refs_8_), channel_id=1, source_target_pairs={{0,4},{2,6},{4,0},{6,2},{8,12},{10,14},{12,8},{14,10},{16,20},{18,... | collective-permute-start | bytes 1572872 | tf_op jit(solution)/shard_map/ppermute | solution.py:488
  358.1 22.3 %collective-permute-start.50 = (bf16[2,256,512]{2,1,0:T(8,128)(2,1)}, bf16[2,256,512]{2,1,0:T(8,128)(2,1)}, u32[]{:S(2)}, u32[]{:S(2)}) collective-permute-start(bf16[2,256,512]{2,1,0:T(8,128)(2,1)} %collective-permute-done.48.refs_5_), channel_id=1, source_target_pairs={{0,2},{2,0},{4,6},{6,4},{8,10},{10,8},{12,14},{14,12},{16,18},{18,... | collective-permute-start | bytes 1572872 | tf_op jit(solution)/shard_map/ppermute | solution.py:488
  365.9 23.8 %collective-permute-start.40 = (bf16[2,256,512]{2,1,0:T(8,128)(2,1)}, bf16[2,256,512]{2,1,0:T(8,128)(2,1)}, u32[]{:S(2)}, u32[]{:S(2)}) collective-permute-start(bf16[2,256,512]{2,1,0:T(8,128)(2,1)} %collective-permute-done.38.refs_1_), channel_id=1, source_target_pairs={{0,2},{2,0},{4,6},{6,4},{8,10},{10,8},{12,14},{14,12},{16,18},{18,... | collective-permute-start | bytes 1572872 | tf_op jit(solution)/shard_map/ppermute | solution.py:488
  368.3 21.4 %collective-permute-start.36 = (bf16[2,256,512]{2,1,0:T(8,128)(2,1)}, bf16[2,256,512]{2,1,0:T(8,128)(2,1)}, u32[]{:S(2)}, u32[]{:S(2)}) collective-permute-start(bf16[2,256,512]{2,1,0:T(8,128)(2,1)} %collective-permute-done.28.refs_0_), channel_id=1, source_target_pairs={{0,2},{2,0},{4,6},{6,4},{8,10},{10,8},{12,14},{14,12},{16,18},{18,... | collective-permute-start | bytes 1572872 | tf_op jit(solution)/shard_map/ppermute | solution.py:488
  376.0 15.6 %collective-permute-start.56 = (bf16[1,256,512]{2,1,0:T(8,128)(2,1)}, bf16[1,256,512]{2,1,0:T(8,128)(2,1)}, u32[]{:S(2)}, u32[]{:S(2)}) collective-permute-start(bf16[1,256,512]{2,1,0:T(8,128)(2,1)} %slice.100), channel_id=1, source_target_pairs={{0,4},{2,6},{4,0},{6,2},{8,12},{10,14},{12,8},{14,10},{16,20},{18,... | collective-permute-start | bytes 786440 | tf_op jit(solution)/shard_map/ppermute | solution.py:488
  379.2 15.4 %collective-permute-start.30 = (bf16[1,256,512]{2,1,0:T(8,128)(2,1)S(1)}, bf16[1,256,512]{2,1,0:T(8,128)(2,1)S(1)}, u32[]{:S(2)}, u32[]{:S(2)}) collective-permute-start(bf16[1,256,512]{2,1,0:T(8,128)(2,1)S(1)} %slice.96), channel_id=1, source_target_pairs={{0,4},{2,6},{4,0},{6,2},{8,12},{10,14},{12,8},{14,10},{16,20},{18,... | collective-permute-start | bytes 786440 | tf_op jit(solution)/shard_map/ppermute | solution.py:488
  380.5 14.5 %collective-permute-start.32 = (bf16[1,256,512]{2,1,0:T(8,128)(2,1)S(1)}, bf16[1,256,512]{2,1,0:T(8,128)(2,1)}, u32[]{:S(2)}, u32[]{:S(2)}) collective-permute-start(bf16[1,256,512]{2,1,0:T(8,128)(2,1)S(1)} %slice.97), channel_id=1, source_target_pairs={{0,8},{2,10},{4,12},{6,14},{8,16},{10,18},{12,20},{14,22},{16,24},... | collective-permute-start | bytes 786440 | tf_op jit(solution)/shard_map/ppermute | solution.py:488
  395.0 14.2 %collective-permute-start.35 = (bf16[1,256,512]{2,1,0:T(8,128)(2,1)}, bf16[1,256,512]{2,1,0:T(8,128)(2,1)}, u32[]{:S(2)}, u32[]{:S(2)}) collective-permute-start(bf16[1,256,512]{2,1,0:T(8,128)(2,1)} %collective-permute-done.32.refs_2_), channel_id=1, source_target_pairs={{0,2},{2,0},{4,6},{6,4},{8,10},{10,8},{12,14},{14,12},{16,18},{18,... | collective-permute-start | bytes 786440 | tf_op jit(solution)/shard_map/ppermute | solution.py:488
  402.0 19.9 %collective-permute-start.53 = (bf16[2,256,512]{2,1,0:T(8,128)(2,1)}, bf16[2,256,512]{2,1,0:T(8,128)(2,1)S(1)}, u32[]{:S(2)}, u32[]{:S(2)}) collective-permute-start(bf16[2,256,512]{2,1,0:T(8,128)(2,1)} %collective-permute-done.51.refs_8_), channel_id=1, source_target_pairs={{0,2},{2,0},{4,6},{6,4},{8,10},{10,8},{12,14},{14,12},{16,18},{18,... | collective-permute-start | bytes 1572872 | tf_op jit(solution)/shard_map/ppermute | solution.py:488
  402.0 19.9 %collective-permute-start.54 = (bf16[2,256,512]{2,1,0:T(8,128)(2,1)S(1)}, bf16[2,256,512]{2,1,0:T(8,128)(2,1)S(1)}, u32[]{:S(2)}, u32[]{:S(2)}) collective-permute-start(bf16[2,256,512]{2,1,0:T(8,128)(2,1)S(1)} %collective-permute-done.52.refs_9_), channel_id=1, source_target_pairs={{0,2},{2,0},{4,6},{6,4},{8,10},{10,8},{12,14},{14,12},{16,18},{18,... | collective-permute-start | bytes 1572872 | tf_op jit(solution)/shard_map/ppermute | solution.py:488
  402.5 19.4 %collective-permute-start.58 = (bf16[2,256,512]{2,1,0:T(8,128)(2,1)S(1)}, bf16[2,256,512]{2,1,0:T(8,128)(2,1)S(1)}, u32[]{:S(2)}, u32[]{:S(2)}) collective-permute-start(bf16[2,256,512]{2,1,0:T(8,128)(2,1)S(1)} %collective-permute-done.55.refs_12_), channel_id=1, source_target_pairs={{0,2},{2,0},{4,6},{6,4},{8,10},{10,8},{12,14},{14,12},{16,18},{18,... | collective-permute-start | bytes 1572872 | tf_op jit(solution)/shard_map/ppermute | solution.py:488
  (48 other events, 968.8 us)

commit v5 on v4

--- a/solution.py
+++ b/solution.py
@@ -294,20 +294,26 @@
     )(places, counts, *owners)
 
 
-def project_kernel(quads, group, grads_ref, basis_ref, other_ref, own_ref, result):
+def project_kernel(quads, where, grads_ref, own_basis, core_basis, other_ref, own_ref, result):
     unit_rows = other_ref.shape[2]
-    result[...] = dot_bf16(grads_ref[0, 0], basis_ref[0], ((1,), (0,))).astype(BF16)
+    for g, basis_ref in enumerate((own_basis, core_basis)):
+
+        @pl.when(pl.program_id(0) == g)
+        def _():
+            result[...] = dot_bf16(grads_ref[0, 0], basis_ref[0], ((1,), (0,))).astype(BF16)
+
     for i, ref in ((0, other_ref), (1, other_ref), (2, own_ref), (3, own_ref)):
         at = pl.multiple_of(quads[i] * unit_rows, unit_rows)
         ref[i % 2, 0] = result[pl.ds(at, unit_rows), :]
 
 
-def project(grads, basis, quads, group, unit_rows):
+def project(grads, bases, quads, where, unit_rows):
     _, mats, _, feats = grads.shape
-    rank = basis.shape[2]
+    rank = bases[0].shape[2]
     rows = QUAD * unit_rows
     out = jax.ShapeDtypeStruct((2, mats, unit_rows, rank), BF16)
-    out_spec = pl.BlockSpec((2, 1, unit_rows, rank), lambda m, q, g: (0, m, 0, 0))
+    out_spec = pl.BlockSpec((2, 1, unit_rows, rank), lambda g, q, w: (0, g ^ w[1], 0, 0))
+    basis_spec = pl.BlockSpec((1, feats, rank), lambda g, q, w: (0, 0, 0))
     return pl.pallas_call(
         project_kernel,
         out_shape=(out, out),
@@ -315,8 +321,9 @@
             num_scalar_prefetch=2,
             grid=(mats,),
             in_specs=[
-                pl.BlockSpec((1, 1, rows, feats), lambda m, q, g: (0, m, g[0], 0)),
-                pl.BlockSpec((1, feats, rank), lambda m, q, g: (m, 0, 0)),
+                pl.BlockSpec((1, 1, rows, feats), lambda g, q, w: (0, g ^ w[1], w[0], 0)),
+                basis_spec,
+                basis_spec,
             ],
             out_specs=(out_spec, out_spec),
             scratch_shapes=[pltpu.VMEM((rows, rank), BF16)],
@@ -327,13 +334,12 @@
             transcendentals=0,
         ),
         name="project",
-    )(quads, group, grads, basis)
-
-
-def expand_kernel(quads, group, *refs, parts):
-    basis_ref = refs[parts]
+    )(quads, where, grads, *bases)
+
+
+def expand_kernel(quads, where, *refs, parts):
     out_ref, joined = refs[-2:]
-    m = pl.program_id(0)
+    m = pl.program_id(0) ^ where[1]
     unit_rows = refs[0].shape[1]
     used = 0
     for i in range(QUAD):
@@ -345,26 +351,30 @@
             low, high = refs[used], refs[used + 1]
             used += 2
             joined[pl.ds(at, unit_rows), :] = jnp.where(m < pl.num_programs(0) // 2, low[0], high[0])
-    out_ref[0] = dot_bf16(joined[...], basis_ref[0], ((1,), (1,))).astype(BF16)
-
-
-def expand(parts, basis, quads, group, target, local_rows):
-    mats, feats, rank = basis.shape
+    for g, basis_ref in enumerate(refs[parts : parts + 2]):
+
+        @pl.when(pl.program_id(0) == g)
+        def _():
+            out_ref[0] = dot_bf16(joined[...], basis_ref[0], ((1,), (1,))).astype(BF16)
+
+
+def expand(parts, bases, quads, where, target, mats, local_rows):
+    _, feats, rank = bases[0].shape
     unit_rows = parts[0][0].shape[1]
     rows = QUAD * unit_rows
     block = (1, unit_rows, rank)
     half = mats // 2
-    in_specs, args = [], [quads, group]
+    in_specs, args = [], [quads, where]
     for part in parts:
         if len(part) == 1:
-            in_specs.append(pl.BlockSpec(block, lambda m, q, g: (m, 0, 0)))
+            in_specs.append(pl.BlockSpec(block, lambda g, q, w: (g ^ w[1], 0, 0)))
         else:
-            in_specs.append(pl.BlockSpec(block, lambda m, q, g: (jnp.minimum(m, half - 1), 0, 0)))
-            in_specs.append(pl.BlockSpec(block, lambda m, q, g: (jnp.maximum(m - half, 0), 0, 0)))
+            in_specs.append(pl.BlockSpec(block, lambda g, q, w: (jnp.minimum(g ^ w[1], half - 1), 0, 0)))
+            in_specs.append(pl.BlockSpec(block, lambda g, q, w: (jnp.maximum((g ^ w[1]) - half, 0), 0, 0)))
         args += part
     pieces = len(in_specs)
-    in_specs.append(pl.BlockSpec((1, feats, rank), lambda m, q, g: (m, 0, 0)))
-    args.append(basis)
+    in_specs += [pl.BlockSpec((1, feats, rank), lambda g, q, w: (0, 0, 0))] * 2
+    args += bases
     aliases = {}
     if target is not None:
         in_specs.append(pl.BlockSpec(memory_space=pl.ANY))
@@ -377,7 +387,7 @@
             num_scalar_prefetch=2,
             grid=(mats,),
             in_specs=in_specs,
-            out_specs=pl.BlockSpec((1, rows, feats), lambda m, q, g: (m, g[0], 0)),
+            out_specs=pl.BlockSpec((1, rows, feats), lambda g, q, w: (g ^ w[1], w[0], 0)),
             scratch_shapes=[pltpu.VMEM((rows, rank), BF16)],
         ),
         input_output_aliases=aliases,
@@ -472,7 +482,7 @@
 
 def shards(grads, raw_proj, bucket_owner, first_moment, second_moment):
     mats, local_rows = grads.shape[1], grads.shape[2]
-    local_feats = raw_proj.shape[1]
+    local_feats, rank = raw_proj.shape[1], raw_proj.shape[2]
     buckets = bucket_owner.shape[1]
     capacity = first_moment.shape[2]
     bucket_rows = local_rows // buckets
@@ -496,13 +506,14 @@
     def to_z(v, layers=1):
         return permute(v, lambda i: (i + layers * QUAD) % replicas)
 
-    quarter = local_feats // QUAD
     my_core = me % 2
+    half = local_feats // 2
+    own = lax.dynamic_slice_in_dim(raw_proj, my_core, 1, 0)
     parts = [
-        lax.dynamic_slice_in_dim(raw_proj, (2 * my_core + i) * quarter, quarter, 1) for i in range(2)
+        lax.dynamic_slice(raw_proj, (my_core, i * half, 0), (1, half, rank)) for i in range(2)
     ]
     my_f = lax.axis_index("fsdp")
-    gram = gram_of([raw_proj])
+    gram = gram_of([own])
     pieces, offsets, early, fresh = [], [my_f * local_feats], [], []
     for shift in range(1, splits):
         base = ((my_f + splits - shift) % splits) * local_feats
@@ -510,13 +521,11 @@
             fetched = lax.ppermute(
                 parts[i], "fsdp", [(j, (j + shift) % splits) for j in range(splits)]
             )
-            for piece, core in ((fetched, my_core), (to_core(fetched), 1 - my_core)):
-                indices.append(len(pieces))
-                pieces.append(piece)
-                offsets.append(base + (2 * core + i) * quarter)
+            indices.append(len(pieces))
+            pieces.append(fetched)
+            offsets.append(base + i * half)
     offsets = jnp.stack(offsets).astype(jnp.int32)
-    if early:
-        gram = gram_of([pieces[i] for i in early], gram)
+    gram = gram_of([pieces[i] for i in early], gram)
 
     same = bucket_owner[:, :, None] == bucket_owner[:, None, :]
     order = jnp.arange(buckets, dtype=jnp.int32)
@@ -550,13 +559,14 @@
     first_unit, second_unit = lax.optimization_barrier((first_unit, second_unit))
 
     state = first_half([pieces[i] for i in fresh], gram)
-    basis = second_half(raw_proj, pieces, offsets, state, splits * local_feats)
+    basis = second_half(own, pieces, offsets, state, splits * local_feats)
+    bases = (basis, to_core(basis))
 
     send_quads = jnp.stack([my_quad ^ flip for flip in (3, 1, 2, 0)]).astype(jnp.int32)
     held = None
     for k in range(1, depth + 1):
-        group = ((my_z + depth - k) % depth).astype(jnp.int32)[None]
-        other, own = project(grads, basis, send_quads, group, unit_rows)
+        where = jnp.stack([(my_z + depth - k) % depth, my_core]).astype(jnp.int32)
+        other, own = project(grads, bases, send_quads, where, unit_rows)
         arrived = to_core(other)
         send = (own[0].astype(F32) + arrived[0].astype(F32)).astype(BF16)
         crossed = to_x(send)
@@ -590,8 +600,10 @@
     part_quads = jnp.stack([my_quad ^ flip for flip in (0, 2, 1, 3)]).astype(jnp.int32)
     weight_delta = None
     for k, parts in enumerate(update_groups):
-        group = ((my_z + depth - k) % depth).astype(jnp.int32)[None]
-        weight_delta = expand(parts, basis, part_quads, group, weight_delta, local_rows)
+        where = jnp.stack([(my_z + depth - k) % depth, my_core]).astype(jnp.int32)
+        weight_delta = expand(
+            parts, bases, part_quads, where, weight_delta, mats, local_rows
+        )
 
     unit = bucket_of // unit_buckets
     back = (my_z + depth - unit // QUAD) % depth

time: 432 us -> 394 us (0.912)
  starting transfers between devices: 121 us -> 91 us
  Pallas kernels: 125 us -> 115 us
    ppermute x59 -> x58, starting transfers between devices: 118 us -> 87.9 us  [permute(): return lax.ppermute(v, 'dp', [(i, target(i)) for i in range(replicas)])]
    ppermute x59 -> x58, waiting for transfers between devices: 130 us -> 138 us  [permute(): return lax.ppermute(v, 'dp', [(i, target(i)) for i in range(replicas)])]
    ppermute x2, waiting for transfers between devices: 22.4 us -> 14.6 us  [shards(): lax.ppermute(parts[i], 'fsdp', [(j, (j + shift) % splits) for j in range(...]
    pallas_call x2, Pallas kernels: 12 us -> 6.87 us  [gram_of(): pl.pallas_call(functools.partial(gram_kernel, pieces=len(pieces)), out_sh...]
    pallas_call x1, Pallas kernels: 22.1 us -> 17.5 us  [second_half(): pl.pallas_call(functools.partial(second_half_kernel, pieces=len(pieces)),...]
  transfers between devices with their start and end apart: 61 -> 60, of which waited for: 17 -> 23; matrix products, arithmetic and copies ran while one was open for 6% -> 7% of each run, Pallas kernels for 16% -> 19%
where the time goes in v5:
time: 394 us; the launch traced here: 393 us
  waiting for transfers between devices  152 us (39%)
  Pallas kernels  115 us (29%)
  starting transfers between devices  91 us (23%)
  other arithmetic  25.6 us (6%)
  local copies, waits for them, and re-layouts  7.6 us (2%)
    ppermute x58, waiting for transfers between devices, permute(): return lax.ppermute(v, 'dp', [(i, target(i)) for i in range(replicas)])  138 us
    ppermute x58, starting transfers between devices, permute(): return lax.ppermute(v, 'dp', [(i, target(i)) for i in range(replicas)])  87.9 us
    pallas_call x4, Pallas kernels, expand(): pl.pallas_call(functools.partial(expand_kernel, parts=pieces), out_shape=...  27.5 us
    pallas_call x4, Pallas kernels, project(): pl.pallas_call(project_kernel, out_shape=(out, out), grid_spec=pltpu.Pref...  26.5 us
    pallas_call x1, Pallas kernels, second_half(): pl.pallas_call(functools.partial(second_half_kernel, pieces=len(pieces)),...  17.5 us
    pallas_call x1, Pallas kernels, first_half(): pl.pallas_call(functools.partial(first_half_kernel, pieces=len(fresh)), o...  16.6 us
    ppermute x2, waiting for transfers between devices, shards(): lax.ppermute(parts[i], 'fsdp', [(j, (j + shift) % splits) for j in range(...  14.6 us
    pallas_call x2, Pallas kernels, collect_moments(): pl.pallas_call(collect_kernel, out_shape=(jax.ShapeDtypeStruct((mats, uni...  12 us
  transfers between devices with their start and end apart: 60, of which 23 were waited for; matrix products, arithmetic and copies ran while one was open for 7% of the time, Pallas kernels for 19%

profile of v5, /device:TPU:0, one launch (start us, length us, event | category | flops | bytes accessed | tf_op | source)
XLA Modules:
  0.0 392.9 jit_solution(7011585041190708563)
XLA Ops:
  2.1 3.1 collective-permute-start.12
  6.9 3.7 gram.2.refs_1_
  10.6 7.4 %collective-permute-done.12.refs_0_.refs_1_ = f32[1,256,512]{2,1,0:T(8,128)} collective-permute-done((f32[1,256,512]{2,1,0:T(8,128)S(1)}, f32[1,256,512]{2,1,0:T(8,128)}, u32[]{:S(2)}, u32[]{:S(2)}) %collective-permute-start.12) | collective-permute-done | bytes 524320 | tf_op jit(solution)/shard_map/ppermute | solution.py:521
  18.0 3.2 gram.3.refs_1_
  21.2 7.2 %collective-permute-done.13.refs_0_.refs_2_ = f32[1,256,512]{2,1,0:T(8,128)} collective-permute-done((f32[1,256,512]{2,1,0:T(8,128)S(1)}, f32[1,256,512]{2,1,0:T(8,128)}, u32[]{:S(2)}, u32[]{:S(2)}) %collective-permute-start.13) | collective-permute-done | bytes 524320 | tf_op jit(solution)/shard_map/ppermute | solution.py:521
  28.4 16.6 %first_half.1 = (f32[1,256,256]{2,1,0:T(8,128)}, f32[1,256,256]{2,1,0:T(8,128)}, f32[1,256,256]{2,1,0:T(8,128)}) custom-call(f32[1,256,512]{2,1,0:T(8,128)} %collective-permute-done.13.refs_0_.refs_2_, f32[1,512,512]{2,1,0:T(8,128)} %gram.3.refs_1_), custom_call_target="tpu_custom_call" | custom-call | flops 20000000000 | bytes 1048576 | tf_op jit(solution)/shard_map/first_half/pallas_call | solution.py:214
  45.0 17.5 %second_half.1.own_basis.refs_4_.refs_6_ = bf16[1,1024,512]{2,1,0:T(8,128)(2,1)} custom-call(s32[3]{0:T(128)} %pad_add_fusion.5.offsets, f32[1,512,512]{2,1,0:T(8,128)} %constant_dynamic-slice_fusion.2.refs_0_, f32[1,256,512]{2,1,0:T(8,128)} %collective-permute-done.12.refs_0_.refs_1_, f32[1,256,512]{2,1,0:T(8,128)} %collective-permute-done.13.refs_0_.refs_2_, ...), custom_call_target="tpu_custom_call" | custom-call | flops 20000000000 | bytes 3145728 | tf_op jit(solution)/shard_map/second_half/pallas_call | solution.py:236
  68.7 6.6 %project.7 = (bf16[2,2,256,512]{3,2,1,0:T(8,128)(2,1)}, bf16[2,2,256,512]{3,2,1,0:T(8,128)(2,1)}) custom-call(s32[4]{0:T(128)} %pad_add_fusion.3.quads, s32[2]{0:T(128)} %get-tuple-element.64.where, bf16[1,2,4096,1024]{3,2,1,0:T(8,128)(2,1)} %grads_ref.7, bf16[1,1024,512]{2,1,0:T(8,128)(2,1)} %second_half.1.own_basis.refs_4_.refs_6_, ...), custom_call_target="tpu_custom_call" | custom-call | flops 2147483648 | bytes 6291456 | tf_op jit(solution)/shard_map/project/pallas_call | solution.py:317
  75.2 6.7 %project.6 = (bf16[2,2,256,512]{3,2,1,0:T(8,128)(2,1)}, bf16[2,2,256,512]{3,2,1,0:T(8,128)(2,1)}) custom-call(s32[4]{0:T(128)} %pad_add_fusion.3.quads, s32[2]{0:T(128)} %get-tuple-element.63.where, bf16[1,2,4096,1024]{3,2,1,0:T(8,128)(2,1)} %grads_ref.7, bf16[1,1024,512]{2,1,0:T(8,128)(2,1)} %second_half.1.own_basis.refs_4_.refs_6_, ...), custom_call_target="tpu_custom_call" | custom-call | flops 2147483648 | bytes 6291456 | tf_op jit(solution)/shard_map/project/pallas_call | solution.py:317
  83.5 6.5 %collective-permute-done.6.refs_1_ = bf16[2,32,16,512]{3,2,1,0:T(8,128)(2,1)} collective-permute-done((bf16[2,32,16,512]{3,2,1,0:T(8,128)(2,1)}, bf16[2,32,16,512]{3,2,1,0:T(8,128)(2,1)}, u32[]{:S(2)}, u32[]{:S(2)}) %collective-permute-start.6) | collective-permute-done | bytes 1048608 | tf_op jit(solution)/shard_map/ppermute | solution.py:498
  90.0 6.5 %project.5 = (bf16[2,2,256,512]{3,2,1,0:T(8,128)(2,1)}, bf16[2,2,256,512]{3,2,1,0:T(8,128)(2,1)}) custom-call(s32[4]{0:T(128)} %pad_add_fusion.3.quads, s32[2]{0:T(128)} %get-tuple-element.61.where, bf16[1,2,4096,1024]{3,2,1,0:T(8,128)(2,1)} %grads_ref.7, bf16[1,1024,512]{2,1,0:T(8,128)(2,1)} %second_half.1.own_basis.refs_4_.refs_6_, ...), custom_call_target="tpu_custom_call" | custom-call | flops 2147483648 | bytes 6291456 | tf_op jit(solution)/shard_map/project/pallas_call | solution.py:317
  97.1 2.1 fusion.17
  101.2 6.7 %project.4 = (bf16[2,2,256,512]{3,2,1,0:T(8,128)(2,1)}, bf16[2,2,256,512]{3,2,1,0:T(8,128)(2,1)}) custom-call(s32[4]{0:T(128)} %pad_add_fusion.3.quads, s32[2]{0:T(128)} %get-tuple-element.62.where, bf16[1,2,4096,1024]{3,2,1,0:T(8,128)(2,1)} %grads_ref.7, bf16[1,1024,512]{2,1,0:T(8,128)(2,1)} %second_half.1.own_basis.refs_4_.refs_6_, ...), custom_call_target="tpu_custom_call" | custom-call | flops 2147483648 | bytes 6291456 | tf_op jit(solution)/shard_map/project/pallas_call | solution.py:317
  107.9 2.0 fusion.16
  109.9 2.5 collective-permute-done.refs_1_
  112.4 10.9 %collective-permute-done.22 = bf16[2,256,512]{2,1,0:T(8,128)(2,1)} collective-permute-done((bf16[2,256,512]{2,1,0:T(8,128)(2,1)}, bf16[2,256,512]{2,1,0:T(8,128)(2,1)}, u32[]{:S(2)}, u32[]{:S(2)}) %collective-permute-start.22) | collective-permute-done | bytes 524320 | tf_op jit(solution)/shard_map/ppermute | solution.py:498
  123.3 2.4 fusion.7
  126.1 1.7 collective-permute-start.20
  130.9 6.0 %collect.3 = (bf16[2,256,512]{2,1,0:T(8,128)(2,1)}, bf16[2,256,512]{2,1,0:T(8,128)(2,1)}, bf16[2,256,512]{2,1,0:T(8,128)(2,1)}, bf16[2,256,512]{2,1,0:T(8,128)(2,1)}) custom-call(s32[4,2,32]{2,1,0:T(2,128)} %get-tuple-element.60.places, s32[4,2]{1,0:T(4,128)} %get-tuple-element.59.counts, bf16[2,32,16,512]{3,2,1,0:T(8,128)(2,1)} %fusion.6.refs_0_, ...), custom_call_target="tpu_custom_call" | custom-call | bytes 8388608 | tf_op jit(solution)/shard_map/collect/pallas_call | solution.py:281
  136.9 2.1 fusion.15
  140.3 2.8 collective-permute-start.10
  144.7 2.4 fusion.9
  148.7 2.3 collective-permute-start.11
  150.9 6.0 %collect.2 = (bf16[2,256,512]{2,1,0:T(8,128)(2,1)}, bf16[2,256,512]{2,1,0:T(8,128)(2,1)}, bf16[2,256,512]{2,1,0:T(8,128)(2,1)}, bf16[2,256,512]{2,1,0:T(8,128)(2,1)}) custom-call(s32[4,2,32]{2,1,0:T(2,128)} %get-tuple-element.60.places, s32[4,2]{1,0:T(4,128)} %get-tuple-element.59.counts, bf16[2,32,16,512]{3,2,1,0:T(8,128)(2,1)} %copy-done.3, ...), custom_call_target="tpu_custom_call" | custom-call | bytes 8388608 | tf_op jit(solution)/shard_map/collect/pallas_call | solution.py:281
  158.7 21.5 %collective-permute-done.10 = bf16[2,256,512]{2,1,0:T(8,128)(2,1)} collective-permute-done((bf16[2,256,512]{2,1,0:T(8,128)(2,1)}, bf16[2,256,512]{2,1,0:T(8,128)(2,1)}, u32[]{:S(2)}, u32[]{:S(2)}) %collective-permute-start.10) | collective-permute-done | bytes 524320 | tf_op jit(solution)/shard_map/ppermute | solution.py:498
  180.2 5.6 %collective-permute-start.5 = (bf16[2,256,512]{2,1,0:T(8,128)(2,1)}, bf16[2,256,512]{2,1,0:T(8,128)(2,1)S(1)}, u32[]{:S(2)}, u32[]{:S(2)}) collective-permute-start(bf16[2,256,512]{2,1,0:T(8,128)(2,1)} %get-tuple-element.31), channel_id=1, source_target_pairs={{0,24},{2,26},{4,28},{6,30},{8,0},{10,2},{12,4},{14,6},{16,8},{18,... | collective-permute-start | bytes 1572872 | tf_op jit(solution)/shard_map/ppermute | solution.py:498
  187.3 20.3 %collective-permute-done.11 = bf16[2,256,512]{2,1,0:T(8,128)(2,1)S(1)} collective-permute-done((bf16[2,256,512]{2,1,0:T(8,128)(2,1)}, bf16[2,256,512]{2,1,0:T(8,128)(2,1)S(1)}, u32[]{:S(2)}, u32[]{:S(2)}) %collective-permute-start.11) | collective-permute-done | bytes 524320 | tf_op jit(solution)/shard_map/ppermute | solution.py:498
  208.1 19.0 %collective-permute-start.25 = (bf16[2,256,512]{2,1,0:T(8,128)(2,1)S(1)}, bf16[2,256,512]{2,1,0:T(8,128)(2,1)S(1)}, u32[]{:S(2)}, u32[]{:S(2)}) collective-permute-start(bf16[2,256,512]{2,1,0:T(8,128)(2,1)S(1)} %fusion.11), channel_id=1, source_target_pairs={{0,8},{2,10},{4,12},{6,14},{8,16},{10,18},{12,20},{14,22},{16,24},... | collective-permute-start | bytes 1572872 | tf_op jit(solution)/shard_map/ppermute | solution.py:498
  228.2 17.5 %collective-permute-done.4 = bf16[2,256,512]{2,1,0:T(8,128)(2,1)S(1)} collective-permute-done((bf16[2,256,512]{2,1,0:T(8,128)(2,1)}, bf16[2,256,512]{2,1,0:T(8,128)(2,1)S(1)}, u32[]{:S(2)}, u32[]{:S(2)}) %collective-permute-start.4) | collective-permute-done | bytes 524320 | tf_op jit(solution)/shard_map/ppermute | solution.py:498
  247.3 22.0 %collective-permute-start.46 = (bf16[2,256,512]{2,1,0:T(8,128)(2,1)S(1)}, bf16[2,256,512]{2,1,0:T(8,128)(2,1)S(1)}, u32[]{:S(2)}, u32[]{:S(2)}) collective-permute-start(bf16[2,256,512]{2,1,0:T(8,128)(2,1)S(1)} %get-tuple-element.50.refs_0_), channel_id=1, source_target_pairs={{0,8},{2,10},{4,12},{6,14},{8,16},{10,18},{12,20},{14,22},{16,24},... | collective-permute-start | bytes 1572872 | tf_op jit(solution)/shard_map/ppermute | solution.py:498
  272.3 9.3 %collective-permute-done.46.refs_4_ = bf16[2,256,512]{2,1,0:T(8,128)(2,1)S(1)} collective-permute-done((bf16[2,256,512]{2,1,0:T(8,128)(2,1)S(1)}, bf16[2,256,512]{2,1,0:T(8,128)(2,1)S(1)}, u32[]{:S(2)}, u32[]{:S(2)}) %collective-permute-start.46) | collective-permute-done | bytes 524320 | tf_op jit(solution)/shard_map/ppermute | solution.py:498
  281.6 2.5 collective-permute-done.43.refs_1_
  285.6 9.7 %collective-permute-done.40.refs_1_ = bf16[2,256,512]{2,1,0:T(8,128)(2,1)S(1)} collective-permute-done((bf16[2,256,512]{2,1,0:T(8,128)(2,1)S(1)}, bf16[2,256,512]{2,1,0:T(8,128)(2,1)S(1)}, u32[]{:S(2)}, u32[]{:S(2)}) %collective-permute-start.40) | collective-permute-done | bytes 524320 | tf_op jit(solution)/shard_map/ppermute | solution.py:498
  295.9 8.2 %collective-permute-done.50.refs_8_ = bf16[2,256,512]{2,1,0:T(8,128)(2,1)} collective-permute-done((bf16[2,256,512]{2,1,0:T(8,128)(2,1)S(1)}, bf16[2,256,512]{2,1,0:T(8,128)(2,1)}, u32[]{:S(2)}, u32[]{:S(2)}) %collective-permute-start.50) | collective-permute-done | bytes 524320 | tf_op jit(solution)/shard_map/ppermute | solution.py:498
  305.9 2.3 collective-permute-start.54
  308.2 7.2 %collective-permute-done.27.refs_0_ = bf16[2,256,512]{2,1,0:T(8,128)(2,1)} collective-permute-done((bf16[2,256,512]{2,1,0:T(8,128)(2,1)}, bf16[2,256,512]{2,1,0:T(8,128)(2,1)}, u32[]{:S(2)}, u32[]{:S(2)}) %collective-permute-start.27) | collective-permute-done | bytes 524320 | tf_op jit(solution)/shard_map/ppermute | solution.py:498
  316.9 2.5 collective-permute-start.28
  321.0 5.7 %collective-permute-done.54.refs_12_ = bf16[2,256,512]{2,1,0:T(8,128)(2,1)S(1)} collective-permute-done((bf16[2,256,512]{2,1,0:T(8,128)(2,1)}, bf16[2,256,512]{2,1,0:T(8,128)(2,1)S(1)}, u32[]{:S(2)}, u32[]{:S(2)}) %collective-permute-start.54) | collective-permute-done | bytes 524320 | tf_op jit(solution)/shard_map/ppermute | solution.py:498
  326.7 4.1 %collective-permute-done.30.refs_1_ = bf16[2,256,512]{2,1,0:T(8,128)(2,1)S(1)} collective-permute-done((bf16[2,256,512]{2,1,0:T(8,128)(2,1)}, bf16[2,256,512]{2,1,0:T(8,128)(2,1)S(1)}, u32[]{:S(2)}, u32[]{:S(2)}) %collective-permute-start.30) | collective-permute-done | bytes 524320 | tf_op jit(solution)/shard_map/ppermute | solution.py:498
  330.7 5.3 %collective-permute-done.28.refs_0_ = bf16[2,256,512]{2,1,0:T(8,128)(2,1)S(1)} collective-permute-done((bf16[2,256,512]{2,1,0:T(8,128)(2,1)}, bf16[2,256,512]{2,1,0:T(8,128)(2,1)S(1)}, u32[]{:S(2)}, u32[]{:S(2)}) %collective-permute-start.28) | collective-permute-done | bytes 524320 | tf_op jit(solution)/shard_map/ppermute | solution.py:498
  342.6 2.6 collective-permute-start.31
  348.5 2.4 collective-permute-start.56
  350.8 2.6 collective-permute-done.29.refs_1_
  354.6 7.0 %expand.4.refs_6_ = bf16[2,4096,1024]{2,1,0:T(8,128)(2,1)} custom-call(s32[4]{0:T(128)} %pad_add_fusion.quads, s32[2]{0:T(128)} %pad_add_fusion.8.where, bf16[2,256,512]{2,1,0:T(8,128)(2,1)} %copy-done.6, bf16[2,256,512]{2,1,0:T(8,128)(2,1)} %copy-done.25, bf16[2,256,512]{2,1,0:T(8,128)(2,1)} %copy-done.26, bf16[2,256,512]{2,1,0:T(8,128)(2,1)} %copy-done.27, ...), custom_call_target="tpu_custom_call" | custom-call | flops 2147483648 | bytes 6291456 | tf_op jit(solution)/shard_map/expand/pallas_call | solution.py:383
  362.4 6.7 %expand.5.refs_6_ = bf16[2,4096,1024]{2,1,0:T(8,128)(2,1)} custom-call(s32[4]{0:T(128)} %pad_add_fusion.quads, s32[2]{0:T(128)} %get-tuple-element.64.where, bf16[2,256,512]{2,1,0:T(8,128)(2,1)} %collective-permute-done.26.refs_0_, bf16[2,256,512]{2,1,0:T(8,128)(2,1)} %collective-permute-done.37.refs_1_, ...), custom_call_target="tpu_custom_call", output_to_operand_aliasing={{}: (8, {})} | custom-call | flops 2147483648 | bytes 6291456 | tf_op jit(solution)/shard_map/expand/pallas_call | solution.py:383
  369.7 6.7 %expand.6.refs_8_ = bf16[2,4096,1024]{2,1,0:T(8,128)(2,1)} custom-call(s32[4]{0:T(128)} %pad_add_fusion.quads, s32[2]{0:T(128)} %get-tuple-element.63.where, bf16[2,256,512]{2,1,0:T(8,128)(2,1)} %collective-permute-done.27.refs_0_, bf16[2,256,512]{2,1,0:T(8,128)(2,1)} %copy-done.8, ...), custom_call_target="tpu_custom_call", output_to_operand_aliasing={{}: (8, {})} | custom-call | flops 2147483648 | bytes 6291456 | tf_op jit(solution)/shard_map/expand/pallas_call | solution.py:383
  376.4 7.0 %expand.7 = bf16[2,4096,1024]{2,1,0:T(8,128)(2,1)} custom-call(s32[4]{0:T(128)} %pad_add_fusion.quads, s32[2]{0:T(128)} %get-tuple-element.61.where, bf16[2,256,512]{2,1,0:T(8,128)(2,1)} %copy-done.7, bf16[1,256,512]{2,1,0:T(8,128)(2,1)} %copy-done.28, bf16[1,256,512]{2,1,0:T(8,128)(2,1)} %collective-permute-done.31.refs_2_, ...), custom_call_target="tpu_custom_call", output_to_operand_aliasing={{}: (10, {})} | custom-call | flops 2147483648 | bytes 6291456 | tf_op jit(solution)/shard_map/expand/pallas_call | solution.py:383
  384.7 8.1 %settle.1 = (f32[2,1,32,16,512]{4,3,2,1,0:T(8,128)}, f32[2,1,32,16,512]{4,3,2,1,0:T(8,128)}) custom-call(s32[2,32]{1,0:T(2,128)} %get-tuple-element.58.piece_of, s32[2,32]{1,0:T(2,128)} %get-tuple-element.57.row_of, s32[2,32]{1,0:T(2,128)} %fusion.29.held, bf16[2,256,512]{2,1,0:T(8,128)(2,1)} %copy-done.4, bf16[2,256,512]{2,1,0:T(8,128)(2,1)} %copy-done.18, ...), custom_call_target="tpu_custom_call" | custom-call | flops 4194304 | bytes 9437184 | tf_op jit(solution)/shard_map/settle/pallas_call | solution.py:452
  (185 shorter events, 51.1 us)
Async XLA Ops:
  2.1 15.9 %collective-permute-start.12 = (f32[1,256,512]{2,1,0:T(8,128)S(1)}, f32[1,256,512]{2,1,0:T(8,128)}, u32[]{:S(2)}, u32[]{:S(2)}) collective-permute-start(f32[1,256,512]{2,1,0:T(8,128)S(1)} %get-tuple-element.56), channel_id=1, source_target_pairs={{0,1},{1,0},{2,3},{3,2},{4,5},{5,4},{6,7},{7,6},{8,9},{9,8},{10,11... | collective-permute-start | bytes 1572872 | tf_op jit(solution)/shard_map/ppermute | solution.py:521
  5.1 23.3 %collective-permute-start.13 = (f32[1,256,512]{2,1,0:T(8,128)S(1)}, f32[1,256,512]{2,1,0:T(8,128)}, u32[]{:S(2)}, u32[]{:S(2)}) collective-permute-start(f32[1,256,512]{2,1,0:T(8,128)S(1)} %get-tuple-element.55), channel_id=1, source_target_pairs={{0,1},{1,0},{2,3},{3,2},{4,5},{5,4},{6,7},{7,6},{8,9},{9,8},{10,11... | collective-permute-start | bytes 1572872 | tf_op jit(solution)/shard_map/ppermute | solution.py:521
  63.7 26.3 %collective-permute-start.6 = (bf16[2,32,16,512]{3,2,1,0:T(8,128)(2,1)}, bf16[2,32,16,512]{3,2,1,0:T(8,128)(2,1)}, u32[]{:S(2)}, u32[]{:S(2)}) collective-permute-start(bf16[2,32,16,512]{3,2,1,0:T(8,128)(2,1)} %fusion.6.refs_0_), channel_id=1, source_target_pairs={{0,4},{2,6},{4,0},{6,2},{8,12},{10,14},{12,8},{14,10},{16,20},{18,... | collective-permute-start | bytes 3145736 | tf_op jit(solution)/shard_map/ppermute | solution.py:498
  65.4 60.2 %collective-permute-start.7 = (bf16[2,32,16,512]{3,2,1,0:T(8,128)(2,1)}, bf16[2,32,16,512]{3,2,1,0:T(8,128)(2,1)}, u32[]{:S(2)}, u32[]{:S(2)}) collective-permute-start(bf16[2,32,16,512]{3,2,1,0:T(8,128)(2,1)} %fusion.6.refs_0_), channel_id=1, source_target_pairs={{0,2},{2,0},{4,6},{6,4},{8,10},{10,8},{12,14},{14,12},{16,18},{18,... | collective-permute-start | bytes 3145736 | tf_op jit(solution)/shard_map/ppermute | solution.py:498
  65.8 46.6 %collective-permute-start = (bf16[2,32,16,512]{3,2,1,0:T(8,128)(2,1)S(1)}, bf16[2,32,16,512]{3,2,1,0:T(8,128)(2,1)S(1)}, u32[]{:S(2)}, u32[]{:S(2)}) collective-permute-start(bf16[2,32,16,512]{3,2,1,0:T(8,128)(2,1)S(1)} %fusion.5.refs_0_), channel_id=1, source_target_pairs={{0,4},{2,6},{4,0},{6,2},{8,12},{10,14},{12,8},{14,10},{16,20},{18,... | collective-permute-start | bytes 3145736 | tf_op jit(solution)/shard_map/ppermute | solution.py:498
  75.2 21.3 %collective-permute-start.21 = (bf16[2,2,256,512]{3,2,1,0:T(8,128)(2,1)}, bf16[2,2,256,512]{3,2,1,0:T(8,128)(2,1)}, u32[]{:S(2)}, u32[]{:S(2)}) collective-permute-start(bf16[2,2,256,512]{3,2,1,0:T(8,128)(2,1)} %get-tuple-element.47), channel_id=1, source_target_pairs={{0,2},{2,0},{4,6},{6,4},{8,10},{10,8},{12,14},{14,12},{16,18},{18,... | collective-permute-start | bytes 3145736 | tf_op jit(solution)/shard_map/ppermute | solution.py:498
  82.0 17.2 %collective-permute-start.19 = (bf16[2,2,256,512]{3,2,1,0:T(8,128)(2,1)}, bf16[2,2,256,512]{3,2,1,0:T(8,128)(2,1)S(1)}, u32[]{:S(2)}, u32[]{:S(2)}) collective-permute-start(bf16[2,2,256,512]{3,2,1,0:T(8,128)(2,1)} %get-tuple-element.45), channel_id=1, source_target_pairs={{0,2},{2,0},{4,6},{6,4},{8,10},{10,8},{12,14},{14,12},{16,18},{18,... | collective-permute-start | bytes 3145736 | tf_op jit(solution)/shard_map/ppermute | solution.py:498
  90.0 36.1 %collective-permute-start.8 = (bf16[2,32,16,512]{3,2,1,0:T(8,128)(2,1)}, bf16[2,32,16,512]{3,2,1,0:T(8,128)(2,1)}, u32[]{:S(2)}, u32[]{:S(2)}) collective-permute-start(bf16[2,32,16,512]{3,2,1,0:T(8,128)(2,1)} %collective-permute-done.6.refs_1_), channel_id=1, source_target_pairs={{0,2},{2,0},{4,6},{6,4},{8,10},{10,8},{12,14},{14,12},{16,18},{18,... | collective-permute-start | bytes 3145736 | tf_op jit(solution)/shard_map/ppermute | solution.py:498
  96.5 31.3 %collective-permute-start.17 = (bf16[2,2,256,512]{3,2,1,0:T(8,128)(2,1)}, bf16[2,2,256,512]{3,2,1,0:T(8,128)(2,1)}, u32[]{:S(2)}, u32[]{:S(2)}) collective-permute-start(bf16[2,2,256,512]{3,2,1,0:T(8,128)(2,1)} %get-tuple-element.43), channel_id=1, source_target_pairs={{0,2},{2,0},{4,6},{6,4},{8,10},{10,8},{12,14},{14,12},{16,18},{18,... | collective-permute-start | bytes 3145736 | tf_op jit(solution)/shard_map/ppermute | solution.py:498
  99.2 24.0 %collective-permute-start.22 = (bf16[2,256,512]{2,1,0:T(8,128)(2,1)}, bf16[2,256,512]{2,1,0:T(8,128)(2,1)}, u32[]{:S(2)}, u32[]{:S(2)}) collective-permute-start(bf16[2,256,512]{2,1,0:T(8,128)(2,1)} %fusion.17), channel_id=1, source_target_pairs={{0,4},{2,6},{4,0},{6,2},{8,12},{10,14},{12,8},{14,10},{16,20},{18,... | collective-permute-start | bytes 1572872 | tf_op jit(solution)/shard_map/ppermute | solution.py:498
  112.4 34.7 %collective-permute-start.1 = (bf16[2,32,16,512]{3,2,1,0:T(8,128)(2,1)S(1)}, bf16[2,32,16,512]{3,2,1,0:T(8,128)(2,1)}, u32[]{:S(2)}, u32[]{:S(2)}) collective-permute-start(bf16[2,32,16,512]{3,2,1,0:T(8,128)(2,1)S(1)} %fusion.5.refs_0_), channel_id=1, source_target_pairs={{0,2},{2,0},{4,6},{6,4},{8,10},{10,8},{12,14},{14,12},{16,18},{18,... | collective-permute-start | bytes 3145736 | tf_op jit(solution)/shard_map/ppermute | solution.py:498
  123.2 25.4 %collective-permute-start.2 = (bf16[2,32,16,512]{3,2,1,0:T(8,128)(2,1)S(1)}, bf16[2,32,16,512]{3,2,1,0:T(8,128)(2,1)}, u32[]{:S(2)}, u32[]{:S(2)}) collective-permute-start(bf16[2,32,16,512]{3,2,1,0:T(8,128)(2,1)S(1)} %collective-permute-done.refs_1_), channel_id=1, source_target_pairs={{0,2},{2,0},{4,6},{6,4},{8,10},{10,8},{12,14},{14,12},{16,18},{18,... | collective-permute-start | bytes 3145736 | tf_op jit(solution)/shard_map/ppermute | solution.py:498
  125.6 31.3 %collective-permute-start.15 = (bf16[2,2,256,512]{3,2,1,0:T(8,128)(2,1)}, bf16[2,2,256,512]{3,2,1,0:T(8,128)(2,1)}, u32[]{:S(2)}, u32[]{:S(2)}) collective-permute-start(bf16[2,2,256,512]{3,2,1,0:T(8,128)(2,1)} %get-tuple-element.41), channel_id=1, source_target_pairs={{0,2},{2,0},{4,6},{6,4},{8,10},{10,8},{12,14},{14,12},{16,18},{18,... | collective-permute-start | bytes 3145736 | tf_op jit(solution)/shard_map/ppermute | solution.py:498
  127.9 15.8 %collective-permute-start.23 = (bf16[2,256,512]{2,1,0:T(8,128)(2,1)}, bf16[2,256,512]{2,1,0:T(8,128)(2,1)}, u32[]{:S(2)}, u32[]{:S(2)}) collective-permute-start(bf16[2,256,512]{2,1,0:T(8,128)(2,1)} %fusion.7), channel_id=1, source_target_pairs={{0,8},{2,10},{4,12},{6,14},{8,16},{10,18},{12,20},{14,22},{16,24},... | collective-permute-start | bytes 1572872 | tf_op jit(solution)/shard_map/ppermute | solution.py:498
  140.3 39.8 %collective-permute-start.10 = (bf16[2,256,512]{2,1,0:T(8,128)(2,1)}, bf16[2,256,512]{2,1,0:T(8,128)(2,1)}, u32[]{:S(2)}, u32[]{:S(2)}) collective-permute-start(bf16[2,256,512]{2,1,0:T(8,128)(2,1)} %get-tuple-element.34), channel_id=1, source_target_pairs={{0,16},{2,18},{4,20},{6,22},{8,24},{10,26},{12,28},{14,30},{16,0},... | collective-permute-start | bytes 1572872 | tf_op jit(solution)/shard_map/ppermute | solution.py:498
  143.6 36.5 %collective-permute-start.18 = (bf16[2,256,512]{2,1,0:T(8,128)(2,1)}, bf16[2,256,512]{2,1,0:T(8,128)(2,1)}, u32[]{:S(2)}, u32[]{:S(2)}) collective-permute-start(bf16[2,256,512]{2,1,0:T(8,128)(2,1)} %fusion.15), channel_id=1, source_target_pairs={{0,4},{2,6},{4,0},{6,2},{8,12},{10,14},{12,8},{14,10},{16,20},{18,... | collective-permute-start | bytes 1572872 | tf_op jit(solution)/shard_map/ppermute | solution.py:498
  147.1 33.1 %collective-permute-start.24 = (bf16[2,256,512]{2,1,0:T(8,128)(2,1)}, bf16[2,256,512]{2,1,0:T(8,128)(2,1)S(1)}, u32[]{:S(2)}, u32[]{:S(2)}) collective-permute-start(bf16[2,256,512]{2,1,0:T(8,128)(2,1)} %fusion.9), channel_id=1, source_target_pairs={{0,8},{2,10},{4,12},{6,14},{8,16},{10,18},{12,20},{14,22},{16,24},... | collective-permute-start | bytes 1572872 | tf_op jit(solution)/shard_map/ppermute | solution.py:498
  148.7 58.9 %collective-permute-start.11 = (bf16[2,256,512]{2,1,0:T(8,128)(2,1)}, bf16[2,256,512]{2,1,0:T(8,128)(2,1)S(1)}, u32[]{:S(2)}, u32[]{:S(2)}) collective-permute-start(bf16[2,256,512]{2,1,0:T(8,128)(2,1)} %get-tuple-element.35), channel_id=1, source_target_pairs={{0,24},{2,26},{4,28},{6,30},{8,0},{10,2},{12,4},{14,6},{16,8},{18,... | collective-permute-start | bytes 1572872 | tf_op jit(solution)/shard_map/ppermute | solution.py:498
  156.9 51.1 %collective-permute-start.9 = (bf16[2,256,512]{2,1,0:T(8,128)(2,1)}, bf16[2,256,512]{2,1,0:T(8,128)(2,1)S(1)}, u32[]{:S(2)}, u32[]{:S(2)}) collective-permute-start(bf16[2,256,512]{2,1,0:T(8,128)(2,1)} %get-tuple-element.33), channel_id=1, source_target_pairs={{0,8},{2,10},{4,12},{6,14},{8,16},{10,18},{12,20},{14,22},{16,24},... | collective-permute-start | bytes 1572872 | tf_op jit(solution)/shard_map/ppermute | solution.py:498
  180.2 48.0 %collective-permute-start.3 = (bf16[2,256,512]{2,1,0:T(8,128)(2,1)}, bf16[2,256,512]{2,1,0:T(8,128)(2,1)S(1)}, u32[]{:S(2)}, u32[]{:S(2)}) collective-permute-start(bf16[2,256,512]{2,1,0:T(8,128)(2,1)} %get-tuple-element.29), channel_id=1, source_target_pairs={{0,8},{2,10},{4,12},{6,14},{8,16},{10,18},{12,20},{14,22},{16,24},... | collective-permute-start | bytes 1572872 | tf_op jit(solution)/shard_map/ppermute | solution.py:498
  180.2 65.6 %collective-permute-start.4 = (bf16[2,256,512]{2,1,0:T(8,128)(2,1)}, bf16[2,256,512]{2,1,0:T(8,128)(2,1)S(1)}, u32[]{:S(2)}, u32[]{:S(2)}) collective-permute-start(bf16[2,256,512]{2,1,0:T(8,128)(2,1)} %get-tuple-element.30), channel_id=1, source_target_pairs={{0,16},{2,18},{4,20},{6,22},{8,24},{10,26},{12,28},{14,30},{16,0},... | collective-permute-start | bytes 1572872 | tf_op jit(solution)/shard_map/ppermute | solution.py:498
  180.2 65.5 %collective-permute-start.5 = (bf16[2,256,512]{2,1,0:T(8,128)(2,1)}, bf16[2,256,512]{2,1,0:T(8,128)(2,1)S(1)}, u32[]{:S(2)}, u32[]{:S(2)}) collective-permute-start(bf16[2,256,512]{2,1,0:T(8,128)(2,1)} %get-tuple-element.31), channel_id=1, source_target_pairs={{0,24},{2,26},{4,28},{6,30},{8,0},{10,2},{12,4},{14,6},{16,8},{18,... | collective-permute-start | bytes 1572872 | tf_op jit(solution)/shard_map/ppermute | solution.py:498
  207.6 38.3 %collective-permute-start.16 = (bf16[2,256,512]{2,1,0:T(8,128)(2,1)S(1)}, bf16[2,256,512]{2,1,0:T(8,128)(2,1)S(1)}, u32[]{:S(2)}, u32[]{:S(2)}) collective-permute-start(bf16[2,256,512]{2,1,0:T(8,128)(2,1)S(1)} %fusion.14), channel_id=1, source_target_pairs={{0,4},{2,6},{4,0},{6,2},{8,12},{10,14},{12,8},{14,10},{16,20},{18,... | collective-permute-start | bytes 1572872 | tf_op jit(solution)/shard_map/ppermute | solution.py:498
  208.1 37.8 %collective-permute-start.25 = (bf16[2,256,512]{2,1,0:T(8,128)(2,1)S(1)}, bf16[2,256,512]{2,1,0:T(8,128)(2,1)S(1)}, u32[]{:S(2)}, u32[]{:S(2)}) collective-permute-start(bf16[2,256,512]{2,1,0:T(8,128)(2,1)S(1)} %fusion.11), channel_id=1, source_target_pairs={{0,8},{2,10},{4,12},{6,14},{8,16},{10,18},{12,20},{14,22},{16,24},... | collective-permute-start | bytes 1572872 | tf_op jit(solution)/shard_map/ppermute | solution.py:498
  247.3 34.3 %collective-permute-start.46 = (bf16[2,256,512]{2,1,0:T(8,128)(2,1)S(1)}, bf16[2,256,512]{2,1,0:T(8,128)(2,1)S(1)}, u32[]{:S(2)}, u32[]{:S(2)}) collective-permute-start(bf16[2,256,512]{2,1,0:T(8,128)(2,1)S(1)} %get-tuple-element.50.refs_0_), channel_id=1, source_target_pairs={{0,8},{2,10},{4,12},{6,14},{8,16},{10,18},{12,20},{14,22},{16,24},... | collective-permute-start | bytes 1572872 | tf_op jit(solution)/shard_map/ppermute | solution.py:498
  269.3 14.8 %collective-permute-start.43 = (bf16[2,256,512]{2,1,0:T(8,128)(2,1)S(1)}, bf16[2,256,512]{2,1,0:T(8,128)(2,1)S(1)}, u32[]{:S(2)}, u32[]{:S(2)}) collective-permute-start(bf16[2,256,512]{2,1,0:T(8,128)(2,1)S(1)} %get-tuple-element.50.refs_0_), channel_id=1, source_target_pairs={{0,4},{2,6},{4,0},{6,2},{8,12},{10,14},{12,8},{14,10},{16,20},{18,... | collective-permute-start | bytes 1572872 | tf_op jit(solution)/shard_map/ppermute | solution.py:498
  271.5 23.8 %collective-permute-start.40 = (bf16[2,256,512]{2,1,0:T(8,128)(2,1)S(1)}, bf16[2,256,512]{2,1,0:T(8,128)(2,1)S(1)}, u32[]{:S(2)}, u32[]{:S(2)}) collective-permute-start(bf16[2,256,512]{2,1,0:T(8,128)(2,1)S(1)} %fusion.13.refs_0_), channel_id=1, source_target_pairs={{0,4},{2,6},{4,0},{6,2},{8,12},{10,14},{12,8},{14,10},{16,20},{18,... | collective-permute-start | bytes 1572872 | tf_op jit(solution)/shard_map/ppermute | solution.py:498
  272.2 23.1 %collective-permute-start.26 = (bf16[2,256,512]{2,1,0:T(8,128)(2,1)S(1)}, bf16[2,256,512]{2,1,0:T(8,128)(2,1)}, u32[]{:S(2)}, u32[]{:S(2)}) collective-permute-start(bf16[2,256,512]{2,1,0:T(8,128)(2,1)S(1)} %fusion.13.refs_0_), channel_id=1, source_target_pairs={{0,8},{2,10},{4,12},{6,14},{8,16},{10,18},{12,20},{14,22},{16,24},... | collective-permute-start | bytes 1572872 | tf_op jit(solution)/shard_map/ppermute | solution.py:498
  284.1 20.0 %collective-permute-start.50 = (bf16[2,256,512]{2,1,0:T(8,128)(2,1)S(1)}, bf16[2,256,512]{2,1,0:T(8,128)(2,1)}, u32[]{:S(2)}, u32[]{:S(2)}) collective-permute-start(bf16[2,256,512]{2,1,0:T(8,128)(2,1)S(1)} %collective-permute-done.46.refs_4_), channel_id=1, source_target_pairs={{0,8},{2,10},{4,12},{6,14},{8,16},{10,18},{12,20},{14,22},{16,24},... | collective-permute-start | bytes 1572872 | tf_op jit(solution)/shard_map/ppermute | solution.py:498
  284.2 20.3 %collective-permute-start.47 = (bf16[2,256,512]{2,1,0:T(8,128)(2,1)S(1)}, bf16[2,256,512]{2,1,0:T(8,128)(2,1)}, u32[]{:S(2)}, u32[]{:S(2)}) collective-permute-start(bf16[2,256,512]{2,1,0:T(8,128)(2,1)S(1)} %collective-permute-done.46.refs_4_), channel_id=1, source_target_pairs={{0,4},{2,6},{4,0},{6,2},{8,12},{10,14},{12,8},{14,10},{16,20},{18,... | collective-permute-start | bytes 1572872 | tf_op jit(solution)/shard_map/ppermute | solution.py:498
  295.3 20.1 %collective-permute-start.27 = (bf16[2,256,512]{2,1,0:T(8,128)(2,1)}, bf16[2,256,512]{2,1,0:T(8,128)(2,1)}, u32[]{:S(2)}, u32[]{:S(2)}) collective-permute-start(bf16[2,256,512]{2,1,0:T(8,128)(2,1)} %collective-permute-done.26.refs_0_), channel_id=1, source_target_pairs={{0,8},{2,10},{4,12},{6,14},{8,16},{10,18},{12,20},{14,22},{16,24},... | collective-permute-start | bytes 1572872 | tf_op jit(solution)/shard_map/ppermute | solution.py:498
  295.5 21.4 %collective-permute-start.48 = (bf16[2,256,512]{2,1,0:T(8,128)(2,1)S(1)}, bf16[2,256,512]{2,1,0:T(8,128)(2,1)}, u32[]{:S(2)}, u32[]{:S(2)}) collective-permute-start(bf16[2,256,512]{2,1,0:T(8,128)(2,1)S(1)} %collective-permute-done.46.refs_4_), channel_id=1, source_target_pairs={{0,2},{2,0},{4,6},{6,4},{8,10},{10,8},{12,14},{14,12},{16,18},{18,... | collective-permute-start | bytes 1572872 | tf_op jit(solution)/shard_map/ppermute | solution.py:498
  304.1 15.3 %collective-permute-start.42 = (bf16[2,256,512]{2,1,0:T(8,128)(2,1)S(1)}, bf16[2,256,512]{2,1,0:T(8,128)(2,1)S(1)}, u32[]{:S(2)}, u32[]{:S(2)}) collective-permute-start(bf16[2,256,512]{2,1,0:T(8,128)(2,1)S(1)} %collective-permute-done.40.refs_1_), channel_id=1, source_target_pairs={{0,2},{2,0},{4,6},{6,4},{8,10},{10,8},{12,14},{14,12},{16,18},{18,... | collective-permute-start | bytes 1572872 | tf_op jit(solution)/shard_map/ppermute | solution.py:498
  304.5 15.1 %collective-permute-start.37 = (bf16[2,256,512]{2,1,0:T(8,128)(2,1)}, bf16[2,256,512]{2,1,0:T(8,128)(2,1)}, u32[]{:S(2)}, u32[]{:S(2)}) collective-permute-start(bf16[2,256,512]{2,1,0:T(8,128)(2,1)} %collective-permute-done.26.refs_0_), channel_id=1, source_target_pairs={{0,4},{2,6},{4,0},{6,2},{8,12},{10,14},{12,8},{14,10},{16,20},{18,... | collective-permute-start | bytes 1572872 | tf_op jit(solution)/shard_map/ppermute | solution.py:498
  305.9 20.8 %collective-permute-start.54 = (bf16[2,256,512]{2,1,0:T(8,128)(2,1)}, bf16[2,256,512]{2,1,0:T(8,128)(2,1)S(1)}, u32[]{:S(2)}, u32[]{:S(2)}) collective-permute-start(bf16[2,256,512]{2,1,0:T(8,128)(2,1)} %collective-permute-done.50.refs_8_), channel_id=1, source_target_pairs={{0,8},{2,10},{4,12},{6,14},{8,16},{10,18},{12,20},{14,22},{16,24},... | collective-permute-start | bytes 1572872 | tf_op jit(solution)/shard_map/ppermute | solution.py:498
  315.4 15.3 %collective-permute-start.30 = (bf16[2,256,512]{2,1,0:T(8,128)(2,1)}, bf16[2,256,512]{2,1,0:T(8,128)(2,1)S(1)}, u32[]{:S(2)}, u32[]{:S(2)}) collective-permute-start(bf16[2,256,512]{2,1,0:T(8,128)(2,1)} %collective-permute-done.27.refs_0_), channel_id=1, source_target_pairs={{0,4},{2,6},{4,0},{6,2},{8,12},{10,14},{12,8},{14,10},{16,20},{18,... | collective-permute-start | bytes 1572872 | tf_op jit(solution)/shard_map/ppermute | solution.py:498
  316.9 19.1 %collective-permute-start.28 = (bf16[2,256,512]{2,1,0:T(8,128)(2,1)}, bf16[2,256,512]{2,1,0:T(8,128)(2,1)S(1)}, u32[]{:S(2)}, u32[]{:S(2)}) collective-permute-start(bf16[2,256,512]{2,1,0:T(8,128)(2,1)} %collective-permute-done.27.refs_0_), channel_id=1, source_target_pairs={{0,8},{2,10},{4,12},{6,14},{8,16},{10,18},{12,20},{14,22},{16,24},... | collective-permute-start | bytes 1572872 | tf_op jit(solution)/shard_map/ppermute | solution.py:498
  319.4 19.6 %collective-permute-start.38 = (bf16[2,256,512]{2,1,0:T(8,128)(2,1)}, bf16[2,256,512]{2,1,0:T(8,128)(2,1)}, u32[]{:S(2)}, u32[]{:S(2)}) collective-permute-start(bf16[2,256,512]{2,1,0:T(8,128)(2,1)} %collective-permute-done.26.refs_0_), channel_id=1, source_target_pairs={{0,2},{2,0},{4,6},{6,4},{8,10},{10,8},{12,14},{14,12},{16,18},{18,... | collective-permute-start | bytes 1572872 | tf_op jit(solution)/shard_map/ppermute | solution.py:498
  319.6 21.5 %collective-permute-start.51 = (bf16[2,256,512]{2,1,0:T(8,128)(2,1)}, bf16[2,256,512]{2,1,0:T(8,128)(2,1)S(1)}, u32[]{:S(2)}, u32[]{:S(2)}) collective-permute-start(bf16[2,256,512]{2,1,0:T(8,128)(2,1)} %collective-permute-done.50.refs_8_), channel_id=1, source_target_pairs={{0,4},{2,6},{4,0},{6,2},{8,12},{10,14},{12,8},{14,10},{16,20},{18,... | collective-permute-start | bytes 1572872 | tf_op jit(solution)/shard_map/ppermute | solution.py:498
  326.7 15.9 %collective-permute-start.49 = (bf16[2,256,512]{2,1,0:T(8,128)(2,1)}, bf16[2,256,512]{2,1,0:T(8,128)(2,1)}, u32[]{:S(2)}, u32[]{:S(2)}) collective-permute-start(bf16[2,256,512]{2,1,0:T(8,128)(2,1)} %collective-permute-done.47.refs_5_), channel_id=1, source_target_pairs={{0,2},{2,0},{4,6},{6,4},{8,10},{10,8},{12,14},{14,12},{16,18},{18,... | collective-permute-start | bytes 1572872 | tf_op jit(solution)/shard_map/ppermute | solution.py:498
  330.7 14.4 %collective-permute-start.39 = (bf16[2,256,512]{2,1,0:T(8,128)(2,1)}, bf16[2,256,512]{2,1,0:T(8,128)(2,1)}, u32[]{:S(2)}, u32[]{:S(2)}) collective-permute-start(bf16[2,256,512]{2,1,0:T(8,128)(2,1)} %collective-permute-done.37.refs_1_), channel_id=1, source_target_pairs={{0,2},{2,0},{4,6},{6,4},{8,10},{10,8},{12,14},{14,12},{16,18},{18,... | collective-permute-start | bytes 1572872 | tf_op jit(solution)/shard_map/ppermute | solution.py:498
  345.1 16.5 %collective-permute-start.36 = (bf16[2,256,512]{2,1,0:T(8,128)(2,1)S(1)}, bf16[2,256,512]{2,1,0:T(8,128)(2,1)S(1)}, u32[]{:S(2)}, u32[]{:S(2)}) collective-permute-start(bf16[2,256,512]{2,1,0:T(8,128)(2,1)S(1)} %collective-permute-done.30.refs_1_), channel_id=1, source_target_pairs={{0,2},{2,0},{4,6},{6,4},{8,10},{10,8},{12,14},{14,12},{16,18},{18,... | collective-permute-start | bytes 1572872 | tf_op jit(solution)/shard_map/ppermute | solution.py:498
  345.7 23.9 %collective-permute-start.32 = (bf16[2,256,512]{2,1,0:T(8,128)(2,1)S(1)}, bf16[2,256,512]{2,1,0:T(8,128)(2,1)}, u32[]{:S(2)}, u32[]{:S(2)}) collective-permute-start(bf16[2,256,512]{2,1,0:T(8,128)(2,1)S(1)} %collective-permute-done.28.refs_0_), channel_id=1, source_target_pairs={{0,2},{2,0},{4,6},{6,4},{8,10},{10,8},{12,14},{14,12},{16,18},{18,... | collective-permute-start | bytes 1572872 | tf_op jit(solution)/shard_map/ppermute | solution.py:498
  354.1 15.0 %collective-permute-start.34 = (bf16[1,256,512]{2,1,0:T(8,128)(2,1)}, bf16[1,256,512]{2,1,0:T(8,128)(2,1)}, u32[]{:S(2)}, u32[]{:S(2)}) collective-permute-start(bf16[1,256,512]{2,1,0:T(8,128)(2,1)} %collective-permute-done.31.refs_2_), channel_id=1, source_target_pairs={{0,2},{2,0},{4,6},{6,4},{8,10},{10,8},{12,14},{14,12},{16,18},{18,... | collective-permute-start | bytes 786440 | tf_op jit(solution)/shard_map/ppermute | solution.py:498
  361.6 21.8 %collective-permute-start.52 = (bf16[2,256,512]{2,1,0:T(8,128)(2,1)}, bf16[2,256,512]{2,1,0:T(8,128)(2,1)S(1)}, u32[]{:S(2)}, u32[]{:S(2)}) collective-permute-start(bf16[2,256,512]{2,1,0:T(8,128)(2,1)} %collective-permute-done.50.refs_8_), channel_id=1, source_target_pairs={{0,2},{2,0},{4,6},{6,4},{8,10},{10,8},{12,14},{14,12},{16,18},{18,... | collective-permute-start | bytes 1572872 | tf_op jit(solution)/shard_map/ppermute | solution.py:498
  361.7 21.8 %collective-permute-start.53 = (bf16[2,256,512]{2,1,0:T(8,128)(2,1)S(1)}, bf16[2,256,512]{2,1,0:T(8,128)(2,1)S(1)}, u32[]{:S(2)}, u32[]{:S(2)}) collective-permute-start(bf16[2,256,512]{2,1,0:T(8,128)(2,1)S(1)} %collective-permute-done.51.refs_9_), channel_id=1, source_target_pairs={{0,2},{2,0},{4,6},{6,4},{8,10},{10,8},{12,14},{14,12},{16,18},{18,... | collective-permute-start | bytes 1572872 | tf_op jit(solution)/shard_map/ppermute | solution.py:498
  362.3 21.2 %collective-permute-start.57 = (bf16[2,256,512]{2,1,0:T(8,128)(2,1)S(1)}, bf16[2,256,512]{2,1,0:T(8,128)(2,1)}, u32[]{:S(2)}, u32[]{:S(2)}) collective-permute-start(bf16[2,256,512]{2,1,0:T(8,128)(2,1)S(1)} %collective-permute-done.54.refs_12_), channel_id=1, source_target_pairs={{0,2},{2,0},{4,6},{6,4},{8,10},{10,8},{12,14},{14,12},{16,18},{18,... | collective-permute-start | bytes 1572872 | tf_op jit(solution)/shard_map/ppermute | solution.py:498
  369.1 14.3 %collective-permute-start.58 = (bf16[1,256,512]{2,1,0:T(8,128)(2,1)}, bf16[1,256,512]{2,1,0:T(8,128)(2,1)S(1)}, u32[]{:S(2)}, u32[]{:S(2)}) collective-permute-start(bf16[1,256,512]{2,1,0:T(8,128)(2,1)} %collective-permute-done.55.refs_13_), channel_id=1, source_target_pairs={{0,2},{2,0},{4,6},{6,4},{8,10},{10,8},{12,14},{14,12},{16,18},{18,... | collective-permute-start | bytes 786440 | tf_op jit(solution)/shard_map/ppermute | solution.py:498
  (44 other events, 931.0 us)

commit v6 on v5

--- a/solution.py
+++ b/solution.py
@@ -509,9 +509,10 @@
     my_core = me % 2
     half = local_feats // 2
     own = lax.dynamic_slice_in_dim(raw_proj, my_core, 1, 0)
-    parts = [
-        lax.dynamic_slice(raw_proj, (my_core, i * half, 0), (1, half, rank)) for i in range(2)
-    ]
+    parts = (
+        lax.dynamic_slice(raw_proj, (my_core, 0, 0), (1, half, rank)),
+        lax.optimization_barrier(own)[:, half:],
+    )
     my_f = lax.axis_index("fsdp")
     gram = gram_of([own])
     pieces, offsets, early, fresh = [], [my_f * local_feats], [], []
@@ -550,10 +551,10 @@
         across = to_x(slots)
         owners = (slots, across, to_core(slots), to_core(across))
         groups = collect_moments(owners, places, quad_counts, depth, unit_rows)
-        total = groups[0]
+        held = groups[depth - 1]
         for k in range(1, depth):
-            total = total + to_z(groups[k], k)
-        return total
+            held = to_z(held) + groups[depth - 1 - k]
+        return held
 
     first_unit, second_unit = unit_moments(first_moment), unit_moments(second_moment)
     first_unit, second_unit = lax.optimization_barrier((first_unit, second_unit))

time: 394 us -> 377 us (0.957)
  starting transfers between devices: 91 us -> 29.9 us
  waiting for transfers between devices: 152 us -> 197 us
    ppermute x58, starting transfers between devices: 87.9 us -> 26.9 us  [permute(): return lax.ppermute(v, 'dp', [(i, target(i)) for i in range(replicas)])]
    ppermute x58, waiting for transfers between devices: 138 us -> 182 us  [permute(): return lax.ppermute(v, 'dp', [(i, target(i)) for i in range(replicas)])]
    unnamed x64 -> x78, local copies, waits for them, and re-layouts: 2.24 us -> 6.41 us
  transfers between devices with their start and end apart: 60 -> 60, of which waited for: 23 -> 24; matrix products, arithmetic and copies ran while one was open for 7% -> 7% of each run, Pallas kernels for 19% -> 19%
where the time goes in v6:
time: 377 us; the launch traced here: 376 us
  waiting for transfers between devices  197 us (52%)
  Pallas kernels  115 us (31%)
  starting transfers between devices  29.9 us (8%)
  other arithmetic  22.3 us (6%)
  local copies, waits for them, and re-layouts  10.2 us (3%)
    ppermute x58, waiting for transfers between devices, permute(): return lax.ppermute(v, 'dp', [(i, target(i)) for i in range(replicas)])  182 us
    pallas_call x4, Pallas kernels, expand(): pl.pallas_call(functools.partial(expand_kernel, parts=pieces), out_shape=...  27.5 us
    ppermute x58, starting transfers between devices, permute(): return lax.ppermute(v, 'dp', [(i, target(i)) for i in range(replicas)])  26.9 us
    pallas_call x4, Pallas kernels, project(): pl.pallas_call(project_kernel, out_shape=(out, out), grid_spec=pltpu.Pref...  26.7 us
    pallas_call x1, Pallas kernels, second_half(): pl.pallas_call(functools.partial(second_half_kernel, pieces=len(pieces)),...  17.4 us
    pallas_call x1, Pallas kernels, first_half(): pl.pallas_call(functools.partial(first_half_kernel, pieces=len(fresh)), o...  16.5 us
    ppermute x2, waiting for transfers between devices, shards(): lax.ppermute(parts[i], 'fsdp', [(j, (j + shift) % splits) for j in range(...  15.4 us
    pallas_call x2, Pallas kernels, collect_moments(): pl.pallas_call(collect_kernel, out_shape=(jax.ShapeDtypeStruct((mats, uni...  12 us
  transfers between devices with their start and end apart: 60, of which 24 were waited for; matrix products, arithmetic and copies ran while one was open for 7% of the time, Pallas kernels for 19%

profile of v6, /device:TPU:0, one launch (start us, length us, event | category | flops | bytes accessed | tf_op | source)
XLA Modules:
  0.0 376.1 jit_solution(5344288688613204425)
XLA Ops:
  3.1 3.0 collective-permute-start.12
  7.1 3.7 gram.2.refs_1_
  10.8 8.4 %collective-permute-done.12.refs_0_.refs_1_ = f32[1,256,512]{2,1,0:T(8,128)} collective-permute-done((f32[1,256,512]{2,1,0:T(8,128)}, f32[1,256,512]{2,1,0:T(8,128)}, u32[]{:S(2)}, u32[]{:S(2)}) %collective-permute-start.12) | collective-permute-done | bytes 524320 | tf_op jit(solution)/shard_map/ppermute | solution.py:522
  19.1 3.2 gram.3.refs_1_
  22.3 7.1 %collective-permute-done.13.refs_0_.refs_2_ = f32[1,256,512]{2,1,0:T(8,128)S(1)} collective-permute-done((f32[1,256,512]{2,1,0:T(8,128)S(1)}, f32[1,256,512]{2,1,0:T(8,128)S(1)}, u32[]{:S(2)}, u32[]{:S(2)}) %collective-permute-start.13) | collective-permute-done | bytes 524320 | tf_op jit(solution)/shard_map/ppermute | solution.py:522
  30.2 16.5 %first_half.1 = (f32[1,256,256]{2,1,0:T(8,128)}, f32[1,256,256]{2,1,0:T(8,128)}, f32[1,256,256]{2,1,0:T(8,128)}) custom-call(f32[1,256,512]{2,1,0:T(8,128)} %copy-done.38, f32[1,512,512]{2,1,0:T(8,128)} %gram.3.refs_1_), custom_call_target="tpu_custom_call" | custom-call | flops 20000000000 | bytes 1048576 | tf_op jit(solution)/shard_map/first_half/pallas_call | solution.py:214
  46.8 17.4 %second_half.1.own_basis.refs_4_.refs_6_ = bf16[1,1024,512]{2,1,0:T(8,128)(2,1)} custom-call(s32[3]{0:T(128)} %pad_add_fusion.5.offsets, f32[1,512,512]{2,1,0:T(8,128)} %copy-done.6, f32[1,256,512]{2,1,0:T(8,128)} %collective-permute-done.12.refs_0_.refs_1_, f32[1,256,512]{2,1,0:T(8,128)} %copy-done.38, f32[1,256,256]{2,1,0:T(8,128)} %get-tuple-element.37.refs_3_, ...), custom_call_target="tpu_custom_call" | custom-call | flops 20000000000 | bytes 3145728 | tf_op jit(solution)/shard_map/second_half/pallas_call | solution.py:236
  64.2 1.9 fusion.6.refs_0_
  66.1 1.8 collective-permute-start.6
  70.7 6.7 %project.7 = (bf16[2,2,256,512]{3,2,1,0:T(8,128)(2,1)}, bf16[2,2,256,512]{3,2,1,0:T(8,128)(2,1)}) custom-call(s32[4]{0:T(128)} %pad_add_fusion.3.quads, s32[2]{0:T(128)} %get-tuple-element.62.where, bf16[1,2,4096,1024]{3,2,1,0:T(8,128)(2,1)} %grads_ref.7, bf16[1,1024,512]{2,1,0:T(8,128)(2,1)} %second_half.1.own_basis.refs_4_.refs_6_, ...), custom_call_target="tpu_custom_call" | custom-call | flops 2147483648 | bytes 6291456 | tf_op jit(solution)/shard_map/project/pallas_call | solution.py:317
  78.3 13.9 %collective-permute-done.6.refs_1_ = bf16[2,32,16,512]{3,2,1,0:T(8,128)(2,1)} collective-permute-done((bf16[2,32,16,512]{3,2,1,0:T(8,128)(2,1)S(1)}, bf16[2,32,16,512]{3,2,1,0:T(8,128)(2,1)}, u32[]{:S(2)}, u32[]{:S(2)}) %collective-permute-start.6) | collective-permute-done | bytes 1048608 | tf_op jit(solution)/shard_map/ppermute | solution.py:498
  92.3 21.9 %collective-permute-done.refs_1_ = bf16[2,32,16,512]{3,2,1,0:T(8,128)(2,1)} collective-permute-done((bf16[2,32,16,512]{3,2,1,0:T(8,128)(2,1)S(1)}, bf16[2,32,16,512]{3,2,1,0:T(8,128)(2,1)}, u32[]{:S(2)}, u32[]{:S(2)}) %collective-permute-start) | collective-permute-done | bytes 1048608 | tf_op jit(solution)/shard_map/ppermute | solution.py:498
  114.1 6.5 %project.6 = (bf16[2,2,256,512]{3,2,1,0:T(8,128)(2,1)}, bf16[2,2,256,512]{3,2,1,0:T(8,128)(2,1)}) custom-call(s32[4]{0:T(128)} %pad_add_fusion.3.quads, s32[2]{0:T(128)} %get-tuple-element.61.where, bf16[1,2,4096,1024]{3,2,1,0:T(8,128)(2,1)} %grads_ref.7, bf16[1,1024,512]{2,1,0:T(8,128)(2,1)} %second_half.1.own_basis.refs_4_.refs_6_, ...), custom_call_target="tpu_custom_call" | custom-call | flops 2147483648 | bytes 6291456 | tf_op jit(solution)/shard_map/project/pallas_call | solution.py:317
  122.2 6.6 %project.5 = (bf16[2,2,256,512]{3,2,1,0:T(8,128)(2,1)}, bf16[2,2,256,512]{3,2,1,0:T(8,128)(2,1)}) custom-call(s32[4]{0:T(128)} %pad_add_fusion.3.quads, s32[2]{0:T(128)} %get-tuple-element.59.where, bf16[1,2,4096,1024]{3,2,1,0:T(8,128)(2,1)} %grads_ref.7, bf16[1,1024,512]{2,1,0:T(8,128)(2,1)} %second_half.1.own_basis.refs_4_.refs_6_, ...), custom_call_target="tpu_custom_call" | custom-call | flops 2147483648 | bytes 6291456 | tf_op jit(solution)/shard_map/project/pallas_call | solution.py:317
  128.7 2.1 fusion.17
  130.9 1.8 collective-permute-start.22
  134.2 6.0 %collect.3 = (bf16[2,256,512]{2,1,0:T(8,128)(2,1)}, bf16[2,256,512]{2,1,0:T(8,128)(2,1)}, bf16[2,256,512]{2,1,0:T(8,128)(2,1)}, bf16[2,256,512]{2,1,0:T(8,128)(2,1)}) custom-call(s32[4,2,32]{2,1,0:T(2,128)} %get-tuple-element.58.places, s32[4,2]{1,0:T(4,128)} %get-tuple-element.57.counts, bf16[2,32,16,512]{3,2,1,0:T(8,128)(2,1)} %copy-done.5, ...), custom_call_target="tpu_custom_call" | custom-call | bytes 8388608 | tf_op jit(solution)/shard_map/collect/pallas_call | solution.py:281
  141.2 2.3 collective-permute-start.9
  143.5 6.0 %collect.2 = (bf16[2,256,512]{2,1,0:T(8,128)(2,1)}, bf16[2,256,512]{2,1,0:T(8,128)(2,1)}, bf16[2,256,512]{2,1,0:T(8,128)(2,1)}, bf16[2,256,512]{2,1,0:T(8,128)(2,1)}) custom-call(s32[4,2,32]{2,1,0:T(2,128)} %get-tuple-element.58.places, s32[4,2]{1,0:T(4,128)} %get-tuple-element.57.counts, bf16[2,32,16,512]{3,2,1,0:T(8,128)(2,1)} %copy-done.4, ...), custom_call_target="tpu_custom_call" | custom-call | bytes 8388608 | tf_op jit(solution)/shard_map/collect/pallas_call | solution.py:281
  149.5 2.3 collective-permute-start.3
  151.8 2.0 fusion.16
  154.2 2.2 fusion.7
  157.7 6.9 %project.4 = (bf16[2,2,256,512]{3,2,1,0:T(8,128)(2,1)}, bf16[2,2,256,512]{3,2,1,0:T(8,128)(2,1)}) custom-call(s32[4]{0:T(128)} %pad_add_fusion.3.quads, s32[2]{0:T(128)} %get-tuple-element.60.where, bf16[1,2,4096,1024]{3,2,1,0:T(8,128)(2,1)} %grads_ref.7, bf16[1,1024,512]{2,1,0:T(8,128)(2,1)} %second_half.1.own_basis.refs_4_.refs_6_, ...), custom_call_target="tpu_custom_call" | custom-call | flops 2147483648 | bytes 6291456 | tf_op jit(solution)/shard_map/project/pallas_call | solution.py:317
  167.8 1.7 collective-permute-done.3
  172.8 7.9 %collective-permute-done.23 = bf16[2,256,512]{2,1,0:T(8,128)(2,1)} collective-permute-done((bf16[2,256,512]{2,1,0:T(8,128)(2,1)}, bf16[2,256,512]{2,1,0:T(8,128)(2,1)}, u32[]{:S(2)}, u32[]{:S(2)}) %collective-permute-start.23) | collective-permute-done | bytes 524320 | tf_op jit(solution)/shard_map/ppermute | solution.py:498
  180.7 1.6 fusion.9
  183.3 8.5 %collective-permute-done.10 = bf16[2,256,512]{2,1,0:T(8,128)(2,1)S(1)} collective-permute-done((bf16[2,256,512]{2,1,0:T(8,128)(2,1)S(1)}, bf16[2,256,512]{2,1,0:T(8,128)(2,1)S(1)}, u32[]{:S(2)}, u32[]{:S(2)}) %collective-permute-start.10) | collective-permute-done | bytes 524320 | tf_op jit(solution)/shard_map/ppermute | solution.py:498
  192.4 10.6 %collective-permute-done.4 = bf16[2,256,512]{2,1,0:T(8,128)(2,1)S(1)} collective-permute-done((bf16[2,256,512]{2,1,0:T(8,128)(2,1)S(1)}, bf16[2,256,512]{2,1,0:T(8,128)(2,1)S(1)}, u32[]{:S(2)}, u32[]{:S(2)}) %collective-permute-start.4) | collective-permute-done | bytes 524320 | tf_op jit(solution)/shard_map/ppermute | solution.py:498
  203.7 10.6 %collective-permute-done.24 = bf16[2,256,512]{2,1,0:T(8,128)(2,1)S(1)} collective-permute-done((bf16[2,256,512]{2,1,0:T(8,128)(2,1)S(1)}, bf16[2,256,512]{2,1,0:T(8,128)(2,1)S(1)}, u32[]{:S(2)}, u32[]{:S(2)}) %collective-permute-start.24) | collective-permute-done | bytes 524320 | tf_op jit(solution)/shard_map/ppermute | solution.py:498
  215.0 10.5 %collective-permute-done.11 = bf16[2,256,512]{2,1,0:T(8,128)(2,1)S(1)} collective-permute-done((bf16[2,256,512]{2,1,0:T(8,128)(2,1)S(1)}, bf16[2,256,512]{2,1,0:T(8,128)(2,1)S(1)}, u32[]{:S(2)}, u32[]{:S(2)}) %collective-permute-start.11) | collective-permute-done | bytes 524320 | tf_op jit(solution)/shard_map/ppermute | solution.py:498
  225.7 11.1 %collective-permute-done.5 = bf16[2,256,512]{2,1,0:T(8,128)(2,1)S(1)} collective-permute-done((bf16[2,256,512]{2,1,0:T(8,128)(2,1)S(1)}, bf16[2,256,512]{2,1,0:T(8,128)(2,1)S(1)}, u32[]{:S(2)}, u32[]{:S(2)}) %collective-permute-start.5) | collective-permute-done | bytes 524320 | tf_op jit(solution)/shard_map/ppermute | solution.py:498
  236.9 10.5 %collective-permute-done.25 = bf16[2,256,512]{2,1,0:T(8,128)(2,1)S(1)} collective-permute-done((bf16[2,256,512]{2,1,0:T(8,128)(2,1)S(1)}, bf16[2,256,512]{2,1,0:T(8,128)(2,1)S(1)}, u32[]{:S(2)}, u32[]{:S(2)}) %collective-permute-start.25) | collective-permute-done | bytes 524320 | tf_op jit(solution)/shard_map/ppermute | solution.py:498
  252.4 12.0 %collective-permute-done.46.refs_4_ = bf16[2,256,512]{2,1,0:T(8,128)(2,1)S(1)} collective-permute-done((bf16[2,256,512]{2,1,0:T(8,128)(2,1)S(1)}, bf16[2,256,512]{2,1,0:T(8,128)(2,1)S(1)}, u32[]{:S(2)}, u32[]{:S(2)}) %collective-permute-start.46) | collective-permute-done | bytes 524320 | tf_op jit(solution)/shard_map/ppermute | solution.py:498
  265.1 8.9 %collective-permute-done.40.refs_1_ = bf16[2,256,512]{2,1,0:T(8,128)(2,1)S(1)} collective-permute-done((bf16[2,256,512]{2,1,0:T(8,128)(2,1)S(1)}, bf16[2,256,512]{2,1,0:T(8,128)(2,1)S(1)}, u32[]{:S(2)}, u32[]{:S(2)}) %collective-permute-start.40) | collective-permute-done | bytes 524320 | tf_op jit(solution)/shard_map/ppermute | solution.py:498
  274.0 1.7 collective-permute-done.26.refs_0_
  275.8 11.1 %collective-permute-done.50.refs_8_ = bf16[2,256,512]{2,1,0:T(8,128)(2,1)} collective-permute-done((bf16[2,256,512]{2,1,0:T(8,128)(2,1)S(1)}, bf16[2,256,512]{2,1,0:T(8,128)(2,1)}, u32[]{:S(2)}, u32[]{:S(2)}) %collective-permute-start.50) | collective-permute-done | bytes 524320 | tf_op jit(solution)/shard_map/ppermute | solution.py:498
  287.5 10.7 %collective-permute-done.27.refs_0_ = bf16[2,256,512]{2,1,0:T(8,128)(2,1)} collective-permute-done((bf16[2,256,512]{2,1,0:T(8,128)(2,1)}, bf16[2,256,512]{2,1,0:T(8,128)(2,1)}, u32[]{:S(2)}, u32[]{:S(2)}) %collective-permute-start.27) | collective-permute-done | bytes 524320 | tf_op jit(solution)/shard_map/ppermute | solution.py:498
  299.5 2.6 collective-permute-done.37.refs_1_
  302.6 6.8 %collective-permute-done.54.refs_12_ = bf16[2,256,512]{2,1,0:T(8,128)(2,1)S(1)} collective-permute-done((bf16[2,256,512]{2,1,0:T(8,128)(2,1)}, bf16[2,256,512]{2,1,0:T(8,128)(2,1)S(1)}, u32[]{:S(2)}, u32[]{:S(2)}) %collective-permute-start.54) | collective-permute-done | bytes 524320 | tf_op jit(solution)/shard_map/ppermute | solution.py:498
  309.3 3.9 %collective-permute-done.30.refs_1_ = bf16[2,256,512]{2,1,0:T(8,128)(2,1)S(1)} collective-permute-done((bf16[2,256,512]{2,1,0:T(8,128)(2,1)}, bf16[2,256,512]{2,1,0:T(8,128)(2,1)S(1)}, u32[]{:S(2)}, u32[]{:S(2)}) %collective-permute-start.30) | collective-permute-done | bytes 524320 | tf_op jit(solution)/shard_map/ppermute | solution.py:498
  313.2 5.9 %collective-permute-done.28.refs_0_ = bf16[2,256,512]{2,1,0:T(8,128)(2,1)S(1)} collective-permute-done((bf16[2,256,512]{2,1,0:T(8,128)(2,1)}, bf16[2,256,512]{2,1,0:T(8,128)(2,1)S(1)}, u32[]{:S(2)}, u32[]{:S(2)}) %collective-permute-start.28) | collective-permute-done | bytes 524320 | tf_op jit(solution)/shard_map/ppermute | solution.py:498
  327.0 4.7 %collective-permute-done.55.refs_13_ = bf16[1,256,512]{2,1,0:T(8,128)(2,1)} collective-permute-done((bf16[1,256,512]{2,1,0:T(8,128)(2,1)}, bf16[1,256,512]{2,1,0:T(8,128)(2,1)}, u32[]{:S(2)}, u32[]{:S(2)}) %collective-permute-start.55) | collective-permute-done | bytes 262176 | tf_op jit(solution)/shard_map/ppermute | solution.py:498
  331.7 4.9 %collective-permute-done.29.refs_1_ = bf16[1,256,512]{2,1,0:T(8,128)(2,1)S(1)} collective-permute-done((bf16[1,256,512]{2,1,0:T(8,128)(2,1)}, bf16[1,256,512]{2,1,0:T(8,128)(2,1)S(1)}, u32[]{:S(2)}, u32[]{:S(2)}) %collective-permute-start.29) | collective-permute-done | bytes 262176 | tf_op jit(solution)/shard_map/ppermute | solution.py:498
  337.6 7.0 %expand.4.refs_6_ = bf16[2,4096,1024]{2,1,0:T(8,128)(2,1)} custom-call(s32[4]{0:T(128)} %pad_add_fusion.quads, s32[2]{0:T(128)} %pad_add_fusion.8.where, bf16[2,256,512]{2,1,0:T(8,128)(2,1)} %copy-done.8, bf16[2,256,512]{2,1,0:T(8,128)(2,1)} %copy-done.31, bf16[2,256,512]{2,1,0:T(8,128)(2,1)} %copy-done.32, bf16[2,256,512]{2,1,0:T(8,128)(2,1)} %copy-done.33, ...), custom_call_target="tpu_custom_call" | custom-call | flops 2147483648 | bytes 6291456 | tf_op jit(solution)/shard_map/expand/pallas_call | solution.py:383
  345.4 6.7 %expand.5.refs_6_ = bf16[2,4096,1024]{2,1,0:T(8,128)(2,1)} custom-call(s32[4]{0:T(128)} %pad_add_fusion.quads, s32[2]{0:T(128)} %get-tuple-element.62.where, bf16[2,256,512]{2,1,0:T(8,128)(2,1)} %collective-permute-done.26.refs_0_, bf16[2,256,512]{2,1,0:T(8,128)(2,1)} %collective-permute-done.37.refs_1_, ...), custom_call_target="tpu_custom_call", output_to_operand_aliasing={{}: (8, {})} | custom-call | flops 2147483648 | bytes 6291456 | tf_op jit(solution)/shard_map/expand/pallas_call | solution.py:383
  352.7 6.7 %expand.6.refs_8_ = bf16[2,4096,1024]{2,1,0:T(8,128)(2,1)} custom-call(s32[4]{0:T(128)} %pad_add_fusion.quads, s32[2]{0:T(128)} %get-tuple-element.61.where, bf16[2,256,512]{2,1,0:T(8,128)(2,1)} %collective-permute-done.27.refs_0_, bf16[2,256,512]{2,1,0:T(8,128)(2,1)} %copy-done.10, ...), custom_call_target="tpu_custom_call", output_to_operand_aliasing={{}: (8, {})} | custom-call | flops 2147483648 | bytes 6291456 | tf_op jit(solution)/shard_map/expand/pallas_call | solution.py:383
  359.5 7.0 %expand.7 = bf16[2,4096,1024]{2,1,0:T(8,128)(2,1)} custom-call(s32[4]{0:T(128)} %pad_add_fusion.quads, s32[2]{0:T(128)} %get-tuple-element.59.where, bf16[2,256,512]{2,1,0:T(8,128)(2,1)} %copy-done.9, bf16[1,256,512]{2,1,0:T(8,128)(2,1)} %copy-done.34, bf16[1,256,512]{2,1,0:T(8,128)(2,1)} %collective-permute-done.31.refs_2_, ...), custom_call_target="tpu_custom_call", output_to_operand_aliasing={{}: (10, {})} | custom-call | flops 2147483648 | bytes 6291456 | tf_op jit(solution)/shard_map/expand/pallas_call | solution.py:383
  367.7 8.2 %settle.1 = (f32[2,1,32,16,512]{4,3,2,1,0:T(8,128)}, f32[2,1,32,16,512]{4,3,2,1,0:T(8,128)}) custom-call(s32[2,32]{1,0:T(2,128)} %get-tuple-element.56.piece_of, s32[2,32]{1,0:T(2,128)} %get-tuple-element.55.row_of, s32[2,32]{1,0:T(2,128)} %fusion.29.held, bf16[2,256,512]{2,1,0:T(8,128)(2,1)} %copy-done.7, bf16[2,256,512]{2,1,0:T(8,128)(2,1)} %copy-done.20, ...), custom_call_target="tpu_custom_call" | custom-call | flops 4194304 | bytes 9437184 | tf_op jit(solution)/shard_map/settle/pallas_call | solution.py:452
  (204 shorter events, 42.9 us)
Async XLA Ops:
  3.1 16.1 %collective-permute-start.12 = (f32[1,256,512]{2,1,0:T(8,128)}, f32[1,256,512]{2,1,0:T(8,128)}, u32[]{:S(2)}, u32[]{:S(2)}) collective-permute-start(f32[1,256,512]{2,1,0:T(8,128)} %constant_dynamic-slice_fusion), channel_id=1, source_target_pairs={{0,1},{1,0},{2,3},{3,2},{4,5},{5,4},{6,7},{7,6},{8,9},{9,8},{10,11... | collective-permute-start | bytes 1572872 | tf_op jit(solution)/shard_map/ppermute | solution.py:522
  6.2 23.2 %collective-permute-start.13 = (f32[1,256,512]{2,1,0:T(8,128)S(1)}, f32[1,256,512]{2,1,0:T(8,128)S(1)}, u32[]{:S(2)}, u32[]{:S(2)}) collective-permute-start(f32[1,256,512]{2,1,0:T(8,128)S(1)} %slice.92), channel_id=1, source_target_pairs={{0,1},{1,0},{2,3},{3,2},{4,5},{5,4},{6,7},{7,6},{8,9},{9,8},{10,11... | collective-permute-start | bytes 1572872 | tf_op jit(solution)/shard_map/ppermute | solution.py:522
  66.1 26.2 %collective-permute-start.6 = (bf16[2,32,16,512]{3,2,1,0:T(8,128)(2,1)S(1)}, bf16[2,32,16,512]{3,2,1,0:T(8,128)(2,1)}, u32[]{:S(2)}, u32[]{:S(2)}) collective-permute-start(bf16[2,32,16,512]{3,2,1,0:T(8,128)(2,1)S(1)} %fusion.6.refs_0_), channel_id=1, source_target_pairs={{0,4},{2,6},{4,0},{6,2},{8,12},{10,14},{12,8},{14,10},{16,20},{18,... | collective-permute-start | bytes 3145736 | tf_op jit(solution)/shard_map/ppermute | solution.py:498
  68.0 46.1 %collective-permute-start = (bf16[2,32,16,512]{3,2,1,0:T(8,128)(2,1)S(1)}, bf16[2,32,16,512]{3,2,1,0:T(8,128)(2,1)}, u32[]{:S(2)}, u32[]{:S(2)}) collective-permute-start(bf16[2,32,16,512]{3,2,1,0:T(8,128)(2,1)S(1)} %fusion.5.refs_0_), channel_id=1, source_target_pairs={{0,4},{2,6},{4,0},{6,2},{8,12},{10,14},{12,8},{14,10},{16,20},{18,... | collective-permute-start | bytes 3145736 | tf_op jit(solution)/shard_map/ppermute | solution.py:498
  77.4 43.3 %collective-permute-start.21 = (bf16[2,2,256,512]{3,2,1,0:T(8,128)(2,1)}, bf16[2,2,256,512]{3,2,1,0:T(8,128)(2,1)}, u32[]{:S(2)}, u32[]{:S(2)}) collective-permute-start(bf16[2,2,256,512]{3,2,1,0:T(8,128)(2,1)} %get-tuple-element.47), channel_id=1, source_target_pairs={{0,2},{2,0},{4,6},{6,4},{8,10},{10,8},{12,14},{14,12},{16,18},{18,... | collective-permute-start | bytes 3145736 | tf_op jit(solution)/shard_map/ppermute | solution.py:498
  77.4 53.5 %collective-permute-start.7 = (bf16[2,32,16,512]{3,2,1,0:T(8,128)(2,1)S(1)}, bf16[2,32,16,512]{3,2,1,0:T(8,128)(2,1)}, u32[]{:S(2)}, u32[]{:S(2)}) collective-permute-start(bf16[2,32,16,512]{3,2,1,0:T(8,128)(2,1)S(1)} %fusion.6.refs_0_), channel_id=1, source_target_pairs={{0,2},{2,0},{4,6},{6,4},{8,10},{10,8},{12,14},{14,12},{16,18},{18,... | collective-permute-start | bytes 3145736 | tf_op jit(solution)/shard_map/ppermute | solution.py:498
  77.9 62.2 %collective-permute-start.1 = (bf16[2,32,16,512]{3,2,1,0:T(8,128)(2,1)S(1)}, bf16[2,32,16,512]{3,2,1,0:T(8,128)(2,1)S(1)}, u32[]{:S(2)}, u32[]{:S(2)}) collective-permute-start(bf16[2,32,16,512]{3,2,1,0:T(8,128)(2,1)S(1)} %fusion.5.refs_0_), channel_id=1, source_target_pairs={{0,2},{2,0},{4,6},{6,4},{8,10},{10,8},{12,14},{14,12},{16,18},{18,... | collective-permute-start | bytes 3145736 | tf_op jit(solution)/shard_map/ppermute | solution.py:498
  92.3 38.6 %collective-permute-start.8 = (bf16[2,32,16,512]{3,2,1,0:T(8,128)(2,1)}, bf16[2,32,16,512]{3,2,1,0:T(8,128)(2,1)}, u32[]{:S(2)}, u32[]{:S(2)}) collective-permute-start(bf16[2,32,16,512]{3,2,1,0:T(8,128)(2,1)} %collective-permute-done.6.refs_1_), channel_id=1, source_target_pairs={{0,2},{2,0},{4,6},{6,4},{8,10},{10,8},{12,14},{14,12},{16,18},{18,... | collective-permute-start | bytes 3145736 | tf_op jit(solution)/shard_map/ppermute | solution.py:498
  114.1 29.4 %collective-permute-start.2 = (bf16[2,32,16,512]{3,2,1,0:T(8,128)(2,1)}, bf16[2,32,16,512]{3,2,1,0:T(8,128)(2,1)}, u32[]{:S(2)}, u32[]{:S(2)}) collective-permute-start(bf16[2,32,16,512]{3,2,1,0:T(8,128)(2,1)} %collective-permute-done.refs_1_), channel_id=1, source_target_pairs={{0,2},{2,0},{4,6},{6,4},{8,10},{10,8},{12,14},{14,12},{16,18},{18,... | collective-permute-start | bytes 3145736 | tf_op jit(solution)/shard_map/ppermute | solution.py:498
  120.7 31.1 %collective-permute-start.19 = (bf16[2,2,256,512]{3,2,1,0:T(8,128)(2,1)}, bf16[2,2,256,512]{3,2,1,0:T(8,128)(2,1)}, u32[]{:S(2)}, u32[]{:S(2)}) collective-permute-start(bf16[2,2,256,512]{3,2,1,0:T(8,128)(2,1)} %get-tuple-element.45), channel_id=1, source_target_pairs={{0,2},{2,0},{4,6},{6,4},{8,10},{10,8},{12,14},{14,12},{16,18},{18,... | collective-permute-start | bytes 3145736 | tf_op jit(solution)/shard_map/ppermute | solution.py:498
  130.9 33.8 %collective-permute-start.17 = (bf16[2,2,256,512]{3,2,1,0:T(8,128)(2,1)}, bf16[2,2,256,512]{3,2,1,0:T(8,128)(2,1)S(1)}, u32[]{:S(2)}, u32[]{:S(2)}) collective-permute-start(bf16[2,2,256,512]{3,2,1,0:T(8,128)(2,1)} %get-tuple-element.43), channel_id=1, source_target_pairs={{0,2},{2,0},{4,6},{6,4},{8,10},{10,8},{12,14},{14,12},{16,18},{18,... | collective-permute-start | bytes 3145736 | tf_op jit(solution)/shard_map/ppermute | solution.py:498
  130.9 23.3 %collective-permute-start.22 = (bf16[2,256,512]{2,1,0:T(8,128)(2,1)}, bf16[2,256,512]{2,1,0:T(8,128)(2,1)}, u32[]{:S(2)}, u32[]{:S(2)}) collective-permute-start(bf16[2,256,512]{2,1,0:T(8,128)(2,1)} %fusion.17), channel_id=1, source_target_pairs={{0,4},{2,6},{4,0},{6,2},{8,12},{10,14},{12,8},{14,10},{16,20},{18,... | collective-permute-start | bytes 1572872 | tf_op jit(solution)/shard_map/ppermute | solution.py:498
  141.2 23.7 %collective-permute-start.9 = (bf16[2,256,512]{2,1,0:T(8,128)(2,1)}, bf16[2,256,512]{2,1,0:T(8,128)(2,1)}, u32[]{:S(2)}, u32[]{:S(2)}) collective-permute-start(bf16[2,256,512]{2,1,0:T(8,128)(2,1)} %get-tuple-element.32), channel_id=1, source_target_pairs={{0,8},{2,10},{4,12},{6,14},{8,16},{10,18},{12,20},{14,22},{16,24},... | collective-permute-start | bytes 1572872 | tf_op jit(solution)/shard_map/ppermute | solution.py:498
  149.5 19.9 %collective-permute-start.3 = (bf16[2,256,512]{2,1,0:T(8,128)(2,1)}, bf16[2,256,512]{2,1,0:T(8,128)(2,1)}, u32[]{:S(2)}, u32[]{:S(2)}) collective-permute-start(bf16[2,256,512]{2,1,0:T(8,128)(2,1)} %get-tuple-element.28), channel_id=1, source_target_pairs={{0,8},{2,10},{4,12},{6,14},{8,16},{10,18},{12,20},{14,22},{16,24},... | collective-permute-start | bytes 1572872 | tf_op jit(solution)/shard_map/ppermute | solution.py:498
  153.8 17.3 %collective-permute-start.20 = (bf16[2,256,512]{2,1,0:T(8,128)(2,1)}, bf16[2,256,512]{2,1,0:T(8,128)(2,1)}, u32[]{:S(2)}, u32[]{:S(2)}) collective-permute-start(bf16[2,256,512]{2,1,0:T(8,128)(2,1)} %fusion.16), channel_id=1, source_target_pairs={{0,4},{2,6},{4,0},{6,2},{8,12},{10,14},{12,8},{14,10},{16,20},{18,... | collective-permute-start | bytes 1572872 | tf_op jit(solution)/shard_map/ppermute | solution.py:498
  156.4 24.2 %collective-permute-start.23 = (bf16[2,256,512]{2,1,0:T(8,128)(2,1)}, bf16[2,256,512]{2,1,0:T(8,128)(2,1)}, u32[]{:S(2)}, u32[]{:S(2)}) collective-permute-start(bf16[2,256,512]{2,1,0:T(8,128)(2,1)} %fusion.7), channel_id=1, source_target_pairs={{0,8},{2,10},{4,12},{6,14},{8,16},{10,18},{12,20},{14,22},{16,24},... | collective-permute-start | bytes 1572872 | tf_op jit(solution)/shard_map/ppermute | solution.py:498
  164.7 18.1 %collective-permute-start.15 = (bf16[2,2,256,512]{3,2,1,0:T(8,128)(2,1)}, bf16[2,2,256,512]{3,2,1,0:T(8,128)(2,1)S(1)}, u32[]{:S(2)}, u32[]{:S(2)}) collective-permute-start(bf16[2,2,256,512]{3,2,1,0:T(8,128)(2,1)} %get-tuple-element.41), channel_id=1, source_target_pairs={{0,2},{2,0},{4,6},{6,4},{8,10},{10,8},{12,14},{14,12},{16,18},{18,... | collective-permute-start | bytes 3145736 | tf_op jit(solution)/shard_map/ppermute | solution.py:498
  164.9 38.8 %collective-permute-start.18 = (bf16[2,256,512]{2,1,0:T(8,128)(2,1)S(1)}, bf16[2,256,512]{2,1,0:T(8,128)(2,1)S(1)}, u32[]{:S(2)}, u32[]{:S(2)}) collective-permute-start(bf16[2,256,512]{2,1,0:T(8,128)(2,1)S(1)} %fusion.15), channel_id=1, source_target_pairs={{0,4},{2,6},{4,0},{6,2},{8,12},{10,14},{12,8},{14,10},{16,20},{18,... | collective-permute-start | bytes 1572872 | tf_op jit(solution)/shard_map/ppermute | solution.py:498
  169.4 22.4 %collective-permute-start.10 = (bf16[2,256,512]{2,1,0:T(8,128)(2,1)S(1)}, bf16[2,256,512]{2,1,0:T(8,128)(2,1)S(1)}, u32[]{:S(2)}, u32[]{:S(2)}) collective-permute-start(bf16[2,256,512]{2,1,0:T(8,128)(2,1)S(1)} %add.215), channel_id=1, source_target_pairs={{0,8},{2,10},{4,12},{6,14},{8,16},{10,18},{12,20},{14,22},{16,24},... | collective-permute-start | bytes 1572872 | tf_op jit(solution)/shard_map/ppermute | solution.py:498
  171.2 31.9 %collective-permute-start.4 = (bf16[2,256,512]{2,1,0:T(8,128)(2,1)S(1)}, bf16[2,256,512]{2,1,0:T(8,128)(2,1)S(1)}, u32[]{:S(2)}, u32[]{:S(2)}) collective-permute-start(bf16[2,256,512]{2,1,0:T(8,128)(2,1)S(1)} %add.212), channel_id=1, source_target_pairs={{0,8},{2,10},{4,12},{6,14},{8,16},{10,18},{12,20},{14,22},{16,24},... | collective-permute-start | bytes 1572872 | tf_op jit(solution)/shard_map/ppermute | solution.py:498
  182.3 32.0 %collective-permute-start.24 = (bf16[2,256,512]{2,1,0:T(8,128)(2,1)S(1)}, bf16[2,256,512]{2,1,0:T(8,128)(2,1)S(1)}, u32[]{:S(2)}, u32[]{:S(2)}) collective-permute-start(bf16[2,256,512]{2,1,0:T(8,128)(2,1)S(1)} %fusion.9), channel_id=1, source_target_pairs={{0,8},{2,10},{4,12},{6,14},{8,16},{10,18},{12,20},{14,22},{16,24},... | collective-permute-start | bytes 1572872 | tf_op jit(solution)/shard_map/ppermute | solution.py:498
  182.9 54.0 %collective-permute-start.16 = (bf16[2,256,512]{2,1,0:T(8,128)(2,1)S(1)}, bf16[2,256,512]{2,1,0:T(8,128)(2,1)S(1)}, u32[]{:S(2)}, u32[]{:S(2)}) collective-permute-start(bf16[2,256,512]{2,1,0:T(8,128)(2,1)S(1)} %fusion.14), channel_id=1, source_target_pairs={{0,4},{2,6},{4,0},{6,2},{8,12},{10,14},{12,8},{14,10},{16,20},{18,... | collective-permute-start | bytes 1572872 | tf_op jit(solution)/shard_map/ppermute | solution.py:498
  192.0 33.6 %collective-permute-start.11 = (bf16[2,256,512]{2,1,0:T(8,128)(2,1)S(1)}, bf16[2,256,512]{2,1,0:T(8,128)(2,1)S(1)}, u32[]{:S(2)}, u32[]{:S(2)}) collective-permute-start(bf16[2,256,512]{2,1,0:T(8,128)(2,1)S(1)} %add.216), channel_id=1, source_target_pairs={{0,8},{2,10},{4,12},{6,14},{8,16},{10,18},{12,20},{14,22},{16,24},... | collective-permute-start | bytes 1572872 | tf_op jit(solution)/shard_map/ppermute | solution.py:498
  203.2 33.6 %collective-permute-start.5 = (bf16[2,256,512]{2,1,0:T(8,128)(2,1)S(1)}, bf16[2,256,512]{2,1,0:T(8,128)(2,1)S(1)}, u32[]{:S(2)}, u32[]{:S(2)}) collective-permute-start(bf16[2,256,512]{2,1,0:T(8,128)(2,1)S(1)} %add.213), channel_id=1, source_target_pairs={{0,8},{2,10},{4,12},{6,14},{8,16},{10,18},{12,20},{14,22},{16,24},... | collective-permute-start | bytes 1572872 | tf_op jit(solution)/shard_map/ppermute | solution.py:498
  214.6 32.8 %collective-permute-start.25 = (bf16[2,256,512]{2,1,0:T(8,128)(2,1)S(1)}, bf16[2,256,512]{2,1,0:T(8,128)(2,1)S(1)}, u32[]{:S(2)}, u32[]{:S(2)}) collective-permute-start(bf16[2,256,512]{2,1,0:T(8,128)(2,1)S(1)} %fusion.11), channel_id=1, source_target_pairs={{0,8},{2,10},{4,12},{6,14},{8,16},{10,18},{12,20},{14,22},{16,24},... | collective-permute-start | bytes 1572872 | tf_op jit(solution)/shard_map/ppermute | solution.py:498
  247.7 16.6 %collective-permute-start.46 = (bf16[2,256,512]{2,1,0:T(8,128)(2,1)S(1)}, bf16[2,256,512]{2,1,0:T(8,128)(2,1)S(1)}, u32[]{:S(2)}, u32[]{:S(2)}) collective-permute-start(bf16[2,256,512]{2,1,0:T(8,128)(2,1)S(1)} %get-tuple-element.50.refs_0_), channel_id=1, source_target_pairs={{0,8},{2,10},{4,12},{6,14},{8,16},{10,18},{12,20},{14,22},{16,24},... | collective-permute-start | bytes 1572872 | tf_op jit(solution)/shard_map/ppermute | solution.py:498
  247.9 16.4 %collective-permute-start.43 = (bf16[2,256,512]{2,1,0:T(8,128)(2,1)S(1)}, bf16[2,256,512]{2,1,0:T(8,128)(2,1)S(1)}, u32[]{:S(2)}, u32[]{:S(2)}) collective-permute-start(bf16[2,256,512]{2,1,0:T(8,128)(2,1)S(1)} %get-tuple-element.50.refs_0_), channel_id=1, source_target_pairs={{0,4},{2,6},{4,0},{6,2},{8,12},{10,14},{12,8},{14,10},{16,20},{18,... | collective-permute-start | bytes 1572872 | tf_op jit(solution)/shard_map/ppermute | solution.py:498
  248.5 16.0 %collective-permute-start.44 = (bf16[2,256,512]{2,1,0:T(8,128)(2,1)S(1)}, bf16[2,256,512]{2,1,0:T(8,128)(2,1)S(1)}, u32[]{:S(2)}, u32[]{:S(2)}) collective-permute-start(bf16[2,256,512]{2,1,0:T(8,128)(2,1)S(1)} %get-tuple-element.50.refs_0_), channel_id=1, source_target_pairs={{0,2},{2,0},{4,6},{6,4},{8,10},{10,8},{12,14},{14,12},{16,18},{18,... | collective-permute-start | bytes 1572872 | tf_op jit(solution)/shard_map/ppermute | solution.py:498
  249.3 24.7 %collective-permute-start.40 = (bf16[2,256,512]{2,1,0:T(8,128)(2,1)S(1)}, bf16[2,256,512]{2,1,0:T(8,128)(2,1)S(1)}, u32[]{:S(2)}, u32[]{:S(2)}) collective-permute-start(bf16[2,256,512]{2,1,0:T(8,128)(2,1)S(1)} %fusion.13.refs_0_), channel_id=1, source_target_pairs={{0,4},{2,6},{4,0},{6,2},{8,12},{10,14},{12,8},{14,10},{16,20},{18,... | collective-permute-start | bytes 1572872 | tf_op jit(solution)/shard_map/ppermute | solution.py:498
  250.8 24.9 %collective-permute-start.26 = (bf16[2,256,512]{2,1,0:T(8,128)(2,1)S(1)}, bf16[2,256,512]{2,1,0:T(8,128)(2,1)}, u32[]{:S(2)}, u32[]{:S(2)}) collective-permute-start(bf16[2,256,512]{2,1,0:T(8,128)(2,1)S(1)} %fusion.13.refs_0_), channel_id=1, source_target_pairs={{0,8},{2,10},{4,12},{6,14},{8,16},{10,18},{12,20},{14,22},{16,24},... | collective-permute-start | bytes 1572872 | tf_op jit(solution)/shard_map/ppermute | solution.py:498
  264.4 22.6 %collective-permute-start.50 = (bf16[2,256,512]{2,1,0:T(8,128)(2,1)S(1)}, bf16[2,256,512]{2,1,0:T(8,128)(2,1)}, u32[]{:S(2)}, u32[]{:S(2)}) collective-permute-start(bf16[2,256,512]{2,1,0:T(8,128)(2,1)S(1)} %collective-permute-done.46.refs_4_), channel_id=1, source_target_pairs={{0,8},{2,10},{4,12},{6,14},{8,16},{10,18},{12,20},{14,22},{16,24},... | collective-permute-start | bytes 1572872 | tf_op jit(solution)/shard_map/ppermute | solution.py:498
  264.5 22.5 %collective-permute-start.47 = (bf16[2,256,512]{2,1,0:T(8,128)(2,1)S(1)}, bf16[2,256,512]{2,1,0:T(8,128)(2,1)}, u32[]{:S(2)}, u32[]{:S(2)}) collective-permute-start(bf16[2,256,512]{2,1,0:T(8,128)(2,1)S(1)} %collective-permute-done.46.refs_4_), channel_id=1, source_target_pairs={{0,4},{2,6},{4,0},{6,2},{8,12},{10,14},{12,8},{14,10},{16,20},{18,... | collective-permute-start | bytes 1572872 | tf_op jit(solution)/shard_map/ppermute | solution.py:498
  275.7 22.5 %collective-permute-start.27 = (bf16[2,256,512]{2,1,0:T(8,128)(2,1)}, bf16[2,256,512]{2,1,0:T(8,128)(2,1)}, u32[]{:S(2)}, u32[]{:S(2)}) collective-permute-start(bf16[2,256,512]{2,1,0:T(8,128)(2,1)} %collective-permute-done.26.refs_0_), channel_id=1, source_target_pairs={{0,8},{2,10},{4,12},{6,14},{8,16},{10,18},{12,20},{14,22},{16,24},... | collective-permute-start | bytes 1572872 | tf_op jit(solution)/shard_map/ppermute | solution.py:498
  275.7 23.0 %collective-permute-start.48 = (bf16[2,256,512]{2,1,0:T(8,128)(2,1)S(1)}, bf16[2,256,512]{2,1,0:T(8,128)(2,1)S(1)}, u32[]{:S(2)}, u32[]{:S(2)}) collective-permute-start(bf16[2,256,512]{2,1,0:T(8,128)(2,1)S(1)} %collective-permute-done.46.refs_4_), channel_id=1, source_target_pairs={{0,2},{2,0},{4,6},{6,4},{8,10},{10,8},{12,14},{14,12},{16,18},{18,... | collective-permute-start | bytes 1572872 | tf_op jit(solution)/shard_map/ppermute | solution.py:498
  287.0 15.1 %collective-permute-start.37 = (bf16[2,256,512]{2,1,0:T(8,128)(2,1)}, bf16[2,256,512]{2,1,0:T(8,128)(2,1)}, u32[]{:S(2)}, u32[]{:S(2)}) collective-permute-start(bf16[2,256,512]{2,1,0:T(8,128)(2,1)} %collective-permute-done.26.refs_0_), channel_id=1, source_target_pairs={{0,4},{2,6},{4,0},{6,2},{8,12},{10,14},{12,8},{14,10},{16,20},{18,... | collective-permute-start | bytes 1572872 | tf_op jit(solution)/shard_map/ppermute | solution.py:498
  287.5 21.9 %collective-permute-start.54 = (bf16[2,256,512]{2,1,0:T(8,128)(2,1)}, bf16[2,256,512]{2,1,0:T(8,128)(2,1)S(1)}, u32[]{:S(2)}, u32[]{:S(2)}) collective-permute-start(bf16[2,256,512]{2,1,0:T(8,128)(2,1)} %collective-permute-done.50.refs_8_), channel_id=1, source_target_pairs={{0,8},{2,10},{4,12},{6,14},{8,16},{10,18},{12,20},{14,22},{16,24},... | collective-permute-start | bytes 1572872 | tf_op jit(solution)/shard_map/ppermute | solution.py:498
  298.2 15.0 %collective-permute-start.30 = (bf16[2,256,512]{2,1,0:T(8,128)(2,1)}, bf16[2,256,512]{2,1,0:T(8,128)(2,1)S(1)}, u32[]{:S(2)}, u32[]{:S(2)}) collective-permute-start(bf16[2,256,512]{2,1,0:T(8,128)(2,1)} %collective-permute-done.27.refs_0_), channel_id=1, source_target_pairs={{0,4},{2,6},{4,0},{6,2},{8,12},{10,14},{12,8},{14,10},{16,20},{18,... | collective-permute-start | bytes 1572872 | tf_op jit(solution)/shard_map/ppermute | solution.py:498
  298.7 20.4 %collective-permute-start.28 = (bf16[2,256,512]{2,1,0:T(8,128)(2,1)}, bf16[2,256,512]{2,1,0:T(8,128)(2,1)S(1)}, u32[]{:S(2)}, u32[]{:S(2)}) collective-permute-start(bf16[2,256,512]{2,1,0:T(8,128)(2,1)} %collective-permute-done.27.refs_0_), channel_id=1, source_target_pairs={{0,8},{2,10},{4,12},{6,14},{8,16},{10,18},{12,20},{14,22},{16,24},... | collective-permute-start | bytes 1572872 | tf_op jit(solution)/shard_map/ppermute | solution.py:498
  298.8 23.4 %collective-permute-start.38 = (bf16[2,256,512]{2,1,0:T(8,128)(2,1)}, bf16[2,256,512]{2,1,0:T(8,128)(2,1)}, u32[]{:S(2)}, u32[]{:S(2)}) collective-permute-start(bf16[2,256,512]{2,1,0:T(8,128)(2,1)} %collective-permute-done.26.refs_0_), channel_id=1, source_target_pairs={{0,2},{2,0},{4,6},{6,4},{8,10},{10,8},{12,14},{14,12},{16,18},{18,... | collective-permute-start | bytes 1572872 | tf_op jit(solution)/shard_map/ppermute | solution.py:498
  302.1 21.9 %collective-permute-start.51 = (bf16[2,256,512]{2,1,0:T(8,128)(2,1)}, bf16[2,256,512]{2,1,0:T(8,128)(2,1)S(1)}, u32[]{:S(2)}, u32[]{:S(2)}) collective-permute-start(bf16[2,256,512]{2,1,0:T(8,128)(2,1)} %collective-permute-done.50.refs_8_), channel_id=1, source_target_pairs={{0,4},{2,6},{4,0},{6,2},{8,12},{10,14},{12,8},{14,10},{16,20},{18,... | collective-permute-start | bytes 1572872 | tf_op jit(solution)/shard_map/ppermute | solution.py:498
  309.3 15.2 %collective-permute-start.49 = (bf16[2,256,512]{2,1,0:T(8,128)(2,1)}, bf16[2,256,512]{2,1,0:T(8,128)(2,1)}, u32[]{:S(2)}, u32[]{:S(2)}) collective-permute-start(bf16[2,256,512]{2,1,0:T(8,128)(2,1)} %collective-permute-done.47.refs_5_), channel_id=1, source_target_pairs={{0,2},{2,0},{4,6},{6,4},{8,10},{10,8},{12,14},{14,12},{16,18},{18,... | collective-permute-start | bytes 1572872 | tf_op jit(solution)/shard_map/ppermute | solution.py:498
  324.5 20.3 %collective-permute-start.36 = (bf16[2,256,512]{2,1,0:T(8,128)(2,1)S(1)}, bf16[2,256,512]{2,1,0:T(8,128)(2,1)S(1)}, u32[]{:S(2)}, u32[]{:S(2)}) collective-permute-start(bf16[2,256,512]{2,1,0:T(8,128)(2,1)S(1)} %collective-permute-done.30.refs_1_), channel_id=1, source_target_pairs={{0,2},{2,0},{4,6},{6,4},{8,10},{10,8},{12,14},{14,12},{16,18},{18,... | collective-permute-start | bytes 1572872 | tf_op jit(solution)/shard_map/ppermute | solution.py:498
  325.2 27.5 %collective-permute-start.32 = (bf16[2,256,512]{2,1,0:T(8,128)(2,1)S(1)}, bf16[2,256,512]{2,1,0:T(8,128)(2,1)}, u32[]{:S(2)}, u32[]{:S(2)}) collective-permute-start(bf16[2,256,512]{2,1,0:T(8,128)(2,1)S(1)} %collective-permute-done.28.refs_0_), channel_id=1, source_target_pairs={{0,2},{2,0},{4,6},{6,4},{8,10},{10,8},{12,14},{14,12},{16,18},{18,... | collective-permute-start | bytes 1572872 | tf_op jit(solution)/shard_map/ppermute | solution.py:498
  337.1 15.0 %collective-permute-start.34 = (bf16[1,256,512]{2,1,0:T(8,128)(2,1)}, bf16[1,256,512]{2,1,0:T(8,128)(2,1)}, u32[]{:S(2)}, u32[]{:S(2)}) collective-permute-start(bf16[1,256,512]{2,1,0:T(8,128)(2,1)} %collective-permute-done.31.refs_2_), channel_id=1, source_target_pairs={{0,2},{2,0},{4,6},{6,4},{8,10},{10,8},{12,14},{14,12},{16,18},{18,... | collective-permute-start | bytes 786440 | tf_op jit(solution)/shard_map/ppermute | solution.py:498
  344.7 21.8 %collective-permute-start.52 = (bf16[2,256,512]{2,1,0:T(8,128)(2,1)}, bf16[2,256,512]{2,1,0:T(8,128)(2,1)S(1)}, u32[]{:S(2)}, u32[]{:S(2)}) collective-permute-start(bf16[2,256,512]{2,1,0:T(8,128)(2,1)} %collective-permute-done.50.refs_8_), channel_id=1, source_target_pairs={{0,2},{2,0},{4,6},{6,4},{8,10},{10,8},{12,14},{14,12},{16,18},{18,... | collective-permute-start | bytes 1572872 | tf_op jit(solution)/shard_map/ppermute | solution.py:498
  344.8 21.8 %collective-permute-start.53 = (bf16[2,256,512]{2,1,0:T(8,128)(2,1)S(1)}, bf16[2,256,512]{2,1,0:T(8,128)(2,1)S(1)}, u32[]{:S(2)}, u32[]{:S(2)}) collective-permute-start(bf16[2,256,512]{2,1,0:T(8,128)(2,1)S(1)} %collective-permute-done.51.refs_9_), channel_id=1, source_target_pairs={{0,2},{2,0},{4,6},{6,4},{8,10},{10,8},{12,14},{14,12},{16,18},{18,... | collective-permute-start | bytes 1572872 | tf_op jit(solution)/shard_map/ppermute | solution.py:498
  345.3 21.2 %collective-permute-start.57 = (bf16[2,256,512]{2,1,0:T(8,128)(2,1)S(1)}, bf16[2,256,512]{2,1,0:T(8,128)(2,1)}, u32[]{:S(2)}, u32[]{:S(2)}) collective-permute-start(bf16[2,256,512]{2,1,0:T(8,128)(2,1)S(1)} %collective-permute-done.54.refs_12_), channel_id=1, source_target_pairs={{0,2},{2,0},{4,6},{6,4},{8,10},{10,8},{12,14},{14,12},{16,18},{18,... | collective-permute-start | bytes 1572872 | tf_op jit(solution)/shard_map/ppermute | solution.py:498
  352.2 14.3 %collective-permute-start.58 = (bf16[1,256,512]{2,1,0:T(8,128)(2,1)}, bf16[1,256,512]{2,1,0:T(8,128)(2,1)S(1)}, u32[]{:S(2)}, u32[]{:S(2)}) collective-permute-start(bf16[1,256,512]{2,1,0:T(8,128)(2,1)} %collective-permute-done.55.refs_13_), channel_id=1, source_target_pairs={{0,2},{2,0},{4,6},{6,4},{8,10},{10,8},{12,14},{14,12},{16,18},{18,... | collective-permute-start | bytes 786440 | tf_op jit(solution)/shard_map/ppermute | solution.py:498
  (51 other events, 871.5 us)

commit v7 on v6

--- a/solution.py
+++ b/solution.py
@@ -551,10 +551,10 @@
         across = to_x(slots)
         owners = (slots, across, to_core(slots), to_core(across))
         groups = collect_moments(owners, places, quad_counts, depth, unit_rows)
-        held = groups[depth - 1]
+        total = groups[0]
         for k in range(1, depth):
-            held = to_z(held) + groups[depth - 1 - k]
-        return held
+            total = total + to_z(groups[k], k)
+        return total
 
     first_unit, second_unit = unit_moments(first_moment), unit_moments(second_moment)
     first_unit, second_unit = lax.optimization_barrier((first_unit, second_unit))

time: 377 us -> 396 us (1.050)
  starting transfers between devices: 29.9 us -> 90.7 us
  waiting for transfers between devices: 197 us -> 153 us
  other arithmetic: 22.3 us -> 26.6 us
    ppermute x58, starting transfers between devices: 26.9 us -> 87.6 us  [permute(): return lax.ppermute(v, 'dp', [(i, target(i)) for i in range(replicas)])]
    ppermute x58, waiting for transfers between devices: 182 us -> 138 us  [permute(): return lax.ppermute(v, 'dp', [(i, target(i)) for i in range(replicas)])]
  transfers between devices with their start and end apart: 60 -> 60, of which waited for: 24 -> 23; matrix products, arithmetic and copies ran while one was open for 7% -> 7% of each run, Pallas kernels for 19% -> 18%
where the time goes in v7:
time: 396 us; the launch traced here: 395 us
  waiting for transfers between devices  153 us (39%)
  Pallas kernels  115 us (29%)
  starting transfers between devices  90.7 us (23%)
  other arithmetic  26.6 us (7%)
  local copies, waits for them, and re-layouts  8.47 us (2%)
    ppermute x58, waiting for transfers between devices, permute(): return lax.ppermute(v, 'dp', [(i, target(i)) for i in range(replicas)])  138 us
    ppermute x58, starting transfers between devices, permute(): return lax.ppermute(v, 'dp', [(i, target(i)) for i in range(replicas)])  87.6 us
    pallas_call x4, Pallas kernels, expand(): pl.pallas_call(functools.partial(expand_kernel, parts=pieces), out_shape=...  27.5 us
    pallas_call x4, Pallas kernels, project(): pl.pallas_call(project_kernel, out_shape=(out, out), grid_spec=pltpu.Pref...  26.5 us
    pallas_call x1, Pallas kernels, second_half(): pl.pallas_call(functools.partial(second_half_kernel, pieces=len(pieces)),...  17.4 us
    pallas_call x1, Pallas kernels, first_half(): pl.pallas_call(functools.partial(first_half_kernel, pieces=len(fresh)), o...  16.5 us
    ppermute x2, waiting for transfers between devices, shards(): lax.ppermute(parts[i], 'fsdp', [(j, (j + shift) % splits) for j in range(...  15.4 us
    pallas_call x2, Pallas kernels, collect_moments(): pl.pallas_call(collect_kernel, out_shape=(jax.ShapeDtypeStruct((mats, uni...  12.1 us
  transfers between devices with their start and end apart: 60, of which 23 were waited for; matrix products, arithmetic and copies ran while one was open for 7% of the time, Pallas kernels for 18%

profile of v7, /device:TPU:0, one launch (start us, length us, event | category | flops | bytes accessed | tf_op | source)
XLA Modules:
  0.0 395.2 jit_solution(8049158900349044413)
XLA Ops:
  3.1 3.0 collective-permute-start.12
  7.1 3.7 gram.2.refs_1_
  10.8 8.4 %collective-permute-done.12.refs_0_.refs_1_ = f32[1,256,512]{2,1,0:T(8,128)} collective-permute-done((f32[1,256,512]{2,1,0:T(8,128)}, f32[1,256,512]{2,1,0:T(8,128)}, u32[]{:S(2)}, u32[]{:S(2)}) %collective-permute-start.12) | collective-permute-done | bytes 524320 | tf_op jit(solution)/shard_map/ppermute | solution.py:522
  19.1 3.2 gram.3.refs_1_
  22.3 7.1 %collective-permute-done.13.refs_0_.refs_2_ = f32[1,256,512]{2,1,0:T(8,128)S(1)} collective-permute-done((f32[1,256,512]{2,1,0:T(8,128)S(1)}, f32[1,256,512]{2,1,0:T(8,128)S(1)}, u32[]{:S(2)}, u32[]{:S(2)}) %collective-permute-start.13) | collective-permute-done | bytes 524320 | tf_op jit(solution)/shard_map/ppermute | solution.py:522
  30.2 16.5 %first_half.1 = (f32[1,256,256]{2,1,0:T(8,128)}, f32[1,256,256]{2,1,0:T(8,128)}, f32[1,256,256]{2,1,0:T(8,128)}) custom-call(f32[1,256,512]{2,1,0:T(8,128)} %copy-done.35, f32[1,512,512]{2,1,0:T(8,128)} %gram.3.refs_1_), custom_call_target="tpu_custom_call" | custom-call | flops 20000000000 | bytes 1048576 | tf_op jit(solution)/shard_map/first_half/pallas_call | solution.py:214
  46.8 17.4 %second_half.1.own_basis.refs_4_.refs_6_ = bf16[1,1024,512]{2,1,0:T(8,128)(2,1)} custom-call(s32[3]{0:T(128)} %pad_add_fusion.5.offsets, f32[1,512,512]{2,1,0:T(8,128)} %copy-done.6, f32[1,256,512]{2,1,0:T(8,128)} %collective-permute-done.12.refs_0_.refs_1_, f32[1,256,512]{2,1,0:T(8,128)} %copy-done.35, f32[1,256,256]{2,1,0:T(8,128)} %get-tuple-element.37.refs_3_, ...), custom_call_target="tpu_custom_call" | custom-call | flops 20000000000 | bytes 3145728 | tf_op jit(solution)/shard_map/second_half/pallas_call | solution.py:236
  64.1 1.9 fusion.6.refs_0_
  70.8 6.6 %project.7 = (bf16[2,2,256,512]{3,2,1,0:T(8,128)(2,1)}, bf16[2,2,256,512]{3,2,1,0:T(8,128)(2,1)}) custom-call(s32[4]{0:T(128)} %pad_add_fusion.3.quads, s32[2]{0:T(128)} %get-tuple-element.62.where, bf16[1,2,4096,1024]{3,2,1,0:T(8,128)(2,1)} %grads_ref.7, bf16[1,1024,512]{2,1,0:T(8,128)(2,1)} %second_half.1.own_basis.refs_4_.refs_6_, ...), custom_call_target="tpu_custom_call" | custom-call | flops 2147483648 | bytes 6291456 | tf_op jit(solution)/shard_map/project/pallas_call | solution.py:317
  77.7 6.7 %project.6 = (bf16[2,2,256,512]{3,2,1,0:T(8,128)(2,1)}, bf16[2,2,256,512]{3,2,1,0:T(8,128)(2,1)}) custom-call(s32[4]{0:T(128)} %pad_add_fusion.3.quads, s32[2]{0:T(128)} %get-tuple-element.61.where, bf16[1,2,4096,1024]{3,2,1,0:T(8,128)(2,1)} %grads_ref.7, bf16[1,1024,512]{2,1,0:T(8,128)(2,1)} %second_half.1.own_basis.refs_4_.refs_6_, ...), custom_call_target="tpu_custom_call" | custom-call | flops 2147483648 | bytes 6291456 | tf_op jit(solution)/shard_map/project/pallas_call | solution.py:317
  85.7 6.6 %collective-permute-done.6.refs_1_ = bf16[2,32,16,512]{3,2,1,0:T(8,128)(2,1)} collective-permute-done((bf16[2,32,16,512]{3,2,1,0:T(8,128)(2,1)S(1)}, bf16[2,32,16,512]{3,2,1,0:T(8,128)(2,1)}, u32[]{:S(2)}, u32[]{:S(2)}) %collective-permute-start.6) | collective-permute-done | bytes 1048608 | tf_op jit(solution)/shard_map/ppermute | solution.py:498
  92.3 6.5 %project.5 = (bf16[2,2,256,512]{3,2,1,0:T(8,128)(2,1)}, bf16[2,2,256,512]{3,2,1,0:T(8,128)(2,1)}) custom-call(s32[4]{0:T(128)} %pad_add_fusion.3.quads, s32[2]{0:T(128)} %get-tuple-element.59.where, bf16[1,2,4096,1024]{3,2,1,0:T(8,128)(2,1)} %grads_ref.7, bf16[1,1024,512]{2,1,0:T(8,128)(2,1)} %second_half.1.own_basis.refs_4_.refs_6_, ...), custom_call_target="tpu_custom_call" | custom-call | flops 2147483648 | bytes 6291456 | tf_op jit(solution)/shard_map/project/pallas_call | solution.py:317
  99.4 2.1 fusion.17
  103.5 6.7 %project.4 = (bf16[2,2,256,512]{3,2,1,0:T(8,128)(2,1)}, bf16[2,2,256,512]{3,2,1,0:T(8,128)(2,1)}) custom-call(s32[4]{0:T(128)} %pad_add_fusion.3.quads, s32[2]{0:T(128)} %get-tuple-element.60.where, bf16[1,2,4096,1024]{3,2,1,0:T(8,128)(2,1)} %grads_ref.7, bf16[1,1024,512]{2,1,0:T(8,128)(2,1)} %second_half.1.own_basis.refs_4_.refs_6_, ...), custom_call_target="tpu_custom_call" | custom-call | flops 2147483648 | bytes 6291456 | tf_op jit(solution)/shard_map/project/pallas_call | solution.py:317
  110.2 2.0 fusion.16
  112.1 2.6 collective-permute-done.refs_1_
  114.7 10.6 %collective-permute-done.22 = bf16[2,256,512]{2,1,0:T(8,128)(2,1)} collective-permute-done((bf16[2,256,512]{2,1,0:T(8,128)(2,1)}, bf16[2,256,512]{2,1,0:T(8,128)(2,1)}, u32[]{:S(2)}, u32[]{:S(2)}) %collective-permute-start.22) | collective-permute-done | bytes 524320 | tf_op jit(solution)/shard_map/ppermute | solution.py:498
  125.4 2.4 fusion.7
  133.0 6.1 %collect.3 = (bf16[2,256,512]{2,1,0:T(8,128)(2,1)}, bf16[2,256,512]{2,1,0:T(8,128)(2,1)}, bf16[2,256,512]{2,1,0:T(8,128)(2,1)}, bf16[2,256,512]{2,1,0:T(8,128)(2,1)}) custom-call(s32[4,2,32]{2,1,0:T(2,128)} %get-tuple-element.58.places, s32[4,2]{1,0:T(4,128)} %get-tuple-element.57.counts, bf16[2,32,16,512]{3,2,1,0:T(8,128)(2,1)} %copy-done.5, ...), custom_call_target="tpu_custom_call" | custom-call | bytes 8388608 | tf_op jit(solution)/shard_map/collect/pallas_call | solution.py:281
  139.2 2.1 fusion.15
  142.5 2.8 collective-permute-start.10
  146.8 2.3 fusion.9
  150.6 2.2 collective-permute-start.11
  152.9 6.0 %collect.2 = (bf16[2,256,512]{2,1,0:T(8,128)(2,1)}, bf16[2,256,512]{2,1,0:T(8,128)(2,1)}, bf16[2,256,512]{2,1,0:T(8,128)(2,1)}, bf16[2,256,512]{2,1,0:T(8,128)(2,1)}) custom-call(s32[4,2,32]{2,1,0:T(2,128)} %get-tuple-element.58.places, s32[4,2]{1,0:T(4,128)} %get-tuple-element.57.counts, bf16[2,32,16,512]{3,2,1,0:T(8,128)(2,1)} %copy-done.4, ...), custom_call_target="tpu_custom_call" | custom-call | bytes 8388608 | tf_op jit(solution)/shard_map/collect/pallas_call | solution.py:281
  160.7 21.6 %collective-permute-done.10 = bf16[2,256,512]{2,1,0:T(8,128)(2,1)} collective-permute-done((bf16[2,256,512]{2,1,0:T(8,128)(2,1)}, bf16[2,256,512]{2,1,0:T(8,128)(2,1)}, u32[]{:S(2)}, u32[]{:S(2)}) %collective-permute-start.10) | collective-permute-done | bytes 524320 | tf_op jit(solution)/shard_map/ppermute | solution.py:498
  182.3 5.4 %collective-permute-start.5 = (bf16[2,256,512]{2,1,0:T(8,128)(2,1)}, bf16[2,256,512]{2,1,0:T(8,128)(2,1)S(1)}, u32[]{:S(2)}, u32[]{:S(2)}) collective-permute-start(bf16[2,256,512]{2,1,0:T(8,128)(2,1)} %get-tuple-element.31), channel_id=1, source_target_pairs={{0,24},{2,26},{4,28},{6,30},{8,0},{10,2},{12,4},{14,6},{16,8},{18,... | collective-permute-start | bytes 1572872 | tf_op jit(solution)/shard_map/ppermute | solution.py:498
  189.2 20.3 %collective-permute-done.11 = bf16[2,256,512]{2,1,0:T(8,128)(2,1)S(1)} collective-permute-done((bf16[2,256,512]{2,1,0:T(8,128)(2,1)}, bf16[2,256,512]{2,1,0:T(8,128)(2,1)S(1)}, u32[]{:S(2)}, u32[]{:S(2)}) %collective-permute-start.11) | collective-permute-done | bytes 524320 | tf_op jit(solution)/shard_map/ppermute | solution.py:498
  210.0 19.2 %collective-permute-start.25 = (bf16[2,256,512]{2,1,0:T(8,128)(2,1)S(1)}, bf16[2,256,512]{2,1,0:T(8,128)(2,1)S(1)}, u32[]{:S(2)}, u32[]{:S(2)}) collective-permute-start(bf16[2,256,512]{2,1,0:T(8,128)(2,1)S(1)} %fusion.11), channel_id=1, source_target_pairs={{0,8},{2,10},{4,12},{6,14},{8,16},{10,18},{12,20},{14,22},{16,24},... | collective-permute-start | bytes 1572872 | tf_op jit(solution)/shard_map/ppermute | solution.py:498
  230.4 17.4 %collective-permute-done.4 = bf16[2,256,512]{2,1,0:T(8,128)(2,1)S(1)} collective-permute-done((bf16[2,256,512]{2,1,0:T(8,128)(2,1)}, bf16[2,256,512]{2,1,0:T(8,128)(2,1)S(1)}, u32[]{:S(2)}, u32[]{:S(2)}) %collective-permute-start.4) | collective-permute-done | bytes 524320 | tf_op jit(solution)/shard_map/ppermute | solution.py:498
  249.4 22.0 %collective-permute-start.46 = (bf16[2,256,512]{2,1,0:T(8,128)(2,1)S(1)}, bf16[2,256,512]{2,1,0:T(8,128)(2,1)S(1)}, u32[]{:S(2)}, u32[]{:S(2)}) collective-permute-start(bf16[2,256,512]{2,1,0:T(8,128)(2,1)S(1)} %get-tuple-element.50.refs_0_), channel_id=1, source_target_pairs={{0,8},{2,10},{4,12},{6,14},{8,16},{10,18},{12,20},{14,22},{16,24},... | collective-permute-start | bytes 1572872 | tf_op jit(solution)/shard_map/ppermute | solution.py:498
  274.4 9.3 %collective-permute-done.46.refs_4_ = bf16[2,256,512]{2,1,0:T(8,128)(2,1)S(1)} collective-permute-done((bf16[2,256,512]{2,1,0:T(8,128)(2,1)S(1)}, bf16[2,256,512]{2,1,0:T(8,128)(2,1)S(1)}, u32[]{:S(2)}, u32[]{:S(2)}) %collective-permute-start.46) | collective-permute-done | bytes 524320 | tf_op jit(solution)/shard_map/ppermute | solution.py:498
  283.7 2.5 collective-permute-done.43.refs_1_
  287.7 9.7 %collective-permute-done.40.refs_1_ = bf16[2,256,512]{2,1,0:T(8,128)(2,1)S(1)} collective-permute-done((bf16[2,256,512]{2,1,0:T(8,128)(2,1)S(1)}, bf16[2,256,512]{2,1,0:T(8,128)(2,1)S(1)}, u32[]{:S(2)}, u32[]{:S(2)}) %collective-permute-start.40) | collective-permute-done | bytes 524320 | tf_op jit(solution)/shard_map/ppermute | solution.py:498
  298.0 8.2 %collective-permute-done.50.refs_8_ = bf16[2,256,512]{2,1,0:T(8,128)(2,1)} collective-permute-done((bf16[2,256,512]{2,1,0:T(8,128)(2,1)S(1)}, bf16[2,256,512]{2,1,0:T(8,128)(2,1)}, u32[]{:S(2)}, u32[]{:S(2)}) %collective-permute-start.50) | collective-permute-done | bytes 524320 | tf_op jit(solution)/shard_map/ppermute | solution.py:498
  308.0 2.3 collective-permute-start.54
  310.2 7.3 %collective-permute-done.27.refs_0_ = bf16[2,256,512]{2,1,0:T(8,128)(2,1)} collective-permute-done((bf16[2,256,512]{2,1,0:T(8,128)(2,1)}, bf16[2,256,512]{2,1,0:T(8,128)(2,1)}, u32[]{:S(2)}, u32[]{:S(2)}) %collective-permute-start.27) | collective-permute-done | bytes 524320 | tf_op jit(solution)/shard_map/ppermute | solution.py:498
  319.0 2.5 collective-permute-start.28
  323.1 5.7 %collective-permute-done.54.refs_12_ = bf16[2,256,512]{2,1,0:T(8,128)(2,1)S(1)} collective-permute-done((bf16[2,256,512]{2,1,0:T(8,128)(2,1)}, bf16[2,256,512]{2,1,0:T(8,128)(2,1)S(1)}, u32[]{:S(2)}, u32[]{:S(2)}) %collective-permute-start.54) | collective-permute-done | bytes 524320 | tf_op jit(solution)/shard_map/ppermute | solution.py:498
  328.8 4.1 %collective-permute-done.30.refs_1_ = bf16[2,256,512]{2,1,0:T(8,128)(2,1)S(1)} collective-permute-done((bf16[2,256,512]{2,1,0:T(8,128)(2,1)}, bf16[2,256,512]{2,1,0:T(8,128)(2,1)S(1)}, u32[]{:S(2)}, u32[]{:S(2)}) %collective-permute-start.30) | collective-permute-done | bytes 524320 | tf_op jit(solution)/shard_map/ppermute | solution.py:498
  332.8 5.3 %collective-permute-done.28.refs_0_ = bf16[2,256,512]{2,1,0:T(8,128)(2,1)S(1)} collective-permute-done((bf16[2,256,512]{2,1,0:T(8,128)(2,1)}, bf16[2,256,512]{2,1,0:T(8,128)(2,1)S(1)}, u32[]{:S(2)}, u32[]{:S(2)}) %collective-permute-start.28) | collective-permute-done | bytes 524320 | tf_op jit(solution)/shard_map/ppermute | solution.py:498
  344.7 2.6 collective-permute-start.31
  350.6 2.4 collective-permute-start.56
  353.0 2.6 collective-permute-done.29.refs_1_
  356.7 7.0 %expand.4.refs_6_ = bf16[2,4096,1024]{2,1,0:T(8,128)(2,1)} custom-call(s32[4]{0:T(128)} %pad_add_fusion.quads, s32[2]{0:T(128)} %pad_add_fusion.8.where, bf16[2,256,512]{2,1,0:T(8,128)(2,1)} %copy-done.8, bf16[2,256,512]{2,1,0:T(8,128)(2,1)} %copy-done.28, bf16[2,256,512]{2,1,0:T(8,128)(2,1)} %copy-done.29, bf16[2,256,512]{2,1,0:T(8,128)(2,1)} %copy-done.30, ...), custom_call_target="tpu_custom_call" | custom-call | flops 2147483648 | bytes 6291456 | tf_op jit(solution)/shard_map/expand/pallas_call | solution.py:383
  364.5 6.7 %expand.5.refs_6_ = bf16[2,4096,1024]{2,1,0:T(8,128)(2,1)} custom-call(s32[4]{0:T(128)} %pad_add_fusion.quads, s32[2]{0:T(128)} %get-tuple-element.62.where, bf16[2,256,512]{2,1,0:T(8,128)(2,1)} %collective-permute-done.26.refs_0_, bf16[2,256,512]{2,1,0:T(8,128)(2,1)} %collective-permute-done.37.refs_1_, ...), custom_call_target="tpu_custom_call", output_to_operand_aliasing={{}: (8, {})} | custom-call | flops 2147483648 | bytes 6291456 | tf_op jit(solution)/shard_map/expand/pallas_call | solution.py:383
  371.8 6.7 %expand.6.refs_8_ = bf16[2,4096,1024]{2,1,0:T(8,128)(2,1)} custom-call(s32[4]{0:T(128)} %pad_add_fusion.quads, s32[2]{0:T(128)} %get-tuple-element.61.where, bf16[2,256,512]{2,1,0:T(8,128)(2,1)} %collective-permute-done.27.refs_0_, bf16[2,256,512]{2,1,0:T(8,128)(2,1)} %copy-done.10, ...), custom_call_target="tpu_custom_call", output_to_operand_aliasing={{}: (8, {})} | custom-call | flops 2147483648 | bytes 6291456 | tf_op jit(solution)/shard_map/expand/pallas_call | solution.py:383
  378.6 7.0 %expand.7 = bf16[2,4096,1024]{2,1,0:T(8,128)(2,1)} custom-call(s32[4]{0:T(128)} %pad_add_fusion.quads, s32[2]{0:T(128)} %get-tuple-element.59.where, bf16[2,256,512]{2,1,0:T(8,128)(2,1)} %copy-done.9, bf16[1,256,512]{2,1,0:T(8,128)(2,1)} %copy-done.31, bf16[1,256,512]{2,1,0:T(8,128)(2,1)} %collective-permute-done.31.refs_2_, ...), custom_call_target="tpu_custom_call", output_to_operand_aliasing={{}: (10, {})} | custom-call | flops 2147483648 | bytes 6291456 | tf_op jit(solution)/shard_map/expand/pallas_call | solution.py:383
  386.8 8.2 %settle.1 = (f32[2,1,32,16,512]{4,3,2,1,0:T(8,128)}, f32[2,1,32,16,512]{4,3,2,1,0:T(8,128)}) custom-call(s32[2,32]{1,0:T(2,128)} %get-tuple-element.56.piece_of, s32[2,32]{1,0:T(2,128)} %get-tuple-element.55.row_of, s32[2,32]{1,0:T(2,128)} %fusion.29.held, bf16[2,256,512]{2,1,0:T(8,128)(2,1)} %copy-done.7, bf16[2,256,512]{2,1,0:T(8,128)(2,1)} %copy-done.21, ...), custom_call_target="tpu_custom_call" | custom-call | flops 4194304 | bytes 9437184 | tf_op jit(solution)/shard_map/settle/pallas_call | solution.py:452
  (194 shorter events, 52.5 us)
Async XLA Ops:
  3.1 16.1 %collective-permute-start.12 = (f32[1,256,512]{2,1,0:T(8,128)}, f32[1,256,512]{2,1,0:T(8,128)}, u32[]{:S(2)}, u32[]{:S(2)}) collective-permute-start(f32[1,256,512]{2,1,0:T(8,128)} %constant_dynamic-slice_fusion), channel_id=1, source_target_pairs={{0,1},{1,0},{2,3},{3,2},{4,5},{5,4},{6,7},{7,6},{8,9},{9,8},{10,11... | collective-permute-start | bytes 1572872 | tf_op jit(solution)/shard_map/ppermute | solution.py:522
  6.2 23.2 %collective-permute-start.13 = (f32[1,256,512]{2,1,0:T(8,128)S(1)}, f32[1,256,512]{2,1,0:T(8,128)S(1)}, u32[]{:S(2)}, u32[]{:S(2)}) collective-permute-start(f32[1,256,512]{2,1,0:T(8,128)S(1)} %slice.92), channel_id=1, source_target_pairs={{0,1},{1,0},{2,3},{3,2},{4,5},{5,4},{6,7},{7,6},{8,9},{9,8},{10,11... | collective-permute-start | bytes 1572872 | tf_op jit(solution)/shard_map/ppermute | solution.py:522
  66.1 26.2 %collective-permute-start.6 = (bf16[2,32,16,512]{3,2,1,0:T(8,128)(2,1)S(1)}, bf16[2,32,16,512]{3,2,1,0:T(8,128)(2,1)}, u32[]{:S(2)}, u32[]{:S(2)}) collective-permute-start(bf16[2,32,16,512]{3,2,1,0:T(8,128)(2,1)S(1)} %fusion.6.refs_0_), channel_id=1, source_target_pairs={{0,4},{2,6},{4,0},{6,2},{8,12},{10,14},{12,8},{14,10},{16,20},{18,... | collective-permute-start | bytes 3145736 | tf_op jit(solution)/shard_map/ppermute | solution.py:498
  67.8 59.9 %collective-permute-start.7 = (bf16[2,32,16,512]{3,2,1,0:T(8,128)(2,1)S(1)}, bf16[2,32,16,512]{3,2,1,0:T(8,128)(2,1)}, u32[]{:S(2)}, u32[]{:S(2)}) collective-permute-start(bf16[2,32,16,512]{3,2,1,0:T(8,128)(2,1)S(1)} %fusion.6.refs_0_), channel_id=1, source_target_pairs={{0,2},{2,0},{4,6},{6,4},{8,10},{10,8},{12,14},{14,12},{16,18},{18,... | collective-permute-start | bytes 3145736 | tf_op jit(solution)/shard_map/ppermute | solution.py:498
  68.1 46.6 %collective-permute-start = (bf16[2,32,16,512]{3,2,1,0:T(8,128)(2,1)S(1)}, bf16[2,32,16,512]{3,2,1,0:T(8,128)(2,1)}, u32[]{:S(2)}, u32[]{:S(2)}) collective-permute-start(bf16[2,32,16,512]{3,2,1,0:T(8,128)(2,1)S(1)} %fusion.5.refs_0_), channel_id=1, source_target_pairs={{0,4},{2,6},{4,0},{6,2},{8,12},{10,14},{12,8},{14,10},{16,20},{18,... | collective-permute-start | bytes 3145736 | tf_op jit(solution)/shard_map/ppermute | solution.py:498
  77.4 21.4 %collective-permute-start.21 = (bf16[2,2,256,512]{3,2,1,0:T(8,128)(2,1)}, bf16[2,2,256,512]{3,2,1,0:T(8,128)(2,1)}, u32[]{:S(2)}, u32[]{:S(2)}) collective-permute-start(bf16[2,2,256,512]{3,2,1,0:T(8,128)(2,1)} %get-tuple-element.47), channel_id=1, source_target_pairs={{0,2},{2,0},{4,6},{6,4},{8,10},{10,8},{12,14},{14,12},{16,18},{18,... | collective-permute-start | bytes 3145736 | tf_op jit(solution)/shard_map/ppermute | solution.py:498
  84.4 17.1 %collective-permute-start.19 = (bf16[2,2,256,512]{3,2,1,0:T(8,128)(2,1)}, bf16[2,2,256,512]{3,2,1,0:T(8,128)(2,1)S(1)}, u32[]{:S(2)}, u32[]{:S(2)}) collective-permute-start(bf16[2,2,256,512]{3,2,1,0:T(8,128)(2,1)} %get-tuple-element.45), channel_id=1, source_target_pairs={{0,2},{2,0},{4,6},{6,4},{8,10},{10,8},{12,14},{14,12},{16,18},{18,... | collective-permute-start | bytes 3145736 | tf_op jit(solution)/shard_map/ppermute | solution.py:498
  92.3 36.0 %collective-permute-start.8 = (bf16[2,32,16,512]{3,2,1,0:T(8,128)(2,1)}, bf16[2,32,16,512]{3,2,1,0:T(8,128)(2,1)}, u32[]{:S(2)}, u32[]{:S(2)}) collective-permute-start(bf16[2,32,16,512]{3,2,1,0:T(8,128)(2,1)} %collective-permute-done.6.refs_1_), channel_id=1, source_target_pairs={{0,2},{2,0},{4,6},{6,4},{8,10},{10,8},{12,14},{14,12},{16,18},{18,... | collective-permute-start | bytes 3145736 | tf_op jit(solution)/shard_map/ppermute | solution.py:498
  98.8 31.2 %collective-permute-start.17 = (bf16[2,2,256,512]{3,2,1,0:T(8,128)(2,1)}, bf16[2,2,256,512]{3,2,1,0:T(8,128)(2,1)}, u32[]{:S(2)}, u32[]{:S(2)}) collective-permute-start(bf16[2,2,256,512]{3,2,1,0:T(8,128)(2,1)} %get-tuple-element.43), channel_id=1, source_target_pairs={{0,2},{2,0},{4,6},{6,4},{8,10},{10,8},{12,14},{14,12},{16,18},{18,... | collective-permute-start | bytes 3145736 | tf_op jit(solution)/shard_map/ppermute | solution.py:498
  101.5 23.9 %collective-permute-start.22 = (bf16[2,256,512]{2,1,0:T(8,128)(2,1)}, bf16[2,256,512]{2,1,0:T(8,128)(2,1)}, u32[]{:S(2)}, u32[]{:S(2)}) collective-permute-start(bf16[2,256,512]{2,1,0:T(8,128)(2,1)} %fusion.17), channel_id=1, source_target_pairs={{0,4},{2,6},{4,0},{6,2},{8,12},{10,14},{12,8},{14,10},{16,20},{18,... | collective-permute-start | bytes 1572872 | tf_op jit(solution)/shard_map/ppermute | solution.py:498
  114.7 34.3 %collective-permute-start.1 = (bf16[2,32,16,512]{3,2,1,0:T(8,128)(2,1)S(1)}, bf16[2,32,16,512]{3,2,1,0:T(8,128)(2,1)}, u32[]{:S(2)}, u32[]{:S(2)}) collective-permute-start(bf16[2,32,16,512]{3,2,1,0:T(8,128)(2,1)S(1)} %fusion.5.refs_0_), channel_id=1, source_target_pairs={{0,2},{2,0},{4,6},{6,4},{8,10},{10,8},{12,14},{14,12},{16,18},{18,... | collective-permute-start | bytes 3145736 | tf_op jit(solution)/shard_map/ppermute | solution.py:498
  125.4 25.3 %collective-permute-start.2 = (bf16[2,32,16,512]{3,2,1,0:T(8,128)(2,1)}, bf16[2,32,16,512]{3,2,1,0:T(8,128)(2,1)}, u32[]{:S(2)}, u32[]{:S(2)}) collective-permute-start(bf16[2,32,16,512]{3,2,1,0:T(8,128)(2,1)} %collective-permute-done.refs_1_), channel_id=1, source_target_pairs={{0,2},{2,0},{4,6},{6,4},{8,10},{10,8},{12,14},{14,12},{16,18},{18,... | collective-permute-start | bytes 3145736 | tf_op jit(solution)/shard_map/ppermute | solution.py:498
  127.7 31.1 %collective-permute-start.15 = (bf16[2,2,256,512]{3,2,1,0:T(8,128)(2,1)}, bf16[2,2,256,512]{3,2,1,0:T(8,128)(2,1)}, u32[]{:S(2)}, u32[]{:S(2)}) collective-permute-start(bf16[2,2,256,512]{3,2,1,0:T(8,128)(2,1)} %get-tuple-element.41), channel_id=1, source_target_pairs={{0,2},{2,0},{4,6},{6,4},{8,10},{10,8},{12,14},{14,12},{16,18},{18,... | collective-permute-start | bytes 3145736 | tf_op jit(solution)/shard_map/ppermute | solution.py:498
  130.0 15.8 %collective-permute-start.23 = (bf16[2,256,512]{2,1,0:T(8,128)(2,1)}, bf16[2,256,512]{2,1,0:T(8,128)(2,1)}, u32[]{:S(2)}, u32[]{:S(2)}) collective-permute-start(bf16[2,256,512]{2,1,0:T(8,128)(2,1)} %fusion.7), channel_id=1, source_target_pairs={{0,8},{2,10},{4,12},{6,14},{8,16},{10,18},{12,20},{14,22},{16,24},... | collective-permute-start | bytes 1572872 | tf_op jit(solution)/shard_map/ppermute | solution.py:498
  142.5 39.8 %collective-permute-start.10 = (bf16[2,256,512]{2,1,0:T(8,128)(2,1)}, bf16[2,256,512]{2,1,0:T(8,128)(2,1)}, u32[]{:S(2)}, u32[]{:S(2)}) collective-permute-start(bf16[2,256,512]{2,1,0:T(8,128)(2,1)} %get-tuple-element.34), channel_id=1, source_target_pairs={{0,16},{2,18},{4,20},{6,22},{8,24},{10,26},{12,28},{14,30},{16,0},... | collective-permute-start | bytes 1572872 | tf_op jit(solution)/shard_map/ppermute | solution.py:498
  145.8 36.5 %collective-permute-start.18 = (bf16[2,256,512]{2,1,0:T(8,128)(2,1)}, bf16[2,256,512]{2,1,0:T(8,128)(2,1)}, u32[]{:S(2)}, u32[]{:S(2)}) collective-permute-start(bf16[2,256,512]{2,1,0:T(8,128)(2,1)} %fusion.15), channel_id=1, source_target_pairs={{0,4},{2,6},{4,0},{6,2},{8,12},{10,14},{12,8},{14,10},{16,20},{18,... | collective-permute-start | bytes 1572872 | tf_op jit(solution)/shard_map/ppermute | solution.py:498
  149.0 33.3 %collective-permute-start.24 = (bf16[2,256,512]{2,1,0:T(8,128)(2,1)}, bf16[2,256,512]{2,1,0:T(8,128)(2,1)S(1)}, u32[]{:S(2)}, u32[]{:S(2)}) collective-permute-start(bf16[2,256,512]{2,1,0:T(8,128)(2,1)} %fusion.9), channel_id=1, source_target_pairs={{0,8},{2,10},{4,12},{6,14},{8,16},{10,18},{12,20},{14,22},{16,24},... | collective-permute-start | bytes 1572872 | tf_op jit(solution)/shard_map/ppermute | solution.py:498
  150.6 58.9 %collective-permute-start.11 = (bf16[2,256,512]{2,1,0:T(8,128)(2,1)}, bf16[2,256,512]{2,1,0:T(8,128)(2,1)S(1)}, u32[]{:S(2)}, u32[]{:S(2)}) collective-permute-start(bf16[2,256,512]{2,1,0:T(8,128)(2,1)} %get-tuple-element.35), channel_id=1, source_target_pairs={{0,24},{2,26},{4,28},{6,30},{8,0},{10,2},{12,4},{14,6},{16,8},{18,... | collective-permute-start | bytes 1572872 | tf_op jit(solution)/shard_map/ppermute | solution.py:498
  158.9 51.1 %collective-permute-start.9 = (bf16[2,256,512]{2,1,0:T(8,128)(2,1)}, bf16[2,256,512]{2,1,0:T(8,128)(2,1)S(1)}, u32[]{:S(2)}, u32[]{:S(2)}) collective-permute-start(bf16[2,256,512]{2,1,0:T(8,128)(2,1)} %get-tuple-element.33), channel_id=1, source_target_pairs={{0,8},{2,10},{4,12},{6,14},{8,16},{10,18},{12,20},{14,22},{16,24},... | collective-permute-start | bytes 1572872 | tf_op jit(solution)/shard_map/ppermute | solution.py:498
  182.3 48.1 %collective-permute-start.3 = (bf16[2,256,512]{2,1,0:T(8,128)(2,1)}, bf16[2,256,512]{2,1,0:T(8,128)(2,1)S(1)}, u32[]{:S(2)}, u32[]{:S(2)}) collective-permute-start(bf16[2,256,512]{2,1,0:T(8,128)(2,1)} %get-tuple-element.29), channel_id=1, source_target_pairs={{0,8},{2,10},{4,12},{6,14},{8,16},{10,18},{12,20},{14,22},{16,24},... | collective-permute-start | bytes 1572872 | tf_op jit(solution)/shard_map/ppermute | solution.py:498
  182.3 65.6 %collective-permute-start.4 = (bf16[2,256,512]{2,1,0:T(8,128)(2,1)}, bf16[2,256,512]{2,1,0:T(8,128)(2,1)S(1)}, u32[]{:S(2)}, u32[]{:S(2)}) collective-permute-start(bf16[2,256,512]{2,1,0:T(8,128)(2,1)} %get-tuple-element.30), channel_id=1, source_target_pairs={{0,16},{2,18},{4,20},{6,22},{8,24},{10,26},{12,28},{14,30},{16,0},... | collective-permute-start | bytes 1572872 | tf_op jit(solution)/shard_map/ppermute | solution.py:498
  182.3 65.6 %collective-permute-start.5 = (bf16[2,256,512]{2,1,0:T(8,128)(2,1)}, bf16[2,256,512]{2,1,0:T(8,128)(2,1)S(1)}, u32[]{:S(2)}, u32[]{:S(2)}) collective-permute-start(bf16[2,256,512]{2,1,0:T(8,128)(2,1)} %get-tuple-element.31), channel_id=1, source_target_pairs={{0,24},{2,26},{4,28},{6,30},{8,0},{10,2},{12,4},{14,6},{16,8},{18,... | collective-permute-start | bytes 1572872 | tf_op jit(solution)/shard_map/ppermute | solution.py:498
  209.5 38.5 %collective-permute-start.16 = (bf16[2,256,512]{2,1,0:T(8,128)(2,1)S(1)}, bf16[2,256,512]{2,1,0:T(8,128)(2,1)S(1)}, u32[]{:S(2)}, u32[]{:S(2)}) collective-permute-start(bf16[2,256,512]{2,1,0:T(8,128)(2,1)S(1)} %fusion.14), channel_id=1, source_target_pairs={{0,4},{2,6},{4,0},{6,2},{8,12},{10,14},{12,8},{14,10},{16,20},{18,... | collective-permute-start | bytes 1572872 | tf_op jit(solution)/shard_map/ppermute | solution.py:498
  210.0 38.0 %collective-permute-start.25 = (bf16[2,256,512]{2,1,0:T(8,128)(2,1)S(1)}, bf16[2,256,512]{2,1,0:T(8,128)(2,1)S(1)}, u32[]{:S(2)}, u32[]{:S(2)}) collective-permute-start(bf16[2,256,512]{2,1,0:T(8,128)(2,1)S(1)} %fusion.11), channel_id=1, source_target_pairs={{0,8},{2,10},{4,12},{6,14},{8,16},{10,18},{12,20},{14,22},{16,24},... | collective-permute-start | bytes 1572872 | tf_op jit(solution)/shard_map/ppermute | solution.py:498
  249.4 34.3 %collective-permute-start.46 = (bf16[2,256,512]{2,1,0:T(8,128)(2,1)S(1)}, bf16[2,256,512]{2,1,0:T(8,128)(2,1)S(1)}, u32[]{:S(2)}, u32[]{:S(2)}) collective-permute-start(bf16[2,256,512]{2,1,0:T(8,128)(2,1)S(1)} %get-tuple-element.50.refs_0_), channel_id=1, source_target_pairs={{0,8},{2,10},{4,12},{6,14},{8,16},{10,18},{12,20},{14,22},{16,24},... | collective-permute-start | bytes 1572872 | tf_op jit(solution)/shard_map/ppermute | solution.py:498
  271.4 14.8 %collective-permute-start.43 = (bf16[2,256,512]{2,1,0:T(8,128)(2,1)S(1)}, bf16[2,256,512]{2,1,0:T(8,128)(2,1)S(1)}, u32[]{:S(2)}, u32[]{:S(2)}) collective-permute-start(bf16[2,256,512]{2,1,0:T(8,128)(2,1)S(1)} %get-tuple-element.50.refs_0_), channel_id=1, source_target_pairs={{0,4},{2,6},{4,0},{6,2},{8,12},{10,14},{12,8},{14,10},{16,20},{18,... | collective-permute-start | bytes 1572872 | tf_op jit(solution)/shard_map/ppermute | solution.py:498
  273.6 23.8 %collective-permute-start.40 = (bf16[2,256,512]{2,1,0:T(8,128)(2,1)S(1)}, bf16[2,256,512]{2,1,0:T(8,128)(2,1)S(1)}, u32[]{:S(2)}, u32[]{:S(2)}) collective-permute-start(bf16[2,256,512]{2,1,0:T(8,128)(2,1)S(1)} %fusion.13.refs_0_), channel_id=1, source_target_pairs={{0,4},{2,6},{4,0},{6,2},{8,12},{10,14},{12,8},{14,10},{16,20},{18,... | collective-permute-start | bytes 1572872 | tf_op jit(solution)/shard_map/ppermute | solution.py:498
  274.3 23.1 %collective-permute-start.26 = (bf16[2,256,512]{2,1,0:T(8,128)(2,1)S(1)}, bf16[2,256,512]{2,1,0:T(8,128)(2,1)}, u32[]{:S(2)}, u32[]{:S(2)}) collective-permute-start(bf16[2,256,512]{2,1,0:T(8,128)(2,1)S(1)} %fusion.13.refs_0_), channel_id=1, source_target_pairs={{0,8},{2,10},{4,12},{6,14},{8,16},{10,18},{12,20},{14,22},{16,24},... | collective-permute-start | bytes 1572872 | tf_op jit(solution)/shard_map/ppermute | solution.py:498
  286.2 20.0 %collective-permute-start.50 = (bf16[2,256,512]{2,1,0:T(8,128)(2,1)S(1)}, bf16[2,256,512]{2,1,0:T(8,128)(2,1)}, u32[]{:S(2)}, u32[]{:S(2)}) collective-permute-start(bf16[2,256,512]{2,1,0:T(8,128)(2,1)S(1)} %collective-permute-done.46.refs_4_), channel_id=1, source_target_pairs={{0,8},{2,10},{4,12},{6,14},{8,16},{10,18},{12,20},{14,22},{16,24},... | collective-permute-start | bytes 1572872 | tf_op jit(solution)/shard_map/ppermute | solution.py:498
  286.3 20.3 %collective-permute-start.47 = (bf16[2,256,512]{2,1,0:T(8,128)(2,1)S(1)}, bf16[2,256,512]{2,1,0:T(8,128)(2,1)}, u32[]{:S(2)}, u32[]{:S(2)}) collective-permute-start(bf16[2,256,512]{2,1,0:T(8,128)(2,1)S(1)} %collective-permute-done.46.refs_4_), channel_id=1, source_target_pairs={{0,4},{2,6},{4,0},{6,2},{8,12},{10,14},{12,8},{14,10},{16,20},{18,... | collective-permute-start | bytes 1572872 | tf_op jit(solution)/shard_map/ppermute | solution.py:498
  297.5 20.1 %collective-permute-start.27 = (bf16[2,256,512]{2,1,0:T(8,128)(2,1)}, bf16[2,256,512]{2,1,0:T(8,128)(2,1)}, u32[]{:S(2)}, u32[]{:S(2)}) collective-permute-start(bf16[2,256,512]{2,1,0:T(8,128)(2,1)} %collective-permute-done.26.refs_0_), channel_id=1, source_target_pairs={{0,8},{2,10},{4,12},{6,14},{8,16},{10,18},{12,20},{14,22},{16,24},... | collective-permute-start | bytes 1572872 | tf_op jit(solution)/shard_map/ppermute | solution.py:498
  297.6 21.4 %collective-permute-start.48 = (bf16[2,256,512]{2,1,0:T(8,128)(2,1)S(1)}, bf16[2,256,512]{2,1,0:T(8,128)(2,1)S(1)}, u32[]{:S(2)}, u32[]{:S(2)}) collective-permute-start(bf16[2,256,512]{2,1,0:T(8,128)(2,1)S(1)} %collective-permute-done.46.refs_4_), channel_id=1, source_target_pairs={{0,2},{2,0},{4,6},{6,4},{8,10},{10,8},{12,14},{14,12},{16,18},{18,... | collective-permute-start | bytes 1572872 | tf_op jit(solution)/shard_map/ppermute | solution.py:498
  306.2 15.3 %collective-permute-start.42 = (bf16[2,256,512]{2,1,0:T(8,128)(2,1)S(1)}, bf16[2,256,512]{2,1,0:T(8,128)(2,1)S(1)}, u32[]{:S(2)}, u32[]{:S(2)}) collective-permute-start(bf16[2,256,512]{2,1,0:T(8,128)(2,1)S(1)} %collective-permute-done.40.refs_1_), channel_id=1, source_target_pairs={{0,2},{2,0},{4,6},{6,4},{8,10},{10,8},{12,14},{14,12},{16,18},{18,... | collective-permute-start | bytes 1572872 | tf_op jit(solution)/shard_map/ppermute | solution.py:498
  306.6 15.1 %collective-permute-start.37 = (bf16[2,256,512]{2,1,0:T(8,128)(2,1)}, bf16[2,256,512]{2,1,0:T(8,128)(2,1)}, u32[]{:S(2)}, u32[]{:S(2)}) collective-permute-start(bf16[2,256,512]{2,1,0:T(8,128)(2,1)} %collective-permute-done.26.refs_0_), channel_id=1, source_target_pairs={{0,4},{2,6},{4,0},{6,2},{8,12},{10,14},{12,8},{14,10},{16,20},{18,... | collective-permute-start | bytes 1572872 | tf_op jit(solution)/shard_map/ppermute | solution.py:498
  308.0 20.8 %collective-permute-start.54 = (bf16[2,256,512]{2,1,0:T(8,128)(2,1)}, bf16[2,256,512]{2,1,0:T(8,128)(2,1)S(1)}, u32[]{:S(2)}, u32[]{:S(2)}) collective-permute-start(bf16[2,256,512]{2,1,0:T(8,128)(2,1)} %collective-permute-done.50.refs_8_), channel_id=1, source_target_pairs={{0,8},{2,10},{4,12},{6,14},{8,16},{10,18},{12,20},{14,22},{16,24},... | collective-permute-start | bytes 1572872 | tf_op jit(solution)/shard_map/ppermute | solution.py:498
  317.5 15.3 %collective-permute-start.30 = (bf16[2,256,512]{2,1,0:T(8,128)(2,1)}, bf16[2,256,512]{2,1,0:T(8,128)(2,1)S(1)}, u32[]{:S(2)}, u32[]{:S(2)}) collective-permute-start(bf16[2,256,512]{2,1,0:T(8,128)(2,1)} %collective-permute-done.27.refs_0_), channel_id=1, source_target_pairs={{0,4},{2,6},{4,0},{6,2},{8,12},{10,14},{12,8},{14,10},{16,20},{18,... | collective-permute-start | bytes 1572872 | tf_op jit(solution)/shard_map/ppermute | solution.py:498
  319.0 19.1 %collective-permute-start.28 = (bf16[2,256,512]{2,1,0:T(8,128)(2,1)}, bf16[2,256,512]{2,1,0:T(8,128)(2,1)S(1)}, u32[]{:S(2)}, u32[]{:S(2)}) collective-permute-start(bf16[2,256,512]{2,1,0:T(8,128)(2,1)} %collective-permute-done.27.refs_0_), channel_id=1, source_target_pairs={{0,8},{2,10},{4,12},{6,14},{8,16},{10,18},{12,20},{14,22},{16,24},... | collective-permute-start | bytes 1572872 | tf_op jit(solution)/shard_map/ppermute | solution.py:498
  321.5 19.6 %collective-permute-start.38 = (bf16[2,256,512]{2,1,0:T(8,128)(2,1)}, bf16[2,256,512]{2,1,0:T(8,128)(2,1)}, u32[]{:S(2)}, u32[]{:S(2)}) collective-permute-start(bf16[2,256,512]{2,1,0:T(8,128)(2,1)} %collective-permute-done.26.refs_0_), channel_id=1, source_target_pairs={{0,2},{2,0},{4,6},{6,4},{8,10},{10,8},{12,14},{14,12},{16,18},{18,... | collective-permute-start | bytes 1572872 | tf_op jit(solution)/shard_map/ppermute | solution.py:498
  321.7 21.5 %collective-permute-start.51 = (bf16[2,256,512]{2,1,0:T(8,128)(2,1)}, bf16[2,256,512]{2,1,0:T(8,128)(2,1)S(1)}, u32[]{:S(2)}, u32[]{:S(2)}) collective-permute-start(bf16[2,256,512]{2,1,0:T(8,128)(2,1)} %collective-permute-done.50.refs_8_), channel_id=1, source_target_pairs={{0,4},{2,6},{4,0},{6,2},{8,12},{10,14},{12,8},{14,10},{16,20},{18,... | collective-permute-start | bytes 1572872 | tf_op jit(solution)/shard_map/ppermute | solution.py:498
  328.8 15.9 %collective-permute-start.49 = (bf16[2,256,512]{2,1,0:T(8,128)(2,1)}, bf16[2,256,512]{2,1,0:T(8,128)(2,1)}, u32[]{:S(2)}, u32[]{:S(2)}) collective-permute-start(bf16[2,256,512]{2,1,0:T(8,128)(2,1)} %collective-permute-done.47.refs_5_), channel_id=1, source_target_pairs={{0,2},{2,0},{4,6},{6,4},{8,10},{10,8},{12,14},{14,12},{16,18},{18,... | collective-permute-start | bytes 1572872 | tf_op jit(solution)/shard_map/ppermute | solution.py:498
  332.8 14.4 %collective-permute-start.39 = (bf16[2,256,512]{2,1,0:T(8,128)(2,1)}, bf16[2,256,512]{2,1,0:T(8,128)(2,1)}, u32[]{:S(2)}, u32[]{:S(2)}) collective-permute-start(bf16[2,256,512]{2,1,0:T(8,128)(2,1)} %collective-permute-done.37.refs_1_), channel_id=1, source_target_pairs={{0,2},{2,0},{4,6},{6,4},{8,10},{10,8},{12,14},{14,12},{16,18},{18,... | collective-permute-start | bytes 1572872 | tf_op jit(solution)/shard_map/ppermute | solution.py:498
  347.3 16.6 %collective-permute-start.36 = (bf16[2,256,512]{2,1,0:T(8,128)(2,1)S(1)}, bf16[2,256,512]{2,1,0:T(8,128)(2,1)S(1)}, u32[]{:S(2)}, u32[]{:S(2)}) collective-permute-start(bf16[2,256,512]{2,1,0:T(8,128)(2,1)S(1)} %collective-permute-done.30.refs_1_), channel_id=1, source_target_pairs={{0,2},{2,0},{4,6},{6,4},{8,10},{10,8},{12,14},{14,12},{16,18},{18,... | collective-permute-start | bytes 1572872 | tf_op jit(solution)/shard_map/ppermute | solution.py:498
  347.8 23.9 %collective-permute-start.32 = (bf16[2,256,512]{2,1,0:T(8,128)(2,1)S(1)}, bf16[2,256,512]{2,1,0:T(8,128)(2,1)}, u32[]{:S(2)}, u32[]{:S(2)}) collective-permute-start(bf16[2,256,512]{2,1,0:T(8,128)(2,1)S(1)} %collective-permute-done.28.refs_0_), channel_id=1, source_target_pairs={{0,2},{2,0},{4,6},{6,4},{8,10},{10,8},{12,14},{14,12},{16,18},{18,... | collective-permute-start | bytes 1572872 | tf_op jit(solution)/shard_map/ppermute | solution.py:498
  356.2 15.0 %collective-permute-start.34 = (bf16[1,256,512]{2,1,0:T(8,128)(2,1)}, bf16[1,256,512]{2,1,0:T(8,128)(2,1)}, u32[]{:S(2)}, u32[]{:S(2)}) collective-permute-start(bf16[1,256,512]{2,1,0:T(8,128)(2,1)} %collective-permute-done.31.refs_2_), channel_id=1, source_target_pairs={{0,2},{2,0},{4,6},{6,4},{8,10},{10,8},{12,14},{14,12},{16,18},{18,... | collective-permute-start | bytes 786440 | tf_op jit(solution)/shard_map/ppermute | solution.py:498
  363.7 21.8 %collective-permute-start.52 = (bf16[2,256,512]{2,1,0:T(8,128)(2,1)}, bf16[2,256,512]{2,1,0:T(8,128)(2,1)S(1)}, u32[]{:S(2)}, u32[]{:S(2)}) collective-permute-start(bf16[2,256,512]{2,1,0:T(8,128)(2,1)} %collective-permute-done.50.refs_8_), channel_id=1, source_target_pairs={{0,2},{2,0},{4,6},{6,4},{8,10},{10,8},{12,14},{14,12},{16,18},{18,... | collective-permute-start | bytes 1572872 | tf_op jit(solution)/shard_map/ppermute | solution.py:498
  363.9 21.8 %collective-permute-start.53 = (bf16[2,256,512]{2,1,0:T(8,128)(2,1)S(1)}, bf16[2,256,512]{2,1,0:T(8,128)(2,1)S(1)}, u32[]{:S(2)}, u32[]{:S(2)}) collective-permute-start(bf16[2,256,512]{2,1,0:T(8,128)(2,1)S(1)} %collective-permute-done.51.refs_9_), channel_id=1, source_target_pairs={{0,2},{2,0},{4,6},{6,4},{8,10},{10,8},{12,14},{14,12},{16,18},{18,... | collective-permute-start | bytes 1572872 | tf_op jit(solution)/shard_map/ppermute | solution.py:498
  364.4 21.2 %collective-permute-start.57 = (bf16[2,256,512]{2,1,0:T(8,128)(2,1)S(1)}, bf16[2,256,512]{2,1,0:T(8,128)(2,1)}, u32[]{:S(2)}, u32[]{:S(2)}) collective-permute-start(bf16[2,256,512]{2,1,0:T(8,128)(2,1)S(1)} %collective-permute-done.54.refs_12_), channel_id=1, source_target_pairs={{0,2},{2,0},{4,6},{6,4},{8,10},{10,8},{12,14},{14,12},{16,18},{18,... | collective-permute-start | bytes 1572872 | tf_op jit(solution)/shard_map/ppermute | solution.py:498
  371.2 14.3 %collective-permute-start.58 = (bf16[1,256,512]{2,1,0:T(8,128)(2,1)}, bf16[1,256,512]{2,1,0:T(8,128)(2,1)S(1)}, u32[]{:S(2)}, u32[]{:S(2)}) collective-permute-start(bf16[1,256,512]{2,1,0:T(8,128)(2,1)} %collective-permute-done.55.refs_13_), channel_id=1, source_target_pairs={{0,2},{2,0},{4,6},{6,4},{8,10},{10,8},{12,14},{14,12},{16,18},{18,... | collective-permute-start | bytes 786440 | tf_op jit(solution)/shard_map/ppermute | solution.py:498
  (48 other events, 957.3 us)
